TPU v7x, 32 devices: a whole 2x2x4 slice. The times are simulated.
32 devices in a mesh: frames: 8 (over z, core), heads: 4 (over y, x).
Axes of the slice: x: 2, y: 2, z: 4, core: 2. Of those that a mesh axis runs over, the one named last changes fastest.
Arguments:
- clip: bfloat16 [16, 8, 128, 320], P('frames', 'heads'), may hold values from -6 to 6
- w_time: bfloat16 [3, 320, 320], replicated, may hold values from -0.1875 to 0.1875
- w_down: bfloat16 [320, 1280], replicated, may hold values from -0.3125 to 0.3125
- w_embed: bfloat16 [320, 1280], replicated, may hold values from -0.3125 to 0.3125
- w_qkv: bfloat16 [1280, 3840], P(None, 'heads'), may hold values from -0.15625 to 0.15625
- w_out: bfloat16 [1280, 1280], P('heads'), may hold values from -0.15625 to 0.15625
- w_up: bfloat16 [1280, 320], replicated, may hold values from -0.15625 to 0.15625
- timestep: int32 [1], replicated, may hold values from 0 to 999
- cotangent: bfloat16 [16, 8, 128, 320], P('frames', 'heads'), may hold values from -6 to 6
Outputs:
- output: bfloat16 [16, 8, 128, 320], P('frames', 'heads')
- grad_clip: float32 [16, 8, 128, 320], P('frames', 'heads')
- grad_time: float32 [3, 320, 320], replicated
- grad_down: float32 [320, 1280], replicated
- grad_embed: float32 [320, 1280], replicated
- grad_qkv: float32 [1280, 3840], P(None, 'heads')
- grad_out: float32 [1280, 1280], P('heads')
- grad_up: float32 [1280, 320], replicated
All inputs are finite; a program needn't handle non-finite values.
Results may differ from a plain program's by a relative error of at most 0.024.
Values may be sent and summed in bfloat16 or wider, within the bound.
No kernel may reach another device: no remote copies, remote signals or barrier semaphores. Data moves between devices by JAX's collectives and lax.ppermute only.
A program may use at most 128 MiB of HBM per device.

v0:
```python
import math

import jax
import jax.numpy as jnp
from jax import lax
from jax.sharding import PartitionSpec as P

HD = 80


def extended(cells, sides, width):
    for axis, dim in sides:
        count = lax.axis_size(axis)
        ends = count - 1
        head = lax.slice_in_dim(cells, 0, width, axis=dim)
        tail = lax.slice_in_dim(cells, cells.shape[dim] - width, cells.shape[dim], axis=dim)
        cells = jnp.concatenate(
            [
                lax.ppermute(tail, axis, [(i, (i + 1) % count) for i in range(ends)]),
                cells,
                lax.ppermute(head, axis, [((i + 1) % count, i) for i in range(ends)]),
            ],
            axis=dim,
        )
    return cells


def matmul(left, right):
    return jnp.dot(left, right, preferred_element_type=jnp.float32)


def inner_rows(left, right):
    return lax.dot_general(
        left, right, (((0,), (0,)), ((), ())), preferred_element_type=jnp.float32
    )


def inner_cols(left, right):
    return lax.dot_general(
        left, right, (((1,), (1,)), ((), ())), preferred_element_type=jnp.float32
    )


def upsample(field):
    return jnp.repeat(jnp.repeat(jnp.repeat(field, 2, 0), 2, 1), 2, 2)


def time_embed(timestep, width):
    half = width // 2
    freqs = jnp.exp(-math.log(10000.0) * jnp.arange(half, dtype=jnp.float32) / half)
    angle = timestep.astype(jnp.float32)[0] * freqs
    return jax.nn.silu(jnp.concatenate([jnp.cos(angle), jnp.sin(angle)])).astype(jnp.bfloat16)


def to_coarse(field):
    local = lax.all_to_all(field, "frames", split_axis=2, concat_axis=0, tiled=True)
    whole = lax.all_gather(local, "heads", axis=1, tiled=True)
    return (local, whole)


def coarse_sum(partial_value):
    return lax.psum_scatter(
        partial_value.astype(jnp.bfloat16), "heads", scatter_dimension=1, tiled=True
    ).astype(jnp.float32)


def to_fine(field):
    return lax.all_to_all(field, "frames", split_axis=0, concat_axis=2, tiled=True)


def shards(clip, w_time, w_down, w_embed, w_qkv, w_out, w_up, timestep, cotangent):
    frames, rows, columns, chans = clip.shape
    width = w_down.shape[1]
    half_f, half_r, half_c = (frames // 2, rows // 2, columns // 2)
    scale = 1.0 / math.sqrt(HD)
    padded = extended(clip, (("frames", 0),), 1)
    branch = jnp.zeros((frames * rows * columns, chans), jnp.float32)
    for tap in range(3):
        branch = branch + matmul(padded[tap : tap + frames].reshape(-1, chans), w_time[tap])
    hidden = (clip.astype(jnp.float32).reshape(-1, chans) + branch).astype(jnp.bfloat16)
    hidden_f = hidden.astype(jnp.float32).reshape(frames, rows, columns, chans)
    pooled = hidden_f.reshape(half_f, 2, half_r, 2, half_c, 2, chans).mean(axis=(1, 3, 5))
    pooled = pooled.astype(jnp.bfloat16).reshape(-1, chans)
    embed = time_embed(timestep, w_embed.shape[0])
    shift = matmul(embed[None, :], w_embed)
    coarse_in = (matmul(pooled, w_down) + shift).astype(jnp.bfloat16)
    coarse_in = coarse_in.reshape(half_f, 1, half_r * half_c, width)
    local_in, full_in = to_coarse(coarse_in)
    coarse_frames, groups, per_group = (full_in.shape[0], full_in.shape[1], full_in.shape[2])
    places = groups * per_group
    token_mat = full_in.reshape(-1, width)
    heads_here = w_qkv.shape[1] // (3 * HD)
    qkv = (
        matmul(token_mat, w_qkv)
        .astype(jnp.bfloat16)
        .reshape(coarse_frames, places, heads_here, 3, HD)
    )
    query = qkv[:, :, :, 0]
    keys = qkv[:, :, :, 1]
    values = qkv[:, :, :, 2]
    scores = jnp.einsum("tpnd,spnd->ntsp", query, keys, preferred_element_type=jnp.float32) * scale
    probs = jax.nn.softmax(scores, axis=2)
    weights = probs.astype(jnp.bfloat16)
    attended = jnp.einsum("ntsp,spnd->tpnd", weights, values, preferred_element_type=jnp.float32)
    attended = attended.astype(jnp.bfloat16).reshape(-1, heads_here * HD)
    mixed = coarse_sum(matmul(attended, w_out).reshape(coarse_frames, groups, per_group, width))
    coarse_out = (local_in.astype(jnp.float32) + mixed).astype(jnp.bfloat16)
    fine_back = to_fine(coarse_out).reshape(-1, width)
    lifted = matmul(fine_back, w_up).reshape(half_f, half_r, half_c, chans)
    output = (hidden_f + upsample(lifted)).astype(jnp.bfloat16)
    upstream = cotangent.astype(jnp.float32)
    pooled_grad = upstream.reshape(half_f, 2, half_r, 2, half_c, 2, chans).sum(axis=(1, 3, 5))
    pooled_grad = pooled_grad.astype(jnp.bfloat16).reshape(-1, chans)
    grad_up_part = inner_rows(fine_back, pooled_grad)
    back_in = (
        inner_cols(pooled_grad, w_up)
        .astype(jnp.bfloat16)
        .reshape(half_f, 1, half_r * half_c, width)
    )
    local_grad, full_grad = to_coarse(back_in)
    grad_mat = full_grad.reshape(-1, width)
    grad_out_part = inner_rows(attended, grad_mat)
    attend_grad = inner_cols(grad_mat, w_out).astype(jnp.bfloat16)
    attend_grad = attend_grad.reshape(coarse_frames, places, heads_here, HD)
    weight_grad = jnp.einsum(
        "tpnd,spnd->ntsp", attend_grad, values, preferred_element_type=jnp.float32
    )
    score_grad = probs * (weight_grad - jnp.sum(probs * weight_grad, axis=2, keepdims=True)) * scale
    score_grad = score_grad.astype(jnp.bfloat16)
    query_grad = jnp.einsum("ntsp,spnd->tpnd", score_grad, keys, preferred_element_type=jnp.float32)
    keys_grad = jnp.einsum("ntsp,tpnd->spnd", score_grad, query, preferred_element_type=jnp.float32)
    values_grad = jnp.einsum(
        "ntsp,tpnd->spnd", weights, attend_grad, preferred_element_type=jnp.float32
    )
    qkv_grad = jnp.stack([query_grad, keys_grad, values_grad], axis=3).astype(jnp.bfloat16)
    qkv_grad = qkv_grad.reshape(-1, heads_here * 3 * HD)
    grad_qkv_part = inner_rows(token_mat, qkv_grad)
    input_grad = coarse_sum(
        inner_cols(qkv_grad, w_qkv).reshape(coarse_frames, groups, per_group, width)
    )
    coarse_grad = (input_grad + local_grad.astype(jnp.float32)).astype(jnp.bfloat16)
    fine_grad = to_fine(coarse_grad).reshape(-1, width)
    column_sum = jnp.sum(fine_grad.astype(jnp.float32), axis=0)
    grad_down_part = inner_rows(pooled, fine_grad)
    spread = inner_cols(fine_grad, w_down).reshape(half_f, half_r, half_c, chans)
    hidden_grad = (upstream + upsample(spread) * 0.125).astype(jnp.bfloat16)
    grad_padded = extended(hidden_grad, (("frames", 0),), 1)
    flat_grad = hidden_grad.reshape(-1, chans)
    grad_clip = flat_grad.astype(jnp.float32)
    taps = []
    for tap in range(3):
        grad_clip = grad_clip + inner_cols(
            grad_padded[2 - tap : 2 - tap + frames].reshape(-1, chans), w_time[tap]
        )
        taps.append(inner_rows(padded[tap : tap + frames].reshape(-1, chans), flat_grad))
    grad_clip = grad_clip.reshape(frames, rows, columns, chans)
    coarse_sums = (
        lax.psum(grad_qkv_part.astype(jnp.bfloat16), "frames").astype(jnp.float32),
        lax.psum(grad_out_part.astype(jnp.bfloat16), "frames").astype(jnp.float32),
    )
    fine_sums = lax.psum(
        (jnp.stack(taps), grad_down_part, grad_up_part, column_sum), ("frames", "heads")
    )
    grad_embed = embed.astype(jnp.float32)[:, None] * fine_sums[3][None, :]
    return (
        output,
        grad_clip,
        fine_sums[0],
        fine_sums[1],
        grad_embed,
        coarse_sums[0],
        coarse_sums[1],
        fine_sums[2],
    )


def solution(mesh):
    return jax.shard_map(
        shards,
        mesh=mesh,
        in_specs=(
            P("frames", "heads", None, None),
            P(),
            P(),
            P(),
            P(None, "heads"),
            P("heads", None),
            P(),
            P(),
            P("frames", "heads", None, None),
        ),
        out_specs=(
            P("frames", "heads", None, None),
            P("frames", "heads", None, None),
            P(),
            P(),
            P(),
            P(None, "heads"),
            P("heads", None),
            P(),
        ),
        check_vma=False,
    )
```

profile of v0, /device:TPU:0, one launch (start us, length us, event | category | flops | bytes accessed | tf_op | source)
XLA Modules:
  0.0 432.7 jit_solution(15819610578393598799)
XLA Ops:
  9.1 3.1 collective-permute-start
  20.1 7.6 %all-to-all-start.2 = ((bf16[8,2,5120]{2,1,0:T(2,128)(2,1)}), bf16[8,2,5120]{2,1,0:T(2,128)(2,1)}, u32[]{:S(2)}, u32[]{:S(2)}) async-start(bf16[8,2,5120]{2,1,0:T(2,128)(2,1)} %reshape.238), calls=%async_computation.2 | async-start | bytes 327680 | tf_op jit(solution)/shard_map/all_to_all | solution.py:56
  45.7 2.5 reshape_reshape.3
  53.8 5.1 %all-to-all-start = ((bf16[8,2,5120]{2,1,0:T(2,128)(2,1)}), bf16[8,2,5120]{2,1,0:T(2,128)(2,1)}, u32[]{:S(2)}, u32[]{:S(2)}) async-start(bf16[8,2,5120]{2,1,0:T(2,128)(2,1)} %reshape.236), calls=%async_computation | async-start | bytes 327680 | tf_op jit(solution)/shard_map/all_to_all | solution.py:56
  62.1 11.6 %all_gather.7 = bf16[8,4,8,1280]{3,2,0,1:T(8,128)(2,1)S(1)} all-gather(bf16[8,1,8,1280]{3,2,0,1:T(8,128)(2,1)S(1)} %bitcast.199), channel_id=1, replica_groups=mesh['frames'=8,'heads'=4] {'heads'}, dimensions={1}, use_global_device_ids=true | all-gather | bytes 819200 | tf_op jit(solution)/shard_map/all_gather | solution.py:57
  77.6 11.5 %all_gather.6 = bf16[8,4,8,1280]{3,2,0,1:T(8,128)(2,1)S(1)} all-gather(bf16[8,1,8,1280]{3,2,0,1:T(8,128)(2,1)S(1)} %bitcast.200), channel_id=1, replica_groups=mesh['frames'=8,'heads'=4] {'heads'}, dimensions={1}, use_global_device_ids=true | all-gather | bytes 819200 | tf_op jit(solution)/shard_map/all_gather | solution.py:57
  91.8 3.3 reshape.210
  101.2 2.2 fusion.9
  108.4 2.2 convolution_bitcast_fusion.1
  113.8 2.3 convolution_convert_fusion.3
  118.6 2.7 convolution_convert_fusion.2
  126.0 2.3 convolution_convert_fusion
  128.3 49.5 %all-reduce.13.cloned.1.call-done = (bf16[8,4,8,1280]{3,2,1,0:T(8,128)(2,1)}, bf16[8,4,8,1280]{3,2,1,0:T(8,128)(2,1)}) async-done(((bf16[8,4,8,1280]{3,2,1,0:T(8,128)(2,1)}, bf16[8,4,8,1280]{3,2,1,0:T(8,128)(2,1)}), (bf16[8,4,8,1280]{3,2,1,0:T(8,128)(2,1)}, bf16[8,4,8,1280]{3,2,1,0:T(8,128)(2,1)})) %all-reduce.13.cloned.1.call-update) | async-done | bytes 1310736
  177.8 2.3 fusion.43
  180.1 4.6 %all-to-all-start.3 = ((bf16[8,1,8,1280]{3,2,1,0:T(8,128)(2,1)}), bf16[8,1,8,1280]{3,2,1,0:T(8,128)(2,1)S(1)}, u32[]{:S(2)}, u32[]{:S(2)}) async-start(bf16[8,1,8,1280]{3,2,1,0:T(8,128)(2,1)} %fusion.43), calls=%async_computation.3 | async-start | bytes 327680 | tf_op jit(solution)/shard_map/all_to_all | solution.py:68
  184.7 2.4 fusion.42
  187.1 6.5 %all-to-all-done.3 = bf16[8,1,8,1280]{3,2,1,0:T(8,128)(2,1)S(1)} async-done(((bf16[8,1,8,1280]{3,2,1,0:T(8,128)(2,1)}), bf16[8,1,8,1280]{3,2,1,0:T(8,128)(2,1)S(1)}, u32[]{:S(2)}, u32[]{:S(2)}) %all-to-all-start.3) | async-done | bytes 163872 | tf_op jit(solution)/shard_map/all_to_all | solution.py:68
  193.5 3.4 all-to-all-start.1
  200.6 5.6 %all-to-all-done.1 = bf16[8,1,8,1280]{3,2,1,0:T(8,128)(2,1)S(1)} async-done(((bf16[8,1,8,1280]{3,2,1,0:T(8,128)(2,1)}), bf16[8,1,8,1280]{3,2,1,0:T(8,128)(2,1)S(1)}, u32[]{:S(2)}, u32[]{:S(2)}) %all-to-all-start.1) | async-done | bytes 163872 | tf_op jit(solution)/shard_map/all_to_all | solution.py:68
  214.0 43.6 %psum.44 = f32[1280]{0:T(1024)S(1)} all-reduce(f32[1280]{0:T(1024)S(1)} %convert_reduce_fusion.1), channel_id=1, replica_groups=mesh['frames'=8,'heads'=4] {'frames','heads'}, use_global_device_ids=true, to_apply=%region_11.12 | all-reduce | flops 1280 | bytes 10240 | tf_op jit(solution)/shard_map/psum | solution.py:161
  259.8 7.7 %all-reduce.11.cloned.1.call-done = (bf16[1280,960]{0,1:T(8,128)(2,1)}, bf16[320,1280]{1,0:T(8,128)(2,1)}) async-done(((bf16[1280,960]{0,1:T(8,128)(2,1)}, bf16[320,1280]{1,0:T(8,128)(2,1)}), (bf16[1280,960]{0,1:T(8,128)(2,1)}, bf16[320,1280]{1,0:T(8,128)(2,1)})) %all-reduce.11.cloned.1.call-update) | async-done | bytes 3276816 | tf_op jit(solution)/shard_map/psum | solution.py:158
  267.4 4.4 %convert_element_type.187 = f32[1280,960]{0,1:T(8,128)} convert(bf16[1280,960]{0,1:T(8,128)(2,1)} %get-tuple-element.59) | non-fusion elementwise | flops 1228800 | bytes 7372800 | tf_op jit(solution)/shard_map/convert_element_type | solution.py:158
  276.5 143.7 %all-reduce.9.cloned.1.call-done = (f32[3,320,320]{2,1,0:T(8,128)}, f32[320,1280]{1,0:T(8,128)}, f32[1280,320]{0,1:T(8,128)}) async-done(((f32[3,320,320]{2,1,0:T(8,128)}, f32[320,1280]{1,0:T(8,128)}, f32[1280,320]{0,1:T(8,128)}), (f32[3,320,320]{2,1,0:T(8,128)}, f32[320,1280]{1,0:T(8,128)}, f32[1280,320]{0,1:T(8,128)})) %all-reduce.9.cloned.1.call-update) | async-done | bytes 4505616 | tf_op jit(solution)/shard_map/psum | solution.py:161
  420.3 2.7 copy.287
  (204 shorter events, 84.8 us)
Async XLA Ops:
  7.2 82.8 %copy-start = (bf16[1280,960]{0,1:T(8,128)(2,1)S(1)}, bf16[1280,960]{0,1:T(8,128)(2,1)}, u32[]{:S(2)}) copy-start(bf16[1280,960]{0,1:T(8,128)(2,1)} %param.13) | copy-start | bytes 7372804
  9.1 21.3 %collective-permute-start = (bf16[1,2,128,320]{2,3,1,0:T(8,128)(2,1)}, bf16[1,2,128,320]{2,3,1,0:T(8,128)(2,1)}, u32[]{:S(2)}, u32[]{:S(2)}) collective-permute-start(bf16[1,2,128,320]{2,3,1,0:T(8,128)(2,1)} %get-tuple-element.73), channel_id=1, source_target_pairs={{0,4},{4,8},{8,12},{12,16},{16,20},{20,24},{24,28},{1,5},{5,9},{9,... | collective-permute-start | bytes 491528 | tf_op jit(solution)/shard_map/ppermute | solution.py:19
  12.1 23.8 %collective-permute-start.1 = (bf16[1,2,128,320]{2,3,1,0:T(8,128)(2,1)}, bf16[1,2,128,320]{2,3,1,0:T(8,128)(2,1)}, u32[]{:S(2)}, u32[]{:S(2)}) collective-permute-start(bf16[1,2,128,320]{2,3,1,0:T(8,128)(2,1)} %get-tuple-element.72), channel_id=1, source_target_pairs={{4,0},{8,4},{12,8},{16,12},{20,16},{24,20},{28,24},{5,1},{9,5},{13... | collective-permute-start | bytes 491528 | tf_op jit(solution)/shard_map/ppermute | solution.py:21
  14.6 13.9 %copy-start.6 = (bf16[2,2,128,320]{2,3,1,0:T(8,128)(2,1)S(1)}, bf16[2,2,128,320]{2,3,1,0:T(8,128)(2,1)}, u32[]{:S(2)}) copy-start(bf16[2,2,128,320]{2,3,1,0:T(8,128)(2,1)} %param.9) | copy-start | bytes 983044
  20.1 33.7 %all-to-all-start.2 = ((bf16[8,2,5120]{2,1,0:T(2,128)(2,1)}), bf16[8,2,5120]{2,1,0:T(2,128)(2,1)}, u32[]{:S(2)}, u32[]{:S(2)}) async-start(bf16[8,2,5120]{2,1,0:T(2,128)(2,1)} %reshape.238), calls=%async_computation.2 | async-start | bytes 327680 | tf_op jit(solution)/shard_map/all_to_all | solution.py:56
  34.0 7.4 %copy-start.12 = (bf16[3,320,320]{2,1,0:T(8,128)(2,1)S(1)}, bf16[3,320,320]{2,1,0:T(8,128)(2,1)}, u32[]{:S(2)}) copy-start(bf16[3,320,320]{2,1,0:T(8,128)(2,1)} %param.10) | copy-start | bytes 1843204
  53.8 22.3 %all-to-all-start = ((bf16[8,2,5120]{2,1,0:T(2,128)(2,1)}), bf16[8,2,5120]{2,1,0:T(2,128)(2,1)}, u32[]{:S(2)}, u32[]{:S(2)}) async-start(bf16[8,2,5120]{2,1,0:T(2,128)(2,1)} %reshape.236), calls=%async_computation | async-start | bytes 327680 | tf_op jit(solution)/shard_map/all_to_all | solution.py:56
  58.9 15.7 %copy-start.8 = (bf16[320,1280]{1,0:T(8,128)(2,1)S(1)}, bf16[320,1280]{1,0:T(8,128)(2,1)}, u32[]{:S(2)}) copy-start(bf16[320,1280]{1,0:T(8,128)(2,1)} %param.14) | copy-start | bytes 2457604
  58.9 118.9 %all-reduce.13.cloned.1.call-start = ((), (), s32[]{:S(2)}) async-start(), calls=%async_computation.6 | async-start | bytes 2621440
  77.5 13.3 %copy-start.15 = (bf16[64,1,1,1280]{3,2,1,0:T(2,128)(2,1)}, bf16[64,1,1,1280]{3,2,1,0:T(2,128)(2,1)S(1)}, u32[]{:S(2)}) copy-start(bf16[64,1,1,1280]{3,2,1,0:T(2,128)(2,1)S(1)} %reshape.237) | copy-start | bytes 491524
  98.1 5.3 %copy-start.22 = (bf16[8,32,4,80]{3,2,1,0:T(4,128)(2,1)S(1)}, bf16[8,32,4,80]{3,2,1,0:T(4,128)(2,1)}, u32[]{:S(2)}) copy-start(bf16[8,32,4,80]{3,2,1,0:T(4,128)(2,1)} %reshape.214) | copy-start | bytes 491524
  107.0 6.8 %copy-start.9 = (bf16[320,1280]{1,0:T(8,128)(2,1)S(1)}, bf16[320,1280]{1,0:T(8,128)(2,1)}, u32[]{:S(2)}) copy-start(bf16[320,1280]{1,0:T(8,128)(2,1)} %param.14) | copy-start | bytes 2457604
  121.4 146.0 %all-reduce.11.cloned.1.call-start = ((), (), s32[]{:S(2)}) async-start(), calls=%async_computation.5 | async-start | bytes 6553600 | tf_op jit(solution)/shard_map/psum | solution.py:158
  128.3 49.5 %copy-start.14 = (bf16[64,1,1,1280]{3,2,1,0:T(2,128)(2,1)S(1)}, bf16[64,1,1,1280]{3,2,1,0:T(2,128)(2,1)}, u32[]{:S(2)}) copy-start(bf16[64,1,1,1280]{3,2,1,0:T(2,128)(2,1)} %reshape.239) | copy-start | bytes 491524
  128.3 56.4 %copy-start.16 = (bf16[64,1,1,1280]{3,2,1,0:T(2,128)(2,1)S(1)}, bf16[64,1,1,1280]{3,2,1,0:T(2,128)(2,1)}, u32[]{:S(2)}) copy-start(bf16[64,1,1,1280]{3,2,1,0:T(2,128)(2,1)} %copy-done.15) | copy-start | bytes 491524
  128.3 68.7 %copy-start.10 = (bf16[320,1280]{1,0:T(8,128)(2,1)S(1)}, bf16[320,1280]{1,0:T(8,128)(2,1)}, u32[]{:S(2)}) copy-start(bf16[320,1280]{1,0:T(8,128)(2,1)} %param.11) | copy-start | bytes 2457604
  180.1 13.5 %all-to-all-start.3 = ((bf16[8,1,8,1280]{3,2,1,0:T(8,128)(2,1)}), bf16[8,1,8,1280]{3,2,1,0:T(8,128)(2,1)S(1)}, u32[]{:S(2)}, u32[]{:S(2)}) async-start(bf16[8,1,8,1280]{3,2,1,0:T(8,128)(2,1)} %fusion.43), calls=%async_computation.3 | async-start | bytes 327680 | tf_op jit(solution)/shard_map/all_to_all | solution.py:68
  184.7 13.0 %copy-start.31 = (bf16[2,2,128,320]{2,3,1,0:T(8,128)(2,1)S(1)}, bf16[2,2,128,320]{2,3,1,0:T(8,128)(2,1)}, u32[]{:S(2)}) copy-start(bf16[2,2,128,320]{2,3,1,0:T(8,128)(2,1)} %param.17) | copy-start | bytes 983044
  193.5 12.7 %all-to-all-start.1 = ((bf16[8,1,8,1280]{3,2,1,0:T(8,128)(2,1)}), bf16[8,1,8,1280]{3,2,1,0:T(8,128)(2,1)S(1)}, u32[]{:S(2)}, u32[]{:S(2)}) async-start(bf16[8,1,8,1280]{3,2,1,0:T(8,128)(2,1)} %fusion.42), calls=%async_computation.1 | async-start | bytes 327680 | tf_op jit(solution)/shard_map/all_to_all | solution.py:68
  196.9 223.4 %all-reduce.9.cloned.1.call-start = ((), (), s32[]{:S(2)}) async-start(), calls=%async_computation.4 | async-start | bytes 9502720 | tf_op jit(solution)/shard_map/psum | solution.py:161
  199.4 6.9 %copy-start.41 = (bf16[64,320]{1,0:T(8,128)(2,1)S(1)}, bf16[64,320]{1,0:T(8,128)(2,1)}, u32[]{:S(2)}) copy-start(bf16[64,320]{1,0:T(8,128)(2,1)} %copy-done.40) | copy-start | bytes 122884
  200.6 7.2 %copy-start.38 = (f32[64,320]{1,0:T(8,128)S(1)}, f32[64,320]{1,0:T(8,128)}, u32[]{:S(2)}) copy-start(f32[64,320]{1,0:T(8,128)} %copy-done.37) | copy-start | bytes 245764
  211.3 61.8 %collective-permute-start.3 = (bf16[1,2,128,320]{2,3,1,0:T(8,128)(2,1)S(1)}, bf16[1,2,128,320]{2,3,1,0:T(8,128)(2,1)S(1)}, u32[]{:S(2)}, u32[]{:S(2)}) collective-permute-start(bf16[1,2,128,320]{2,3,1,0:T(8,128)(2,1)S(1)} %get-tuple-element.70), channel_id=1, source_target_pairs={{0,4},{4,8},{8,12},{12,16},{16,20},{20,24},{24,28},{1,5},{5,9},{9,... | collective-permute-start | bytes 491528 | tf_op jit(solution)/shard_map/ppermute | solution.py:19
  212.6 60.5 %collective-permute-start.2 = (bf16[1,2,128,320]{2,3,1,0:T(8,128)(2,1)S(1)}, bf16[1,2,128,320]{2,3,1,0:T(8,128)(2,1)S(1)}, u32[]{:S(2)}, u32[]{:S(2)}) collective-permute-start(bf16[1,2,128,320]{2,3,1,0:T(8,128)(2,1)S(1)} %get-tuple-element.71), channel_id=1, source_target_pairs={{4,0},{8,4},{12,8},{16,12},{20,16},{24,20},{28,24},{5,1},{9,5},{13... | collective-permute-start | bytes 491528 | tf_op jit(solution)/shard_map/ppermute | solution.py:21
  (31 other events, 66.6 us)
Sparse Core Ops, SparseCore 0:
  121.5 56.2 all-reduce.12
  180.8 86.5 all-reduce.10
  274.1 146.1 all-reduce.8
where the time goes:
time: 434 us; the launch traced here: 433 us
  waiting for transfers between devices  213 us (49%)
  blocking collectives  66.7 us (15%)
  local copies, waits for them, and re-layouts  55 us (13%)
  matrix products  32.1 us (7%)
  starting transfers between devices  27.9 us (6%)
  other arithmetic  22.9 us (5%)
  between operations  15.2 us (4%)
    psum x1, waiting for transfers between devices, shards(): lax.psum((jnp.stack(taps), grad_down_part, grad_up_part, column_sum), ('f...  144 us
    unnamed x4, waiting for transfers between devices  49.5 us
    psum x1, blocking collectives, shards(): lax.psum((jnp.stack(taps), grad_down_part, grad_up_part, column_sum), ('f...  43.6 us
    all_gather x2, blocking collectives, to_coarse(): whole = lax.all_gather(local, 'heads', axis=1, tiled=True)  23.1 us
    unnamed x103, local copies, waits for them, and re-layouts  22.5 us
    all_to_all x2, starting transfers between devices, to_coarse(): lax.all_to_all(field, 'frames', split_axis=2, concat_axis=0, tiled=True)  12.7 us
    all_to_all x2, waiting for transfers between devices, to_fine(): lax.all_to_all(field, 'frames', split_axis=0, concat_axis=2, tiled=True)  12.1 us
    dot_general x8, matrix products, matmul(): return jnp.dot(left, right, preferred_element_type=jnp.float32)  9.45 us
  transfers between devices with their start and end apart: 11, of which 5 were waited for; matrix products, arithmetic and copies ran while one was open for 15% of the time, Pallas kernels for 0%

commit v1 on v0

v1 whole, which is shorter than its diff:
```python
import functools
import math

import jax
import jax.numpy as jnp
from jax import lax
from jax.experimental import pallas as pl
from jax.experimental.pallas import tpu as pltpu
from jax.sharding import PartitionSpec as P

HD = 80
SLOT = 128
BF = jnp.bfloat16
F32 = jnp.float32


def nn(a, b):
    return lax.dot_general(a, b, (((1,), (0,)), ((), ())), preferred_element_type=F32)


def nt(a, b):
    return lax.dot_general(a, b, (((1,), (1,)), ((), ())), preferred_element_type=F32)


def tn(a, b):
    return lax.dot_general(a, b, (((0,), (0,)), ((), ())), preferred_element_type=F32)


def round_up(value, step):
    return -(-value // step) * step


def call(kernel, out_shape, **kw):
    return pl.pallas_call(
        kernel,
        out_shape=out_shape,
        compiler_params=pltpu.CompilerParams(vmem_limit_bytes=56 * 1024 * 1024),
        **kw,
    )


def smem():
    return pl.BlockSpec(memory_space=pltpu.SMEM)


def vmem():
    return pl.BlockSpec(memory_space=pltpu.VMEM)


def sds(shape, dtype):
    return jax.ShapeDtypeStruct(shape, dtype)


def bit_list(count):
    bits = []
    while (1 << len(bits)) < count:
        bits.append(1 << len(bits))
    return bits


def reversed_bits(value, count):
    n = len(bit_list(count))
    out = 0
    for i in range(n):
        out = out + (((value >> i) & 1) << (n - 1 - i))
    return out


def swap(x, axis, bit):
    n = lax.axis_size(axis)
    return lax.ppermute(x, axis, [(i, i ^ bit) for i in range(n)])


def time_embed(timestep, width):
    half = width // 2
    freqs = jnp.exp(-math.log(10000.0) * jnp.arange(half, dtype=F32) / half)
    angle = timestep.astype(F32)[0] * freqs
    return jax.nn.silu(jnp.concatenate([jnp.cos(angle), jnp.sin(angle)])).astype(BF)


def pool_matrix(half_c, columns):
    row = lax.broadcasted_iota(jnp.int32, (half_c, 2 * columns), 0)
    col = lax.broadcasted_iota(jnp.int32, (half_c, 2 * columns), 1)
    col = jnp.where(col >= columns, col - columns, col)
    return jnp.where((col >> 1) == row, 1.0, 0.0).astype(BF)


def lift_matrix(half_c, columns):
    row = lax.broadcasted_iota(jnp.int32, (2 * columns, half_c), 0)
    col = lax.broadcasted_iota(jnp.int32, (2 * columns, half_c), 1)
    row = jnp.where(row >= columns, row - columns, row)
    return jnp.where((row >> 1) == col, 1.0, 0.0).astype(BF)


def pool_kernel(me, clip, cot, keep, send, tmp):
    half_c = tmp.shape[1]
    half = half_c // 2
    quart = half // 2
    columns = clip.shape[1] // 2
    pool = pool_matrix(half_c, columns)
    tmp[0] = nn(pool, clip[0]) * 0.25
    tmp[1] = nn(pool, clip[1]) * 0.25
    tmp[2] = nn(pool, cot[0]) + nn(pool, cot[1])
    core = me[0] & 1
    for color in range(2):
        for item in range(3):
            base = pl.multiple_of(core * half + color * quart, quart)
            keep[color, item] = tmp[item, pl.ds(base, quart), :].astype(BF)
            base = pl.multiple_of((1 - core) * half + color * quart, quart)
            send[color, item] = tmp[item, pl.ds(base, quart), :].astype(BF)


def weight_kernel(w_down, w_embed, embed, w_qkv, w_out, w_up, down, mix, out_mix, direct):
    chans = w_down.shape[0]
    padded = down.shape[0]
    shift = nn(embed[...], w_embed[...])
    high = shift.astype(BF)
    low = (shift - high.astype(F32)).astype(BF)
    down[0:chans, :] = w_down[...]
    row = lax.broadcasted_iota(jnp.int32, (padded - chans, shift.shape[1]), 0)
    tail = jnp.where(row == 0, high.astype(F32), jnp.where(row == 1, low.astype(F32), 0.0))
    down[chans:padded, :] = tail.astype(BF)
    full = down[...]
    pieces = w_qkv.shape[1] // HD
    prod = nn(full, w_qkv[...])
    mix[...] = jnp.zeros(mix.shape, BF)
    for i in range(pieces):
        mix[:, i * SLOT : i * SLOT + HD] = prod[:, i * HD : (i + 1) * HD].astype(BF)
    up = w_up[...]
    small = nn(w_out[...], up)
    out_mix[...] = jnp.zeros(out_mix.shape, BF)
    for i in range(pieces // 3):
        out_mix[i * SLOT : i * SLOT + HD, :] = small[i * HD : (i + 1) * HD, :].astype(BF)
    direct[...] = nn(full, up).astype(BF)


def fine_kernel(clip, clip_lo, clip_hi, cot, cot_lo, cot_hi, w_time, hidden, base, taps):
    frames = clip.shape[0]

    def pick(body, lo, hi, t):
        return lo[...] if t < 0 else (hi[...] if t >= frames else body[t])

    chans = w_time.shape[1]
    taps[3 * chans :, :] = jnp.zeros((taps.shape[0] - 3 * chans, chans), BF)
    for tap in range(3):
        acc = None
        for t in range(frames):
            part = tn(pick(clip, clip_lo, clip_hi, t + tap - 1), cot[t])
            acc = part if acc is None else acc + part
        taps[tap * chans : (tap + 1) * chans, :] = acc.astype(BF)
    for t in range(frames):
        acc = clip[t].astype(F32)
        grad = cot[t].astype(F32)
        for tap in range(3):
            acc = acc + nn(pick(clip, clip_lo, clip_hi, t + tap - 1), w_time[tap])
            grad = grad + nt(pick(cot, cot_lo, cot_hi, t + 1 - tap), w_time[tap])
        hidden[t] = acc.astype(BF)
        base[t] = grad


def coarse_kernel(
    me, first, second, w_time, mix, out_mix, direct, local, grad_mix, grad_att, gram, tap_keep, tap_send,
    shifted, centre, pooled, upper, qkv, att_grad, att, qkv_grad, fields, mix_acc, att_acc, gram_acc, tap_acc,
    *, coarse_frames, heads_axis,
):
    step = pl.program_id(0)
    frame = me[0]
    quart = first.shape[2]
    chans = first.shape[3]
    padded = pooled.shape[1]
    tokens = coarse_frames * quart
    chips = coarse_frames // 2
    heads = att.shape[1] // SLOT
    scale = 1.0 / math.sqrt(HD)
    part = 1.0 / heads_axis

    @pl.when(step == 0)
    def _():
        mix_acc[...] = jnp.zeros(mix_acc.shape, F32)
        att_acc[...] = jnp.zeros(att_acc.shape, F32)
        gram_acc[...] = jnp.zeros(gram_acc.shape, F32)
        tap_acc[...] = jnp.zeros(tap_acc.shape, F32)
        lane = lax.broadcasted_iota(jnp.int32, (2 * tokens, padded - chans), 1)
        pooled[:, chans:padded] = jnp.where(lane < 2, 1.0, 0.0).astype(BF)

    def entry(index):
        gap = index ^ frame
        return (reversed_bits(gap >> 1, chips) * 2 + (gap & 1)) * 3

    for color, source in ((0, first), (1, second)):
        before = jnp.zeros((quart, chans), F32)
        here = source[0, entry(0)].astype(F32)
        for u in range(coarse_frames):
            at = entry(u)
            last = source[0, at + 1].astype(F32)
            after = source[0, entry(u + 1)].astype(F32) if u + 1 < coarse_frames else jnp.zeros((quart, chans), F32)
            rows = pl.ds(color * tokens + u * quart, quart)
            mid = 0.5 * (here + last)
            shifted[0, rows, :] = (0.5 * (before + here)).astype(BF)
            shifted[1, rows, :] = mid.astype(BF)
            shifted[2, rows, :] = (0.5 * (last + after)).astype(BF)
            centre[rows, :] = mid
            upper[rows, :] = source[0, at + 2]
            before, here = last, after
    acc = centre[...]
    for tap in range(3):
        acc = acc + nn(shifted[tap], w_time[tap])
    pooled[:, 0:chans] = acc.astype(BF)
    qkv[...] = nn(pooled[...], mix[...]).astype(BF)
    att_grad[...] = nt(upper[...], out_mix[...]).astype(BF)
    row = lax.broadcasted_iota(jnp.int32, (tokens, tokens), 0)
    col = lax.broadcasted_iota(jnp.int32, (tokens, tokens), 1)
    same = (row & (quart - 1)) == (col & (quart - 1))
    for color in range(2):
        rows = slice(color * tokens, (color + 1) * tokens)
        for n in range(heads):
            q = qkv[rows, (3 * n) * SLOT : (3 * n + 1) * SLOT]
            k = qkv[rows, (3 * n + 1) * SLOT : (3 * n + 2) * SLOT]
            v = qkv[rows, (3 * n + 2) * SLOT : (3 * n + 3) * SLOT]
            da = att_grad[rows, n * SLOT : (n + 1) * SLOT]
            scores = jnp.where(same, nt(q, k) * scale, -jnp.inf)
            peak = jnp.max(scores, axis=1, keepdims=True)
            ex = jnp.exp(scores - peak)
            probs = ex / jnp.sum(ex, axis=1, keepdims=True)
            weights = probs.astype(BF)
            att[rows, n * SLOT : (n + 1) * SLOT] = nn(weights, v).astype(BF)
            dw = nt(da, v)
            inner = jnp.sum(probs * dw, axis=1, keepdims=True)
            ds = (probs * (dw - inner) * scale).astype(BF)
            qkv_grad[rows, (3 * n) * SLOT : (3 * n + 1) * SLOT] = nn(ds, k).astype(BF)
            qkv_grad[rows, (3 * n + 1) * SLOT : (3 * n + 2) * SLOT] = tn(ds, q).astype(BF)
            qkv_grad[rows, (3 * n + 2) * SLOT : (3 * n + 3) * SLOT] = tn(weights, da).astype(BF)
    lifted = nn(att[...], out_mix[...]) + nn(pooled[...], direct[...]) * part
    spread = nt(qkv_grad[...], mix[...]) + nt(upper[...], direct[...]) * part
    spread = spread[:, 0:chans]
    fields[0] = lifted.astype(BF).reshape(2 * coarse_frames, quart, chans)
    fields[1] = spread.astype(BF).reshape(2 * coarse_frames, quart, chans)
    mine = (frame >> 1) * 2
    for color in range(2):
        for i in range(2):
            local[0, i, color] = fields[0, color * coarse_frames + mine + i]
        for i in range(4):
            at = jnp.clip(mine + i - 1, 0, coarse_frames - 1)
            local[0, 2 + i, color] = fields[1, color * coarse_frames + at]
    mix_acc[...] += tn(pooled[...], qkv_grad[...])
    att_acc[...] += tn(att[...], upper[...])
    gram_acc[...] += tn(pooled[...], upper[...])
    spread16 = spread.astype(BF)
    for tap in range(3):
        tap_acc[tap * chans : (tap + 1) * chans, :] += tn(shifted[tap], spread16)

    @pl.when(step == heads_axis - 1)
    def _():
        for i in range(3 * heads):
            grad_mix[:, i * HD : (i + 1) * HD] = mix_acc[:, i * SLOT : i * SLOT + HD].astype(BF)
        for n in range(heads):
            grad_att[n * HD : (n + 1) * HD, :] = att_acc[n * SLOT : n * SLOT + HD, :].astype(BF)
        gram[...] = gram_acc[...].astype(BF)
        rows = tap_keep.shape[0]
        tap_keep[...] = tap_acc[pl.ds(pl.multiple_of(frame * rows, rows), rows), :].astype(BF)
        tap_send[...] = tap_acc[pl.ds(pl.multiple_of((frame ^ 1) * rows, rows), rows), :].astype(BF)


def slice_kernel(
    me, mix_a, mix_b, att_a, att_b, gram_a, gram_b, tap_a, tap_b, tap_c, w_qkv, w_up, w_out, down,
    grad_mix, grad_att, down_t, up, taps, *, heads_axis,
):
    del me
    chans = gram_a.shape[1]
    part = 1.0 / heads_axis
    g = (mix_a[...].astype(F32) + mix_b[...].astype(F32)).astype(BF)
    a = (att_a[...].astype(F32) + att_b[...].astype(F32)).astype(BF)
    s = (gram_a[...].astype(F32) + gram_b[...].astype(F32)).astype(BF)
    grad_mix[...] = g
    grad_att[...] = a
    down_t[...] = nt(w_qkv[...], g) + nt(w_up[...], s) * part
    up[:, 0:chans] = tn(w_out[...], a) + tn(down[...], s) * part
    up[:, chans:] = jnp.zeros((up.shape[0], up.shape[1] - chans), F32)
    taps[:, 0:chans] = tap_a[...].astype(F32) + tap_b[...].astype(F32) + tap_c[...].astype(F32)
    taps[:, chans:] = jnp.zeros((taps.shape[0], taps.shape[1] - chans), F32)


def split_grad_kernel(down, grad_mix, grad_att, w_up, qkv_out, att_out):
    qkv_out[...] = tn(down[...], grad_mix[...])
    att_out[...] = nt(grad_att[...], w_up[...])


def finish_kernel(me, hidden, base, own, other, w_time, output, grad_clip, rows, *, coarse_frames):
    frame = me[0]
    core = frame & 1
    half = own.shape[1]
    columns = hidden.shape[1] // 2
    for i in range(4):
        rows[i, pl.ds(pl.multiple_of(core * half, half), half), :] = own[i].astype(F32)
        rows[i, pl.ds(pl.multiple_of((1 - core) * half, half), half), :] = other[i].astype(F32)
    lift = lift_matrix(2 * half, columns)
    fine = nn(lift, rows[0].astype(BF))
    for t in range(2):
        output[t] = (hidden[t].astype(F32) + fine).astype(BF)
    before = (rows[1] * jnp.where(frame == 0, 0.0, 1.0)).astype(BF)
    here = rows[2].astype(BF)
    after = (rows[3] * jnp.where(frame == coarse_frames - 1, 0.0, 1.0)).astype(BF)
    mid = rows[2] + nt(here, w_time[1])
    even = mid + nt(here, w_time[0]) + nt(before, w_time[2])
    odd = mid + nt(after, w_time[0]) + nt(here, w_time[2])
    for t, value in ((0, even), (1, odd)):
        high = value.astype(BF)
        low = (value - high.astype(F32)).astype(BF)
        grad_clip[t] = base[t] + (nn(lift, high) + nn(lift, low)) * 0.125


def gather_kernel(me, embed, *refs, layout, aligned):
    pieces = refs[:4]
    refs = refs[4:]
    time_out, up_out = refs[0], refs[1]
    frame, head = me[0], me[1]
    chips, heads_axis, r1, p1, r3, split = layout
    chans = up_out.shape[2]
    down_rows = refs[-1] if aligned else refs[2]
    devices = 2 * chips * heads_axis
    for core in range(2):
        for idx in range(chips * heads_axis):
            hi, zi = idx // chips, idx % chips
            colors = []
            for color in range(2):
                src = pieces[2 * core + color]
                off = hi if color == 0 else reversed_bits(hi, heads_axis)
                colors.append(src[off, zi].astype(F32))
            value = jnp.concatenate(colors, axis=0)
            owner = (frame ^ (reversed_bits(zi, chips) * 2 + core)) * heads_axis + (head ^ hi)
            down_rows[owner] = value[0:r1]
            up_out[owner] = value[p1 : p1 + r1, 0:chans]

            @pl.when(owner < time_out.shape[0])
            def _():
                time_out[owner] = value[2 * p1 : 2 * p1 + r3, 0:chans]

    if aligned:
        down_out, embed_out = refs[2], refs[3]
        table = down_rows[...].reshape(devices * r1, down_rows.shape[2]).astype(BF)
        lanes = table.shape[1]
        eye = (lax.broadcasted_iota(jnp.int32, (lanes, lanes), 0) == lax.broadcasted_iota(jnp.int32, (lanes, lanes), 1))
        flipped = nt(eye.astype(F32).astype(BF), table)
        down_out[...] = flipped[0:chans]
        embed_out[...] = embed[...] * flipped[chans : chans + 1]


def double(x, axis, bits, dim):
    for bit in bits:
        x = jnp.concatenate([x, swap(x, axis, bit)], axis=dim)
    return x


def shards(clip, w_time, w_down, w_embed, w_qkv, w_out, w_up, timestep, cotangent):
    nf = lax.axis_size("frames")
    nh = lax.axis_size("heads")
    f = lax.axis_index("frames")
    h = lax.axis_index("heads")
    me = jnp.stack([f, h]).astype(jnp.int32)
    frames, rows, columns, chans = clip.shape
    width = w_down.shape[1]
    half_c = columns // 2
    half = half_c // 2
    quart = half // 2
    chips = nf // 2
    padded = round_up(chans + 2, 128)
    pieces = w_qkv.shape[1] // HD
    heads = pieces // 3
    chip_bits = [2 * b for b in reversed(bit_list(chips))]
    head_bits = bit_list(nh)

    clip2 = clip.reshape(frames, rows * columns, chans)
    cot2 = cotangent.reshape(frames, rows * columns, chans)

    keep, send = call(
        pool_kernel,
        [sds((2, 3, quart, chans), BF)] * 2,
        in_specs=[smem(), vmem(), vmem()],
        out_specs=[vmem()] * 2,
        scratch_shapes=[pltpu.VMEM((3, half_c, chans), F32)],
    )(me, clip2, cot2)
    block = jnp.concatenate([keep, swap(send, "frames", 1)], axis=1)
    block = double(block, "frames", chip_bits, 1)
    first = block[0]
    second = block[1]
    first = first[None]
    second = second[None]
    for a, b in zip(head_bits, reversed(head_bits)):
        first_in = swap(first, "heads", a)
        second_in = swap(second, "heads", b)
        first = jnp.concatenate([first, first_in], axis=0)
        second = jnp.concatenate([second, second_in], axis=0)

    embed = time_embed(timestep, w_embed.shape[0])
    down, mix, out_mix, direct = call(
        weight_kernel,
        [
            sds((padded, width), BF),
            sds((padded, pieces * SLOT), BF),
            sds((heads * SLOT, chans), BF),
            sds((padded, chans), BF),
        ],
    )(w_down, w_embed, embed[None, :], w_qkv, w_out, w_up)

    tail = jnp.stack([clip2[-1], cot2[-1]])
    head = jnp.stack([clip2[0], cot2[0]])
    lo = lax.ppermute(tail, "frames", [(i, i + 1) for i in range(nf - 1)])
    hi = lax.ppermute(head, "frames", [(i + 1, i) for i in range(nf - 1)])
    tap_rows = round_up(3 * chans, nf * nh * 8)
    hidden, base, taps = call(
        fine_kernel,
        [
            sds(clip2.shape, BF),
            sds(clip2.shape, F32),
            sds((tap_rows, chans), BF),
        ],
    )(clip2, lo[0], hi[0], cot2, lo[1], hi[1], w_time)
    share = tap_rows // nf
    bits = bit_list(nf)
    taps = taps.reshape([2] * len(bits) + [share, chans])
    for i in range(len(bits)):
        axis = len(bits) - 1 - i
        mine = (f >> i) & 1
        other = lax.dynamic_index_in_dim(taps, 1 - mine, axis, keepdims=False)
        same = lax.dynamic_index_in_dim(taps, mine, axis, keepdims=False)
        got = swap(other, "frames", 1 << i)
        taps = (same.astype(F32) + got.astype(F32)).astype(BF)

    blk = pl.BlockSpec((1, nf * 3, quart, chans), lambda g: (g, 0, 0, 0))
    mirrored = pl.BlockSpec((1, nf * 3, quart, chans), lambda g: (reversed_bits(g, nh), 0, 0, 0))
    total = 2 * nf * quart

    def whole(*shape):
        return pl.BlockSpec(shape, lambda g: (0,) * len(shape))

    local, mix_g, att_g, gram, tap_keep, tap_send = call(
        functools.partial(coarse_kernel, coarse_frames=nf, heads_axis=nh),
        [
            sds((nh, 6, 2, quart, chans), BF),
            sds((padded, pieces * HD), BF),
            sds((heads * HD, chans), BF),
            sds((padded, chans), BF),
            sds((share, chans), BF),
            sds((share, chans), BF),
        ],
        grid=(nh,),
        in_specs=[
            smem(),
            blk,
            mirrored,
            whole(*w_time.shape),
            whole(*mix.shape),
            whole(*out_mix.shape),
            whole(*direct.shape),
        ],
        out_specs=[
            pl.BlockSpec((1, 6, 2, quart, chans), lambda g: (g, 0, 0, 0, 0)),
            whole(padded, pieces * HD),
            whole(heads * HD, chans),
            whole(padded, chans),
            whole(share, chans),
            whole(share, chans),
        ],
        scratch_shapes=[
            pltpu.VMEM((3, total, chans), BF),
            pltpu.VMEM((total, chans), F32),
            pltpu.VMEM((total, padded), BF),
            pltpu.VMEM((total, chans), BF),
            pltpu.VMEM((total, pieces * SLOT), BF),
            pltpu.VMEM((total, heads * SLOT), BF),
            pltpu.VMEM((total, heads * SLOT), BF),
            pltpu.VMEM((total, pieces * SLOT), BF),
            pltpu.VMEM((2, 2 * nf, quart, chans), BF),
            pltpu.VMEM((padded, pieces * SLOT), F32),
            pltpu.VMEM((heads * SLOT, chans), F32),
            pltpu.VMEM((padded, chans), F32),
            pltpu.VMEM((tap_rows, chans), F32),
        ],
    )(me, first, second, w_time, mix, out_mix, direct)

    mix_o = swap(mix_g, "frames", 1)
    att_o = swap(att_g, "frames", 1)
    gram_o = swap(gram, "frames", 1)
    tap_o = swap(tap_send, "frames", 1)

    rows_here = width // nf
    out_cols = lax.dynamic_slice_in_dim(w_out, f * rows_here, rows_here, axis=1)
    down_cols = lax.dynamic_slice_in_dim(down, f * rows_here, rows_here, axis=1)
    grid_spec = pltpu.PrefetchScalarGridSpec(
        num_scalar_prefetch=1,
        grid=(1,),
        in_specs=[pl.BlockSpec(x.shape, lambda g, m: (0, 0)) for x in (mix_g, mix_o, att_g, att_o, gram, gram_o, tap_keep, tap_o, taps)]
        + [
            pl.BlockSpec((rows_here, w_qkv.shape[1]), lambda g, m: (m[0], 0)),
            pl.BlockSpec((rows_here, chans), lambda g, m: (m[0], 0)),
            pl.BlockSpec(out_cols.shape, lambda g, m: (0, 0)),
            pl.BlockSpec(down_cols.shape, lambda g, m: (0, 0)),
        ],
        out_specs=[
            pl.BlockSpec(mix_g.shape, lambda g, m: (0, 0)),
            pl.BlockSpec(att_g.shape, lambda g, m: (0, 0)),
            pl.BlockSpec((rows_here, padded), lambda g, m: (0, 0)),
            pl.BlockSpec((rows_here, padded), lambda g, m: (0, 0)),
            pl.BlockSpec((share, padded), lambda g, m: (0, 0)),
        ],
    )
    mix_s, att_s, down_s, up_s, tap_s = call(
        functools.partial(slice_kernel, heads_axis=nh),
        [
            sds(mix_g.shape, BF),
            sds(att_g.shape, BF),
            sds((rows_here, padded), F32),
            sds((rows_here, padded), F32),
            sds((share, padded), F32),
        ],
        grid_spec=grid_spec,
    )(me, mix_g, mix_o, att_g, att_o, gram, gram_o, tap_keep, tap_o, taps, w_qkv, w_up, out_cols, down_cols)

    r1 = rows_here // nh
    p1 = round_up(r1, 8)
    r3 = share // nh
    piece_rows = round_up(2 * p1 + r3, 32)

    def fit(x, count):
        x = x.astype(BF).reshape(nh, count, padded)
        return jnp.pad(x, ((0, 0), (0, round_up(count, 8) - count), (0, 0)))

    parts = jnp.concatenate([fit(down_s, r1), fit(up_s, r1), fit(tap_s, r3)], axis=1)
    parts = jnp.pad(parts, ((0, 0), (0, piece_rows - parts.shape[1]), (0, 0)))
    mine = lax.dynamic_index_in_dim(parts, h, 0, keepdims=False).astype(F32)
    for d in range(1, nh):
        mine = mine + swap(lax.dynamic_index_in_dim(parts, h ^ d, 0, keepdims=False), "heads", d).astype(F32)
    piece = mine.astype(BF).reshape(2, 1, piece_rows // 2, padded)
    piece = double(piece, "frames", chip_bits, 1)
    p_first = piece[0][None]
    p_second = piece[1][None]
    for a, b in zip(head_bits, reversed(head_bits)):
        a_in = swap(p_first, "heads", a)
        b_in = swap(p_second, "heads", b)
        p_first = jnp.concatenate([p_first, a_in], axis=0)
        p_second = jnp.concatenate([p_second, b_in], axis=0)
    q_first = swap(p_first, "frames", 1)
    q_second = swap(p_second, "frames", 1)

    own = local[0].astype(F32)
    for d in range(1, nh):
        own = own + swap(local[d], "heads", d).astype(F32)
    own = own.astype(BF).reshape(6, half, chans)
    core = f & 1

    def four(which):
        return jnp.concatenate(
            [
                lax.dynamic_slice_in_dim(own, which, 1, axis=0),
                lax.dynamic_slice_in_dim(own, 2 + which, 3, axis=0),
            ]
        )

    mine4 = four(core)
    other4 = swap(four(1 - core), "frames", 1)
    output, grad_clip = call(
        functools.partial(finish_kernel, coarse_frames=nf),
        [sds(clip2.shape, BF), sds(clip2.shape, F32)],
        in_specs=[smem()] + [vmem()] * 5,
        out_specs=[vmem()] * 2,
        scratch_shapes=[pltpu.VMEM((4, half_c, chans), F32)],
    )(me, hidden, base, mine4, other4, w_time)

    step = 256
    grad_qkv, grad_out = call(
        split_grad_kernel,
        [sds((width, pieces * HD), F32), sds((heads * HD, width), F32)],
        grid=(width // step,),
        in_specs=[
            pl.BlockSpec((padded, step), lambda g: (0, g)),
            whole(*mix_s.shape),
            whole(*att_s.shape),
            pl.BlockSpec((step, chans), lambda g: (g, 0)),
        ],
        out_specs=[
            pl.BlockSpec((step, pieces * HD), lambda g: (g, 0)),
            pl.BlockSpec((heads * HD, step), lambda g: (0, g)),
        ],
    )(down, mix_s, att_s, w_up)

    devices = nf * nh
    aligned = r1 % 8 == 0
    layout = (chips, nh, r1, p1, r3, piece_rows // 2)
    time_rows = 3 * chans // r3
    outs = [sds((time_rows, r3, chans), F32), sds((devices, r1, chans), F32)]
    scratch = []
    if aligned:
        outs += [sds((chans, width), F32), sds((w_embed.shape[0], width), F32)]
        scratch = [pltpu.VMEM((devices, r1, padded), F32)]
    else:
        outs += [sds((devices, r1, padded), F32)]
    embed_col = embed.astype(F32)[:, None]
    got = call(
        functools.partial(gather_kernel, layout=layout, aligned=aligned),
        outs,
        in_specs=[smem()] + [vmem()] * 5,
        out_specs=[vmem()] * len(outs),
        scratch_shapes=scratch,
    )(me, embed_col, p_first, p_second, q_first, q_second)
    grad_time = got[0].reshape(w_time.shape)
    grad_up = got[1].reshape(width, chans)
    if aligned:
        grad_down, grad_embed = got[2], got[3]
    else:
        table = got[2].reshape(width, padded)
        grad_down = table[:, :chans].T
        grad_embed = embed_col * table[:, chans][None, :]
    return (
        output.reshape(clip.shape),
        grad_clip.reshape(clip.shape),
        grad_time,
        grad_down,
        grad_embed,
        grad_qkv,
        grad_out,
        grad_up,
    )


def solution(mesh):
    return jax.shard_map(
        shards,
        mesh=mesh,
        in_specs=(
            P("frames", "heads", None, None),
            P(),
            P(),
            P(),
            P(None, "heads"),
            P("heads", None),
            P(),
            P(),
            P("frames", "heads", None, None),
        ),
        out_specs=(
            P("frames", "heads", None, None),
            P("frames", "heads", None, None),
            P(),
            P(),
            P(),
            P(None, "heads"),
            P("heads", None),
            P(),
        ),
        check_vma=False,
    )
```

time: 434 us -> 204 us (0.47)
  waiting for transfers between devices: 213 us -> 49.8 us
  blocking collectives: 66.7 us -> 0 us
  Pallas kernels: 0 us -> 66.4 us
  matrix products: 32.1 us -> 0 us
  local copies, waits for them, and re-layouts: 55 us -> 37.8 us
  between operations: 15.2 us -> 1.68 us
  other arithmetic: 22.9 us -> 13.4 us
  starting transfers between devices: 27.9 us -> 33.7 us
    psum x2 -> x0, waiting for transfers between devices: 151 us -> none  [the longest x1 144 us: shards(): lax.psum((jnp.stack(taps), grad_down_part, grad_up_part, column_sum), ('f...]
    pallas_call x0 -> x8, Pallas kernels: none -> 66.4 us  [the longest x1 33.6 us: shards(): call(functools.partial(coarse_kernel, coarse_frames=nf, heads_axis=nh), [...]
    ppermute x4 -> x31, waiting for transfers between devices: 0.01 us -> 49.8 us  [the longest x29 49.8 us: swap(): return lax.ppermute(x, axis, [(i, i ^ bit) for i in range(n)])]
    unnamed x4 -> x0, waiting for transfers between devices: 49.5 us -> none
    psum x1 -> x0, blocking collectives: 43.6 us -> none  [shards(): lax.psum((jnp.stack(taps), grad_down_part, grad_up_part, column_sum), ('f...]
    dot_general x28 -> x0, matrix products: 32.1 us -> none  [the longest x8 9.45 us: matmul(): return jnp.dot(left, right, preferred_element_type=jnp.float32)]
    ppermute x4 -> x31, starting transfers between devices: 6.93 us -> 33.7 us  [the longest x29 28.7 us: swap(): return lax.ppermute(x, axis, [(i, i ^ bit) for i in range(n)])]
    all_gather x2 -> x0, blocking collectives: 23.1 us -> none  [to_coarse(): whole = lax.all_gather(local, 'heads', axis=1, tiled=True)]
  transfers between devices with their start and end apart: 11 -> 31, of which waited for: 5 -> 13; matrix products, arithmetic and copies ran while one was open for 15% -> 20% of each run, Pallas kernels for 0% -> 28%
where the time goes in v1:
time: 204 us; the launch traced here: 203 us
  Pallas kernels  66.4 us (33%)
  waiting for transfers between devices  49.8 us (24%)
  local copies, waits for them, and re-layouts  37.8 us (19%)
  starting transfers between devices  33.7 us (17%)
  other arithmetic  13.4 us (7%)
    ppermute x29, waiting for transfers between devices, swap(): return lax.ppermute(x, axis, [(i, i ^ bit) for i in range(n)])  49.8 us
    pallas_call x1, Pallas kernels, shards(): call(functools.partial(coarse_kernel, coarse_frames=nf, heads_axis=nh), [...  33.6 us
    ppermute x29, starting transfers between devices, swap(): return lax.ppermute(x, axis, [(i, i ^ bit) for i in range(n)])  28.7 us
    unnamed x49, local copies, waits for them, and re-layouts  23.1 us
    pallas_call x1, Pallas kernels, shards(): call(split_grad_kernel, [sds((width, pieces * HD), F32), sds((heads * HD,...  7.09 us
    pallas_call x1, Pallas kernels, shards(): call(weight_kernel, [sds((padded, width), BF), sds((padded, pieces * SLOT...  5.74 us
    pallas_call x1, Pallas kernels, shards(): call(functools.partial(gather_kernel, layout=layout, aligned=aligned), ou...  5.19 us
    pallas_call x1, Pallas kernels, shards(): call(fine_kernel, [sds(clip2.shape, BF), sds(clip2.shape, F32), sds((tap_...  4.94 us
  transfers between devices with their start and end apart: 31, of which 13 were waited for; matrix products, arithmetic and copies ran while one was open for 20% of the time, Pallas kernels for 28%

profile of v1, /device:TPU:0, one launch (start us, length us, event | category | flops | bytes accessed | tf_op | source)
XLA Modules:
  0.0 202.9 jit_solution(16075583641951842092)
XLA Ops:
  5.4 3.8 %collective-permute-start = (bf16[2,256,320]{2,1,0:T(8,128)(2,1)}, bf16[2,256,320]{2,1,0:T(8,128)(2,1)}, u32[]{:S(2)}, u32[]{:S(2)}) collective-permute-start(bf16[2,256,320]{2,1,0:T(8,128)(2,1)} %pad_maximum_fusion.6), channel_id=1, source_target_pairs={{0,4},{4,8},{8,12},{12,16},{16,20},{20,24},{24,28},{1,5},{5,9},{9,... | collective-permute-start | bytes 983048 | tf_op jit(solution)/shard_map/ppermute | solution.py:407
  11.7 2.2 %shard_map.153 = (bf16[2,3,16,320]{3,2,1,0:T(8,128)(2,1)}, bf16[2,3,16,320]{3,2,1,0:T(8,128)(2,1)}) custom-call(s32[2]{0:T(128)} %pad_add_fusion.me, bf16[2,256,320]{2,1,0:T(8,128)(2,1)} %bitcast.67, bf16[2,256,320]{2,1,0:T(8,128)(2,1)} %bitcast.69), custom_call_target="tpu_custom_call" | custom-call | tf_op jit(solution)/shard_map/pallas_call | solution.py:375
  19.6 2.6 %collective-permute-start.3 = (bf16[2,6,16,320]{3,2,1,0:T(8,128)(2,1)}, bf16[2,6,16,320]{3,2,1,0:T(8,128)(2,1)S(1)}, u32[]{:S(2)}, u32[]{:S(2)}) collective-permute-start(bf16[2,6,16,320]{3,2,1,0:T(8,128)(2,1)} %pad_maximum_fusion.13), channel_id=1, source_target_pairs={{0,16},{4,20},{8,24},{12,28},{16,0},{20,4},{24,8},{28,12},{1,17},{... | collective-permute-start | bytes 368648 | tf_op jit(solution)/shard_map/ppermute | solution.py:71
  23.5 3.4 %copy.81.w_qkv = bf16[1280,960]{1,0:T(8,128)(2,1)} copy(bf16[1280,960]{0,1:T(8,128)(2,1)S(1)} %copy-done.2) | data formatting | bytes 4915200 | tf_op args[4]
  27.0 2.6 %collective-permute-done.3 = bf16[2,6,16,320]{3,2,1,0:T(8,128)(2,1)S(1)} collective-permute-done((bf16[2,6,16,320]{3,2,1,0:T(8,128)(2,1)}, bf16[2,6,16,320]{3,2,1,0:T(8,128)(2,1)S(1)}, u32[]{:S(2)}, u32[]{:S(2)}) %collective-permute-start.3) | collective-permute-done | bytes 122912 | tf_op jit(solution)/shard_map/ppermute | solution.py:71
  32.3 5.4 %collective-permute-done.4 = bf16[2,12,16,320]{3,2,1,0:T(8,128)(2,1)S(1)} collective-permute-done((bf16[2,12,16,320]{3,2,1,0:T(8,128)(2,1)S(1)}, bf16[2,12,16,320]{3,2,1,0:T(8,128)(2,1)S(1)}, u32[]{:S(2)}, u32[]{:S(2)}) %collective-permute-start.4) | collective-permute-done | bytes 245792 | tf_op jit(solution)/shard_map/ppermute | solution.py:71
  41.4 4.9 %shard_map.152 = (bf16[2,256,320]{2,1,0:T(8,128)(2,1)}, f32[2,256,320]{2,1,0:T(8,128)}, bf16[1024,320]{1,0:T(8,128)(2,1)}) custom-call(bf16[2,256,320]{2,1,0:T(8,128)(2,1)} %bitcast.68, bf16[256,320]{1,0:T(8,128)(2,1)} %get-tuple-element.111.clip_lo, bf16[256,320]{1,0:T(8,128)(2,1)} %get-tuple-element.109.clip_hi, bf16[2,256,320]{2,1,0:T(8,128)(2,1)} %bitcast.70, ...), custom_call_target="tpu_custom_call" | custom-call | tf_op jit(solution)/shard_map/pallas_call | solution.py:410
  49.8 5.7 %shard_map.154 = (bf16[384,1280]{1,0:T(8,128)(2,1)}, bf16[384,1536]{1,0:T(8,128)(2,1)}, bf16[512,320]{1,0:T(8,128)(2,1)}, bf16[384,320]{1,0:T(8,128)(2,1)}) custom-call(bf16[320,1280]{1,0:T(8,128)(2,1)} %w_down.1, bf16[320,1280]{1,0:T(8,128)(2,1)} %w_embed.1, bf16[1,320]{1,0:T(2,128)(2,1)} %fusion.14.embed, bf16[1280,960]{1,0:T(8,128)(2,1)} %copy.81.w_qkv, ...), custom_call_target="tpu_custom_call" | custom-call | tf_op jit(solution)/shard_map/pallas_call | solution.py:395
  58.8 12.7 %collective-permute-done.8 = bf16[2,24,16,320]{3,2,1,0:T(8,128)(2,1)S(1)} collective-permute-done((bf16[2,24,16,320]{3,2,1,0:T(8,128)(2,1)S(1)}, bf16[2,24,16,320]{3,2,1,0:T(8,128)(2,1)S(1)}, u32[]{:S(2)}, u32[]{:S(2)}) %collective-permute-start.8) | collective-permute-done | bytes 491552 | tf_op jit(solution)/shard_map/ppermute | solution.py:71
  74.0 33.6 %shard_map.155 = (bf16[4,6,2,16,320]{4,3,2,1,0:T(8,128)(2,1)}, bf16[384,960]{1,0:T(8,128)(2,1)}, bf16[320,320]{1,0:T(8,128)(2,1)}, bf16[384,320]{1,0:T(8,128)(2,...) custom-call(s32[2]{0:T(128)} %pad_add_fusion.me, bf16[4,24,16,320]{3,2,1,0:T(8,128)(2,1)} %pad_maximum_fusion.first, ...), custom_call_target="tpu_custom_call" | custom-call | tf_op jit(solution)/shard_map/pallas_call | solution.py:436
  111.1 3.2 %collective-permute-start.19 = (bf16[128,320]{1,0:T(8,128)(2,1)S(1)}, bf16[128,320]{1,0:T(8,128)(2,1)S(1)}, u32[]{:S(2)}, u32[]{:S(2)}) collective-permute-start(bf16[128,320]{1,0:T(8,128)(2,1)S(1)} %dynamic-slice_bitcast_fusion.4), channel_id=1, source_target_pairs={{0,16},{4,20},{8,24},{12,28},{16,0},{20,4},{24,8},{28,12},{1,17},{... | collective-permute-start | bytes 245768 | tf_op jit(solution)/shard_map/ppermute | solution.py:71
  116.8 3.1 %collective-permute-done.19 = bf16[128,320]{1,0:T(8,128)(2,1)S(1)} collective-permute-done((bf16[128,320]{1,0:T(8,128)(2,1)S(1)}, bf16[128,320]{1,0:T(8,128)(2,1)S(1)}, u32[]{:S(2)}, u32[]{:S(2)}) %collective-permute-start.19) | collective-permute-done | bytes 81952 | tf_op jit(solution)/shard_map/ppermute | solution.py:71
  122.6 4.3 %shard_map.157 = (bf16[384,960]{1,0:T(8,128)(2,1)}, bf16[320,320]{1,0:T(8,128)(2,1)}, f32[160,384]{1,0:T(8,128)}, f32[160,384]{1,0:T(8,128)}, f32[128,384]{1,0:T(8,128)}) custom-call(s32[2]{0:T(128)} %pad_add_fusion.me, bf16[384,960]{1,0:T(8,128)(2,1)} %get-tuple-element.46.mix_a, bf16[384,960]{1,0:T(8,128)(2,1)} %copy.87.mix_b, ...), custom_call_target="tpu_custom_call" | custom-call | tf_op jit(solution)/shard_map/pallas_call | solution.py:507
  131.1 2.3 %collective-permute-start.22 = (bf16[128,384]{1,0:T(8,128)(2,1)S(1)}, bf16[128,384]{1,0:T(8,128)(2,1)S(1)}, u32[]{:S(2)}, u32[]{:S(2)}) collective-permute-start(bf16[128,384]{1,0:T(8,128)(2,1)S(1)} %get-tuple-element.107), channel_id=1, source_target_pairs={{0,3},{1,2},{2,1},{3,0},{4,7},{5,6},{6,5},{7,4},{8,11},{9,10},{10,... | collective-permute-start | bytes 294920 | tf_op jit(solution)/shard_map/ppermute | solution.py:71
  137.8 6.2 %collective-permute-done.23 = bf16[2,1,64,384]{3,2,1,0:T(8,128)(2,1)S(1)} collective-permute-done((bf16[2,1,64,384]{3,2,1,0:T(8,128)(2,1)S(1)}, bf16[2,1,64,384]{3,2,1,0:T(8,128)(2,1)S(1)}, u32[]{:S(2)}, u32[]{:S(2)}) %collective-permute-start.23) | collective-permute-done | bytes 98336 | tf_op jit(solution)/shard_map/ppermute | solution.py:71
  144.3 5.5 %collective-permute-done.24 = bf16[2,2,64,384]{3,2,1,0:T(8,128)(2,1)S(1)} collective-permute-done((bf16[2,2,64,384]{3,2,1,0:T(8,128)(2,1)S(1)}, bf16[2,2,64,384]{3,2,1,0:T(8,128)(2,1)S(1)}, u32[]{:S(2)}, u32[]{:S(2)}) %collective-permute-start.24) | collective-permute-done | bytes 196640 | tf_op jit(solution)/shard_map/ppermute | solution.py:71
  152.2 4.9 %collective-permute-done.27 = bf16[1,4,64,384]{3,2,1,0:T(8,128)(2,1)S(1)} collective-permute-done((bf16[1,4,64,384]{3,2,1,0:T(8,128)(2,1)S(1)}, bf16[1,4,64,384]{3,2,1,0:T(8,128)(2,1)S(1)}, u32[]{:S(2)}, u32[]{:S(2)}) %collective-permute-start.27) | collective-permute-done | bytes 196640 | tf_op jit(solution)/shard_map/ppermute | solution.py:71
  164.1 2.6 %collective-permute-done.28 = bf16[2,4,64,384]{3,2,1,0:T(8,128)(2,1)S(1)} collective-permute-done((bf16[2,4,64,384]{3,2,1,0:T(8,128)(2,1)S(1)}, bf16[2,4,64,384]{3,2,1,0:T(8,128)(2,1)S(1)}, u32[]{:S(2)}, u32[]{:S(2)}) %collective-permute-start.28) | collective-permute-done | bytes 393248 | tf_op jit(solution)/shard_map/ppermute | solution.py:71
  173.8 3.3 %shard_map.156 = (bf16[2,256,320]{2,1,0:T(8,128)(2,1)}, f32[2,256,320]{2,1,0:T(8,128)}) custom-call(s32[2]{0:T(128)} %pad_add_fusion.me, bf16[2,256,320]{2,1,0:T(8,128)(2,1)} %get-tuple-element.36.hidden, f32[2,256,320]{2,1,0:T(8,128)} %get-tuple-element.37.base, bf16[4,32,320]{2,1,0:T(8,128)(2,1)} %pad_maximum_fusion.14.own, ...), custom_call_target="tpu_custom_call" | custom-call | tf_op jit(solution)/shard_map/pallas_call | solution.py:561
  177.1 2.3 %copy.93 = f32[2,2,128,320]{2,3,1,0:T(8,128)} copy(f32[2,2,128,320]{3,2,1,0:T(8,128)} %bitcast.78) | data formatting | bytes 1310720
  180.3 7.1 %shard_map.159 = (f32[1280,960]{1,0:T(8,128)}, f32[320,1280]{1,0:T(8,128)}) custom-call(bf16[384,1280]{1,0:T(8,128)(2,1)} %get-tuple-element.52.down, bf16[384,960]{1,0:T(8,128)(2,1)} %get-tuple-element.59.grad_mix, bf16[320,320]{1,0:T(8,128)(2,1)} %get-tuple-element.60.grad_att, bf16[1280,320]{1,0:T(8,128)(2,1)} %copy.82.w_up), custom_call_target="tpu_custom_call" | custom-call | tf_op jit(solution)/shard_map/pallas_call | solution.py:570
  187.4 5.8 %copy.94 = f32[1280,960]{0,1:T(8,128)} copy(f32[1280,960]{1,0:T(8,128)} %get-tuple-element.93) | data formatting | bytes 9830400
  195.0 5.2 %shard_map.158 = (f32[30,32,320]{2,1,0:T(8,128)}, f32[32,40,320]{2,1,0:T(8,128)}, f32[320,1280]{1,0:T(8,128)}, f32[320,1280]{1,0:T(8,128)}) custom-call(s32[2]{0:T(128)} %pad_add_fusion.me, f32[320,1]{1,0:T(8,128)} %copy.90.embed, bf16[4,4,64,384]{3,2,1,0:T(8,128)(2,1)} %copy-done.1, bf16[4,4,64,384]{3,2,1,0:T(8,128)(2,1)} %copy-done, ...), custom_call_target="tpu_custom_call" | custom-call | tf_op jit(solution)/shard_map/pallas_call | solution.py:598
  200.2 2.7 %copy.95 = f32[1280,320]{0,1:T(8,128)} copy(f32[1280,320]{1,0:T(8,128)} %bitcast.71) | data formatting | bytes 3276800
  (148 shorter events, 65.6 us)
Async XLA Ops:
  2.9 27.6 %collective-permute-start.1 = (bf16[2,256,320]{2,1,0:T(8,128)(2,1)}, bf16[2,256,320]{2,1,0:T(8,128)(2,1)}, u32[]{:S(2)}, u32[]{:S(2)}) collective-permute-start(bf16[2,256,320]{2,1,0:T(8,128)(2,1)} %pad_maximum_fusion.7), channel_id=1, source_target_pairs={{4,0},{8,4},{12,8},{16,12},{20,16},{24,20},{28,24},{5,1},{9,5},{13... | collective-permute-start | bytes 983048 | tf_op jit(solution)/shard_map/ppermute | solution.py:408
  5.4 34.2 %collective-permute-start = (bf16[2,256,320]{2,1,0:T(8,128)(2,1)}, bf16[2,256,320]{2,1,0:T(8,128)(2,1)}, u32[]{:S(2)}, u32[]{:S(2)}) collective-permute-start(bf16[2,256,320]{2,1,0:T(8,128)(2,1)} %pad_maximum_fusion.6), channel_id=1, source_target_pairs={{0,4},{4,8},{8,12},{12,16},{16,20},{20,24},{24,28},{1,5},{5,9},{9,... | collective-permute-start | bytes 983048 | tf_op jit(solution)/shard_map/ppermute | solution.py:407
  19.6 10.0 %collective-permute-start.3 = (bf16[2,6,16,320]{3,2,1,0:T(8,128)(2,1)}, bf16[2,6,16,320]{3,2,1,0:T(8,128)(2,1)S(1)}, u32[]{:S(2)}, u32[]{:S(2)}) collective-permute-start(bf16[2,6,16,320]{3,2,1,0:T(8,128)(2,1)} %pad_maximum_fusion.13), channel_id=1, source_target_pairs={{0,16},{4,20},{8,24},{12,28},{16,0},{20,4},{24,8},{28,12},{1,17},{... | collective-permute-start | bytes 368648 | tf_op jit(solution)/shard_map/ppermute | solution.py:71
  29.7 8.1 %collective-permute-start.4 = (bf16[2,12,16,320]{3,2,1,0:T(8,128)(2,1)S(1)}, bf16[2,12,16,320]{3,2,1,0:T(8,128)(2,1)S(1)}, u32[]{:S(2)}, u32[]{:S(2)}) collective-permute-start(bf16[2,12,16,320]{3,2,1,0:T(8,128)(2,1)S(1)} %pad_maximum_fusion.11), channel_id=1, source_target_pairs={{0,8},{4,12},{8,0},{12,4},{16,24},{20,28},{24,16},{28,20},{1,9},{5... | collective-permute-start | bytes 737288 | tf_op jit(solution)/shard_map/ppermute | solution.py:71
  37.9 17.7 %collective-permute-start.7 = (bf16[1,24,16,320]{3,2,1,0:T(8,128)(2,1)S(1)}, bf16[1,24,16,320]{3,2,1,0:T(8,128)(2,1)S(1)}, u32[]{:S(2)}, u32[]{:S(2)}) collective-permute-start(bf16[1,24,16,320]{3,2,1,0:T(8,128)(2,1)S(1)} %get-tuple-element.101), channel_id=1, source_target_pairs={{0,2},{1,3},{2,0},{3,1},{4,6},{5,7},{6,4},{7,5},{8,10},{9,11},{10,... | collective-permute-start | bytes 737288 | tf_op jit(solution)/shard_map/ppermute | solution.py:71
  46.4 9.9 %collective-permute-start.5 = (bf16[1,24,16,320]{3,2,1,0:T(8,128)(2,1)S(1)}, bf16[1,24,16,320]{3,2,1,0:T(8,128)(2,1)S(1)}, u32[]{:S(2)}, u32[]{:S(2)}) collective-permute-start(bf16[1,24,16,320]{3,2,1,0:T(8,128)(2,1)S(1)} %get-tuple-element.102), channel_id=1, source_target_pairs={{0,1},{1,0},{2,3},{3,2},{4,5},{5,4},{6,7},{7,6},{8,9},{9,8},{10,11... | collective-permute-start | bytes 737288 | tf_op jit(solution)/shard_map/ppermute | solution.py:71
  49.1 7.8 %collective-permute-start.17 = (bf16[2,2,128,320]{3,2,0,1:T(8,128)(2,1)S(1)}, bf16[2,2,128,320]{3,2,0,1:T(8,128)(2,1)S(1)}, u32[]{:S(2)}, u32[]{:S(2)}) collective-permute-start(bf16[2,2,128,320]{3,2,0,1:T(8,128)(2,1)S(1)} %bitcast.85), channel_id=1, source_target_pairs={{0,4},{4,0},{8,12},{12,8},{16,20},{20,16},{24,28},{28,24},{1,5},{5... | collective-permute-start | bytes 983048 | tf_op jit(solution)/shard_map/ppermute | solution.py:71
  55.7 15.8 %collective-permute-start.8 = (bf16[2,24,16,320]{3,2,1,0:T(8,128)(2,1)S(1)}, bf16[2,24,16,320]{3,2,1,0:T(8,128)(2,1)S(1)}, u32[]{:S(2)}, u32[]{:S(2)}) collective-permute-start(bf16[2,24,16,320]{3,2,1,0:T(8,128)(2,1)S(1)} %pad_maximum_fusion.5), channel_id=1, source_target_pairs={{0,1},{1,0},{2,3},{3,2},{4,5},{5,4},{6,7},{7,6},{8,9},{9,8},{10,11... | collective-permute-start | bytes 1474568 | tf_op jit(solution)/shard_map/ppermute | solution.py:71
  56.4 16.3 %collective-permute-start.6 = (bf16[2,24,16,320]{3,2,1,0:T(8,128)(2,1)S(1)}, bf16[2,24,16,320]{3,2,1,0:T(8,128)(2,1)S(1)}, u32[]{:S(2)}, u32[]{:S(2)}) collective-permute-start(bf16[2,24,16,320]{3,2,1,0:T(8,128)(2,1)S(1)} %pad_maximum_fusion.4), channel_id=1, source_target_pairs={{0,2},{1,3},{2,0},{3,1},{4,6},{5,7},{6,4},{7,5},{8,10},{9,11},{10,... | collective-permute-start | bytes 1474568 | tf_op jit(solution)/shard_map/ppermute | solution.py:71
  57.0 54.0 %collective-permute-start.18 = (bf16[2,128,320]{2,1,0:T(8,128)(2,1)S(1)}, bf16[2,128,320]{2,1,0:T(8,128)(2,1)S(1)}, u32[]{:S(2)}, u32[]{:S(2)}) collective-permute-start(bf16[2,128,320]{2,1,0:T(8,128)(2,1)S(1)} %dynamic-slice_bitcast_fusion), channel_id=1, source_target_pairs={{0,8},{4,12},{8,0},{12,4},{16,24},{20,28},{24,16},{28,20},{1,9},{5... | collective-permute-start | bytes 491528 | tf_op jit(solution)/shard_map/ppermute | solution.py:71
  109.2 11.4 %collective-permute-start.13 = (bf16[384,960]{0,1:T(8,128)(2,1)S(1)}, bf16[384,960]{0,1:T(8,128)(2,1)S(1)}, u32[]{:S(2)}, u32[]{:S(2)}) collective-permute-start(bf16[384,960]{0,1:T(8,128)(2,1)S(1)} %copy.83), channel_id=1, source_target_pairs={{0,4},{4,0},{8,12},{12,8},{16,20},{20,16},{24,28},{28,24},{1,5},{5... | collective-permute-start | bytes 2211848 | tf_op jit(solution)/shard_map/ppermute | solution.py:71
  111.1 8.7 %collective-permute-start.19 = (bf16[128,320]{1,0:T(8,128)(2,1)S(1)}, bf16[128,320]{1,0:T(8,128)(2,1)S(1)}, u32[]{:S(2)}, u32[]{:S(2)}) collective-permute-start(bf16[128,320]{1,0:T(8,128)(2,1)S(1)} %dynamic-slice_bitcast_fusion.4), channel_id=1, source_target_pairs={{0,16},{4,20},{8,24},{12,28},{16,0},{20,4},{24,8},{28,12},{1,17},{... | collective-permute-start | bytes 245768 | tf_op jit(solution)/shard_map/ppermute | solution.py:71
  114.3 7.4 %collective-permute-start.15 = (bf16[384,320]{1,0:T(8,128)(2,1)S(1)}, bf16[384,320]{1,0:T(8,128)(2,1)S(1)}, u32[]{:S(2)}, u32[]{:S(2)}) collective-permute-start(bf16[384,320]{1,0:T(8,128)(2,1)S(1)} %copy-done.12), channel_id=1, source_target_pairs={{0,4},{4,0},{8,12},{12,8},{16,20},{20,16},{24,28},{28,24},{1,5},{5... | collective-permute-start | bytes 737288 | tf_op jit(solution)/shard_map/ppermute | solution.py:71
  130.6 6.6 %collective-permute-start.21 = (bf16[128,384]{1,0:T(8,128)(2,1)S(1)}, bf16[128,384]{1,0:T(8,128)(2,1)S(1)}, u32[]{:S(2)}, u32[]{:S(2)}) collective-permute-start(bf16[128,384]{1,0:T(8,128)(2,1)S(1)} %get-tuple-element.106), channel_id=1, source_target_pairs={{0,2},{1,3},{2,0},{3,1},{4,6},{5,7},{6,4},{7,5},{8,10},{9,11},{10,... | collective-permute-start | bytes 294920 | tf_op jit(solution)/shard_map/ppermute | solution.py:71
  137.3 6.7 %collective-permute-start.23 = (bf16[2,1,64,384]{3,2,1,0:T(8,128)(2,1)S(1)}, bf16[2,1,64,384]{3,2,1,0:T(8,128)(2,1)S(1)}, u32[]{:S(2)}, u32[]{:S(2)}) collective-permute-start(bf16[2,1,64,384]{3,2,1,0:T(8,128)(2,1)S(1)} %bitcast.72), channel_id=1, source_target_pairs={{0,16},{4,20},{8,24},{12,28},{16,0},{20,4},{24,8},{28,12},{1,17},{... | collective-permute-start | bytes 294920 | tf_op jit(solution)/shard_map/ppermute | solution.py:71
  149.9 7.2 %collective-permute-start.27 = (bf16[1,4,64,384]{3,2,1,0:T(8,128)(2,1)S(1)}, bf16[1,4,64,384]{3,2,1,0:T(8,128)(2,1)S(1)}, u32[]{:S(2)}, u32[]{:S(2)}) collective-permute-start(bf16[1,4,64,384]{3,2,1,0:T(8,128)(2,1)S(1)} %get-tuple-element.103), channel_id=1, source_target_pairs={{0,2},{1,3},{2,0},{3,1},{4,6},{5,7},{6,4},{7,5},{8,10},{9,11},{10,... | collective-permute-start | bytes 589832 | tf_op jit(solution)/shard_map/ppermute | solution.py:71
  151.1 7.9 %collective-permute-start.25 = (bf16[1,4,64,384]{3,2,1,0:T(8,128)(2,1)S(1)}, bf16[1,4,64,384]{3,2,1,0:T(8,128)(2,1)S(1)}, u32[]{:S(2)}, u32[]{:S(2)}) collective-permute-start(bf16[1,4,64,384]{3,2,1,0:T(8,128)(2,1)S(1)} %get-tuple-element.104), channel_id=1, source_target_pairs={{0,1},{1,0},{2,3},{3,2},{4,5},{5,4},{6,7},{7,6},{8,9},{9,8},{10,11... | collective-permute-start | bytes 589832 | tf_op jit(solution)/shard_map/ppermute | solution.py:71
  157.2 9.6 %collective-permute-start.28 = (bf16[2,4,64,384]{3,2,1,0:T(8,128)(2,1)S(1)}, bf16[2,4,64,384]{3,2,1,0:T(8,128)(2,1)S(1)}, u32[]{:S(2)}, u32[]{:S(2)}) collective-permute-start(bf16[2,4,64,384]{3,2,1,0:T(8,128)(2,1)S(1)} %pad_maximum_fusion.10), channel_id=1, source_target_pairs={{0,1},{1,0},{2,3},{3,2},{4,5},{5,4},{6,7},{7,6},{8,9},{9,8},{10,11... | collective-permute-start | bytes 1179656 | tf_op jit(solution)/shard_map/ppermute | solution.py:71
  159.0 8.2 %collective-permute-start.26 = (bf16[2,4,64,384]{3,2,1,0:T(8,128)(2,1)S(1)}, bf16[2,4,64,384]{3,2,1,0:T(8,128)(2,1)S(1)}, u32[]{:S(2)}, u32[]{:S(2)}) collective-permute-start(bf16[2,4,64,384]{3,2,1,0:T(8,128)(2,1)S(1)} %pad_maximum_fusion.9), channel_id=1, source_target_pairs={{0,2},{1,3},{2,0},{3,1},{4,6},{5,7},{6,4},{7,5},{8,10},{9,11},{10,... | collective-permute-start | bytes 1179656 | tf_op jit(solution)/shard_map/ppermute | solution.py:71
  160.6 9.9 %collective-permute-start.10 = (bf16[6,2,16,320]{3,2,1,0:T(8,128)(2,1)}, bf16[6,2,16,320]{3,2,1,0:T(8,128)(2,1)}, u32[]{:S(2)}, u32[]{:S(2)}) collective-permute-start(bf16[6,2,16,320]{3,2,1,0:T(8,128)(2,1)} %get-tuple-element.100), channel_id=1, source_target_pairs={{0,2},{1,3},{2,0},{3,1},{4,6},{5,7},{6,4},{7,5},{8,10},{9,11},{10,... | collective-permute-start | bytes 368648 | tf_op jit(solution)/shard_map/ppermute | solution.py:71
  161.8 8.7 %collective-permute-start.11 = (bf16[6,2,16,320]{3,2,1,0:T(8,128)(2,1)S(1)}, bf16[6,2,16,320]{3,2,1,0:T(8,128)(2,1)}, u32[]{:S(2)}, u32[]{:S(2)}) collective-permute-start(bf16[6,2,16,320]{3,2,1,0:T(8,128)(2,1)S(1)} %get-tuple-element.99), channel_id=1, source_target_pairs={{0,3},{1,2},{2,1},{3,0},{4,7},{5,6},{6,5},{7,4},{8,11},{9,10},{10,... | collective-permute-start | bytes 368648 | tf_op jit(solution)/shard_map/ppermute | solution.py:71
  163.3 7.2 %collective-permute-start.9 = (bf16[6,2,16,320]{3,2,1,0:T(8,128)(2,1)S(1)}, bf16[6,2,16,320]{3,2,1,0:T(8,128)(2,1)}, u32[]{:S(2)}, u32[]{:S(2)}) collective-permute-start(bf16[6,2,16,320]{3,2,1,0:T(8,128)(2,1)S(1)} %get-tuple-element.98), channel_id=1, source_target_pairs={{0,1},{1,0},{2,3},{3,2},{4,5},{5,4},{6,7},{7,6},{8,9},{9,8},{10,11... | collective-permute-start | bytes 368648 | tf_op jit(solution)/shard_map/ppermute | solution.py:71
  166.8 26.3 %collective-permute-start.30 = (bf16[4,4,64,384]{3,2,1,0:T(8,128)(2,1)S(1)}, bf16[4,4,64,384]{3,2,1,0:T(8,128)(2,1)S(1)}, u32[]{:S(2)}, u32[]{:S(2)}) collective-permute-start(bf16[4,4,64,384]{3,2,1,0:T(8,128)(2,1)S(1)} %pad_maximum_fusion.3.refs_1_), channel_id=1, source_target_pairs={{0,4},{4,0},{8,12},{12,8},{16,20},{20,16},{24,28},{28,24},{1,5},{5... | collective-permute-start | bytes 2359304 | tf_op jit(solution)/shard_map/ppermute | solution.py:71
  167.3 25.9 %collective-permute-start.29 = (bf16[4,4,64,384]{3,2,1,0:T(8,128)(2,1)S(1)}, bf16[4,4,64,384]{3,2,1,0:T(8,128)(2,1)S(1)}, u32[]{:S(2)}, u32[]{:S(2)}) collective-permute-start(bf16[4,4,64,384]{3,2,1,0:T(8,128)(2,1)S(1)} %pad_maximum_fusion.2.refs_0_), channel_id=1, source_target_pairs={{0,4},{4,0},{8,12},{12,8},{16,20},{20,16},{24,28},{28,24},{1,5},{5... | collective-permute-start | bytes 2359304 | tf_op jit(solution)/shard_map/ppermute | solution.py:71
  (26 other events, 130.9 us)

commit v2 on v1

v2 whole, which is shorter than its diff:
```python
import functools
import math

import jax
import jax.numpy as jnp
from jax import lax
from jax.experimental import pallas as pl
from jax.experimental.pallas import tpu as pltpu
from jax.sharding import PartitionSpec as P

HD = 80
SLOT = 128
BF = jnp.bfloat16
F32 = jnp.float32


def nn(a, b):
    return lax.dot_general(a, b, (((1,), (0,)), ((), ())), preferred_element_type=F32)


def nt(a, b):
    return lax.dot_general(a, b, (((1,), (1,)), ((), ())), preferred_element_type=F32)


def tn(a, b):
    return lax.dot_general(a, b, (((0,), (0,)), ((), ())), preferred_element_type=F32)


def round_up(value, step):
    return -(-value // step) * step


def call(kernel, out_shape, **kw):
    return pl.pallas_call(
        kernel,
        out_shape=out_shape,
        compiler_params=pltpu.CompilerParams(vmem_limit_bytes=56 * 1024 * 1024),
        **kw,
    )


def smem():
    return pl.BlockSpec(memory_space=pltpu.SMEM)


def vmem():
    return pl.BlockSpec(memory_space=pltpu.VMEM)


def sds(shape, dtype):
    return jax.ShapeDtypeStruct(shape, dtype)


def bit_list(count):
    bits = []
    while (1 << len(bits)) < count:
        bits.append(1 << len(bits))
    return bits


def reversed_bits(value, count):
    n = len(bit_list(count))
    out = 0
    for i in range(n):
        out = out + (((value >> i) & 1) << (n - 1 - i))
    return out


def swap(x, axis, bit):
    n = lax.axis_size(axis)
    return lax.ppermute(x, axis, [(i, i ^ bit) for i in range(n)])


def time_embed(timestep, width):
    half = width // 2
    freqs = jnp.exp(-math.log(10000.0) * jnp.arange(half, dtype=F32) / half)
    angle = timestep.astype(F32)[0] * freqs
    return jax.nn.silu(jnp.concatenate([jnp.cos(angle), jnp.sin(angle)])).astype(BF)


def pool_matrix(half_c, columns):
    row = lax.broadcasted_iota(jnp.int32, (half_c, columns), 0)
    col = lax.broadcasted_iota(jnp.int32, (half_c, columns), 1)
    return jnp.where((col >> 1) == row, 1.0, 0.0).astype(BF)


def pool_kernel(me, clip, cot, keep, send, tmp):
    half_c = tmp.shape[1]
    half = half_c // 2
    quart = half // 2
    pool = pool_matrix(half_c, clip.shape[3])
    for t in range(2):
        tmp[t] = (nt(pool, clip[t, 0]) + nt(pool, clip[t, 1])) * 0.25
    tmp[2] = (nt(pool, cot[0, 0]) + nt(pool, cot[0, 1])) + (nt(pool, cot[1, 0]) + nt(pool, cot[1, 1]))
    core = me[0] & 1
    for color in range(2):
        for item in range(3):
            base = pl.multiple_of(core * half + color * quart, quart)
            keep[color, item] = tmp[item, pl.ds(base, quart), :].astype(BF)
            base = pl.multiple_of((1 - core) * half + color * quart, quart)
            send[color, item] = tmp[item, pl.ds(base, quart), :].astype(BF)


def edge_kernel(clip, cot, after, head, tail):
    del after
    for r in range(2):
        head[r] = clip[0, r]
        head[2 + r] = cot[0, r]
        tail[r] = clip[1, r]
        tail[2 + r] = cot[1, r]


def weight_kernel(w_down, w_embed, embed, w_qkv, w_out, w_up, down, mix, out_mix, direct):
    chans = w_down.shape[0]
    padded = down.shape[0]
    shift = nn(embed[...], w_embed[...])
    high = shift.astype(BF)
    low = (shift - high.astype(F32)).astype(BF)
    down[0:chans, :] = w_down[...]
    row = lax.broadcasted_iota(jnp.int32, (padded - chans, shift.shape[1]), 0)
    tail = jnp.where(row == 0, high.astype(F32), jnp.where(row == 1, low.astype(F32), 0.0))
    down[chans:padded, :] = tail.astype(BF)
    full = down[...]
    pieces = w_qkv.shape[0] // HD
    prod = nt(full, w_qkv[...])
    mix[...] = jnp.zeros(mix.shape, BF)
    for i in range(pieces):
        mix[:, i * SLOT : i * SLOT + HD] = prod[:, i * HD : (i + 1) * HD].astype(BF)
    up = w_up[...]
    small = nt(w_out[...], up)
    out_mix[...] = jnp.zeros(out_mix.shape, BF)
    for i in range(pieces // 3):
        out_mix[i * SLOT : i * SLOT + HD, :] = small[i * HD : (i + 1) * HD, :].astype(BF)
    direct[...] = nt(full, up).astype(BF)


def fine_kernel(clip, cot, lo, hi, w_time, hidden, base, taps, wide, grad):
    chans = w_time.shape[1]
    columns = clip.shape[3]
    for t in range(4):
        for r in range(2):
            at = slice((2 * t + r) * columns, (2 * t + r + 1) * columns)
            if t in (0, 3):
                halo = lo if t == 0 else hi
                wide[:, at] = halo[r]
                grad[:, at] = halo[2 + r]
            else:
                wide[:, at] = clip[t - 1, r]
                grad[:, at] = cot[t - 1, r]
    cells = 2 * columns
    taps[3 * chans :, :] = jnp.zeros((taps.shape[0] - 3 * chans, chans), BF)
    here = grad[:, cells : 3 * cells]
    for tap in range(3):
        taps[tap * chans : (tap + 1) * chans, :] = nt(wide[:, tap * cells : (tap + 2) * cells], here).astype(BF)
    acc = wide[:, cells : 3 * cells].astype(F32)
    back = here.astype(F32)
    for tap in range(3):
        acc = acc + tn(w_time[tap], wide[:, tap * cells : (tap + 2) * cells])
        back = back + nn(w_time[tap], grad[:, (2 - tap) * cells : (4 - tap) * cells])
    for t in range(2):
        for r in range(2):
            at = slice((2 * t + r) * columns, (2 * t + r + 1) * columns)
            hidden[t, r] = acc[:, at].astype(BF)
            base[t, r] = back[:, at]


def coarse_kernel(
    me, first, second, w_time, mix, out_mix, direct, q_rows, u_rows, o_rows, d_rows, taps,
    local, grad_mix, grad_att, keep, send,
    shifted, centre, pooled, upper, qkv, att_grad, att, qkv_grad, fields, spread_all, rows_down, rows_up, rows_tap,
    *, coarse_frames, heads_axis, rest,
):
    step = pl.program_id(0)
    frame = me[0]
    quart = first.shape[2]
    chans = first.shape[3]
    padded = pooled.shape[1]
    tokens = coarse_frames * quart
    total = 2 * tokens
    chips = coarse_frames // 2
    heads = att.shape[1] // SLOT
    scale = 1.0 / math.sqrt(HD)
    part = 1.0 / heads_axis
    here_rows = pl.ds(pl.multiple_of(step * total, total), total)

    @pl.when(step == 0)
    def _():
        lane = lax.broadcasted_iota(jnp.int32, (pooled.shape[0], padded - chans), 1)
        pooled[:, chans:padded] = jnp.where(lane < 2, 1.0, 0.0).astype(BF)
        shifted[:, 3 * chans :] = jnp.zeros((shifted.shape[0], shifted.shape[1] - 3 * chans), BF)

    def entry(index):
        gap = index ^ frame
        return (reversed_bits(gap >> 1, chips) * 2 + (gap & 1)) * 3

    for color, source in ((0, first), (1, second)):
        before = jnp.zeros((quart, chans), F32)
        here = source[0, entry(0)].astype(F32)
        for u in range(coarse_frames):
            at = entry(u)
            last = source[0, at + 1].astype(F32)
            after = source[0, entry(u + 1)].astype(F32) if u + 1 < coarse_frames else jnp.zeros((quart, chans), F32)
            offset = color * tokens + u * quart
            rows = pl.ds(pl.multiple_of(step * total + offset, quart), quart)
            mid = 0.5 * (here + last)
            shifted[rows, 0:chans] = (0.5 * (before + here)).astype(BF)
            shifted[rows, chans : 2 * chans] = mid.astype(BF)
            shifted[rows, 2 * chans : 3 * chans] = (0.5 * (last + after)).astype(BF)
            centre[offset : offset + quart, :] = mid
            upper[rows, :] = source[0, at + 2]
            before, here = last, after
    pool = (centre[...] + nn(shifted[here_rows, 0 : 3 * chans], w_time[...])).astype(BF)
    pooled[here_rows, 0:chans] = pool
    lines = pooled[here_rows, :]
    ups = upper[here_rows, :]
    qkv[...] = nn(lines, mix[...]).astype(BF)
    att_grad[...] = nt(ups, out_mix[...]).astype(BF)
    row = lax.broadcasted_iota(jnp.int32, (tokens, tokens), 0)
    col = lax.broadcasted_iota(jnp.int32, (tokens, tokens), 1)
    same = (row & (quart - 1)) == (col & (quart - 1))
    for color in range(2):
        rows = slice(color * tokens, (color + 1) * tokens)
        out = pl.ds(pl.multiple_of(step * total + color * tokens, tokens), tokens)
        for n in range(heads):
            q = qkv[rows, (3 * n) * SLOT : (3 * n + 1) * SLOT]
            k = qkv[rows, (3 * n + 1) * SLOT : (3 * n + 2) * SLOT]
            v = qkv[rows, (3 * n + 2) * SLOT : (3 * n + 3) * SLOT]
            da = att_grad[rows, n * SLOT : (n + 1) * SLOT]
            scores = jnp.where(same, nt(q, k) * scale, -jnp.inf)
            peak = jnp.max(scores, axis=1, keepdims=True)
            ex = jnp.exp(scores - peak)
            probs = ex * (1.0 / jnp.sum(ex, axis=1, keepdims=True))
            weights = probs.astype(BF)
            att[out, n * SLOT : (n + 1) * SLOT] = nn(weights, v).astype(BF)
            dw = nt(da, v)
            inner = jnp.sum(probs * dw, axis=1, keepdims=True)
            ds = (probs * (dw - inner) * scale).astype(BF)
            qkv_grad[out, (3 * n) * SLOT : (3 * n + 1) * SLOT] = nn(ds, k).astype(BF)
            qkv_grad[out, (3 * n + 1) * SLOT : (3 * n + 2) * SLOT] = tn(ds, q).astype(BF)
            qkv_grad[out, (3 * n + 2) * SLOT : (3 * n + 3) * SLOT] = tn(weights, da).astype(BF)
    lifted = nn(att[here_rows, :], out_mix[...]) + nn(lines, direct[...]) * part
    spread = nt(qkv_grad[here_rows, :], mix[...]) + nt(ups, direct[...]) * part
    spread = spread[:, 0:chans].astype(BF)
    spread_all[here_rows, :] = spread
    fields[0] = lifted.astype(BF).reshape(2 * coarse_frames, quart, chans)
    fields[1] = spread.reshape(2 * coarse_frames, quart, chans)
    mine = (frame >> 1) * 2
    for color in range(2):
        for i in range(2):
            local[0, i, color] = fields[0, color * coarse_frames + mine + i]
        for i in range(4):
            at = jnp.clip(mine + i - 1, 0, coarse_frames - 1)
            local[0, 2 + i, color] = fields[1, color * coarse_frames + at]

    @pl.when(step == heads_axis - 1)
    def _():
        g = tn(pooled[...], qkv_grad[...])
        for i in range(3 * heads):
            grad_mix[:, i * HD : (i + 1) * HD] = g[:, i * SLOT : i * SLOT + HD].astype(BF)
        a = tn(att[...], upper[...])
        for n in range(heads):
            grad_att[n * HD : (n + 1) * HD, :] = a[n * SLOT : n * SLOT + HD, :].astype(BF)
        s = tn(pooled[...], upper[...]).astype(BF)
        pair = rows_tap.shape[0]
        own = shifted[:, pl.ds(pl.multiple_of((frame >> 1) * pair, pair), pair)]
        rows_tap[:, 0:chans] = tn(own, spread_all[...])
        rows_tap[:, chans:] = jnp.zeros((pair, padded - chans), F32)
        rows_down[...] = nt(q_rows[...], grad_mix[...]) + nt(u_rows[...], s) * part
        rows_up[:, 0:chans] = nn(o_rows[...], grad_att[...]) + nn(d_rows[...], s) * part
        rows_up[:, chans:] = jnp.zeros((rows_up.shape[0], padded - chans), F32)
        core = frame & 1
        p1, r3, piece = rest
        extra = jnp.zeros((piece - 2 * p1 - r3, padded), F32)
        for dest, which in ((keep, core), (send, 1 - core)):
            for j in range(heads_axis):
                at = pl.ds(pl.multiple_of((which * heads_axis + j) * p1, p1), p1)
                tap = rows_tap[pl.ds(pl.multiple_of((which * heads_axis + j) * r3, r3), r3), :]
                if dest is keep:
                    more = jnp.concatenate([taps[j * r3 : (j + 1) * r3, :].astype(F32), jnp.zeros((r3, padded - chans), F32)], axis=1)
                    tap = tap + more
                parts = [rows_down[at, :], rows_up[at, :], tap]
                if piece > 2 * p1 + r3:
                    parts.append(extra)
                dest[j] = jnp.concatenate(parts, axis=0).astype(BF)


def order_kernel(me, keep, got, *outs):
    head = me[1]
    for d, out in enumerate(outs):
        at = head ^ d
        out[...] = (keep[at].astype(F32) + got[at].astype(F32)).astype(BF)


def sum_kernel(*refs):
    acc = refs[0][...].astype(F32)
    for ref in refs[1:-1]:
        acc = acc + ref[...].astype(F32)
    refs[-1][...] = acc.astype(BF)


def split_grad_kernel(down, mix_a, mix_b, att_a, att_b, w_up, qkv_out, att_out, flipped):
    @pl.when(pl.program_id(0) == 0)
    def _():
        flipped[...] = (mix_a[...].astype(F32) + mix_b[...].astype(F32)).T.astype(BF)

    qkv_out[...] = nn(flipped[...], down[...])
    att_out[...] = nn((att_a[...].astype(F32) + att_b[...].astype(F32)).astype(BF), w_up[...])


def finish_kernel(me, hidden, base, own, other, w_time, output, grad_clip, rows, *, coarse_frames):
    frame = me[0]
    core = frame & 1
    half = own.shape[1]
    columns = hidden.shape[3]
    for i in range(4):
        rows[i, pl.ds(pl.multiple_of(core * half, half), half), :] = own[i].astype(F32)
        rows[i, pl.ds(pl.multiple_of((1 - core) * half, half), half), :] = other[i].astype(F32)
    lift = pool_matrix(2 * half, columns)
    fine = tn(rows[0].astype(BF), lift)
    for t in range(2):
        for r in range(2):
            output[t, r] = (hidden[t, r].astype(F32) + fine).astype(BF)
    before = (rows[1] * jnp.where(frame == 0, 0.0, 1.0)).astype(BF)
    here = rows[2].astype(BF)
    after = (rows[3] * jnp.where(frame == coarse_frames - 1, 0.0, 1.0)).astype(BF)
    mid = rows[2] + nt(here, w_time[1])
    even = mid + nt(here, w_time[0]) + nt(before, w_time[2])
    odd = mid + nt(after, w_time[0]) + nt(here, w_time[2])
    for t, value in ((0, even), (1, odd)):
        high = value.astype(BF)
        low = (value - high.astype(F32)).astype(BF)
        add = (tn(high, lift) + tn(low, lift)) * 0.125
        for r in range(2):
            grad_clip[t, r] = base[t, r] + add


def gather_kernel(me, embed, *refs, layout, aligned):
    pieces = refs[:4]
    time_out, down_rows, up_rows = refs[4], refs[-2], refs[-1]
    frame, head = me[0], me[1]
    chips, heads_axis, r1, p1, r3 = layout
    chans = time_out.shape[2]
    devices = 2 * chips * heads_axis
    for core in range(2):
        for idx in range(chips * heads_axis):
            hi, zi = idx // chips, idx % chips
            colors = []
            for color in range(2):
                src = pieces[2 * core + color]
                off = hi if color == 0 else reversed_bits(hi, heads_axis)
                colors.append(src[off, zi].astype(F32))
            value = jnp.concatenate(colors, axis=0)
            owner = (frame ^ (reversed_bits(zi, chips) * 2 + core)) * heads_axis + (head ^ hi)
            down_rows[owner] = value[0:r1]
            up_rows[owner] = value[p1 : p1 + r1]

            @pl.when(owner < time_out.shape[0])
            def _():
                time_out[owner] = value[2 * p1 : 2 * p1 + r3, 0:chans]

    if aligned:
        down_out, embed_out, up_out = refs[5], refs[6], refs[7]
        lanes = down_rows.shape[2]
        eye = (lax.broadcasted_iota(jnp.int32, (lanes, lanes), 0) == lax.broadcasted_iota(jnp.int32, (lanes, lanes), 1))
        eye = eye.astype(F32).astype(BF)
        flipped = nt(eye, down_rows[...].reshape(devices * r1, lanes).astype(BF))
        down_out[...] = flipped[0:chans]
        embed_out[...] = embed[...] * flipped[chans : chans + 1]
        up_out[...] = nt(eye, up_rows[...].reshape(devices * r1, lanes).astype(BF))[0:chans]


def double(x, axis, bits, dim):
    for bit in bits:
        got = swap(x, axis, bit)
        x = jnp.concatenate([x, got], axis=dim)
    return x


def cross(first, second, bits):
    for a, b in zip(bits, reversed(bits)):
        first_in = swap(first, "heads", a)
        second_in = swap(second, "heads", b)
        first = jnp.concatenate([first, first_in], axis=0)
        second = jnp.concatenate([second, second_in], axis=0)
    return first, second


def body(clip, w_time, w_down, w_embed, w_qkv, w_out, w_up, timestep, cotangent):
    nf = lax.axis_size("frames")
    nh = lax.axis_size("heads")
    f = lax.axis_index("frames")
    h = lax.axis_index("heads")
    me = jnp.stack([f, h]).astype(jnp.int32)
    _, _, columns, chans = clip.shape
    width = w_down.shape[1]
    half_c = columns // 2
    half = half_c // 2
    quart = half // 2
    chips = nf // 2
    padded = round_up(chans + 2, 128)
    pieces = w_qkv.shape[1] // HD
    heads = pieces // 3
    chip_bits = [2 * b for b in reversed(bit_list(chips))]
    head_bits = bit_list(nh)
    devices = nf * nh

    clip_t = clip.transpose(0, 1, 3, 2)
    cot_t = cotangent.transpose(0, 1, 3, 2)
    w_qkv_t = w_qkv.T
    w_up_t = w_up.T

    keep, send = call(
        pool_kernel,
        [sds((2, 3, quart, chans), BF)] * 2,
        in_specs=[smem(), vmem(), vmem()],
        out_specs=[vmem()] * 2,
        scratch_shapes=[pltpu.VMEM((3, half_c, chans), F32)],
    )(me, clip_t, cot_t)
    keep_in = swap(send, "frames", 1)
    block = jnp.concatenate([keep, keep_in], axis=1)
    block = double(block, "frames", chip_bits, 1)
    first, second = cross(block[0][None], block[1][None], head_bits)

    embed = time_embed(timestep, w_embed.shape[0])
    down, mix, out_mix, direct = call(
        weight_kernel,
        [
            sds((padded, width), BF),
            sds((padded, pieces * SLOT), BF),
            sds((heads * SLOT, chans), BF),
            sds((padded, chans), BF),
        ],
    )(w_down, w_embed, embed[None, :], w_qkv_t, w_out, w_up_t)

    head, tail = call(
        edge_kernel,
        [sds((4, chans, columns), BF)] * 2,
        in_specs=[vmem(), vmem(), pl.BlockSpec(memory_space=pl.ANY)],
        out_specs=[vmem()] * 2,
    )(clip_t, cot_t, keep)
    lo = lax.ppermute(tail, "frames", [(i, i + 1) for i in range(nf - 1)])
    hi = lax.ppermute(head, "frames", [(i + 1, i) for i in range(nf - 1)])
    tap_rows = round_up(3 * chans, devices * 8)
    hidden, base, taps = call(
        fine_kernel,
        [
            sds(clip_t.shape, BF),
            sds(clip_t.shape, F32),
            sds((tap_rows, chans), BF),
        ],
        scratch_shapes=[pltpu.VMEM((chans, 8 * columns), BF)] * 2,
    )(clip_t, cot_t, lo, hi, w_time)
    share = tap_rows // nf
    bits = bit_list(nf)
    taps = taps.reshape([2] * len(bits) + [share, chans])
    for i in range(len(bits)):
        axis = len(bits) - 1 - i
        mine = (f >> i) & 1
        other = lax.dynamic_index_in_dim(taps, 1 - mine, axis, keepdims=False)
        same = lax.dynamic_index_in_dim(taps, mine, axis, keepdims=False)
        got = swap(other, "frames", 1 << i)
        taps = (same.astype(F32) + got.astype(F32)).astype(BF)

    chip_rows = 2 * width // nf
    r1 = width // devices
    p1 = round_up(r1, 8)
    r3 = share // nh
    piece_rows = round_up(2 * p1 + r3, 16)
    start = (f >> 1) * chip_rows

    def rows_of(x, axis):
        x = lax.dynamic_slice_in_dim(x, start, chip_rows, axis=axis)
        x = x.T if axis == 1 else x
        x = x.reshape(2 * nh, r1, x.shape[1])
        return jnp.pad(x, ((0, 0), (0, p1 - r1), (0, 0))).reshape(2 * nh * p1, x.shape[2])

    q_rows = rows_of(w_qkv, 0)
    u_rows = rows_of(w_up, 0)
    o_rows = rows_of(w_out, 1)
    d_rows = rows_of(down, 1)

    blk = pl.BlockSpec((1, nf * 3, quart, chans), lambda g: (g, 0, 0, 0))
    mirrored = pl.BlockSpec((1, nf * 3, quart, chans), lambda g: (reversed_bits(g, nh), 0, 0, 0))
    total = 2 * nf * quart
    every = nh * total

    def whole(*shape):
        return pl.BlockSpec(shape, lambda g: (0,) * len(shape))

    w_time2 = w_time.reshape(3 * chans, chans)
    statics = (w_time2, mix, out_mix, direct, q_rows, u_rows, o_rows, d_rows, taps)
    local, mix_g, att_g, d_keep, d_send = call(
        functools.partial(coarse_kernel, coarse_frames=nf, heads_axis=nh, rest=(p1, r3, piece_rows)),
        [
            sds((nh, 6, 2, quart, chans), BF),
            sds((padded, pieces * HD), BF),
            sds((heads * HD, chans), BF),
            sds((nh, piece_rows, padded), BF),
            sds((nh, piece_rows, padded), BF),
        ],
        grid=(nh,),
        in_specs=[smem(), blk, mirrored] + [whole(*x.shape) for x in statics],
        out_specs=[
            pl.BlockSpec((1, 6, 2, quart, chans), lambda g: (g, 0, 0, 0, 0)),
            whole(padded, pieces * HD),
            whole(heads * HD, chans),
            whole(nh, piece_rows, padded),
            whole(nh, piece_rows, padded),
        ],
        scratch_shapes=[
            pltpu.VMEM((every, tap_rows), BF),
            pltpu.VMEM((total, chans), F32),
            pltpu.VMEM((every, padded), BF),
            pltpu.VMEM((every, chans), BF),
            pltpu.VMEM((total, pieces * SLOT), BF),
            pltpu.VMEM((total, heads * SLOT), BF),
            pltpu.VMEM((every, heads * SLOT), BF),
            pltpu.VMEM((every, pieces * SLOT), BF),
            pltpu.VMEM((2, 2 * nf, quart, chans), BF),
            pltpu.VMEM((every, chans), BF),
            pltpu.VMEM((2 * nh * p1, padded), F32),
            pltpu.VMEM((2 * nh * p1, padded), F32),
            pltpu.VMEM((2 * share, padded), F32),
        ],
    )(me, first, second, *statics)

    d_got = swap(d_send, "frames", 1)
    ordered = call(
        order_kernel,
        [sds((piece_rows, padded), BF)] * nh,
        in_specs=[smem(), vmem(), vmem()],
        out_specs=[vmem()] * nh,
    )(me, d_keep, d_got)
    got = []
    for d in range(1, nh):
        got.append(swap(ordered[d], "heads", d))
    piece = call(sum_kernel, sds((piece_rows, padded), BF))(ordered[0], *got)
    piece = piece.reshape(2, 1, piece_rows // 2, padded)
    piece = double(piece, "frames", chip_bits, 1)
    p_first, p_second = cross(piece[0][None], piece[1][None], head_bits)
    q_first = swap(p_first, "frames", 1)
    q_second = swap(p_second, "frames", 1)

    got = []
    for d in range(1, nh):
        got.append(swap(local[d], "heads", d))
    own = call(sum_kernel, sds(local.shape[1:], BF))(local[0], *got)
    own = own.reshape(6, half, chans)
    core = f & 1

    def four(which):
        return jnp.concatenate(
            [
                lax.dynamic_slice_in_dim(own, which, 1, axis=0),
                lax.dynamic_slice_in_dim(own, 2 + which, 3, axis=0),
            ]
        )

    mine4 = four(core)
    other4 = swap(four(1 - core), "frames", 1)
    output, grad_clip = call(
        functools.partial(finish_kernel, coarse_frames=nf),
        [sds(clip_t.shape, BF), sds(clip_t.shape, F32)],
        in_specs=[smem()] + [vmem()] * 5,
        out_specs=[vmem()] * 2,
        scratch_shapes=[pltpu.VMEM((4, half_c, chans), F32)],
    )(me, hidden, base, mine4, other4, w_time)

    mix_o = swap(mix_g, "frames", 1)
    att_o = swap(att_g, "frames", 1)
    step = 256
    grad_qkv, grad_out = call(
        split_grad_kernel,
        [sds((pieces * HD, width), F32), sds((heads * HD, width), F32)],
        grid=(width // step,),
        in_specs=[
            pl.BlockSpec((padded, step), lambda g: (0, g)),
            whole(*mix_g.shape),
            whole(*mix_g.shape),
            whole(*att_g.shape),
            whole(*att_g.shape),
            pl.BlockSpec((chans, step), lambda g: (0, g)),
        ],
        out_specs=[
            pl.BlockSpec((pieces * HD, step), lambda g: (0, g)),
            pl.BlockSpec((heads * HD, step), lambda g: (0, g)),
        ],
        scratch_shapes=[pltpu.VMEM((pieces * HD, padded), BF)],
    )(down, mix_g, mix_o, att_g, att_o, w_up_t)

    output, grad_clip, grad_qkv, grad_out, q_second = lax.optimization_barrier(
        (output, grad_clip, grad_qkv, grad_out, q_second)
    )
    aligned = r1 % 8 == 0
    layout = (chips, nh, r1, p1, r3)
    outs = [sds((3 * chans // r3, r3, chans), F32)]
    table = (devices, r1, padded)
    scratch = []
    if aligned:
        outs += [sds((chans, width), F32), sds((w_embed.shape[0], width), F32), sds((chans, width), F32)]
        scratch = [pltpu.VMEM(table, F32)] * 2
    else:
        outs += [sds(table, F32)] * 2
    embed_col = embed.astype(F32)[:, None]
    got = call(
        functools.partial(gather_kernel, layout=layout, aligned=aligned),
        outs,
        in_specs=[smem()] + [vmem()] * 5,
        out_specs=[vmem()] * len(outs),
        scratch_shapes=scratch,
    )(me, embed_col, p_first, p_second, q_first, q_second)
    grad_time = got[0].reshape(w_time.shape)
    if aligned:
        grad_down, grad_embed, grad_up = got[1], got[2], got[3].T
    else:
        down_rows = got[1].reshape(width, padded)
        grad_down = down_rows[:, :chans].T
        grad_embed = embed_col * down_rows[:, chans][None, :]
        grad_up = got[2].reshape(width, padded)[:, :chans]
    return (
        output.transpose(0, 1, 3, 2),
        grad_clip.transpose(0, 1, 3, 2),
        grad_time,
        grad_down,
        grad_embed,
        grad_qkv.T,
        grad_out,
        grad_up,
    )


def solution(mesh):
    return jax.shard_map(
        body,
        mesh=mesh,
        in_specs=(
            P("frames", "heads", None, None),
            P(),
            P(),
            P(),
            P(None, "heads"),
            P("heads", None),
            P(),
            P(),
            P("frames", "heads", None, None),
        ),
        out_specs=(
            P("frames", "heads", None, None),
            P("frames", "heads", None, None),
            P(),
            P(),
            P(),
            P(None, "heads"),
            P("heads", None),
            P(),
        ),
        check_vma=False,
    )
```

time: 204 us -> 182 us (0.89)
  local copies, waits for them, and re-layouts: 37.8 us -> 21 us
  Pallas kernels: 66.4 us -> 70.8 us
  starting transfers between devices: 33.7 us -> 29.7 us
  other arithmetic: 13.4 us -> 10.3 us
    unnamed x49 -> x36, local copies, waits for them, and re-layouts: 23.1 us -> 8.6 us
    pallas_call x8 -> x11, Pallas kernels: 66.4 us -> 70.8 us  [the longest x1 35.4 us: body(): call(functools.partial(coarse_kernel, coarse_frames=nf, heads_axis=nh, re...]
    convert_element_type x9 -> x4, other arithmetic: 5.01 us -> 0.92 us  [the longest x3 0.85 us: body(): taps = (same.astype(F32) + got.astype(F32)).astype(BF)]
    squeeze x6 -> x3, local copies, waits for them, and re-layouts: 4.4 us -> 0.88 us  [the longest x1 0.83 us: body(): got.append(swap(local[d], 'heads', d))]
    concatenate x13 -> x12, other arithmetic: 4.76 us -> 7.37 us  [the longest x4 3.2 us: cross(): second = jnp.concatenate([second, second_in], axis=0)]
    ppermute x29 -> x28, starting transfers between devices: 28.7 us -> 26.5 us  [swap(): return lax.ppermute(x, axis, [(i, i ^ bit) for i in range(n)])]
    ppermute x29 -> x28, waiting for transfers between devices: 49.8 us -> 48 us  [swap(): return lax.ppermute(x, axis, [(i, i ^ bit) for i in range(n)])]
    dynamic_slice x4 -> x5, local copies, waits for them, and re-layouts: 4.73 us -> 5.03 us  [the longest x3 3.79 us: rows_of(): x = lax.dynamic_slice_in_dim(x, start, chip_rows, axis=axis)]
  transfers between devices with their start and end apart: 31 -> 30, of which waited for: 13 -> 17; matrix products, arithmetic and copies ran while one was open for 20% -> 13% of each run, Pallas kernels for 28% -> 13%
where the time goes in v2:
time: 182 us
  Pallas kernels  70.8 us (39%)
  waiting for transfers between devices  48 us (26%)
  starting transfers between devices  29.7 us (16%)
  local copies, waits for them, and re-layouts  21 us (12%)
  other arithmetic  10.3 us (6%)
    ppermute x28, waiting for transfers between devices, swap(): return lax.ppermute(x, axis, [(i, i ^ bit) for i in range(n)])  48 us
    pallas_call x1, Pallas kernels, body(): call(functools.partial(coarse_kernel, coarse_frames=nf, heads_axis=nh, re...  35.4 us
    ppermute x28, starting transfers between devices, swap(): return lax.ppermute(x, axis, [(i, i ^ bit) for i in range(n)])  26.5 us
    unnamed x36, local copies, waits for them, and re-layouts  8.6 us
    pallas_call x1, Pallas kernels, body(): call(split_grad_kernel, [sds((pieces * HD, width), F32), sds((heads * HD,...  7.45 us
    pallas_call x1, Pallas kernels, body(): call(weight_kernel, [sds((padded, width), BF), sds((padded, pieces * SLOT...  5.65 us
    pallas_call x1, Pallas kernels, body(): call(functools.partial(gather_kernel, layout=layout, aligned=aligned), ou...  5.31 us
    pallas_call x1, Pallas kernels, body(): call(fine_kernel, [sds(clip_t.shape, BF), sds(clip_t.shape, F32), sds((ta...  4.36 us
  transfers between devices with their start and end apart: 30, of which 17 were waited for; matrix products, arithmetic and copies ran while one was open for 13% of the time, Pallas kernels for 13%

profile of v2, /device:TPU:0, one launch (start us, length us, event | category | flops | bytes accessed | tf_op | source)
XLA Modules:
  0.0 181.5 jit_solution(4173268950472017968)
XLA Ops:
  1.3 2.1 %shard_map.152 = (bf16[2,3,16,320]{3,2,1,0:T(8,128)(2,1)}, bf16[2,3,16,320]{3,2,1,0:T(8,128)(2,1)}) custom-call(s32[2]{0:T(128)} %pad_add_fusion.me, bf16[2,2,320,128]{3,2,1,0:T(8,128)(2,1)} %bitcast.53, bf16[2,2,320,128]{3,2,1,0:T(8,128)(2,1)} %bitcast.56), custom_call_target="tpu_custom_call" | custom-call | tf_op jit(solution)/shard_map/pallas_call | solution.py:412
  3.9 1.9 %shard_map.153 = (bf16[4,320,128]{2,1,0:T(8,128)(2,1)}, bf16[4,320,128]{2,1,0:T(8,128)(2,1)}) custom-call(bf16[2,2,320,128]{3,2,1,0:T(8,128)(2,1)} %bitcast.54, bf16[2,2,320,128]{3,2,1,0:T(8,128)(2,1)} %bitcast.57, bf16[2,3,16,320]{3,2,1,0:T(8,128)(2,1)} %get-tuple-element.41.after), custom_call_target="tpu_custom_call" | custom-call | tf_op jit(solution)/shard_map/pallas_call | solution.py:435
  5.8 1.9 %collective-permute-start = (bf16[4,320,128]{2,1,0:T(8,128)(2,1)}, bf16[4,320,128]{2,1,0:T(8,128)(2,1)S(1)}, u32[]{:S(2)}, u32[]{:S(2)}) collective-permute-start(bf16[4,320,128]{2,1,0:T(8,128)(2,1)} %get-tuple-element.42), channel_id=1, source_target_pairs={{0,4},{4,8},{8,12},{12,16},{16,20},{20,24},{24,28},{1,5},{5,9},{9,... | collective-permute-start | bytes 983048 | tf_op jit(solution)/shard_map/ppermute | solution.py:441
  14.5 6.0 %collective-permute-start.3 = (bf16[2,6,16,320]{3,2,1,0:T(8,128)(2,1)S(1)}, bf16[2,6,16,320]{3,2,1,0:T(8,128)(2,1)S(1)}, u32[]{:S(2)}, u32[]{:S(2)}) collective-permute-start(bf16[2,6,16,320]{3,2,1,0:T(8,128)(2,1)S(1)} %pad_maximum_fusion.11), channel_id=1, source_target_pairs={{0,16},{4,20},{8,24},{12,28},{16,0},{20,4},{24,8},{28,12},{1,17},{... | collective-permute-start | bytes 368648 | tf_op jit(solution)/shard_map/ppermute | solution.py:71
  24.0 5.7 %shard_map.155 = (bf16[384,1280]{1,0:T(8,128)(2,1)}, bf16[384,1536]{1,0:T(8,128)(2,1)}, bf16[512,320]{1,0:T(8,128)(2,1)}, bf16[384,320]{1,0:T(8,128)(2,1)}) custom-call(bf16[320,1280]{1,0:T(8,128)(2,1)} %w_down.1, bf16[320,1280]{1,0:T(8,128)(2,1)} %w_embed.1, bf16[1,320]{1,0:T(2,128)(2,1)} %fusion.3.embed, bf16[960,1280]{1,0:T(8,128)(2,1)} %bitcast.52, ...), custom_call_target="tpu_custom_call" | custom-call | tf_op jit(solution)/shard_map/pallas_call | solution.py:425
  34.3 4.4 %shard_map.154 = (bf16[2,2,320,128]{3,2,1,0:T(8,128)(2,1)}, f32[2,2,320,128]{3,2,1,0:T(8,128)}, bf16[1024,320]{1,0:T(8,128)(2,1)}) custom-call(bf16[2,2,320,128]{3,2,1,0:T(8,128)(2,1)} %bitcast.55, bf16[2,2,320,128]{3,2,1,0:T(8,128)(2,1)} %bitcast.58, bf16[4,320,128]{2,1,0:T(8,128)(2,1)} %copy-done.6, bf16[4,320,128]{2,1,0:T(8,128)(2,1)} %copy-done.7, ...), custom_call_target="tpu_custom_call" | custom-call | tf_op jit(solution)/shard_map/pallas_call | solution.py:444
  44.2 5.5 %collective-permute-done.7 = bf16[1,24,16,320]{3,2,1,0:T(8,128)(2,1)S(1)} collective-permute-done((bf16[1,24,16,320]{3,2,1,0:T(8,128)(2,1)S(1)}, bf16[1,24,16,320]{3,2,1,0:T(8,128)(2,1)S(1)}, u32[]{:S(2)}, u32[]{:S(2)}) %collective-permute-start.7) | collective-permute-done | bytes 245792 | tf_op jit(solution)/shard_map/ppermute | solution.py:71
  54.4 5.5 %collective-permute-done.11 = bf16[128,320]{1,0:T(8,128)(2,1)S(1)} collective-permute-done((bf16[128,320]{1,0:T(8,128)(2,1)S(1)}, bf16[128,320]{1,0:T(8,128)(2,1)S(1)}, u32[]{:S(2)}, u32[]{:S(2)}) %collective-permute-start.11) | collective-permute-done | bytes 81952 | tf_op jit(solution)/shard_map/ppermute | solution.py:71
  60.5 4.1 %collective-permute-done.8 = bf16[2,24,16,320]{3,2,1,0:T(8,128)(2,1)S(1)} collective-permute-done((bf16[2,24,16,320]{3,2,1,0:T(8,128)(2,1)S(1)}, bf16[2,24,16,320]{3,2,1,0:T(8,128)(2,1)S(1)}, u32[]{:S(2)}, u32[]{:S(2)}) %collective-permute-start.8) | collective-permute-done | bytes 491552 | tf_op jit(solution)/shard_map/ppermute | solution.py:71
  67.3 35.4 %shard_map.156 = (bf16[4,6,2,16,320]{4,3,2,1,0:T(8,128)(2,1)}, bf16[384,960]{1,0:T(8,128)(2,1)}, bf16[320,320]{1,0:T(8,128)(2,1)}, bf16[4,112,384]{2,1,0:T(8,128)(2,1)}, bf16[4,112,384]{2,1,0:T(8,128)(2,1)}) custom-call(s32[2]{0:T(128)} %pad_add_fusion.me, bf16[4,24,16,320]{3,2,1,0:T(8,128)(2,1)} %pad_maximum_fusion.first, ...), custom_call_target="tpu_custom_call" | custom-call | tf_op jit(solution)/shard_map/pallas_call | solution.py:492
  102.8 1.9 %collective-permute-done.18.got = bf16[4,112,384]{2,1,0:T(8,128)(2,1)S(1)} collective-permute-done((bf16[4,112,384]{2,1,0:T(8,128)(2,1)}, bf16[4,112,384]{2,1,0:T(8,128)(2,1)S(1)}, u32[]{:S(2)}, u32[]{:S(2)}) %collective-permute-start.18) | collective-permute-done | bytes 344096 | tf_op jit(solution)/shard_map/ppermute | solution.py:71
  105.4 1.8 %shard_map.160 = (bf16[112,384]{1,0:T(8,128)(2,1)}, bf16[112,384]{1,0:T(8,128)(2,1)}, bf16[112,384]{1,0:T(8,128)(2,1)}, bf16[112,384]{1,0:T(8,128)(2,1)}) custom-call(s32[2]{0:T(128)} %pad_add_fusion.me, bf16[4,112,384]{2,1,0:T(8,128)(2,1)} %get-tuple-element.59.keep, bf16[4,112,384]{2,1,0:T(8,128)(2,1)} %copy-done.5), custom_call_target="tpu_custom_call" | custom-call | tf_op jit(solution)/shard_map/pallas_call | solution.py:528
  112.0 2.3 %collective-permute-done.20.refs_2_ = bf16[112,384]{1,0:T(8,128)(2,1)S(1)} collective-permute-done((bf16[112,384]{1,0:T(8,128)(2,1)}, bf16[112,384]{1,0:T(8,128)(2,1)S(1)}, u32[]{:S(2)}, u32[]{:S(2)}) %collective-permute-start.20) | collective-permute-done | bytes 86048 | tf_op jit(solution)/shard_map/ppermute | solution.py:71
  116.4 1.7 shard_map.161
  118.5 6.0 %collective-permute-done.22 = bf16[2,1,56,384]{3,2,1,0:T(8,128)(2,1)S(1)} collective-permute-done((bf16[2,1,56,384]{3,2,1,0:T(8,128)(2,1)}, bf16[2,1,56,384]{3,2,1,0:T(8,128)(2,1)S(1)}, u32[]{:S(2)}, u32[]{:S(2)}) %collective-permute-start.22) | collective-permute-done | bytes 86048 | tf_op jit(solution)/shard_map/ppermute | solution.py:71
  125.5 5.4 %collective-permute-done.23 = bf16[2,2,56,384]{3,2,1,0:T(8,128)(2,1)S(1)} collective-permute-done((bf16[2,2,56,384]{3,2,1,0:T(8,128)(2,1)S(1)}, bf16[2,2,56,384]{3,2,1,0:T(8,128)(2,1)S(1)}, u32[]{:S(2)}, u32[]{:S(2)}) %collective-permute-start.23) | collective-permute-done | bytes 172064 | tf_op jit(solution)/shard_map/ppermute | solution.py:71
  133.6 3.8 %collective-permute-done.24 = bf16[1,4,56,384]{3,2,1,0:T(8,128)(2,1)S(1)} collective-permute-done((bf16[1,4,56,384]{3,2,1,0:T(8,128)(2,1)S(1)}, bf16[1,4,56,384]{3,2,1,0:T(8,128)(2,1)S(1)}, u32[]{:S(2)}, u32[]{:S(2)}) %collective-permute-start.24) | collective-permute-done | bytes 172064 | tf_op jit(solution)/shard_map/ppermute | solution.py:71
  144.4 2.4 %collective-permute-done.25 = bf16[2,4,56,384]{3,2,1,0:T(8,128)(2,1)} collective-permute-done((bf16[2,4,56,384]{3,2,1,0:T(8,128)(2,1)}, bf16[2,4,56,384]{3,2,1,0:T(8,128)(2,1)}, u32[]{:S(2)}, u32[]{:S(2)}) %collective-permute-start.25) | collective-permute-done | bytes 344096 | tf_op jit(solution)/shard_map/ppermute | solution.py:71
  148.0 2.0 %collective-permute-done.28 = bf16[2,4,56,384]{3,2,1,0:T(8,128)(2,1)S(1)} collective-permute-done((bf16[2,4,56,384]{3,2,1,0:T(8,128)(2,1)}, bf16[2,4,56,384]{3,2,1,0:T(8,128)(2,1)S(1)}, u32[]{:S(2)}, u32[]{:S(2)}) %collective-permute-start.28) | collective-permute-done | bytes 344096 | tf_op jit(solution)/shard_map/ppermute | solution.py:71
  153.0 3.6 %collective-permute-done.13.refs_2_ = bf16[6,2,16,320]{3,2,1,0:T(8,128)(2,1)S(1)} collective-permute-done((bf16[6,2,16,320]{3,2,1,0:T(8,128)(2,1)}, bf16[6,2,16,320]{3,2,1,0:T(8,128)(2,1)S(1)}, u32[]{:S(2)}, u32[]{:S(2)}) %collective-permute-start.13) | collective-permute-done | bytes 122912 | tf_op jit(solution)/shard_map/ppermute | solution.py:71
  158.1 1.9 %shard_map.157 = bf16[6,2,16,320]{3,2,1,0:T(8,128)(2,1)} custom-call(bf16[6,2,16,320]{3,2,1,0:T(8,128)(2,1)} %get-tuple-element.79.refs_0_, bf16[6,2,16,320]{3,2,1,0:T(8,128)(2,1)} %copy-done.10, bf16[6,2,16,320]{3,2,1,0:T(8,128)(2,1)} %copy-done.9, bf16[6,2,16,320]{3,2,1,0:T(8,128)(2,1)} %collective-permute-done.14.refs_3_), custom_call_target="tpu_custom_call" | custom-call | tf_op jit(solution)/shard_map/pallas_call | solution.py:547
  163.7 3.1 %shard_map.158 = (bf16[2,2,320,128]{3,2,1,0:T(8,128)(2,1)}, f32[2,2,320,128]{3,2,1,0:T(8,128)}) custom-call(s32[2]{0:T(128)} %pad_add_fusion.me, bf16[2,2,320,128]{3,2,1,0:T(8,128)(2,1)} %get-tuple-element.44.hidden, f32[2,2,320,128]{3,2,1,0:T(8,128)} %get-tuple-element.45.base, bf16[4,32,320]{2,1,0:T(8,128)(2,1)} %pad_maximum_fusion.12.own, ...), custom_call_target="tpu_custom_call" | custom-call | tf_op jit(solution)/shard_map/pallas_call | solution.py:561
  168.7 7.4 %shard_map.159 = (f32[960,1280]{1,0:T(8,128)}, f32[320,1280]{1,0:T(8,128)}) custom-call(bf16[384,1280]{1,0:T(8,128)(2,1)} %get-tuple-element.50.down, bf16[384,960]{1,0:T(8,128)(2,1)} %get-tuple-element.55.mix_a, bf16[384,960]{1,0:T(8,128)(2,1)} %copy.50.mix_b, bf16[320,320]{1,0:T(8,128)(2,1)} %get-tuple-element.56.att_a, bf16[320,320]{1,0:T(8,128)(2,1)} %copy-done.8, ...), custom_call_target="tpu_custom_call" | custom-call | tf_op jit(solution)/shard_map/pallas_call | solution.py:572
  176.2 5.3 %shard_map.162 = (f32[30,32,320]{2,1,0:T(8,128)}, f32[320,1280]{1,0:T(8,128)}, f32[320,1280]{1,0:T(8,128)}, f32[320,1280]{1,0:T(8,128)}) custom-call(s32[2]{0:T(128)} %pad_add_fusion.me, f32[320,1]{1,0:T(8,128)} %copy.51.embed, bf16[4,4,56,384]{3,2,1,0:T(8,128)(2,1)} %copy-done.2, bf16[4,4,56,384]{3,2,1,0:T(8,128)(2,1)} %copy-done.1, ...), custom_call_target="tpu_custom_call" | custom-call | tf_op jit(solution)/shard_map/pallas_call | solution.py:605
  (122 shorter events, 58.8 us)
Async XLA Ops:
  3.4 11.1 %collective-permute-start.2 = (bf16[2,3,16,320]{3,2,1,0:T(8,128)(2,1)}, bf16[2,3,16,320]{3,2,1,0:T(8,128)(2,1)S(1)}, u32[]{:S(2)}, u32[]{:S(2)}) collective-permute-start(bf16[2,3,16,320]{3,2,1,0:T(8,128)(2,1)} %get-tuple-element.46), channel_id=1, source_target_pairs={{0,4},{4,0},{8,12},{12,8},{16,20},{20,16},{24,28},{28,24},{1,5},{5... | collective-permute-start | bytes 184328 | tf_op jit(solution)/shard_map/ppermute | solution.py:71
  5.8 27.1 %collective-permute-start = (bf16[4,320,128]{2,1,0:T(8,128)(2,1)}, bf16[4,320,128]{2,1,0:T(8,128)(2,1)S(1)}, u32[]{:S(2)}, u32[]{:S(2)}) collective-permute-start(bf16[4,320,128]{2,1,0:T(8,128)(2,1)} %get-tuple-element.42), channel_id=1, source_target_pairs={{0,4},{4,8},{8,12},{12,16},{16,20},{20,24},{24,28},{1,5},{5,9},{9,... | collective-permute-start | bytes 983048 | tf_op jit(solution)/shard_map/ppermute | solution.py:441
  7.8 25.1 %collective-permute-start.1 = (bf16[4,320,128]{2,1,0:T(8,128)(2,1)}, bf16[4,320,128]{2,1,0:T(8,128)(2,1)S(1)}, u32[]{:S(2)}, u32[]{:S(2)}) collective-permute-start(bf16[4,320,128]{2,1,0:T(8,128)(2,1)} %get-tuple-element.43), channel_id=1, source_target_pairs={{4,0},{8,4},{12,8},{16,12},{20,16},{24,20},{28,24},{5,1},{9,5},{13... | collective-permute-start | bytes 983048 | tf_op jit(solution)/shard_map/ppermute | solution.py:442
  14.5 16.7 %collective-permute-start.3 = (bf16[2,6,16,320]{3,2,1,0:T(8,128)(2,1)S(1)}, bf16[2,6,16,320]{3,2,1,0:T(8,128)(2,1)S(1)}, u32[]{:S(2)}, u32[]{:S(2)}) collective-permute-start(bf16[2,6,16,320]{3,2,1,0:T(8,128)(2,1)S(1)} %pad_maximum_fusion.11), channel_id=1, source_target_pairs={{0,16},{4,20},{8,24},{12,28},{16,0},{20,4},{24,8},{28,12},{1,17},{... | collective-permute-start | bytes 368648 | tf_op jit(solution)/shard_map/ppermute | solution.py:71
  31.4 8.7 %collective-permute-start.4 = (bf16[2,12,16,320]{3,2,1,0:T(8,128)(2,1)S(1)}, bf16[2,12,16,320]{3,2,1,0:T(8,128)(2,1)S(1)}, u32[]{:S(2)}, u32[]{:S(2)}) collective-permute-start(bf16[2,12,16,320]{3,2,1,0:T(8,128)(2,1)S(1)} %pad_maximum_fusion.9), channel_id=1, source_target_pairs={{0,8},{4,12},{8,0},{12,4},{16,24},{20,28},{24,16},{28,20},{1,9},{5... | collective-permute-start | bytes 737288 | tf_op jit(solution)/shard_map/ppermute | solution.py:71
  40.2 9.5 %collective-permute-start.7 = (bf16[1,24,16,320]{3,2,1,0:T(8,128)(2,1)S(1)}, bf16[1,24,16,320]{3,2,1,0:T(8,128)(2,1)S(1)}, u32[]{:S(2)}, u32[]{:S(2)}) collective-permute-start(bf16[1,24,16,320]{3,2,1,0:T(8,128)(2,1)S(1)} %get-tuple-element.80), channel_id=1, source_target_pairs={{0,2},{1,3},{2,0},{3,1},{4,6},{5,7},{6,4},{7,5},{8,10},{9,11},{10,... | collective-permute-start | bytes 737288 | tf_op jit(solution)/shard_map/ppermute | solution.py:71
  41.8 9.6 %collective-permute-start.5 = (bf16[1,24,16,320]{3,2,1,0:T(8,128)(2,1)S(1)}, bf16[1,24,16,320]{3,2,1,0:T(8,128)(2,1)S(1)}, u32[]{:S(2)}, u32[]{:S(2)}) collective-permute-start(bf16[1,24,16,320]{3,2,1,0:T(8,128)(2,1)S(1)} %get-tuple-element.81), channel_id=1, source_target_pairs={{0,1},{1,0},{2,3},{3,2},{4,5},{5,4},{6,7},{7,6},{8,9},{9,8},{10,11... | collective-permute-start | bytes 737288 | tf_op jit(solution)/shard_map/ppermute | solution.py:71
  43.4 9.6 %collective-permute-start.10 = (bf16[2,128,320]{2,1,0:T(8,128)(2,1)S(1)}, bf16[2,128,320]{2,1,0:T(8,128)(2,1)S(1)}, u32[]{:S(2)}, u32[]{:S(2)}) collective-permute-start(bf16[2,128,320]{2,1,0:T(8,128)(2,1)S(1)} %dynamic-slice_bitcast_fusion.1), channel_id=1, source_target_pairs={{0,8},{4,12},{8,0},{12,4},{16,24},{20,28},{24,16},{28,20},{1,9},{5... | collective-permute-start | bytes 491528 | tf_op jit(solution)/shard_map/ppermute | solution.py:71
  49.8 14.9 %collective-permute-start.8 = (bf16[2,24,16,320]{3,2,1,0:T(8,128)(2,1)S(1)}, bf16[2,24,16,320]{3,2,1,0:T(8,128)(2,1)S(1)}, u32[]{:S(2)}, u32[]{:S(2)}) collective-permute-start(bf16[2,24,16,320]{3,2,1,0:T(8,128)(2,1)S(1)} %pad_maximum_fusion.5), channel_id=1, source_target_pairs={{0,1},{1,0},{2,3},{3,2},{4,5},{5,4},{6,7},{7,6},{8,9},{9,8},{10,11... | collective-permute-start | bytes 1474568 | tf_op jit(solution)/shard_map/ppermute | solution.py:71
  51.4 14.6 %collective-permute-start.6 = (bf16[2,24,16,320]{3,2,1,0:T(8,128)(2,1)S(1)}, bf16[2,24,16,320]{3,2,1,0:T(8,128)(2,1)S(1)}, u32[]{:S(2)}, u32[]{:S(2)}) collective-permute-start(bf16[2,24,16,320]{3,2,1,0:T(8,128)(2,1)S(1)} %pad_maximum_fusion.4), channel_id=1, source_target_pairs={{0,2},{1,3},{2,0},{3,1},{4,6},{5,7},{6,4},{7,5},{8,10},{9,11},{10,... | collective-permute-start | bytes 1474568 | tf_op jit(solution)/shard_map/ppermute | solution.py:71
  53.1 6.7 %collective-permute-start.11 = (bf16[128,320]{1,0:T(8,128)(2,1)S(1)}, bf16[128,320]{1,0:T(8,128)(2,1)S(1)}, u32[]{:S(2)}, u32[]{:S(2)}) collective-permute-start(bf16[128,320]{1,0:T(8,128)(2,1)S(1)} %dynamic-slice_bitcast_fusion.2), channel_id=1, source_target_pairs={{0,16},{4,20},{8,24},{12,28},{16,0},{20,4},{24,8},{28,12},{1,17},{... | collective-permute-start | bytes 245768 | tf_op jit(solution)/shard_map/ppermute | solution.py:71
  108.6 5.7 %collective-permute-start.20 = (bf16[112,384]{1,0:T(8,128)(2,1)}, bf16[112,384]{1,0:T(8,128)(2,1)S(1)}, u32[]{:S(2)}, u32[]{:S(2)}) collective-permute-start(bf16[112,384]{1,0:T(8,128)(2,1)} %get-tuple-element.63), channel_id=1, source_target_pairs={{0,2},{1,3},{2,0},{3,1},{4,6},{5,7},{6,4},{7,5},{8,10},{9,11},{10,... | collective-permute-start | bytes 258056 | tf_op jit(solution)/shard_map/ppermute | solution.py:71
  110.1 5.6 %collective-permute-start.21 = (bf16[112,384]{1,0:T(8,128)(2,1)}, bf16[112,384]{1,0:T(8,128)(2,1)S(1)}, u32[]{:S(2)}, u32[]{:S(2)}) collective-permute-start(bf16[112,384]{1,0:T(8,128)(2,1)} %get-tuple-element.64), channel_id=1, source_target_pairs={{0,3},{1,2},{2,1},{3,0},{4,7},{5,6},{6,5},{7,4},{8,11},{9,10},{10,... | collective-permute-start | bytes 258056 | tf_op jit(solution)/shard_map/ppermute | solution.py:71
  118.1 6.5 %collective-permute-start.22 = (bf16[2,1,56,384]{3,2,1,0:T(8,128)(2,1)}, bf16[2,1,56,384]{3,2,1,0:T(8,128)(2,1)S(1)}, u32[]{:S(2)}, u32[]{:S(2)}) collective-permute-start(bf16[2,1,56,384]{3,2,1,0:T(8,128)(2,1)} %bitcast.63), channel_id=1, source_target_pairs={{0,16},{4,20},{8,24},{12,28},{16,0},{20,4},{24,8},{28,12},{1,17},{... | collective-permute-start | bytes 258056 | tf_op jit(solution)/shard_map/ppermute | solution.py:71
  132.9 7.2 %collective-permute-start.27 = (bf16[1,4,56,384]{3,2,1,0:T(8,128)(2,1)S(1)}, bf16[1,4,56,384]{3,2,1,0:T(8,128)(2,1)S(1)}, u32[]{:S(2)}, u32[]{:S(2)}) collective-permute-start(bf16[1,4,56,384]{3,2,1,0:T(8,128)(2,1)S(1)} %get-tuple-element.82), channel_id=1, source_target_pairs={{0,1},{1,0},{2,3},{3,2},{4,5},{5,4},{6,7},{7,6},{8,9},{9,8},{10,11... | collective-permute-start | bytes 516104 | tf_op jit(solution)/shard_map/ppermute | solution.py:71
  138.1 8.7 %collective-permute-start.25 = (bf16[2,4,56,384]{3,2,1,0:T(8,128)(2,1)}, bf16[2,4,56,384]{3,2,1,0:T(8,128)(2,1)}, u32[]{:S(2)}, u32[]{:S(2)}) collective-permute-start(bf16[2,4,56,384]{3,2,1,0:T(8,128)(2,1)} %pad_maximum_fusion.7), channel_id=1, source_target_pairs={{0,1},{1,0},{2,3},{3,2},{4,5},{5,4},{6,7},{7,6},{8,9},{9,8},{10,11... | collective-permute-start | bytes 1032200 | tf_op jit(solution)/shard_map/ppermute | solution.py:71
  141.0 9.0 %collective-permute-start.28 = (bf16[2,4,56,384]{3,2,1,0:T(8,128)(2,1)}, bf16[2,4,56,384]{3,2,1,0:T(8,128)(2,1)S(1)}, u32[]{:S(2)}, u32[]{:S(2)}) collective-permute-start(bf16[2,4,56,384]{3,2,1,0:T(8,128)(2,1)} %pad_maximum_fusion.8), channel_id=1, source_target_pairs={{0,2},{1,3},{2,0},{3,1},{4,6},{5,7},{6,4},{7,5},{8,10},{9,11},{10,... | collective-permute-start | bytes 1032200 | tf_op jit(solution)/shard_map/ppermute | solution.py:71
  142.8 8.5 %collective-permute-start.14 = (bf16[6,2,16,320]{3,2,1,0:T(8,128)(2,1)}, bf16[6,2,16,320]{3,2,1,0:T(8,128)(2,1)}, u32[]{:S(2)}, u32[]{:S(2)}) collective-permute-start(bf16[6,2,16,320]{3,2,1,0:T(8,128)(2,1)} %get-tuple-element.76), channel_id=1, source_target_pairs={{0,3},{1,2},{2,1},{3,0},{4,7},{5,6},{6,5},{7,4},{8,11},{9,10},{10,... | collective-permute-start | bytes 368648 | tf_op jit(solution)/shard_map/ppermute | solution.py:71
  144.3 22.6 %collective-permute-start.16 = (bf16[384,960]{0,1:T(8,128)(2,1)S(1)}, bf16[384,960]{0,1:T(8,128)(2,1)S(1)}, u32[]{:S(2)}, u32[]{:S(2)}) collective-permute-start(bf16[384,960]{0,1:T(8,128)(2,1)S(1)} %copy.49), channel_id=1, source_target_pairs={{0,4},{4,0},{8,12},{12,8},{16,20},{20,16},{24,28},{28,24},{1,5},{5... | collective-permute-start | bytes 2211848 | tf_op jit(solution)/shard_map/ppermute | solution.py:71
  147.9 28.3 %collective-permute-start.26 = (bf16[4,4,56,384]{3,2,1,0:T(8,128)(2,1)S(1)}, bf16[4,4,56,384]{3,2,1,0:T(8,128)(2,1)}, u32[]{:S(2)}, u32[]{:S(2)}) collective-permute-start(bf16[4,4,56,384]{3,2,1,0:T(8,128)(2,1)S(1)} %pad_maximum_fusion.2.refs_1_), channel_id=1, source_target_pairs={{0,4},{4,0},{8,12},{12,8},{16,20},{20,16},{24,28},{28,24},{1,5},{5... | collective-permute-start | bytes 2064392 | tf_op jit(solution)/shard_map/ppermute | solution.py:71
  150.1 26.1 %collective-permute-start.29 = (bf16[4,4,56,384]{3,2,1,0:T(8,128)(2,1)S(1)}, bf16[4,4,56,384]{3,2,1,0:T(8,128)(2,1)}, u32[]{:S(2)}, u32[]{:S(2)}) collective-permute-start(bf16[4,4,56,384]{3,2,1,0:T(8,128)(2,1)S(1)} %pad_maximum_fusion.3.refs_0_), channel_id=1, source_target_pairs={{0,4},{4,0},{8,12},{12,8},{16,20},{20,16},{24,28},{28,24},{1,5},{5... | collective-permute-start | bytes 2064392 | tf_op jit(solution)/shard_map/ppermute | solution.py:71
  150.2 6.5 %collective-permute-start.13 = (bf16[6,2,16,320]{3,2,1,0:T(8,128)(2,1)}, bf16[6,2,16,320]{3,2,1,0:T(8,128)(2,1)S(1)}, u32[]{:S(2)}, u32[]{:S(2)}) collective-permute-start(bf16[6,2,16,320]{3,2,1,0:T(8,128)(2,1)} %get-tuple-element.77), channel_id=1, source_target_pairs={{0,2},{1,3},{2,0},{3,1},{4,6},{5,7},{6,4},{7,5},{8,10},{9,11},{10,... | collective-permute-start | bytes 368648 | tf_op jit(solution)/shard_map/ppermute | solution.py:71
  151.3 6.1 %collective-permute-start.12 = (bf16[6,2,16,320]{3,2,1,0:T(8,128)(2,1)}, bf16[6,2,16,320]{3,2,1,0:T(8,128)(2,1)S(1)}, u32[]{:S(2)}, u32[]{:S(2)}) collective-permute-start(bf16[6,2,16,320]{3,2,1,0:T(8,128)(2,1)} %get-tuple-element.78), channel_id=1, source_target_pairs={{0,1},{1,0},{2,3},{3,2},{4,5},{5,4},{6,7},{7,6},{8,9},{9,8},{10,11... | collective-permute-start | bytes 368648 | tf_op jit(solution)/shard_map/ppermute | solution.py:71
  156.6 11.4 %collective-permute-start.17 = (bf16[320,320]{1,0:T(8,128)(2,1)}, bf16[320,320]{1,0:T(8,128)(2,1)S(1)}, u32[]{:S(2)}, u32[]{:S(2)}) collective-permute-start(bf16[320,320]{1,0:T(8,128)(2,1)} %get-tuple-element.56.att_a), channel_id=1, source_target_pairs={{0,4},{4,0},{8,12},{12,8},{16,20},{20,16},{24,28},{28,24},{1,5},{5... | collective-permute-start | bytes 614408 | tf_op jit(solution)/shard_map/ppermute | solution.py:71
  (21 other events, 87.6 us)

commit v3 on v2

--- a/solution.py
+++ b/solution.py
@@ -7,6 +7,7 @@
 from jax.experimental import pallas as pl
 from jax.experimental.pallas import tpu as pltpu
 from jax.sharding import PartitionSpec as P
+
 
 HD = 80
 SLOT = 128
@@ -165,15 +166,16 @@
 
 
 def coarse_kernel(
-    me, first, second, w_time, mix, out_mix, direct, q_rows, u_rows, o_rows, d_rows, taps,
+    me, first_a, first_b, second_a, second_b, w_time, mix, out_mix, direct, q_rows, u_rows, o_rows, d_rows, taps,
     local, grad_mix, grad_att, keep, send,
-    shifted, centre, pooled, upper, qkv, att_grad, att, qkv_grad, fields, spread_all, rows_down, rows_up, rows_tap,
+    stage, shifted, centre, pooled, upper, qkv, att_grad, att, qkv_grad, score, slope, weight, delta, fields, spread_all,
+    rows_down, rows_up, rows_tap,
     *, coarse_frames, heads_axis, rest,
 ):
     step = pl.program_id(0)
     frame = me[0]
-    quart = first.shape[2]
-    chans = first.shape[3]
+    quart = stage.shape[2]
+    chans = stage.shape[3]
     padded = pooled.shape[1]
     tokens = coarse_frames * quart
     total = 2 * tokens
@@ -193,13 +195,21 @@
         gap = index ^ frame
         return (reversed_bits(gap >> 1, chips) * 2 + (gap & 1)) * 3
 
-    for color, source in ((0, first), (1, second)):
+    for color, sources in ((0, (first_a, first_b)), (1, (second_a, second_b))):
+        place = step if color == 0 else reversed_bits(step, heads_axis)
+        for late in range(2):
+
+            @pl.when((place >= heads_axis // 2) == bool(late))
+            def _():
+                stage[color] = sources[late][0]
+
+    for color in range(2):
         before = jnp.zeros((quart, chans), F32)
-        here = source[0, entry(0)].astype(F32)
+        here = stage[color, entry(0)].astype(F32)
         for u in range(coarse_frames):
             at = entry(u)
-            last = source[0, at + 1].astype(F32)
-            after = source[0, entry(u + 1)].astype(F32) if u + 1 < coarse_frames else jnp.zeros((quart, chans), F32)
+            last = stage[color, at + 1].astype(F32)
+            after = stage[color, entry(u + 1)].astype(F32) if u + 1 < coarse_frames else jnp.zeros((quart, chans), F32)
             offset = color * tokens + u * quart
             rows = pl.ds(pl.multiple_of(step * total + offset, quart), quart)
             mid = 0.5 * (here + last)
@@ -207,7 +217,7 @@
             shifted[rows, chans : 2 * chans] = mid.astype(BF)
             shifted[rows, 2 * chans : 3 * chans] = (0.5 * (last + after)).astype(BF)
             centre[offset : offset + quart, :] = mid
-            upper[rows, :] = source[0, at + 2]
+            upper[rows, :] = stage[color, at + 2]
             before, here = last, after
     pool = (centre[...] + nn(shifted[here_rows, 0 : 3 * chans], w_time[...])).astype(BF)
     pooled[here_rows, 0:chans] = pool
@@ -218,39 +228,50 @@
     row = lax.broadcasted_iota(jnp.int32, (tokens, tokens), 0)
     col = lax.broadcasted_iota(jnp.int32, (tokens, tokens), 1)
     same = (row & (quart - 1)) == (col & (quart - 1))
-    for color in range(2):
-        rows = slice(color * tokens, (color + 1) * tokens)
+    cases = [(color, n) for color in range(2) for n in range(heads)]
+
+    def part_of(color, n, which):
+        return qkv[color * tokens : (color + 1) * tokens, (3 * n + which) * SLOT : (3 * n + which + 1) * SLOT]
+
+    def grad_of(color, n):
+        return att_grad[color * tokens : (color + 1) * tokens, n * SLOT : (n + 1) * SLOT]
+
+    for i, (color, n) in enumerate(cases):
+        score[i] = nt(part_of(color, n, 0), part_of(color, n, 1))
+        slope[i] = nt(grad_of(color, n), part_of(color, n, 2))
+    for i, (color, n) in enumerate(cases):
+        scores = jnp.where(same, score[i] * scale, -jnp.inf)
+        ex = jnp.exp(scores - jnp.max(scores, axis=1, keepdims=True))
+        probs = ex * (1.0 / jnp.sum(ex, axis=1, keepdims=True))
+        dw = slope[i]
+        inner = jnp.sum(probs * dw, axis=1, keepdims=True)
+        weight[i] = probs.astype(BF)
+        delta[i] = (probs * (dw - inner) * scale).astype(BF)
+    for i, (color, n) in enumerate(cases):
         out = pl.ds(pl.multiple_of(step * total + color * tokens, tokens), tokens)
-        for n in range(heads):
-            q = qkv[rows, (3 * n) * SLOT : (3 * n + 1) * SLOT]
-            k = qkv[rows, (3 * n + 1) * SLOT : (3 * n + 2) * SLOT]
-            v = qkv[rows, (3 * n + 2) * SLOT : (3 * n + 3) * SLOT]
-            da = att_grad[rows, n * SLOT : (n + 1) * SLOT]
-            scores = jnp.where(same, nt(q, k) * scale, -jnp.inf)
-            peak = jnp.max(scores, axis=1, keepdims=True)
-            ex = jnp.exp(scores - peak)
-            probs = ex * (1.0 / jnp.sum(ex, axis=1, keepdims=True))
-            weights = probs.astype(BF)
-            att[out, n * SLOT : (n + 1) * SLOT] = nn(weights, v).astype(BF)
-            dw = nt(da, v)
-            inner = jnp.sum(probs * dw, axis=1, keepdims=True)
-            ds = (probs * (dw - inner) * scale).astype(BF)
-            qkv_grad[out, (3 * n) * SLOT : (3 * n + 1) * SLOT] = nn(ds, k).astype(BF)
-            qkv_grad[out, (3 * n + 1) * SLOT : (3 * n + 2) * SLOT] = tn(ds, q).astype(BF)
-            qkv_grad[out, (3 * n + 2) * SLOT : (3 * n + 3) * SLOT] = tn(weights, da).astype(BF)
-    lifted = nn(att[here_rows, :], out_mix[...]) + nn(lines, direct[...]) * part
+        att[out, n * SLOT : (n + 1) * SLOT] = nn(weight[i], part_of(color, n, 2)).astype(BF)
+        qkv_grad[out, (3 * n) * SLOT : (3 * n + 1) * SLOT] = nn(delta[i], part_of(color, n, 1)).astype(BF)
+        qkv_grad[out, (3 * n + 1) * SLOT : (3 * n + 2) * SLOT] = tn(delta[i], part_of(color, n, 0)).astype(BF)
+        qkv_grad[out, (3 * n + 2) * SLOT : (3 * n + 3) * SLOT] = tn(weight[i], grad_of(color, n)).astype(BF)
     spread = nt(qkv_grad[here_rows, :], mix[...]) + nt(ups, direct[...]) * part
     spread = spread[:, 0:chans].astype(BF)
     spread_all[here_rows, :] = spread
-    fields[0] = lifted.astype(BF).reshape(2 * coarse_frames, quart, chans)
-    fields[1] = spread.reshape(2 * coarse_frames, quart, chans)
+    fields[...] = spread.reshape(2 * coarse_frames, quart, chans)
     mine = (frame >> 1) * 2
+    att_rows, line_rows = [], []
+    for color in range(2):
+        rows = pl.ds(pl.multiple_of(step * total + color * tokens + mine * quart, 2 * quart), 2 * quart)
+        att_rows.append(att[rows, :])
+        line_rows.append(pooled[rows, :])
+    lifted = nn(jnp.concatenate(att_rows, axis=0), out_mix[...])
+    lifted = lifted + nn(jnp.concatenate(line_rows, axis=0), direct[...]) * part
+    lifted = lifted.astype(BF).reshape(4, quart, chans)
     for color in range(2):
         for i in range(2):
-            local[0, i, color] = fields[0, color * coarse_frames + mine + i]
+            local[0, i, color] = lifted[2 * color + i]
         for i in range(4):
             at = jnp.clip(mine + i - 1, 0, coarse_frames - 1)
-            local[0, 2 + i, color] = fields[1, color * coarse_frames + at]
+            local[0, 2 + i, color] = fields[color * coarse_frames + at]
 
     @pl.when(step == heads_axis - 1)
     def _():
@@ -298,6 +319,20 @@
     refs[-1][...] = acc.astype(BF)
 
 
+def local_kernel(me, *refs):
+    parts, (mine, send, acc) = refs[:-3], refs[-3:]
+    core = me[0] & 1
+    for i in range(acc.shape[0]):
+        value = parts[0][i].astype(F32)
+        for ref in parts[1:]:
+            value = value + ref[i].astype(F32)
+        acc[i] = value
+    for dest, which in ((mine, core), (send, 1 - core)):
+        dest[0] = acc[which].astype(BF)
+        for i in range(3):
+            dest[1 + i] = acc[2 + which + i].astype(BF)
+
+
 def split_grad_kernel(down, mix_a, mix_b, att_a, att_b, w_up, qkv_out, att_out, flipped):
     @pl.when(pl.program_id(0) == 0)
     def _():
@@ -335,8 +370,8 @@
 
 
 def gather_kernel(me, embed, *refs, layout, aligned):
-    pieces = refs[:4]
-    time_out, down_rows, up_rows = refs[4], refs[-2], refs[-1]
+    pieces = refs[:8]
+    time_out, down_rows, up_rows = refs[8], refs[-2], refs[-1]
     frame, head = me[0], me[1]
     chips, heads_axis, r1, p1, r3 = layout
     chans = time_out.shape[2]
@@ -346,9 +381,10 @@
             hi, zi = idx // chips, idx % chips
             colors = []
             for color in range(2):
-                src = pieces[2 * core + color]
                 off = hi if color == 0 else reversed_bits(hi, heads_axis)
-                colors.append(src[off, zi].astype(F32))
+                edge = heads_axis // 2
+                src = pieces[4 * core + 2 * color + off // edge]
+                colors.append(src[off % edge, zi].astype(F32))
             value = jnp.concatenate(colors, axis=0)
             owner = (frame ^ (reversed_bits(zi, chips) * 2 + core)) * heads_axis + (head ^ hi)
             down_rows[owner] = value[0:r1]
@@ -359,7 +395,7 @@
                 time_out[owner] = value[2 * p1 : 2 * p1 + r3, 0:chans]
 
     if aligned:
-        down_out, embed_out, up_out = refs[5], refs[6], refs[7]
+        down_out, embed_out, up_out = refs[9], refs[10], refs[11]
         lanes = down_rows.shape[2]
         eye = (lax.broadcasted_iota(jnp.int32, (lanes, lanes), 0) == lax.broadcasted_iota(jnp.int32, (lanes, lanes), 1))
         eye = eye.astype(F32).astype(BF)
@@ -377,12 +413,13 @@
 
 
 def cross(first, second, bits):
-    for a, b in zip(bits, reversed(bits)):
+    for i, (a, b) in enumerate(zip(bits, reversed(bits))):
         first_in = swap(first, "heads", a)
         second_in = swap(second, "heads", b)
-        first = jnp.concatenate([first, first_in], axis=0)
-        second = jnp.concatenate([second, second_in], axis=0)
-    return first, second
+        if i + 1 < len(bits):
+            first = jnp.concatenate([first, first_in], axis=0)
+            second = jnp.concatenate([second, second_in], axis=0)
+    return first, first_in, second, second_in
 
 
 def body(clip, w_time, w_down, w_embed, w_qkv, w_out, w_up, timestep, cotangent):
@@ -419,7 +456,7 @@
     keep_in = swap(send, "frames", 1)
     block = jnp.concatenate([keep, keep_in], axis=1)
     block = double(block, "frames", chip_bits, 1)
-    first, second = cross(block[0][None], block[1][None], head_bits)
+    first, second = block[0][None], block[1][None]
 
     embed = time_embed(timestep, w_embed.shape[0])
     down, mix, out_mix, direct = call(
@@ -466,7 +503,8 @@
     p1 = round_up(r1, 8)
     r3 = share // nh
     piece_rows = round_up(2 * p1 + r3, 16)
-    start = (f >> 1) * chip_rows
+    start, first, second = lax.optimization_barrier(((f >> 1) * chip_rows, first, second))
+    sides = cross(first, second, head_bits)
 
     def rows_of(x, axis):
         x = lax.dynamic_slice_in_dim(x, start, chip_rows, axis=axis)
@@ -479,8 +517,17 @@
     o_rows = rows_of(w_out, 1)
     d_rows = rows_of(down, 1)
 
-    blk = pl.BlockSpec((1, nf * 3, quart, chans), lambda g: (g, 0, 0, 0))
-    mirrored = pl.BlockSpec((1, nf * 3, quart, chans), lambda g: (reversed_bits(g, nh), 0, 0, 0))
+    edge = nh // 2
+
+    def side(mirrored, late):
+        def index(g):
+            at = reversed_bits(g, nh) if mirrored else g
+            at = jnp.maximum(at - edge, 0) if late else jnp.minimum(at, edge - 1)
+            return (at, 0, 0, 0)
+
+        return pl.BlockSpec((1, nf * 3, quart, chans), index)
+
+    side_specs = [side(False, False), side(False, True), side(True, False), side(True, True)]
     total = 2 * nf * quart
     every = nh * total
 
@@ -499,7 +546,7 @@
             sds((nh, piece_rows, padded), BF),
         ],
         grid=(nh,),
-        in_specs=[smem(), blk, mirrored] + [whole(*x.shape) for x in statics],
+        in_specs=[smem()] + side_specs + [whole(*x.shape) for x in statics],
         out_specs=[
             pl.BlockSpec((1, 6, 2, quart, chans), lambda g: (g, 0, 0, 0, 0)),
             whole(padded, pieces * HD),
@@ -508,6 +555,7 @@
             whole(nh, piece_rows, padded),
         ],
         scratch_shapes=[
+            pltpu.VMEM((2, nf * 3, quart, chans), BF),
             pltpu.VMEM((every, tap_rows), BF),
             pltpu.VMEM((total, chans), F32),
             pltpu.VMEM((every, padded), BF),
@@ -516,13 +564,17 @@
             pltpu.VMEM((total, heads * SLOT), BF),
             pltpu.VMEM((every, heads * SLOT), BF),
             pltpu.VMEM((every, pieces * SLOT), BF),
-            pltpu.VMEM((2, 2 * nf, quart, chans), BF),
+            pltpu.VMEM((2 * heads, total // 2, total // 2), F32),
+            pltpu.VMEM((2 * heads, total // 2, total // 2), F32),
+            pltpu.VMEM((2 * heads, total // 2, total // 2), BF),
+            pltpu.VMEM((2 * heads, total // 2, total // 2), BF),
+            pltpu.VMEM((2 * nf, quart, chans), BF),
             pltpu.VMEM((every, chans), BF),
             pltpu.VMEM((2 * nh * p1, padded), F32),
             pltpu.VMEM((2 * nh * p1, padded), F32),
             pltpu.VMEM((2 * share, padded), F32),
         ],
-    )(me, first, second, *statics)
+    )(me, *sides, *statics)
 
     d_got = swap(d_send, "frames", 1)
     ordered = call(
@@ -537,27 +589,25 @@
     piece = call(sum_kernel, sds((piece_rows, padded), BF))(ordered[0], *got)
     piece = piece.reshape(2, 1, piece_rows // 2, padded)
     piece = double(piece, "frames", chip_bits, 1)
-    p_first, p_second = cross(piece[0][None], piece[1][None], head_bits)
-    q_first = swap(p_first, "frames", 1)
-    q_second = swap(p_second, "frames", 1)
+    shares = cross(piece[0][None], piece[1][None], head_bits)
+    mates = []
+    for x in shares:
+        mates.append(swap(x, "frames", 1))
 
     got = []
     for d in range(1, nh):
         got.append(swap(local[d], "heads", d))
-    own = call(sum_kernel, sds(local.shape[1:], BF))(local[0], *got)
-    own = own.reshape(6, half, chans)
-    core = f & 1
-
-    def four(which):
-        return jnp.concatenate(
-            [
-                lax.dynamic_slice_in_dim(own, which, 1, axis=0),
-                lax.dynamic_slice_in_dim(own, 2 + which, 3, axis=0),
-            ]
-        )
-
-    mine4 = four(core)
-    other4 = swap(four(1 - core), "frames", 1)
+    four = sds((4, 2, quart, chans), BF)
+    mine4, send4 = call(
+        local_kernel,
+        [four, four],
+        in_specs=[smem()] + [vmem()] * nh,
+        out_specs=[vmem()] * 2,
+        scratch_shapes=[pltpu.VMEM(local.shape[1:], F32)],
+    )(me, local[0], *got)
+    other4 = swap(send4, "frames", 1)
+    mine4 = mine4.reshape(4, half, chans)
+    other4 = other4.reshape(4, half, chans)
     output, grad_clip = call(
         functools.partial(finish_kernel, coarse_frames=nf),
         [sds(clip_t.shape, BF), sds(clip_t.shape, F32)],
@@ -588,8 +638,8 @@
         scratch_shapes=[pltpu.VMEM((pieces * HD, padded), BF)],
     )(down, mix_g, mix_o, att_g, att_o, w_up_t)
 
-    output, grad_clip, grad_qkv, grad_out, q_second = lax.optimization_barrier(
-        (output, grad_clip, grad_qkv, grad_out, q_second)
+    output, grad_clip, grad_qkv, grad_out, mates[3] = lax.optimization_barrier(
+        (output, grad_clip, grad_qkv, grad_out, mates[3])
     )
     aligned = r1 % 8 == 0
     layout = (chips, nh, r1, p1, r3)
@@ -605,10 +655,10 @@
     got = call(
         functools.partial(gather_kernel, layout=layout, aligned=aligned),
         outs,
-        in_specs=[smem()] + [vmem()] * 5,
+        in_specs=[smem()] + [vmem()] * 9,
         out_specs=[vmem()] * len(outs),
         scratch_shapes=scratch,
-    )(me, embed_col, p_first, p_second, q_first, q_second)
+    )(me, embed_col, *shares, *mates)
     grad_time = got[0].reshape(w_time.shape)
     if aligned:
         grad_down, grad_embed, grad_up = got[1], got[2], got[3].T

time: 182 us -> 164 us (0.901)
  Pallas kernels: 70.8 us -> 55.7 us
  other arithmetic: 10.3 us -> 6.03 us
  waiting for transfers between devices: 48 us -> 46 us
    pallas_call x1, Pallas kernels: 35.4 us -> 20.3 us  [body(): call(functools.partial(coarse_kernel, coarse_frames=nf, heads_axis=nh, re...]
    concatenate x4 -> x1, other arithmetic: 3.2 us -> 0.04 us  [cross(): second = jnp.concatenate([second, second_in], axis=0)]
    concatenate x0 -> x2, local copies, waits for them, and re-layouts: none -> 2.02 us  [the longest x1 1.01 us: cross(): first = jnp.concatenate([first, first_in], axis=0)]
    ppermute x28 -> x30, waiting for transfers between devices: 48 us -> 46 us  [swap(): return lax.ppermute(x, axis, [(i, i ^ bit) for i in range(n)])]
    ppermute x28 -> x30, starting transfers between devices: 26.5 us -> 27.8 us  [swap(): return lax.ppermute(x, axis, [(i, i ^ bit) for i in range(n)])]
    unnamed x36 -> x54, local copies, waits for them, and re-layouts: 8.6 us -> 9.56 us
  transfers between devices with their start and end apart: 30 -> 32, of which waited for: 17 -> 17; matrix products, arithmetic and copies ran while one was open for 13% -> 12% of each run, Pallas kernels for 13% -> 15%
where the time goes in v3:
time: 164 us; the launch traced here: 163 us
  Pallas kernels  55.7 us (34%)
  waiting for transfers between devices  46 us (28%)
  starting transfers between devices  31 us (19%)
  local copies, waits for them, and re-layouts  22.2 us (14%)
  other arithmetic  6.03 us (4%)
  between operations  1.67 us (1%)
    ppermute x30, waiting for transfers between devices, swap(): return lax.ppermute(x, axis, [(i, i ^ bit) for i in range(n)])  46 us
    ppermute x30, starting transfers between devices, swap(): return lax.ppermute(x, axis, [(i, i ^ bit) for i in range(n)])  27.8 us
    pallas_call x1, Pallas kernels, body(): call(functools.partial(coarse_kernel, coarse_frames=nf, heads_axis=nh, re...  20.3 us
    unnamed x54, local copies, waits for them, and re-layouts  9.56 us
    pallas_call x1, Pallas kernels, body(): call(split_grad_kernel, [sds((pieces * HD, width), F32), sds((heads * HD,...  7.45 us
    pallas_call x1, Pallas kernels, body(): call(weight_kernel, [sds((padded, width), BF), sds((padded, pieces * SLOT...  5.65 us
    pallas_call x1, Pallas kernels, body(): call(functools.partial(gather_kernel, layout=layout, aligned=aligned), ou...  5.29 us
    pallas_call x1, Pallas kernels, body(): call(fine_kernel, [sds(clip_t.shape, BF), sds(clip_t.shape, F32), sds((ta...  4.36 us
  transfers between devices with their start and end apart: 32, of which 17 were waited for; matrix products, arithmetic and copies ran while one was open for 12% of the time, Pallas kernels for 15%

profile of v3, /device:TPU:0, one launch (start us, length us, event | category | flops | bytes accessed | tf_op | source)
XLA Modules:
  0.0 162.7 jit_solution(2668571757492070571)
XLA Ops:
  1.2 2.1 %shard_map.152 = (bf16[2,3,16,320]{3,2,1,0:T(8,128)(2,1)}, bf16[2,3,16,320]{3,2,1,0:T(8,128)(2,1)}) custom-call(s32[2]{0:T(128)} %pad_add_fusion.me, bf16[2,2,320,128]{3,2,1,0:T(8,128)(2,1)} %bitcast.54, bf16[2,2,320,128]{3,2,1,0:T(8,128)(2,1)} %bitcast.57), custom_call_target="tpu_custom_call" | custom-call | tf_op jit(solution)/shard_map/pallas_call | solution.py:449
  3.9 1.9 %shard_map.153 = (bf16[4,320,128]{2,1,0:T(8,128)(2,1)}, bf16[4,320,128]{2,1,0:T(8,128)(2,1)}) custom-call(bf16[2,2,320,128]{3,2,1,0:T(8,128)(2,1)} %bitcast.55, bf16[2,2,320,128]{3,2,1,0:T(8,128)(2,1)} %bitcast.58, bf16[2,3,16,320]{3,2,1,0:T(8,128)(2,1)} %get-tuple-element.46.after), custom_call_target="tpu_custom_call" | custom-call | tf_op jit(solution)/shard_map/pallas_call | solution.py:472
  5.8 1.9 %collective-permute-start = (bf16[4,320,128]{2,1,0:T(8,128)(2,1)}, bf16[4,320,128]{2,1,0:T(8,128)(2,1)S(1)}, u32[]{:S(2)}, u32[]{:S(2)}) collective-permute-start(bf16[4,320,128]{2,1,0:T(8,128)(2,1)} %get-tuple-element.47), channel_id=1, source_target_pairs={{0,4},{4,8},{8,12},{12,16},{16,20},{20,24},{24,28},{1,5},{5,9},{9,... | collective-permute-start | bytes 983048 | tf_op jit(solution)/shard_map/ppermute | solution.py:478
  11.6 6.0 %collective-permute-start.3 = (bf16[2,6,16,320]{3,2,1,0:T(8,128)(2,1)S(1)}, bf16[2,6,16,320]{3,2,1,0:T(8,128)(2,1)S(1)}, u32[]{:S(2)}, u32[]{:S(2)}) collective-permute-start(bf16[2,6,16,320]{3,2,1,0:T(8,128)(2,1)S(1)} %pad_maximum_fusion.5), channel_id=1, source_target_pairs={{0,16},{4,20},{8,24},{12,28},{16,0},{20,4},{24,8},{28,12},{1,17},{... | collective-permute-start | bytes 368648 | tf_op jit(solution)/shard_map/ppermute | solution.py:72
  18.2 5.6 %shard_map.155 = (bf16[384,1280]{1,0:T(8,128)(2,1)}, bf16[384,1536]{1,0:T(8,128)(2,1)}, bf16[512,320]{1,0:T(8,128)(2,1)}, bf16[384,320]{1,0:T(8,128)(2,1)}) custom-call(bf16[320,1280]{1,0:T(8,128)(2,1)} %w_down.1, bf16[320,1280]{1,0:T(8,128)(2,1)} %w_embed.1, bf16[1,320]{1,0:T(2,128)(2,1)} %fusion.3.embed, bf16[960,1280]{1,0:T(8,128)(2,1)} %bitcast.53, ...), custom_call_target="tpu_custom_call" | custom-call | tf_op jit(solution)/shard_map/pallas_call | solution.py:462
  23.8 1.6 copy.45
  28.7 4.4 %shard_map.154 = (bf16[2,2,320,128]{3,2,1,0:T(8,128)(2,1)}, f32[2,2,320,128]{3,2,1,0:T(8,128)}, bf16[1024,320]{1,0:T(8,128)(2,1)}) custom-call(bf16[2,2,320,128]{3,2,1,0:T(8,128)(2,1)} %bitcast.56, bf16[2,2,320,128]{3,2,1,0:T(8,128)(2,1)} %bitcast.59, bf16[4,320,128]{2,1,0:T(8,128)(2,1)} %copy-done.13, bf16[4,320,128]{2,1,0:T(8,128)(2,1)} %copy-done.14, ...), custom_call_target="tpu_custom_call" | custom-call | tf_op jit(solution)/shard_map/pallas_call | solution.py:481
  45.9 3.3 %collective-permute-done.7 = bf16[1,24,16,320]{3,2,1,0:T(8,128)(2,1)} collective-permute-done((bf16[1,24,16,320]{3,2,1,0:T(8,128)(2,1)S(1)}, bf16[1,24,16,320]{3,2,1,0:T(8,128)(2,1)}, u32[]{:S(2)}, u32[]{:S(2)}) %collective-permute-start.7) | collective-permute-done | bytes 245792 | tf_op jit(solution)/shard_map/ppermute | solution.py:72
  55.5 4.7 %collective-permute-done.11 = bf16[128,320]{1,0:T(8,128)(2,1)S(1)} collective-permute-done((bf16[128,320]{1,0:T(8,128)(2,1)S(1)}, bf16[128,320]{1,0:T(8,128)(2,1)S(1)}, u32[]{:S(2)}, u32[]{:S(2)}) %collective-permute-start.11) | collective-permute-done | bytes 81952 | tf_op jit(solution)/shard_map/ppermute | solution.py:72
  60.8 4.0 %collective-permute-done.8.second_b = bf16[2,24,16,320]{3,2,1,0:T(8,128)(2,1)S(1)} collective-permute-done((bf16[2,24,16,320]{3,2,1,0:T(8,128)(2,1)S(1)}, bf16[2,24,16,320]{3,2,1,0:T(8,128)(2,1)S(1)}, u32[]{:S(2)}, u32[]{:S(2)}) %collective-permute-start.8) | collective-permute-done | bytes 491552 | tf_op jit(solution)/shard_map/ppermute | solution.py:72
  67.1 20.3 %shard_map.156 = (bf16[4,6,2,16,320]{4,3,2,1,0:T(8,128)(2,1)}, bf16[384,960]{1,0:T(8,128)(2,1)}, bf16[320,320]{1,0:T(8,128)(2,1)}, bf16[4,112,384]{2,1,0:T(8,128)(2,1)}, bf16[4,112,384]{2,1,0:T(8,128)(2,1)}) custom-call(s32[2]{0:T(128)} %pad_add_fusion.me, bf16[2,24,16,320]{3,2,1,0:T(8,128)(2,1)} %copy-done.3, bf16[2,24,16,320]{3,2,1,0:T(8,128)(2,1)} %copy-done.7, ...), custom_call_target="tpu_custom_call" | custom-call | tf_op jit(solution)/shard_map/pallas_call | solution.py:539
  87.5 1.9 %collective-permute-done.18.got = bf16[4,112,384]{2,1,0:T(8,128)(2,1)S(1)} collective-permute-done((bf16[4,112,384]{2,1,0:T(8,128)(2,1)}, bf16[4,112,384]{2,1,0:T(8,128)(2,1)S(1)}, u32[]{:S(2)}, u32[]{:S(2)}) %collective-permute-start.18) | collective-permute-done | bytes 344096 | tf_op jit(solution)/shard_map/ppermute | solution.py:72
  90.1 1.8 %shard_map.160 = (bf16[112,384]{1,0:T(8,128)(2,1)}, bf16[112,384]{1,0:T(8,128)(2,1)}, bf16[112,384]{1,0:T(8,128)(2,1)}, bf16[112,384]{1,0:T(8,128)(2,1)}) custom-call(s32[2]{0:T(128)} %pad_add_fusion.me, bf16[4,112,384]{2,1,0:T(8,128)(2,1)} %get-tuple-element.69.keep, bf16[4,112,384]{2,1,0:T(8,128)(2,1)} %copy-done.12), custom_call_target="tpu_custom_call" | custom-call | tf_op jit(solution)/shard_map/pallas_call | solution.py:580
  96.7 2.4 %collective-permute-done.20.refs_2_ = bf16[112,384]{1,0:T(8,128)(2,1)S(1)} collective-permute-done((bf16[112,384]{1,0:T(8,128)(2,1)}, bf16[112,384]{1,0:T(8,128)(2,1)S(1)}, u32[]{:S(2)}, u32[]{:S(2)}) %collective-permute-start.20) | collective-permute-done | bytes 86048 | tf_op jit(solution)/shard_map/ppermute | solution.py:72
  101.2 1.7 %shard_map.161 = bf16[112,384]{1,0:T(8,128)(2,1)} custom-call(bf16[112,384]{1,0:T(8,128)(2,1)} %get-tuple-element.71.refs_0_, bf16[112,384]{1,0:T(8,128)(2,1)} %copy-done.20, bf16[112,384]{1,0:T(8,128)(2,1)} %copy-done.21, bf16[112,384]{1,0:T(8,128)(2,1)} %copy-done.22), custom_call_target="tpu_custom_call" | custom-call | tf_op jit(solution)/shard_map/pallas_call | solution.py:589
  104.0 4.4 %collective-permute-done.22 = bf16[2,1,56,384]{3,2,1,0:T(8,128)(2,1)S(1)} collective-permute-done((bf16[2,1,56,384]{3,2,1,0:T(8,128)(2,1)}, bf16[2,1,56,384]{3,2,1,0:T(8,128)(2,1)S(1)}, u32[]{:S(2)}, u32[]{:S(2)}) %collective-permute-start.22) | collective-permute-done | bytes 86048 | tf_op jit(solution)/shard_map/ppermute | solution.py:72
  110.9 3.9 %collective-permute-done.23 = bf16[2,2,56,384]{3,2,1,0:T(8,128)(2,1)S(1)} collective-permute-done((bf16[2,2,56,384]{3,2,1,0:T(8,128)(2,1)S(1)}, bf16[2,2,56,384]{3,2,1,0:T(8,128)(2,1)S(1)}, u32[]{:S(2)}, u32[]{:S(2)}) %collective-permute-start.23) | collective-permute-done | bytes 172064 | tf_op jit(solution)/shard_map/ppermute | solution.py:72
  117.9 3.4 %collective-permute-done.24 = bf16[1,4,56,384]{3,2,1,0:T(8,128)(2,1)S(1)} collective-permute-done((bf16[1,4,56,384]{3,2,1,0:T(8,128)(2,1)S(1)}, bf16[1,4,56,384]{3,2,1,0:T(8,128)(2,1)S(1)}, u32[]{:S(2)}, u32[]{:S(2)}) %collective-permute-start.24) | collective-permute-done | bytes 172064 | tf_op jit(solution)/shard_map/ppermute | solution.py:72
  127.7 5.7 %collective-permute-done.14.refs_3_ = bf16[6,2,16,320]{3,2,1,0:T(8,128)(2,1)S(1)} collective-permute-done((bf16[6,2,16,320]{3,2,1,0:T(8,128)(2,1)S(1)}, bf16[6,2,16,320]{3,2,1,0:T(8,128)(2,1)S(1)}, u32[]{:S(2)}, u32[]{:S(2)}) %collective-permute-start.14) | collective-permute-done | bytes 122912 | tf_op jit(solution)/shard_map/ppermute | solution.py:72
  134.0 3.1 %collective-permute-done.13.refs_2_ = bf16[6,2,16,320]{3,2,1,0:T(8,128)(2,1)S(1)} collective-permute-done((bf16[6,2,16,320]{3,2,1,0:T(8,128)(2,1)S(1)}, bf16[6,2,16,320]{3,2,1,0:T(8,128)(2,1)S(1)}, u32[]{:S(2)}, u32[]{:S(2)}) %collective-permute-start.13) | collective-permute-done | bytes 122912 | tf_op jit(solution)/shard_map/ppermute | solution.py:72
  139.2 1.9 %shard_map.157 = (bf16[4,2,16,320]{3,2,1,0:T(8,128)(2,1)}, bf16[4,2,16,320]{3,2,1,0:T(8,128)(2,1)}) custom-call(s32[2]{0:T(128)} %pad_add_fusion.me, bf16[6,2,16,320]{3,2,1,0:T(8,128)(2,1)} %get-tuple-element.89.refs_0_, bf16[6,2,16,320]{3,2,1,0:T(8,128)(2,1)} %copy-done.18, bf16[6,2,16,320]{3,2,1,0:T(8,128)(2,1)} %copy-done.17, ...), custom_call_target="tpu_custom_call" | custom-call | tf_op jit(solution)/shard_map/pallas_call | solution.py:601
  144.2 3.1 %shard_map.158 = (bf16[2,2,320,128]{3,2,1,0:T(8,128)(2,1)}, f32[2,2,320,128]{3,2,1,0:T(8,128)}) custom-call(s32[2]{0:T(128)} %pad_add_fusion.me, bf16[2,2,320,128]{3,2,1,0:T(8,128)(2,1)} %get-tuple-element.49.hidden, f32[2,2,320,128]{3,2,1,0:T(8,128)} %get-tuple-element.50.base, bf16[4,32,320]{2,1,0:T(8,128)(2,1)} %bitcast.66, bf16[4,32,320]{2,1,0:T(8,128)(2,1)} %bitcast.67, ...), custom_call_target="tpu_custom_call" | custom-call | tf_op jit(solution)/shard_map/pallas_call | solution.py:611
  149.2 7.5 %shard_map.159 = (f32[960,1280]{1,0:T(8,128)}, f32[320,1280]{1,0:T(8,128)}) custom-call(bf16[384,1280]{1,0:T(8,128)(2,1)} %get-tuple-element.58.down, bf16[384,960]{1,0:T(8,128)(2,1)} %get-tuple-element.65.mix_a, bf16[384,960]{1,0:T(8,128)(2,1)} %copy.50.mix_b, bf16[320,320]{1,0:T(8,128)(2,1)} %get-tuple-element.66.att_a, bf16[320,320]{1,0:T(8,128)(2,1)} %copy-done.15, ...), custom_call_target="tpu_custom_call" | custom-call | tf_op jit(solution)/shard_map/pallas_call | solution.py:622
  157.4 5.3 %shard_map.162 = (f32[30,32,320]{2,1,0:T(8,128)}, f32[320,1280]{1,0:T(8,128)}, f32[320,1280]{1,0:T(8,128)}, f32[320,1280]{1,0:T(8,128)}) custom-call(s32[2]{0:T(128)} %pad_add_fusion.me, f32[320,1]{1,0:T(8,128)} %copy.51.embed, bf16[2,4,56,384]{3,2,1,0:T(8,128)(2,1)} %copy-done.2, bf16[2,4,56,384]{3,2,1,0:T(8,128)(2,1)} %copy-done.10, ...), custom_call_target="tpu_custom_call" | custom-call | tf_op jit(solution)/shard_map/pallas_call | solution.py:655
  (136 shorter events, 58.9 us)
Async XLA Ops:
  3.4 7.3 %collective-permute-start.2 = (bf16[2,3,16,320]{3,2,1,0:T(8,128)(2,1)}, bf16[2,3,16,320]{3,2,1,0:T(8,128)(2,1)S(1)}, u32[]{:S(2)}, u32[]{:S(2)}) collective-permute-start(bf16[2,3,16,320]{3,2,1,0:T(8,128)(2,1)} %get-tuple-element.51), channel_id=1, source_target_pairs={{0,4},{4,0},{8,12},{12,8},{16,20},{20,16},{24,28},{28,24},{1,5},{5... | collective-permute-start | bytes 184328 | tf_op jit(solution)/shard_map/ppermute | solution.py:72
  5.8 21.4 %collective-permute-start = (bf16[4,320,128]{2,1,0:T(8,128)(2,1)}, bf16[4,320,128]{2,1,0:T(8,128)(2,1)S(1)}, u32[]{:S(2)}, u32[]{:S(2)}) collective-permute-start(bf16[4,320,128]{2,1,0:T(8,128)(2,1)} %get-tuple-element.47), channel_id=1, source_target_pairs={{0,4},{4,8},{8,12},{12,16},{16,20},{20,24},{24,28},{1,5},{5,9},{9,... | collective-permute-start | bytes 983048 | tf_op jit(solution)/shard_map/ppermute | solution.py:478
  7.7 19.5 %collective-permute-start.1 = (bf16[4,320,128]{2,1,0:T(8,128)(2,1)}, bf16[4,320,128]{2,1,0:T(8,128)(2,1)S(1)}, u32[]{:S(2)}, u32[]{:S(2)}) collective-permute-start(bf16[4,320,128]{2,1,0:T(8,128)(2,1)} %get-tuple-element.48), channel_id=1, source_target_pairs={{4,0},{8,4},{12,8},{16,12},{20,16},{24,20},{28,24},{5,1},{9,5},{13... | collective-permute-start | bytes 983048 | tf_op jit(solution)/shard_map/ppermute | solution.py:479
  11.6 14.9 %collective-permute-start.3 = (bf16[2,6,16,320]{3,2,1,0:T(8,128)(2,1)S(1)}, bf16[2,6,16,320]{3,2,1,0:T(8,128)(2,1)S(1)}, u32[]{:S(2)}, u32[]{:S(2)}) collective-permute-start(bf16[2,6,16,320]{3,2,1,0:T(8,128)(2,1)S(1)} %pad_maximum_fusion.5), channel_id=1, source_target_pairs={{0,16},{4,20},{8,24},{12,28},{16,0},{20,4},{24,8},{28,12},{1,17},{... | collective-permute-start | bytes 368648 | tf_op jit(solution)/shard_map/ppermute | solution.py:72
  26.6 7.8 %collective-permute-start.4 = (bf16[2,12,16,320]{3,2,1,0:T(8,128)(2,1)S(1)}, bf16[2,12,16,320]{3,2,1,0:T(8,128)(2,1)S(1)}, u32[]{:S(2)}, u32[]{:S(2)}) collective-permute-start(bf16[2,12,16,320]{3,2,1,0:T(8,128)(2,1)S(1)} %pad_maximum_fusion.3), channel_id=1, source_target_pairs={{0,8},{4,12},{8,0},{12,4},{16,24},{20,28},{24,16},{28,20},{1,9},{5... | collective-permute-start | bytes 737288 | tf_op jit(solution)/shard_map/ppermute | solution.py:72
  34.3 9.9 %collective-permute-start.9 = (bf16[2,2,128,320]{3,2,0,1:T(8,128)(2,1)S(1)}, bf16[2,2,128,320]{3,2,0,1:T(8,128)(2,1)S(1)}, u32[]{:S(2)}, u32[]{:S(2)}) collective-permute-start(bf16[2,2,128,320]{3,2,0,1:T(8,128)(2,1)S(1)} %bitcast.65), channel_id=1, source_target_pairs={{0,4},{4,0},{8,12},{12,8},{16,20},{20,16},{24,28},{28,24},{1,5},{5... | collective-permute-start | bytes 983048 | tf_op jit(solution)/shard_map/ppermute | solution.py:72
  38.5 12.3 %collective-permute-start.5 = (bf16[1,24,16,320]{3,2,1,0:T(8,128)(2,1)S(1)}, bf16[1,24,16,320]{3,2,1,0:T(8,128)(2,1)}, u32[]{:S(2)}, u32[]{:S(2)}) collective-permute-start(bf16[1,24,16,320]{3,2,1,0:T(8,128)(2,1)S(1)} %get-tuple-element.52), channel_id=1, source_target_pairs={{0,1},{1,0},{2,3},{3,2},{4,5},{5,4},{6,7},{7,6},{8,9},{9,8},{10,11... | collective-permute-start | bytes 737288 | tf_op jit(solution)/shard_map/ppermute | solution.py:72
  40.0 9.2 %collective-permute-start.7 = (bf16[1,24,16,320]{3,2,1,0:T(8,128)(2,1)S(1)}, bf16[1,24,16,320]{3,2,1,0:T(8,128)(2,1)}, u32[]{:S(2)}, u32[]{:S(2)}) collective-permute-start(bf16[1,24,16,320]{3,2,1,0:T(8,128)(2,1)S(1)} %get-tuple-element.53), channel_id=1, source_target_pairs={{0,2},{1,3},{2,0},{3,1},{4,6},{5,7},{6,4},{7,5},{8,10},{9,11},{10,... | collective-permute-start | bytes 737288 | tf_op jit(solution)/shard_map/ppermute | solution.py:72
  44.4 9.1 %collective-permute-start.10 = (bf16[2,128,320]{2,1,0:T(8,128)(2,1)S(1)}, bf16[2,128,320]{2,1,0:T(8,128)(2,1)S(1)}, u32[]{:S(2)}, u32[]{:S(2)}) collective-permute-start(bf16[2,128,320]{2,1,0:T(8,128)(2,1)S(1)} %dynamic-slice_bitcast_fusion.1), channel_id=1, source_target_pairs={{0,8},{4,12},{8,0},{12,4},{16,24},{20,28},{24,16},{28,20},{1,9},{5... | collective-permute-start | bytes 491528 | tf_op jit(solution)/shard_map/ppermute | solution.py:72
  50.2 14.6 %collective-permute-start.8 = (bf16[2,24,16,320]{3,2,1,0:T(8,128)(2,1)S(1)}, bf16[2,24,16,320]{3,2,1,0:T(8,128)(2,1)S(1)}, u32[]{:S(2)}, u32[]{:S(2)}) collective-permute-start(bf16[2,24,16,320]{3,2,1,0:T(8,128)(2,1)S(1)} %constant_dynamic-update-slice_fusion.6.second_a), channel_id=1, source_target_pairs={{0,1},{1,0},{2,3},{3,2},{4,5},{5,4},{6,7},{7,6},{8,9},{9,8},{10,11... | collective-permute-start | bytes 1474568 | tf_op jit(solution)/shard_map/ppermute | solution.py:72
  51.9 14.4 %collective-permute-start.6 = (bf16[2,24,16,320]{3,2,1,0:T(8,128)(2,1)S(1)}, bf16[2,24,16,320]{3,2,1,0:T(8,128)(2,1)S(1)}, u32[]{:S(2)}, u32[]{:S(2)}) collective-permute-start(bf16[2,24,16,320]{3,2,1,0:T(8,128)(2,1)S(1)} %constant_dynamic-update-slice_fusion.4.first_a), channel_id=1, source_target_pairs={{0,2},{1,3},{2,0},{3,1},{4,6},{5,7},{6,4},{7,5},{8,10},{9,11},{10,... | collective-permute-start | bytes 1474568 | tf_op jit(solution)/shard_map/ppermute | solution.py:72
  53.6 6.6 %collective-permute-start.11 = (bf16[128,320]{1,0:T(8,128)(2,1)S(1)}, bf16[128,320]{1,0:T(8,128)(2,1)S(1)}, u32[]{:S(2)}, u32[]{:S(2)}) collective-permute-start(bf16[128,320]{1,0:T(8,128)(2,1)S(1)} %dynamic-slice_bitcast_fusion.2), channel_id=1, source_target_pairs={{0,16},{4,20},{8,24},{12,28},{16,0},{20,4},{24,8},{28,12},{1,17},{... | collective-permute-start | bytes 245768 | tf_op jit(solution)/shard_map/ppermute | solution.py:72
  93.4 5.7 %collective-permute-start.20 = (bf16[112,384]{1,0:T(8,128)(2,1)}, bf16[112,384]{1,0:T(8,128)(2,1)S(1)}, u32[]{:S(2)}, u32[]{:S(2)}) collective-permute-start(bf16[112,384]{1,0:T(8,128)(2,1)} %get-tuple-element.73), channel_id=1, source_target_pairs={{0,2},{1,3},{2,0},{3,1},{4,6},{5,7},{6,4},{7,5},{8,10},{9,11},{10,... | collective-permute-start | bytes 258056 | tf_op jit(solution)/shard_map/ppermute | solution.py:72
  102.9 5.6 %collective-permute-start.22 = (bf16[2,1,56,384]{3,2,1,0:T(8,128)(2,1)}, bf16[2,1,56,384]{3,2,1,0:T(8,128)(2,1)S(1)}, u32[]{:S(2)}, u32[]{:S(2)}) collective-permute-start(bf16[2,1,56,384]{3,2,1,0:T(8,128)(2,1)} %bitcast.62), channel_id=1, source_target_pairs={{0,16},{4,20},{8,24},{12,28},{16,0},{20,4},{24,8},{28,12},{1,17},{... | collective-permute-start | bytes 258056 | tf_op jit(solution)/shard_map/ppermute | solution.py:72
  116.9 6.7 %collective-permute-start.27 = (bf16[1,4,56,384]{3,2,1,0:T(8,128)(2,1)S(1)}, bf16[1,4,56,384]{3,2,1,0:T(8,128)(2,1)}, u32[]{:S(2)}, u32[]{:S(2)}) collective-permute-start(bf16[1,4,56,384]{3,2,1,0:T(8,128)(2,1)S(1)} %get-tuple-element.92), channel_id=1, source_target_pairs={{0,1},{1,0},{2,3},{3,2},{4,5},{5,4},{6,7},{7,6},{8,9},{9,8},{10,11... | collective-permute-start | bytes 516104 | tf_op jit(solution)/shard_map/ppermute | solution.py:72
  117.8 25.3 %collective-permute-start.16 = (bf16[384,960]{0,1:T(8,128)(2,1)S(1)}, bf16[384,960]{0,1:T(8,128)(2,1)S(1)}, u32[]{:S(2)}, u32[]{:S(2)}) collective-permute-start(bf16[384,960]{0,1:T(8,128)(2,1)S(1)} %copy.49), channel_id=1, source_target_pairs={{0,4},{4,0},{8,12},{12,8},{16,20},{20,16},{24,28},{28,24},{1,5},{5... | collective-permute-start | bytes 2211848 | tf_op jit(solution)/shard_map/ppermute | solution.py:72
  121.4 19.7 %collective-permute-start.25 = (bf16[2,4,56,384]{3,2,1,0:T(8,128)(2,1)S(1)}, bf16[2,4,56,384]{3,2,1,0:T(8,128)(2,1)S(1)}, u32[]{:S(2)}, u32[]{:S(2)}) collective-permute-start(bf16[2,4,56,384]{3,2,1,0:T(8,128)(2,1)S(1)} %pad_maximum_fusion.1.refs_2_), channel_id=1, source_target_pairs={{0,1},{1,0},{2,3},{3,2},{4,5},{5,4},{6,7},{7,6},{8,9},{9,8},{10,11... | collective-permute-start | bytes 1032200 | tf_op jit(solution)/shard_map/ppermute | solution.py:72
  124.5 18.2 %collective-permute-start.28 = (bf16[2,4,56,384]{3,2,1,0:T(8,128)(2,1)S(1)}, bf16[2,4,56,384]{3,2,1,0:T(8,128)(2,1)S(1)}, u32[]{:S(2)}, u32[]{:S(2)}) collective-permute-start(bf16[2,4,56,384]{3,2,1,0:T(8,128)(2,1)S(1)} %pad_maximum_fusion.2.refs_0_), channel_id=1, source_target_pairs={{0,2},{1,3},{2,0},{3,1},{4,6},{5,7},{6,4},{7,5},{8,10},{9,11},{10,... | collective-permute-start | bytes 1032200 | tf_op jit(solution)/shard_map/ppermute | solution.py:72
  126.4 7.0 %collective-permute-start.14 = (bf16[6,2,16,320]{3,2,1,0:T(8,128)(2,1)S(1)}, bf16[6,2,16,320]{3,2,1,0:T(8,128)(2,1)S(1)}, u32[]{:S(2)}, u32[]{:S(2)}) collective-permute-start(bf16[6,2,16,320]{3,2,1,0:T(8,128)(2,1)S(1)} %get-tuple-element.86), channel_id=1, source_target_pairs={{0,3},{1,2},{2,1},{3,0},{4,7},{5,6},{6,5},{7,4},{8,11},{9,10},{10,... | collective-permute-start | bytes 368648 | tf_op jit(solution)/shard_map/ppermute | solution.py:72
  126.7 10.3 %collective-permute-start.13 = (bf16[6,2,16,320]{3,2,1,0:T(8,128)(2,1)S(1)}, bf16[6,2,16,320]{3,2,1,0:T(8,128)(2,1)S(1)}, u32[]{:S(2)}, u32[]{:S(2)}) collective-permute-start(bf16[6,2,16,320]{3,2,1,0:T(8,128)(2,1)S(1)} %get-tuple-element.87), channel_id=1, source_target_pairs={{0,2},{1,3},{2,0},{3,1},{4,6},{5,7},{6,4},{7,5},{8,10},{9,11},{10,... | collective-permute-start | bytes 368648 | tf_op jit(solution)/shard_map/ppermute | solution.py:72
  141.1 15.5 %collective-permute-start.26 = (bf16[2,4,56,384]{3,2,1,0:T(8,128)(2,1)S(1)}, bf16[2,4,56,384]{3,2,1,0:T(8,128)(2,1)S(1)}, u32[]{:S(2)}, u32[]{:S(2)}) collective-permute-start(bf16[2,4,56,384]{3,2,1,0:T(8,128)(2,1)S(1)} %collective-permute-done.25.refs_3_), channel_id=1, source_target_pairs={{0,4},{4,0},{8,12},{12,8},{16,20},{20,16},{24,28},{28,24},{1,5},{5... | collective-permute-start | bytes 1032200 | tf_op jit(solution)/shard_map/ppermute | solution.py:72
  141.6 15.1 %collective-permute-start.31 = (bf16[2,4,56,384]{3,2,1,0:T(8,128)(2,1)S(1)}, bf16[2,4,56,384]{3,2,1,0:T(8,128)(2,1)}, u32[]{:S(2)}, u32[]{:S(2)}) collective-permute-start(bf16[2,4,56,384]{3,2,1,0:T(8,128)(2,1)S(1)} %pad_maximum_fusion.1.refs_2_), channel_id=1, source_target_pairs={{0,4},{4,0},{8,12},{12,8},{16,20},{20,16},{24,28},{28,24},{1,5},{5... | collective-permute-start | bytes 1032200 | tf_op jit(solution)/shard_map/ppermute | solution.py:72
  142.6 14.1 %collective-permute-start.29 = (bf16[2,4,56,384]{3,2,1,0:T(8,128)(2,1)S(1)}, bf16[2,4,56,384]{3,2,1,0:T(8,128)(2,1)}, u32[]{:S(2)}, u32[]{:S(2)}) collective-permute-start(bf16[2,4,56,384]{3,2,1,0:T(8,128)(2,1)S(1)} %pad_maximum_fusion.2.refs_0_), channel_id=1, source_target_pairs={{0,4},{4,0},{8,12},{12,8},{16,20},{20,16},{24,28},{28,24},{1,5},{5... | collective-permute-start | bytes 1032200 | tf_op jit(solution)/shard_map/ppermute | solution.py:72
  142.8 13.9 %collective-permute-start.30 = (bf16[2,4,56,384]{3,2,1,0:T(8,128)(2,1)S(1)}, bf16[2,4,56,384]{3,2,1,0:T(8,128)(2,1)}, u32[]{:S(2)}, u32[]{:S(2)}) collective-permute-start(bf16[2,4,56,384]{3,2,1,0:T(8,128)(2,1)S(1)} %collective-permute-done.28.refs_1_), channel_id=1, source_target_pairs={{0,4},{4,0},{8,12},{12,8},{16,20},{20,16},{24,28},{28,24},{1,5},{5... | collective-permute-start | bytes 1032200 | tf_op jit(solution)/shard_map/ppermute | solution.py:72
  (31 other events, 190.7 us)

commit v4 on v3

--- a/solution.py
+++ b/solution.py
@@ -83,6 +83,17 @@
     row = lax.broadcasted_iota(jnp.int32, (half_c, columns), 0)
     col = lax.broadcasted_iota(jnp.int32, (half_c, columns), 1)
     return jnp.where((col >> 1) == row, 1.0, 0.0).astype(BF)
+
+
+def fold(x):
+    half = x.shape[0] // 2
+    return jnp.concatenate([x[:half], x[half:]], axis=1).astype(BF)
+
+
+def unfold(x):
+    half = x.shape[1] // 2
+    x = x.astype(F32)
+    return jnp.concatenate([x[:, :half], x[:, half:]], axis=0)
 
 
 def pool_kernel(me, clip, cot, keep, send, tmp):
@@ -97,9 +108,9 @@
     for color in range(2):
         for item in range(3):
             base = pl.multiple_of(core * half + color * quart, quart)
-            keep[color, item] = tmp[item, pl.ds(base, quart), :].astype(BF)
+            keep[color, item] = fold(tmp[item, pl.ds(base, quart), :])
             base = pl.multiple_of((1 - core) * half + color * quart, quart)
-            send[color, item] = tmp[item, pl.ds(base, quart), :].astype(BF)
+            send[color, item] = fold(tmp[item, pl.ds(base, quart), :])
 
 
 def edge_kernel(clip, cot, after, head, tail):
@@ -166,16 +177,21 @@
 
 
 def coarse_kernel(
-    me, first_a, first_b, second_a, second_b, w_time, mix, out_mix, direct, q_rows, u_rows, o_rows, d_rows, taps,
-    local, grad_mix, grad_att, keep, send,
+    me, first_a, first_b, second_a, second_b, w_time, mix, out_mix, direct, taps, *refs,
+    coarse_frames, heads_axis, rest,
+):
+    p1, r3, piece, panes, shift = rest
+    windows = [refs[i * panes : (i + 1) * panes] for i in range(4)]
+    local = refs[4 * panes : 4 * panes + heads_axis]
+    grad_mix, grad_att, keep, send = refs[4 * panes + heads_axis : 4 * panes + heads_axis + 4]
+    (
     stage, shifted, centre, pooled, upper, qkv, att_grad, att, qkv_grad, score, slope, weight, delta, fields, spread_all,
     rows_down, rows_up, rows_tap,
-    *, coarse_frames, heads_axis, rest,
-):
+    ) = refs[4 * panes + heads_axis + 4 :]
     step = pl.program_id(0)
     frame = me[0]
-    quart = stage.shape[2]
-    chans = stage.shape[3]
+    quart = 2 * stage.shape[2]
+    chans = stage.shape[3] // 2
     padded = pooled.shape[1]
     tokens = coarse_frames * quart
     total = 2 * tokens
@@ -205,11 +221,11 @@
 
     for color in range(2):
         before = jnp.zeros((quart, chans), F32)
-        here = stage[color, entry(0)].astype(F32)
+        here = unfold(stage[color, entry(0)])
         for u in range(coarse_frames):
             at = entry(u)
-            last = stage[color, at + 1].astype(F32)
-            after = stage[color, entry(u + 1)].astype(F32) if u + 1 < coarse_frames else jnp.zeros((quart, chans), F32)
+            last = unfold(stage[color, at + 1])
+            after = unfold(stage[color, entry(u + 1)]) if u + 1 < coarse_frames else jnp.zeros((quart, chans), F32)
             offset = color * tokens + u * quart
             rows = pl.ds(pl.multiple_of(step * total + offset, quart), quart)
             mid = 0.5 * (here + last)
@@ -217,7 +233,7 @@
             shifted[rows, chans : 2 * chans] = mid.astype(BF)
             shifted[rows, 2 * chans : 3 * chans] = (0.5 * (last + after)).astype(BF)
             centre[offset : offset + quart, :] = mid
-            upper[rows, :] = stage[color, at + 2]
+            upper[rows, :] = unfold(stage[color, at + 2]).astype(BF)
             before, here = last, after
     pool = (centre[...] + nn(shifted[here_rows, 0 : 3 * chans], w_time[...])).astype(BF)
     pooled[here_rows, 0:chans] = pool
@@ -266,12 +282,16 @@
     lifted = nn(jnp.concatenate(att_rows, axis=0), out_mix[...])
     lifted = lifted + nn(jnp.concatenate(line_rows, axis=0), direct[...]) * part
     lifted = lifted.astype(BF).reshape(4, quart, chans)
-    for color in range(2):
-        for i in range(2):
-            local[0, i, color] = lifted[2 * color + i]
-        for i in range(4):
-            at = jnp.clip(mine + i - 1, 0, coarse_frames - 1)
-            local[0, 2 + i, color] = fields[color * coarse_frames + at]
+    for d in range(heads_axis):
+
+        @pl.when(step == d)
+        def _():
+            for color in range(2):
+                for i in range(2):
+                    local[d][i, color] = lifted[2 * color + i]
+                for i in range(4):
+                    at = jnp.clip(mine + i - 1, 0, coarse_frames - 1)
+                    local[d][2 + i, color] = fields[color * coarse_frames + at]
 
     @pl.when(step == heads_axis - 1)
     def _():
@@ -286,15 +306,18 @@
         own = shifted[:, pl.ds(pl.multiple_of((frame >> 1) * pair, pair), pair)]
         rows_tap[:, 0:chans] = tn(own, spread_all[...])
         rows_tap[:, chans:] = jnp.zeros((pair, padded - chans), F32)
-        rows_down[...] = nt(q_rows[...], grad_mix[...]) + nt(u_rows[...], s) * part
-        rows_up[:, 0:chans] = nn(o_rows[...], grad_att[...]) + nn(d_rows[...], s) * part
+        q_win, u_win, o_win, d_win = [jnp.concatenate([ref[...] for ref in group], axis=1) for group in windows]
+        down_t = nn(grad_mix[...], q_win) + nn(s, u_win) * part
+        rows_down[...] = down_t.astype(BF).T.astype(F32)
+        up_t = tn(grad_att[...], o_win) + tn(s, d_win) * part
+        rows_up[:, 0:chans] = up_t.astype(BF).T.astype(F32)
         rows_up[:, chans:] = jnp.zeros((rows_up.shape[0], padded - chans), F32)
         core = frame & 1
-        p1, r3, piece = rest
+        base = ((frame >> 1) * shift) & (SLOT - 1)
         extra = jnp.zeros((piece - 2 * p1 - r3, padded), F32)
         for dest, which in ((keep, core), (send, 1 - core)):
             for j in range(heads_axis):
-                at = pl.ds(pl.multiple_of((which * heads_axis + j) * p1, p1), p1)
+                at = pl.ds(pl.multiple_of(base + (which * heads_axis + j) * p1, 8), p1)
                 tap = rows_tap[pl.ds(pl.multiple_of((which * heads_axis + j) * r3, r3), r3), :]
                 if dest is keep:
                     more = jnp.concatenate([taps[j * r3 : (j + 1) * r3, :].astype(F32), jnp.zeros((r3, padded - chans), F32)], axis=1)
@@ -333,13 +356,19 @@
             dest[1 + i] = acc[2 + which + i].astype(BF)
 
 
-def split_grad_kernel(down, mix_a, mix_b, att_a, att_b, w_up, qkv_out, att_out, flipped):
+def split_grad_kernel(down, mix_a, mix_b, *refs, late):
+    if late:
+        _, qkv_out, flipped = refs
+    else:
+        att_a, att_b, w_up, qkv_out, att_out, flipped = refs
+
     @pl.when(pl.program_id(0) == 0)
     def _():
         flipped[...] = (mix_a[...].astype(F32) + mix_b[...].astype(F32)).T.astype(BF)
+        if not late:
+            att_out[...] = nn((att_a[...].astype(F32) + att_b[...].astype(F32)).astype(BF), w_up[...])
 
     qkv_out[...] = nn(flipped[...], down[...])
-    att_out[...] = nn((att_a[...].astype(F32) + att_b[...].astype(F32)).astype(BF), w_up[...])
 
 
 def finish_kernel(me, hidden, base, own, other, w_time, output, grad_clip, rows, *, coarse_frames):
@@ -448,7 +477,7 @@
 
     keep, send = call(
         pool_kernel,
-        [sds((2, 3, quart, chans), BF)] * 2,
+        [sds((2, 3, quart // 2, 2 * chans), BF)] * 2,
         in_specs=[smem(), vmem(), vmem()],
         out_specs=[vmem()] * 2,
         scratch_shapes=[pltpu.VMEM((3, half_c, chans), F32)],
@@ -503,59 +532,60 @@
     p1 = round_up(r1, 8)
     r3 = share // nh
     piece_rows = round_up(2 * p1 + r3, 16)
-    start, first, second = lax.optimization_barrier(((f >> 1) * chip_rows, first, second))
     sides = cross(first, second, head_bits)
-
-    def rows_of(x, axis):
-        x = lax.dynamic_slice_in_dim(x, start, chip_rows, axis=axis)
-        x = x.T if axis == 1 else x
-        x = x.reshape(2 * nh, r1, x.shape[1])
-        return jnp.pad(x, ((0, 0), (0, p1 - r1), (0, 0))).reshape(2 * nh * p1, x.shape[2])
-
-    q_rows = rows_of(w_qkv, 0)
-    u_rows = rows_of(w_up, 0)
-    o_rows = rows_of(w_out, 1)
-    d_rows = rows_of(down, 1)
+    simple = r1 == p1
+    if simple:
+        panes = -(-(chip_rows + SLOT - math.gcd(chip_rows, SLOT)) // SLOT)
+        shift = chip_rows
+        cells = (w_qkv_t, w_up_t, w_out, down)
+    else:
+        panes = -(-(2 * nh * p1) // SLOT)
+        shift = 0
+        start = (f >> 1) * chip_rows
+
+        def columns_of(x):
+            x = lax.dynamic_slice_in_dim(x, start, chip_rows, axis=1).reshape(x.shape[0], 2 * nh, r1)
+            x = jnp.pad(x, ((0, 0), (0, 0), (0, p1 - r1))).reshape(x.shape[0], 2 * nh * p1)
+            return jnp.pad(x, ((0, 0), (0, panes * SLOT - x.shape[1])))
+
+        cells = tuple(columns_of(x) for x in (w_qkv_t, w_up_t, w_out, down))
+
+    def pane(x, i):
+        return pl.BlockSpec((x.shape[0], SLOT), lambda g, m: (0, ((m[0] >> 1) * shift) // SLOT + i))
 
     edge = nh // 2
 
     def side(mirrored, late):
-        def index(g):
+        def index(g, m):
             at = reversed_bits(g, nh) if mirrored else g
             at = jnp.maximum(at - edge, 0) if late else jnp.minimum(at, edge - 1)
             return (at, 0, 0, 0)
 
-        return pl.BlockSpec((1, nf * 3, quart, chans), index)
+        return pl.BlockSpec((1, nf * 3, quart // 2, 2 * chans), index)
 
     side_specs = [side(False, False), side(False, True), side(True, False), side(True, True)]
     total = 2 * nf * quart
     every = nh * total
 
     def whole(*shape):
-        return pl.BlockSpec(shape, lambda g: (0,) * len(shape))
+        return pl.BlockSpec(shape, lambda *g: (0,) * len(shape))
 
     w_time2 = w_time.reshape(3 * chans, chans)
-    statics = (w_time2, mix, out_mix, direct, q_rows, u_rows, o_rows, d_rows, taps)
-    local, mix_g, att_g, d_keep, d_send = call(
-        functools.partial(coarse_kernel, coarse_frames=nf, heads_axis=nh, rest=(p1, r3, piece_rows)),
-        [
-            sds((nh, 6, 2, quart, chans), BF),
-            sds((padded, pieces * HD), BF),
-            sds((heads * HD, chans), BF),
-            sds((nh, piece_rows, padded), BF),
-            sds((nh, piece_rows, padded), BF),
-        ],
+    statics = (w_time2, mix, out_mix, direct, taps)
+    window = panes * SLOT
+    outs = [sds((6, 2, quart, chans), BF)] * nh + [
+        sds((padded, pieces * HD), BF),
+        sds((heads * HD, chans), BF),
+        sds((nh, piece_rows, padded), BF),
+        sds((nh, piece_rows, padded), BF),
+    ]
+    grid_spec = pltpu.PrefetchScalarGridSpec(
+        num_scalar_prefetch=1,
         grid=(nh,),
-        in_specs=[smem()] + side_specs + [whole(*x.shape) for x in statics],
-        out_specs=[
-            pl.BlockSpec((1, 6, 2, quart, chans), lambda g: (g, 0, 0, 0, 0)),
-            whole(padded, pieces * HD),
-            whole(heads * HD, chans),
-            whole(nh, piece_rows, padded),
-            whole(nh, piece_rows, padded),
-        ],
+        in_specs=side_specs + [whole(*x.shape) for x in statics] + [pane(x, i) for x in cells for i in range(panes)],
+        out_specs=[whole(*x.shape) for x in outs],
         scratch_shapes=[
-            pltpu.VMEM((2, nf * 3, quart, chans), BF),
+            pltpu.VMEM((2, nf * 3, quart // 2, 2 * chans), BF),
             pltpu.VMEM((every, tap_rows), BF),
             pltpu.VMEM((total, chans), F32),
             pltpu.VMEM((every, padded), BF),
@@ -570,11 +600,19 @@
             pltpu.VMEM((2 * heads, total // 2, total // 2), BF),
             pltpu.VMEM((2 * nf, quart, chans), BF),
             pltpu.VMEM((every, chans), BF),
-            pltpu.VMEM((2 * nh * p1, padded), F32),
-            pltpu.VMEM((2 * nh * p1, padded), F32),
+            pltpu.VMEM((window, padded), F32),
+            pltpu.VMEM((window, padded), F32),
             pltpu.VMEM((2 * share, padded), F32),
         ],
-    )(me, *sides, *statics)
+    )
+    rest = (p1, r3, piece_rows, panes, shift)
+    results = call(
+        functools.partial(coarse_kernel, coarse_frames=nf, heads_axis=nh, rest=rest),
+        outs,
+        grid_spec=grid_spec,
+    )(me, *sides, *statics, *[x for x in cells for _ in range(panes)])
+    local = results[:nh]
+    mix_g, att_g, d_keep, d_send = results[nh:]
 
     d_got = swap(d_send, "frames", 1)
     ordered = call(
@@ -603,7 +641,7 @@
         [four, four],
         in_specs=[smem()] + [vmem()] * nh,
         out_specs=[vmem()] * 2,
-        scratch_shapes=[pltpu.VMEM(local.shape[1:], F32)],
+        scratch_shapes=[pltpu.VMEM(local[0].shape, F32)],
     )(me, local[0], *got)
     other4 = swap(send4, "frames", 1)
     mine4 = mine4.reshape(4, half, chans)
@@ -619,24 +657,41 @@
     mix_o = swap(mix_g, "frames", 1)
     att_o = swap(att_g, "frames", 1)
     step = 256
+    early = 2
+    wide = sds((pieces * HD, width), F32)
+    scratch = [pltpu.VMEM((pieces * HD, padded), BF)]
     grad_qkv, grad_out = call(
-        split_grad_kernel,
-        [sds((pieces * HD, width), F32), sds((heads * HD, width), F32)],
-        grid=(width // step,),
+        functools.partial(split_grad_kernel, late=False),
+        [wide, sds((heads * HD, width), F32)],
+        grid=(early,),
         in_specs=[
             pl.BlockSpec((padded, step), lambda g: (0, g)),
             whole(*mix_g.shape),
             whole(*mix_g.shape),
             whole(*att_g.shape),
             whole(*att_g.shape),
-            pl.BlockSpec((chans, step), lambda g: (0, g)),
+            whole(*w_up_t.shape),
         ],
         out_specs=[
             pl.BlockSpec((pieces * HD, step), lambda g: (0, g)),
-            pl.BlockSpec((heads * HD, step), lambda g: (0, g)),
+            whole(heads * HD, width),
         ],
-        scratch_shapes=[pltpu.VMEM((pieces * HD, padded), BF)],
+        scratch_shapes=scratch,
     )(down, mix_g, mix_o, att_g, att_o, w_up_t)
+    grad_qkv = call(
+        functools.partial(split_grad_kernel, late=True),
+        wide,
+        grid=(width // step - early,),
+        in_specs=[
+            pl.BlockSpec((padded, step), lambda g: (0, g + early)),
+            whole(*mix_g.shape),
+            whole(*mix_g.shape),
+            pl.BlockSpec(memory_space=pl.ANY),
+        ],
+        out_specs=pl.BlockSpec((pieces * HD, step), lambda g: (0, g + early)),
+        scratch_shapes=scratch,
+        input_output_aliases={3: 0},
+    )(down, mix_g, mix_o, grad_qkv)
 
     output, grad_clip, grad_qkv, grad_out, mates[3] = lax.optimization_barrier(
         (output, grad_clip, grad_qkv, grad_out, mates[3])

time: 164 us -> 157 us (0.957)
  local copies, waits for them, and re-layouts: 22.2 us -> 10.4 us
  starting transfers between devices: 31 us -> 36.8 us
  Pallas kernels: 55.7 us -> 59.7 us
  waiting for transfers between devices: 46 us -> 42.1 us
    ppermute x30, starting transfers between devices: 27.8 us -> 33.1 us  [swap(): return lax.ppermute(x, axis, [(i, i ^ bit) for i in range(n)])]
    ppermute x30, waiting for transfers between devices: 46 us -> 42.1 us  [swap(): return lax.ppermute(x, axis, [(i, i ^ bit) for i in range(n)])]
    dynamic_slice x3 -> x0, local copies, waits for them, and re-layouts: 3.75 us -> none  [rows_of(): x = lax.dynamic_slice_in_dim(x, start, chip_rows, axis=axis)]
    unnamed x54 -> x51, local copies, waits for them, and re-layouts: 9.56 us -> 6.6 us
    pallas_call x2 -> x3, Pallas kernels: 9.58 us -> 11.6 us  [the longest x1 4.75 us: body(): call(functools.partial(split_grad_kernel, late=True), wide, grid=(width /...]
    concatenate x2 -> x0, local copies, waits for them, and re-layouts: 2.02 us -> none  [the longest x1 1.01 us: cross(): first = jnp.concatenate([first, first_in], axis=0)]
    pallas_call x1, Pallas kernels: 20.3 us -> 22.3 us  [body(): call(functools.partial(coarse_kernel, coarse_frames=nf, heads_axis=nh, re...]
  transfers between devices with their start and end apart: 32 -> 32, of which waited for: 17 -> 13; matrix products, arithmetic and copies ran while one was open for 12% -> 5% of each run, Pallas kernels for 15% -> 16%
where the time goes in v4:
time: 157 us
  Pallas kernels  59.7 us (38%)
  waiting for transfers between devices  42.1 us (27%)
  starting transfers between devices  36.8 us (23%)
  local copies, waits for them, and re-layouts  10.4 us (7%)
  other arithmetic  5.96 us (4%)
  between operations  1.66 us (1%)
    ppermute x30, waiting for transfers between devices, swap(): return lax.ppermute(x, axis, [(i, i ^ bit) for i in range(n)])  42.1 us
    ppermute x30, starting transfers between devices, swap(): return lax.ppermute(x, axis, [(i, i ^ bit) for i in range(n)])  33.1 us
    pallas_call x1, Pallas kernels, body(): call(functools.partial(coarse_kernel, coarse_frames=nf, heads_axis=nh, re...  22.3 us
    unnamed x51, local copies, waits for them, and re-layouts  6.6 us
    pallas_call x1, Pallas kernels, body(): call(weight_kernel, [sds((padded, width), BF), sds((padded, pieces * SLOT...  5.66 us
    pallas_call x1, Pallas kernels, body(): call(functools.partial(gather_kernel, layout=layout, aligned=aligned), ou...  5.28 us
    pallas_call x1, Pallas kernels, body(): call(functools.partial(split_grad_kernel, late=True), wide, grid=(width /...  4.75 us
    pallas_call x1, Pallas kernels, body(): call(functools.partial(split_grad_kernel, late=False), [wide, sds((heads...  4.7 us
  transfers between devices with their start and end apart: 32, of which 13 were waited for; matrix products, arithmetic and copies ran while one was open for 5% of the time, Pallas kernels for 16%

profile of v4, /device:TPU:0, one launch (start us, length us, event | category | flops | bytes accessed | tf_op | source)
XLA Modules:
  0.0 156.6 jit_solution(10887620711902689118)
XLA Ops:
  1.3 2.2 %shard_map.152 = (bf16[2,3,8,640]{3,2,1,0:T(8,128)(2,1)}, bf16[2,3,8,640]{3,2,1,0:T(8,128)(2,1)}) custom-call(s32[2]{0:T(128)} %pad_add_fusion.me, bf16[2,2,320,128]{3,2,1,0:T(8,128)(2,1)} %bitcast.50, bf16[2,2,320,128]{3,2,1,0:T(8,128)(2,1)} %bitcast.53), custom_call_target="tpu_custom_call" | custom-call | tf_op jit(solution)/shard_map/pallas_call | solution.py:478
  3.4 1.9 %shard_map.153 = (bf16[4,320,128]{2,1,0:T(8,128)(2,1)}, bf16[4,320,128]{2,1,0:T(8,128)(2,1)}) custom-call(bf16[2,2,320,128]{3,2,1,0:T(8,128)(2,1)} %bitcast.51, bf16[2,2,320,128]{3,2,1,0:T(8,128)(2,1)} %bitcast.54, bf16[2,3,8,640]{3,2,1,0:T(8,128)(2,1)} %get-tuple-element.46.after), custom_call_target="tpu_custom_call" | custom-call | tf_op jit(solution)/shard_map/pallas_call | solution.py:501
  5.4 2.4 %collective-permute-start = (bf16[4,320,128]{2,1,0:T(8,128)(2,1)}, bf16[4,320,128]{2,1,0:T(8,128)(2,1)S(1)}, u32[]{:S(2)}, u32[]{:S(2)}) collective-permute-start(bf16[4,320,128]{2,1,0:T(8,128)(2,1)} %get-tuple-element.47), channel_id=1, source_target_pairs={{0,4},{4,8},{8,12},{12,16},{16,20},{20,24},{24,28},{1,5},{5,9},{9,... | collective-permute-start | bytes 983048 | tf_op jit(solution)/shard_map/ppermute | solution.py:507
  9.1 3.4 %collective-permute-start.2 = (bf16[2,3,8,640]{3,2,1,0:T(8,128)(2,1)}, bf16[2,3,8,640]{3,2,1,0:T(8,128)(2,1)S(1)}, u32[]{:S(2)}, u32[]{:S(2)}) collective-permute-start(bf16[2,3,8,640]{3,2,1,0:T(8,128)(2,1)} %get-tuple-element.51), channel_id=1, source_target_pairs={{0,4},{4,0},{8,12},{12,8},{16,20},{20,16},{24,28},{28,24},{1,5},{5... | collective-permute-start | bytes 184328 | tf_op jit(solution)/shard_map/ppermute | solution.py:72
  14.8 2.7 %collective-permute-start.3 = (bf16[2,6,8,640]{3,2,1,0:T(8,128)(2,1)S(1)}, bf16[2,6,8,640]{3,2,1,0:T(8,128)(2,1)S(1)}, u32[]{:S(2)}, u32[]{:S(2)}) collective-permute-start(bf16[2,6,8,640]{3,2,1,0:T(8,128)(2,1)S(1)} %pad_maximum_fusion.7), channel_id=1, source_target_pairs={{0,16},{4,20},{8,24},{12,28},{16,0},{20,4},{24,8},{28,12},{1,17},{... | collective-permute-start | bytes 368648 | tf_op jit(solution)/shard_map/ppermute | solution.py:72
  17.6 7.9 %collective-permute-done.3 = bf16[2,6,8,640]{3,2,1,0:T(8,128)(2,1)S(1)} collective-permute-done((bf16[2,6,8,640]{3,2,1,0:T(8,128)(2,1)S(1)}, bf16[2,6,8,640]{3,2,1,0:T(8,128)(2,1)S(1)}, u32[]{:S(2)}, u32[]{:S(2)}) %collective-permute-start.3) | collective-permute-done | bytes 122912 | tf_op jit(solution)/shard_map/ppermute | solution.py:72
  27.9 4.4 %shard_map.154 = (bf16[2,2,320,128]{3,2,1,0:T(8,128)(2,1)}, f32[2,2,320,128]{3,2,1,0:T(8,128)}, bf16[1024,320]{1,0:T(8,128)(2,1)}) custom-call(bf16[2,2,320,128]{3,2,1,0:T(8,128)(2,1)} %bitcast.52, bf16[2,2,320,128]{3,2,1,0:T(8,128)(2,1)} %bitcast.55, bf16[4,320,128]{2,1,0:T(8,128)(2,1)} %copy-done.11, bf16[4,320,128]{2,1,0:T(8,128)(2,1)} %copy-done.12, ...), custom_call_target="tpu_custom_call" | custom-call | tf_op jit(solution)/shard_map/pallas_call | solution.py:510
  36.9 2.1 %collective-permute-start.10 = (bf16[2,128,320]{2,1,0:T(8,128)(2,1)S(1)}, bf16[2,128,320]{2,1,0:T(8,128)(2,1)S(1)}, u32[]{:S(2)}, u32[]{:S(2)}) collective-permute-start(bf16[2,128,320]{2,1,0:T(8,128)(2,1)S(1)} %dynamic-slice_bitcast_fusion), channel_id=1, source_target_pairs={{0,8},{4,12},{8,0},{12,4},{16,24},{20,28},{24,16},{28,20},{1,9},{5... | collective-permute-start | bytes 491528 | tf_op jit(solution)/shard_map/ppermute | solution.py:72
  39.0 3.1 %collective-permute-done.5 = bf16[1,24,8,640]{3,2,1,0:T(8,128)(2,1)S(1)} collective-permute-done((bf16[1,24,8,640]{3,2,1,0:T(8,128)(2,1)S(1)}, bf16[1,24,8,640]{3,2,1,0:T(8,128)(2,1)S(1)}, u32[]{:S(2)}, u32[]{:S(2)}) %collective-permute-start.5) | collective-permute-done | bytes 245792 | tf_op jit(solution)/shard_map/ppermute | solution.py:72
  45.5 2.8 %collective-permute-start.11 = (bf16[128,320]{1,0:T(8,128)(2,1)S(1)}, bf16[128,320]{1,0:T(8,128)(2,1)S(1)}, u32[]{:S(2)}, u32[]{:S(2)}) collective-permute-start(bf16[128,320]{1,0:T(8,128)(2,1)S(1)} %dynamic-slice_bitcast_fusion.1), channel_id=1, source_target_pairs={{0,16},{4,20},{8,24},{12,28},{16,0},{20,4},{24,8},{28,12},{1,17},{... | collective-permute-start | bytes 245768 | tf_op jit(solution)/shard_map/ppermute | solution.py:72
  48.9 5.7 %shard_map.155 = (bf16[384,1280]{1,0:T(8,128)(2,1)}, bf16[384,1536]{1,0:T(8,128)(2,1)}, bf16[512,320]{1,0:T(8,128)(2,1)}, bf16[384,320]{1,0:T(8,128)(2,1)}) custom-call(bf16[320,1280]{1,0:T(8,128)(2,1)} %w_down.1, bf16[320,1280]{1,0:T(8,128)(2,1)} %w_embed.1, bf16[1,320]{1,0:T(2,128)(2,1)} %fusion.3.embed, bf16[960,1280]{1,0:T(8,128)(2,1)} %bitcast.39, ...), custom_call_target="tpu_custom_call" | custom-call | tf_op jit(solution)/shard_map/pallas_call | solution.py:491
  57.2 22.3 %shard_map.156 = (bf16[6,2,16,320]{3,2,1,0:T(8,128)(2,1)}, bf16[6,2,16,320]{3,2,1,0:T(8,128)(2,1)}, bf16[6,2,16,320]{3,2,1,0:T(8,128)(2,1)}, bf16[6,2,16,320]{3,...) custom-call(s32[2]{0:T(128)} %pad_add_fusion.me, ...), custom_call_target="tpu_custom_call" | custom-call | tf_op jit(solution)/shard_map/pallas_call | solution.py:609
  88.8 3.2 %collective-permute-done.20.refs_2_ = bf16[112,384]{1,0:T(8,128)(2,1)S(1)} collective-permute-done((bf16[112,384]{1,0:T(8,128)(2,1)}, bf16[112,384]{1,0:T(8,128)(2,1)S(1)}, u32[]{:S(2)}, u32[]{:S(2)}) %collective-permute-start.20) | collective-permute-done | bytes 86048 | tf_op jit(solution)/shard_map/ppermute | solution.py:72
  94.4 2.7 %collective-permute-start.22 = (bf16[2,1,56,384]{3,2,1,0:T(8,128)(2,1)}, bf16[2,1,56,384]{3,2,1,0:T(8,128)(2,1)S(1)}, u32[]{:S(2)}, u32[]{:S(2)}) collective-permute-start(bf16[2,1,56,384]{3,2,1,0:T(8,128)(2,1)} %bitcast.57), channel_id=1, source_target_pairs={{0,16},{4,20},{8,24},{12,28},{16,0},{20,4},{24,8},{28,12},{1,17},{... | collective-permute-start | bytes 258056 | tf_op jit(solution)/shard_map/ppermute | solution.py:72
  97.1 2.9 %collective-permute-done.22 = bf16[2,1,56,384]{3,2,1,0:T(8,128)(2,1)S(1)} collective-permute-done((bf16[2,1,56,384]{3,2,1,0:T(8,128)(2,1)}, bf16[2,1,56,384]{3,2,1,0:T(8,128)(2,1)S(1)}, u32[]{:S(2)}, u32[]{:S(2)}) %collective-permute-start.22) | collective-permute-done | bytes 86048 | tf_op jit(solution)/shard_map/ppermute | solution.py:72
  100.9 2.1 %collective-permute-start.23 = (bf16[2,2,56,384]{3,2,1,0:T(8,128)(2,1)S(1)}, bf16[2,2,56,384]{3,2,1,0:T(8,128)(2,1)S(1)}, u32[]{:S(2)}, u32[]{:S(2)}) collective-permute-start(bf16[2,2,56,384]{3,2,1,0:T(8,128)(2,1)S(1)} %pad_maximum_fusion.6), channel_id=1, source_target_pairs={{0,8},{4,12},{8,0},{12,4},{16,24},{20,28},{24,16},{28,20},{1,9},{5... | collective-permute-start | bytes 516104 | tf_op jit(solution)/shard_map/ppermute | solution.py:72
  103.0 3.4 %collective-permute-done.23 = bf16[2,2,56,384]{3,2,1,0:T(8,128)(2,1)S(1)} collective-permute-done((bf16[2,2,56,384]{3,2,1,0:T(8,128)(2,1)S(1)}, bf16[2,2,56,384]{3,2,1,0:T(8,128)(2,1)S(1)}, u32[]{:S(2)}, u32[]{:S(2)}) %collective-permute-start.23) | collective-permute-done | bytes 172064 | tf_op jit(solution)/shard_map/ppermute | solution.py:72
  109.8 3.1 %collective-permute-done.24 = bf16[1,4,56,384]{3,2,1,0:T(8,128)(2,1)S(1)} collective-permute-done((bf16[1,4,56,384]{3,2,1,0:T(8,128)(2,1)S(1)}, bf16[1,4,56,384]{3,2,1,0:T(8,128)(2,1)S(1)}, u32[]{:S(2)}, u32[]{:S(2)}) %collective-permute-start.24) | collective-permute-done | bytes 172064 | tf_op jit(solution)/shard_map/ppermute | solution.py:72
  117.4 7.0 %collective-permute-done.12.refs_1_ = bf16[6,2,16,320]{3,2,1,0:T(8,128)(2,1)S(1)} collective-permute-done((bf16[6,2,16,320]{3,2,1,0:T(8,128)(2,1)S(1)}, bf16[6,2,16,320]{3,2,1,0:T(8,128)(2,1)S(1)}, u32[]{:S(2)}, u32[]{:S(2)}) %collective-permute-start.12) | collective-permute-done | bytes 122912 | tf_op jit(solution)/shard_map/ppermute | solution.py:72
  125.5 5.0 %collective-permute-done.14.refs_3_ = bf16[6,2,16,320]{3,2,1,0:T(8,128)(2,1)S(1)} collective-permute-done((bf16[6,2,16,320]{3,2,1,0:T(8,128)(2,1)S(1)}, bf16[6,2,16,320]{3,2,1,0:T(8,128)(2,1)S(1)}, u32[]{:S(2)}, u32[]{:S(2)}) %collective-permute-start.14) | collective-permute-done | bytes 122912 | tf_op jit(solution)/shard_map/ppermute | solution.py:72
  136.2 3.1 %shard_map.158 = (bf16[2,2,320,128]{3,2,1,0:T(8,128)(2,1)}, f32[2,2,320,128]{3,2,1,0:T(8,128)}) custom-call(s32[2]{0:T(128)} %pad_add_fusion.me, bf16[2,2,320,128]{3,2,1,0:T(8,128)(2,1)} %get-tuple-element.49.hidden, f32[2,2,320,128]{3,2,1,0:T(8,128)} %get-tuple-element.50.base, bf16[4,32,320]{2,1,0:T(8,128)(2,1)} %bitcast.61, bf16[4,32,320]{2,1,0:T(8,128)(2,1)} %bitcast.62, ...), custom_call_target="tpu_custom_call" | custom-call | tf_op jit(solution)/shard_map/pallas_call | solution.py:649
  141.2 4.7 %shard_map.159 = (f32[960,1280]{1,0:T(8,128)}, f32[320,1280]{1,0:T(8,128)}) custom-call(bf16[384,1280]{1,0:T(8,128)(2,1)} %get-tuple-element.56.refs_9_.refs_10_.refs_11_.down, bf16[384,960]{1,0:T(8,128)(2,1)} %get-tuple-element.65.mix_a, bf16[384,960]{1,0:T(8,128)(2,1)} %copy.37.mix_b, bf16[320,320]{1,0:T(8,128)(2,1)} %get-tuple-element.66.refs_0_, ...), custom_call_target="tpu_custom_call" | custom-call | tf_op jit(solution)/shard_map/pallas_call | solution.py:663
  145.9 4.8 %shard_map.160 = f32[960,1280]{1,0:T(8,128)} custom-call(bf16[384,1280]{1,0:T(8,128)(2,1)} %get-tuple-element.56.refs_9_.refs_10_.refs_11_.down, bf16[384,960]{1,0:T(8,128)(2,1)} %get-tuple-element.65.mix_a, bf16[384,960]{1,0:T(8,128)(2,1)} %copy.37.mix_b, f32[960,1280]{1,0:T(8,128)} %get-tuple-element.67.refs_0_), custom_call_target="tpu_custom_call", output_to_operand_aliasing={{}: (3, {})} | custom-call | tf_op jit(solution)/shard_map/pallas_call | solution.py:681
  151.4 5.3 %shard_map.163 = (f32[30,32,320]{2,1,0:T(8,128)}, f32[320,1280]{1,0:T(8,128)}, f32[320,1280]{1,0:T(8,128)}, f32[320,1280]{1,0:T(8,128)}) custom-call(s32[2]{0:T(128)} %pad_add_fusion.me, f32[320,1]{1,0:T(8,128)} %copy.38.embed, bf16[2,4,56,384]{3,2,1,0:T(8,128)(2,1)} %copy-done.4, bf16[2,4,56,384]{3,2,1,0:T(8,128)(2,1)} %copy-done.8, ...), custom_call_target="tpu_custom_call" | custom-call | tf_op jit(solution)/shard_map/pallas_call | solution.py:710
  (128 shorter events, 47.0 us)
Async XLA Ops:
  5.4 21.1 %collective-permute-start = (bf16[4,320,128]{2,1,0:T(8,128)(2,1)}, bf16[4,320,128]{2,1,0:T(8,128)(2,1)S(1)}, u32[]{:S(2)}, u32[]{:S(2)}) collective-permute-start(bf16[4,320,128]{2,1,0:T(8,128)(2,1)} %get-tuple-element.47), channel_id=1, source_target_pairs={{0,4},{4,8},{8,12},{12,16},{16,20},{20,24},{24,28},{1,5},{5,9},{9,... | collective-permute-start | bytes 983048 | tf_op jit(solution)/shard_map/ppermute | solution.py:507
  7.8 18.7 %collective-permute-start.1 = (bf16[4,320,128]{2,1,0:T(8,128)(2,1)}, bf16[4,320,128]{2,1,0:T(8,128)(2,1)S(1)}, u32[]{:S(2)}, u32[]{:S(2)}) collective-permute-start(bf16[4,320,128]{2,1,0:T(8,128)(2,1)} %get-tuple-element.48), channel_id=1, source_target_pairs={{4,0},{8,4},{12,8},{16,12},{20,16},{24,20},{28,24},{5,1},{9,5},{13... | collective-permute-start | bytes 983048 | tf_op jit(solution)/shard_map/ppermute | solution.py:508
  14.8 10.7 %collective-permute-start.3 = (bf16[2,6,8,640]{3,2,1,0:T(8,128)(2,1)S(1)}, bf16[2,6,8,640]{3,2,1,0:T(8,128)(2,1)S(1)}, u32[]{:S(2)}, u32[]{:S(2)}) collective-permute-start(bf16[2,6,8,640]{3,2,1,0:T(8,128)(2,1)S(1)} %pad_maximum_fusion.7), channel_id=1, source_target_pairs={{0,16},{4,20},{8,24},{12,28},{16,0},{20,4},{24,8},{28,12},{1,17},{... | collective-permute-start | bytes 368648 | tf_op jit(solution)/shard_map/ppermute | solution.py:72
  26.4 7.3 %collective-permute-start.4 = (bf16[2,12,8,640]{3,2,1,0:T(8,128)(2,1)S(1)}, bf16[2,12,8,640]{3,2,1,0:T(8,128)(2,1)S(1)}, u32[]{:S(2)}, u32[]{:S(2)}) collective-permute-start(bf16[2,12,8,640]{3,2,1,0:T(8,128)(2,1)S(1)} %pad_maximum_fusion.5), channel_id=1, source_target_pairs={{0,8},{4,12},{8,0},{12,4},{16,24},{20,28},{24,16},{28,20},{1,9},{5... | collective-permute-start | bytes 737288 | tf_op jit(solution)/shard_map/ppermute | solution.py:72
  33.7 8.4 %collective-permute-start.5 = (bf16[1,24,8,640]{3,2,1,0:T(8,128)(2,1)S(1)}, bf16[1,24,8,640]{3,2,1,0:T(8,128)(2,1)S(1)}, u32[]{:S(2)}, u32[]{:S(2)}) collective-permute-start(bf16[1,24,8,640]{3,2,1,0:T(8,128)(2,1)S(1)} %get-tuple-element.87), channel_id=1, source_target_pairs={{0,1},{1,0},{2,3},{3,2},{4,5},{5,4},{6,7},{7,6},{8,9},{9,8},{10,11... | collective-permute-start | bytes 737288 | tf_op jit(solution)/shard_map/ppermute | solution.py:72
  35.3 8.5 %collective-permute-start.7 = (bf16[1,24,8,640]{3,2,1,0:T(8,128)(2,1)S(1)}, bf16[1,24,8,640]{3,2,1,0:T(8,128)(2,1)S(1)}, u32[]{:S(2)}, u32[]{:S(2)}) collective-permute-start(bf16[1,24,8,640]{3,2,1,0:T(8,128)(2,1)S(1)} %get-tuple-element.86), channel_id=1, source_target_pairs={{0,2},{1,3},{2,0},{3,1},{4,6},{5,7},{6,4},{7,5},{8,10},{9,11},{10,... | collective-permute-start | bytes 737288 | tf_op jit(solution)/shard_map/ppermute | solution.py:72
  36.9 8.5 %collective-permute-start.10 = (bf16[2,128,320]{2,1,0:T(8,128)(2,1)S(1)}, bf16[2,128,320]{2,1,0:T(8,128)(2,1)S(1)}, u32[]{:S(2)}, u32[]{:S(2)}) collective-permute-start(bf16[2,128,320]{2,1,0:T(8,128)(2,1)S(1)} %dynamic-slice_bitcast_fusion), channel_id=1, source_target_pairs={{0,8},{4,12},{8,0},{12,4},{16,24},{20,28},{24,16},{28,20},{1,9},{5... | collective-permute-start | bytes 491528 | tf_op jit(solution)/shard_map/ppermute | solution.py:72
  42.2 13.1 %collective-permute-start.6 = (bf16[2,24,8,640]{3,2,1,0:T(8,128)(2,1)S(1)}, bf16[2,24,8,640]{3,2,1,0:T(8,128)(2,1)S(1)}, u32[]{:S(2)}, u32[]{:S(2)}) collective-permute-start(bf16[2,24,8,640]{3,2,1,0:T(8,128)(2,1)S(1)} %pad_maximum_fusion.first_a), channel_id=1, source_target_pairs={{0,2},{1,3},{2,0},{3,1},{4,6},{5,7},{6,4},{7,5},{8,10},{9,11},{10,... | collective-permute-start | bytes 1474568 | tf_op jit(solution)/shard_map/ppermute | solution.py:72
  43.9 12.5 %collective-permute-start.8 = (bf16[2,24,8,640]{3,2,1,0:T(8,128)(2,1)S(1)}, bf16[2,24,8,640]{3,2,1,0:T(8,128)(2,1)S(1)}, u32[]{:S(2)}, u32[]{:S(2)}) collective-permute-start(bf16[2,24,8,640]{3,2,1,0:T(8,128)(2,1)S(1)} %pad_maximum_fusion.1.second_a), channel_id=1, source_target_pairs={{0,1},{1,0},{2,3},{3,2},{4,5},{5,4},{6,7},{7,6},{8,9},{9,8},{10,11... | collective-permute-start | bytes 1474568 | tf_op jit(solution)/shard_map/ppermute | solution.py:72
  45.5 9.1 %collective-permute-start.11 = (bf16[128,320]{1,0:T(8,128)(2,1)S(1)}, bf16[128,320]{1,0:T(8,128)(2,1)S(1)}, u32[]{:S(2)}, u32[]{:S(2)}) collective-permute-start(bf16[128,320]{1,0:T(8,128)(2,1)S(1)} %dynamic-slice_bitcast_fusion.1), channel_id=1, source_target_pairs={{0,16},{4,20},{8,24},{12,28},{16,0},{20,4},{24,8},{28,12},{1,17},{... | collective-permute-start | bytes 245768 | tf_op jit(solution)/shard_map/ppermute | solution.py:72
  85.5 6.5 %collective-permute-start.20 = (bf16[112,384]{1,0:T(8,128)(2,1)}, bf16[112,384]{1,0:T(8,128)(2,1)S(1)}, u32[]{:S(2)}, u32[]{:S(2)}) collective-permute-start(bf16[112,384]{1,0:T(8,128)(2,1)} %get-tuple-element.73), channel_id=1, source_target_pairs={{0,2},{1,3},{2,0},{3,1},{4,6},{5,7},{6,4},{7,5},{8,10},{9,11},{10,... | collective-permute-start | bytes 258056 | tf_op jit(solution)/shard_map/ppermute | solution.py:72
  86.0 6.0 %collective-permute-start.21 = (bf16[112,384]{1,0:T(8,128)(2,1)}, bf16[112,384]{1,0:T(8,128)(2,1)S(1)}, u32[]{:S(2)}, u32[]{:S(2)}) collective-permute-start(bf16[112,384]{1,0:T(8,128)(2,1)} %get-tuple-element.74), channel_id=1, source_target_pairs={{0,3},{1,2},{2,1},{3,0},{4,7},{5,6},{6,5},{7,4},{8,11},{9,10},{10,... | collective-permute-start | bytes 258056 | tf_op jit(solution)/shard_map/ppermute | solution.py:72
  94.4 5.6 %collective-permute-start.22 = (bf16[2,1,56,384]{3,2,1,0:T(8,128)(2,1)}, bf16[2,1,56,384]{3,2,1,0:T(8,128)(2,1)S(1)}, u32[]{:S(2)}, u32[]{:S(2)}) collective-permute-start(bf16[2,1,56,384]{3,2,1,0:T(8,128)(2,1)} %bitcast.57), channel_id=1, source_target_pairs={{0,16},{4,20},{8,24},{12,28},{16,0},{20,4},{24,8},{28,12},{1,17},{... | collective-permute-start | bytes 258056 | tf_op jit(solution)/shard_map/ppermute | solution.py:72
  108.5 6.3 %collective-permute-start.27 = (bf16[1,4,56,384]{3,2,1,0:T(8,128)(2,1)S(1)}, bf16[1,4,56,384]{3,2,1,0:T(8,128)(2,1)S(1)}, u32[]{:S(2)}, u32[]{:S(2)}) collective-permute-start(bf16[1,4,56,384]{3,2,1,0:T(8,128)(2,1)S(1)} %get-tuple-element.88), channel_id=1, source_target_pairs={{0,1},{1,0},{2,3},{3,2},{4,5},{5,4},{6,7},{7,6},{8,9},{9,8},{10,11... | collective-permute-start | bytes 516104 | tf_op jit(solution)/shard_map/ppermute | solution.py:72
  109.7 25.4 %collective-permute-start.16 = (bf16[384,960]{0,1:T(8,128)(2,1)S(1)}, bf16[384,960]{0,1:T(8,128)(2,1)S(1)}, u32[]{:S(2)}, u32[]{:S(2)}) collective-permute-start(bf16[384,960]{0,1:T(8,128)(2,1)S(1)} %copy.35), channel_id=1, source_target_pairs={{0,4},{4,0},{8,12},{12,8},{16,20},{20,16},{24,28},{28,24},{1,5},{5... | collective-permute-start | bytes 2211848 | tf_op jit(solution)/shard_map/ppermute | solution.py:72
  112.9 20.1 %collective-permute-start.25 = (bf16[2,4,56,384]{3,2,1,0:T(8,128)(2,1)S(1)}, bf16[2,4,56,384]{3,2,1,0:T(8,128)(2,1)S(1)}, u32[]{:S(2)}, u32[]{:S(2)}) collective-permute-start(bf16[2,4,56,384]{3,2,1,0:T(8,128)(2,1)S(1)} %pad_maximum_fusion.3.refs_2_), channel_id=1, source_target_pairs={{0,1},{1,0},{2,3},{3,2},{4,5},{5,4},{6,7},{7,6},{8,9},{9,8},{10,11... | collective-permute-start | bytes 1032200 | tf_op jit(solution)/shard_map/ppermute | solution.py:72
  114.9 19.8 %collective-permute-start.28 = (bf16[2,4,56,384]{3,2,1,0:T(8,128)(2,1)S(1)}, bf16[2,4,56,384]{3,2,1,0:T(8,128)(2,1)S(1)}, u32[]{:S(2)}, u32[]{:S(2)}) collective-permute-start(bf16[2,4,56,384]{3,2,1,0:T(8,128)(2,1)S(1)} %pad_maximum_fusion.4.refs_0_), channel_id=1, source_target_pairs={{0,2},{1,3},{2,0},{3,1},{4,6},{5,7},{6,4},{7,5},{8,10},{9,11},{10,... | collective-permute-start | bytes 1032200 | tf_op jit(solution)/shard_map/ppermute | solution.py:72
  116.1 8.3 %collective-permute-start.12 = (bf16[6,2,16,320]{3,2,1,0:T(8,128)(2,1)S(1)}, bf16[6,2,16,320]{3,2,1,0:T(8,128)(2,1)S(1)}, u32[]{:S(2)}, u32[]{:S(2)}) collective-permute-start(bf16[6,2,16,320]{3,2,1,0:T(8,128)(2,1)S(1)} %copy-done.23), channel_id=1, source_target_pairs={{0,1},{1,0},{2,3},{3,2},{4,5},{5,4},{6,7},{7,6},{8,9},{9,8},{10,11... | collective-permute-start | bytes 368648 | tf_op jit(solution)/shard_map/ppermute | solution.py:72
  116.2 9.3 %collective-permute-start.13 = (bf16[6,2,16,320]{3,2,1,0:T(8,128)(2,1)S(1)}, bf16[6,2,16,320]{3,2,1,0:T(8,128)(2,1)S(1)}, u32[]{:S(2)}, u32[]{:S(2)}) collective-permute-start(bf16[6,2,16,320]{3,2,1,0:T(8,128)(2,1)S(1)} %copy-done.22), channel_id=1, source_target_pairs={{0,2},{1,3},{2,0},{3,1},{4,6},{5,7},{6,4},{7,5},{8,10},{9,11},{10,... | collective-permute-start | bytes 368648 | tf_op jit(solution)/shard_map/ppermute | solution.py:72
  124.5 6.0 %collective-permute-start.14 = (bf16[6,2,16,320]{3,2,1,0:T(8,128)(2,1)S(1)}, bf16[6,2,16,320]{3,2,1,0:T(8,128)(2,1)S(1)}, u32[]{:S(2)}, u32[]{:S(2)}) collective-permute-start(bf16[6,2,16,320]{3,2,1,0:T(8,128)(2,1)S(1)} %copy-done.21), channel_id=1, source_target_pairs={{0,3},{1,2},{2,1},{3,0},{4,7},{5,6},{6,5},{7,4},{8,11},{9,10},{10,... | collective-permute-start | bytes 368648 | tf_op jit(solution)/shard_map/ppermute | solution.py:72
  133.1 17.5 %collective-permute-start.26 = (bf16[2,4,56,384]{3,2,1,0:T(8,128)(2,1)S(1)}, bf16[2,4,56,384]{3,2,1,0:T(8,128)(2,1)S(1)}, u32[]{:S(2)}, u32[]{:S(2)}) collective-permute-start(bf16[2,4,56,384]{3,2,1,0:T(8,128)(2,1)S(1)} %collective-permute-done.25.refs_3_), channel_id=1, source_target_pairs={{0,4},{4,0},{8,12},{12,8},{16,20},{20,16},{24,28},{28,24},{1,5},{5... | collective-permute-start | bytes 1032200 | tf_op jit(solution)/shard_map/ppermute | solution.py:72
  133.6 17.1 %collective-permute-start.29 = (bf16[2,4,56,384]{3,2,1,0:T(8,128)(2,1)S(1)}, bf16[2,4,56,384]{3,2,1,0:T(8,128)(2,1)}, u32[]{:S(2)}, u32[]{:S(2)}) collective-permute-start(bf16[2,4,56,384]{3,2,1,0:T(8,128)(2,1)S(1)} %pad_maximum_fusion.4.refs_0_), channel_id=1, source_target_pairs={{0,4},{4,0},{8,12},{12,8},{16,20},{20,16},{24,28},{28,24},{1,5},{5... | collective-permute-start | bytes 1032200 | tf_op jit(solution)/shard_map/ppermute | solution.py:72
  134.6 16.1 %collective-permute-start.31 = (bf16[2,4,56,384]{3,2,1,0:T(8,128)(2,1)S(1)}, bf16[2,4,56,384]{3,2,1,0:T(8,128)(2,1)}, u32[]{:S(2)}, u32[]{:S(2)}) collective-permute-start(bf16[2,4,56,384]{3,2,1,0:T(8,128)(2,1)S(1)} %pad_maximum_fusion.3.refs_2_), channel_id=1, source_target_pairs={{0,4},{4,0},{8,12},{12,8},{16,20},{20,16},{24,28},{28,24},{1,5},{5... | collective-permute-start | bytes 1032200 | tf_op jit(solution)/shard_map/ppermute | solution.py:72
  134.7 15.9 %collective-permute-start.30 = (bf16[2,4,56,384]{3,2,1,0:T(8,128)(2,1)S(1)}, bf16[2,4,56,384]{3,2,1,0:T(8,128)(2,1)}, u32[]{:S(2)}, u32[]{:S(2)}) collective-permute-start(bf16[2,4,56,384]{3,2,1,0:T(8,128)(2,1)S(1)} %collective-permute-done.28.refs_1_), channel_id=1, source_target_pairs={{0,4},{4,0},{8,12},{12,8},{16,20},{20,16},{24,28},{28,24},{1,5},{5... | collective-permute-start | bytes 1032200 | tf_op jit(solution)/shard_map/ppermute | solution.py:72
  (32 other events, 208.9 us)

commit v5 on v4

--- a/solution.py
+++ b/solution.py
@@ -122,7 +122,11 @@
         tail[2 + r] = cot[1, r]
 
 
-def weight_kernel(w_down, w_embed, embed, w_qkv, w_out, w_up, down, mix, out_mix, direct):
+def weight_kernel(w_down, w_embed, embed, w_qkv, w_out, w_up, down, mix, out_mix, direct, column):
+    wide = embed.shape[1]
+    eye = lax.broadcasted_iota(jnp.int32, (wide, wide), 0) == lax.broadcasted_iota(jnp.int32, (wide, wide), 1)
+    line = jnp.broadcast_to(embed[...].astype(F32), (SLOT, wide)).astype(BF)
+    column[...] = nt(eye.astype(F32).astype(BF), line)
     chans = w_down.shape[0]
     padded = down.shape[0]
     shift = nn(embed[...], w_embed[...])
@@ -146,7 +150,7 @@
     direct[...] = nt(full, up).astype(BF)
 
 
-def fine_kernel(clip, cot, lo, hi, w_time, hidden, base, taps, wide, grad):
+def fine_kernel(me, clip, cot, lo, hi, w_time, hidden, base, keep, send, wide, grad, taps):
     chans = w_time.shape[1]
     columns = clip.shape[3]
     for t in range(4):
@@ -160,10 +164,15 @@
                 wide[:, at] = clip[t - 1, r]
                 grad[:, at] = cot[t - 1, r]
     cells = 2 * columns
-    taps[3 * chans :, :] = jnp.zeros((taps.shape[0] - 3 * chans, chans), BF)
+    taps[3 * chans :, :] = jnp.zeros((taps.shape[0] - 3 * chans, chans), F32)
     here = grad[:, cells : 3 * cells]
     for tap in range(3):
-        taps[tap * chans : (tap + 1) * chans, :] = nt(wide[:, tap * cells : (tap + 2) * cells], here).astype(BF)
+        taps[tap * chans : (tap + 1) * chans, :] = nt(wide[:, tap * cells : (tap + 2) * cells], here)
+    core = me[0] & 1
+    share = keep.shape[1]
+    for z in range(keep.shape[0]):
+        keep[z] = taps[pl.ds(pl.multiple_of((2 * z + core) * share, share), share), :].astype(BF)
+        send[z] = taps[pl.ds(pl.multiple_of((2 * z + 1 - core) * share, share), share), :].astype(BF)
     acc = wide[:, cells : 3 * cells].astype(F32)
     back = here.astype(F32)
     for tap in range(3):
@@ -176,8 +185,14 @@
             base[t, r] = back[:, at]
 
 
+def tap_kernel(me, keep, got, *outs):
+    for d, out in enumerate(outs):
+        at = (me[0] >> 1) ^ d
+        out[...] = (keep[at].astype(F32) + got[at].astype(F32)).astype(BF)
+
+
 def coarse_kernel(
-    me, first_a, first_b, second_a, second_b, w_time, mix, out_mix, direct, taps, *refs,
+    me, first_a, first_b, second_a, second_b, w_time, mix, out_mix, direct, *refs,
     coarse_frames, heads_axis, rest,
 ):
     p1, r3, piece, panes, shift = rest
@@ -298,6 +313,8 @@
         g = tn(pooled[...], qkv_grad[...])
         for i in range(3 * heads):
             grad_mix[:, i * HD : (i + 1) * HD] = g[:, i * SLOT : i * SLOT + HD].astype(BF)
+        used = 3 * heads * HD
+        grad_mix[:, used:] = jnp.zeros((padded, grad_mix.shape[1] - used), BF)
         a = tn(att[...], upper[...])
         for n in range(heads):
             grad_att[n * HD : (n + 1) * HD, :] = a[n * SLOT : n * SLOT + HD, :].astype(BF)
@@ -307,7 +324,7 @@
         rows_tap[:, 0:chans] = tn(own, spread_all[...])
         rows_tap[:, chans:] = jnp.zeros((pair, padded - chans), F32)
         q_win, u_win, o_win, d_win = [jnp.concatenate([ref[...] for ref in group], axis=1) for group in windows]
-        down_t = nn(grad_mix[...], q_win) + nn(s, u_win) * part
+        down_t = nn(grad_mix[:, 0:used], q_win) + nn(s, u_win) * part
         rows_down[...] = down_t.astype(BF).T.astype(F32)
         up_t = tn(grad_att[...], o_win) + tn(s, d_win) * part
         rows_up[:, 0:chans] = up_t.astype(BF).T.astype(F32)
@@ -319,20 +336,25 @@
             for j in range(heads_axis):
                 at = pl.ds(pl.multiple_of(base + (which * heads_axis + j) * p1, 8), p1)
                 tap = rows_tap[pl.ds(pl.multiple_of((which * heads_axis + j) * r3, r3), r3), :]
-                if dest is keep:
-                    more = jnp.concatenate([taps[j * r3 : (j + 1) * r3, :].astype(F32), jnp.zeros((r3, padded - chans), F32)], axis=1)
-                    tap = tap + more
                 parts = [rows_down[at, :], rows_up[at, :], tap]
                 if piece > 2 * p1 + r3:
                     parts.append(extra)
                 dest[j] = jnp.concatenate(parts, axis=0).astype(BF)
 
 
-def order_kernel(me, keep, got, *outs):
+def order_kernel(me, keep, got, *refs, at, taps):
+    parts, outs = refs[:taps], refs[taps:]
     head = me[1]
+    rows = parts[0].shape[0] // len(outs)
+    chans = parts[0].shape[1]
     for d, out in enumerate(outs):
-        at = head ^ d
-        out[...] = (keep[at].astype(F32) + got[at].astype(F32)).astype(BF)
+        value = keep[head ^ d].astype(F32) + got[head ^ d].astype(F32)
+        here = pl.ds(pl.multiple_of((head ^ d) * rows, rows), rows)
+        tap = value[at : at + rows, 0:chans]
+        for ref in parts:
+            tap = tap + ref[here, :].astype(F32)
+        out[...] = value.astype(BF)
+        out[at : at + rows, 0:chans] = tap.astype(BF)
 
 
 def sum_kernel(*refs):
@@ -364,7 +386,7 @@
 
     @pl.when(pl.program_id(0) == 0)
     def _():
-        flipped[...] = (mix_a[...].astype(F32) + mix_b[...].astype(F32)).T.astype(BF)
+        flipped[...] = (mix_a[...].astype(F32) + mix_b[...].astype(F32)).astype(BF).T[0 : flipped.shape[0]]
         if not late:
             att_out[...] = nn((att_a[...].astype(F32) + att_b[...].astype(F32)).astype(BF), w_up[...])
 
@@ -430,7 +452,7 @@
         eye = eye.astype(F32).astype(BF)
         flipped = nt(eye, down_rows[...].reshape(devices * r1, lanes).astype(BF))
         down_out[...] = flipped[0:chans]
-        embed_out[...] = embed[...] * flipped[chans : chans + 1]
+        embed_out[...] = embed[:, 0:1] * flipped[chans : chans + 1]
         up_out[...] = nt(eye, up_rows[...].reshape(devices * r1, lanes).astype(BF))[0:chans]
 
 
@@ -481,20 +503,21 @@
         in_specs=[smem(), vmem(), vmem()],
         out_specs=[vmem()] * 2,
         scratch_shapes=[pltpu.VMEM((3, half_c, chans), F32)],
-    )(me, clip_t, cot_t)
+    )(f.astype(jnp.int32).reshape(1), clip_t, cot_t)
     keep_in = swap(send, "frames", 1)
     block = jnp.concatenate([keep, keep_in], axis=1)
     block = double(block, "frames", chip_bits, 1)
     first, second = block[0][None], block[1][None]
 
     embed = time_embed(timestep, w_embed.shape[0])
-    down, mix, out_mix, direct = call(
+    down, mix, out_mix, direct, embed_col = call(
         weight_kernel,
         [
             sds((padded, width), BF),
             sds((padded, pieces * SLOT), BF),
             sds((heads * SLOT, chans), BF),
             sds((padded, chans), BF),
+            sds((embed.shape[0], SLOT), F32),
         ],
     )(w_down, w_embed, embed[None, :], w_qkv_t, w_out, w_up_t)
 
@@ -507,25 +530,29 @@
     lo = lax.ppermute(tail, "frames", [(i, i + 1) for i in range(nf - 1)])
     hi = lax.ppermute(head, "frames", [(i + 1, i) for i in range(nf - 1)])
     tap_rows = round_up(3 * chans, devices * 8)
-    hidden, base, taps = call(
+    hidden, base, tap_keep, tap_send = call(
         fine_kernel,
         [
             sds(clip_t.shape, BF),
             sds(clip_t.shape, F32),
-            sds((tap_rows, chans), BF),
+            sds((chips, tap_rows // nf, chans), BF),
+            sds((chips, tap_rows // nf, chans), BF),
         ],
-        scratch_shapes=[pltpu.VMEM((chans, 8 * columns), BF)] * 2,
-    )(clip_t, cot_t, lo, hi, w_time)
+        in_specs=[smem()] + [vmem()] * 5,
+        out_specs=[vmem()] * 4,
+        scratch_shapes=[pltpu.VMEM((chans, 8 * columns), BF)] * 2 + [pltpu.VMEM((tap_rows, chans), F32)],
+    )(me, clip_t, cot_t, lo, hi, w_time)
     share = tap_rows // nf
-    bits = bit_list(nf)
-    taps = taps.reshape([2] * len(bits) + [share, chans])
-    for i in range(len(bits)):
-        axis = len(bits) - 1 - i
-        mine = (f >> i) & 1
-        other = lax.dynamic_index_in_dim(taps, 1 - mine, axis, keepdims=False)
-        same = lax.dynamic_index_in_dim(taps, mine, axis, keepdims=False)
-        got = swap(other, "frames", 1 << i)
-        taps = (same.astype(F32) + got.astype(F32)).astype(BF)
+    tap_got = swap(tap_send, "frames", 1)
+    tap_parts = call(
+        tap_kernel,
+        [sds((share, chans), BF)] * chips,
+        in_specs=[smem(), vmem(), vmem()],
+        out_specs=[vmem()] * chips,
+    )(me, tap_keep, tap_got)
+    taps = [tap_parts[0]]
+    for d in range(1, chips):
+        taps.append(swap(tap_parts[d], "frames", 2 * d))
 
     chip_rows = 2 * width // nf
     r1 = width // devices
@@ -571,10 +598,10 @@
         return pl.BlockSpec(shape, lambda *g: (0,) * len(shape))
 
     w_time2 = w_time.reshape(3 * chans, chans)
-    statics = (w_time2, mix, out_mix, direct, taps)
+    statics = (w_time2, mix, out_mix, direct)
     window = panes * SLOT
     outs = [sds((6, 2, quart, chans), BF)] * nh + [
-        sds((padded, pieces * HD), BF),
+        sds((padded, round_up(pieces * HD, SLOT)), BF),
         sds((heads * HD, chans), BF),
         sds((nh, piece_rows, padded), BF),
         sds((nh, piece_rows, padded), BF),
@@ -616,11 +643,11 @@
 
     d_got = swap(d_send, "frames", 1)
     ordered = call(
-        order_kernel,
+        functools.partial(order_kernel, at=2 * p1, taps=chips),
         [sds((piece_rows, padded), BF)] * nh,
-        in_specs=[smem(), vmem(), vmem()],
+        in_specs=[smem()] + [vmem()] * (2 + chips),
         out_specs=[vmem()] * nh,
-    )(me, d_keep, d_got)
+    )(me, d_keep, d_got, *taps)
     got = []
     for d in range(1, nh):
         got.append(swap(ordered[d], "heads", d))
@@ -706,7 +733,6 @@
         scratch = [pltpu.VMEM(table, F32)] * 2
     else:
         outs += [sds(table, F32)] * 2
-    embed_col = embed.astype(F32)[:, None]
     got = call(
         functools.partial(gather_kernel, layout=layout, aligned=aligned),
         outs,
@@ -720,7 +746,7 @@
     else:
         down_rows = got[1].reshape(width, padded)
         grad_down = down_rows[:, :chans].T
-        grad_embed = embed_col * down_rows[:, chans][None, :]
+        grad_embed = embed_col[:, 0:1] * down_rows[:, chans][None, :]
         grad_up = got[2].reshape(width, padded)[:, :chans]
     return (
         output.transpose(0, 1, 3, 2),

time: 157 us -> 173 us (1.10)
  waiting for transfers between devices: 42.1 us -> 53.3 us
  starting transfers between devices: 36.8 us -> 42.8 us
  local copies, waits for them, and re-layouts: 10.4 us -> 7.44 us
  Pallas kernels: 59.7 us -> 62 us
    ppermute x30 -> x31, waiting for transfers between devices: 42.1 us -> 49.9 us  [swap(): return lax.ppermute(x, axis, [(i, i ^ bit) for i in range(n)])]
    ppermute x30 -> x31, starting transfers between devices: 33.1 us -> 40.2 us  [swap(): return lax.ppermute(x, axis, [(i, i ^ bit) for i in range(n)])]
    ppermute x1, waiting for transfers between devices: 0.01 us -> 3.41 us  [body(): hi = lax.ppermute(head, 'frames', [(i + 1, i) for i in range(nf - 1)])]
    pallas_call x2 -> x3, Pallas kernels: 6.2 us -> 8.45 us  [the longest x1 4.54 us: body(): call(fine_kernel, [sds(clip_t.shape, BF), sds(clip_t.shape, F32), sds((ch...]
    unnamed x51 -> x69, local copies, waits for them, and re-layouts: 6.6 us -> 7.33 us
  transfers between devices with their start and end apart: 32 -> 33, of which waited for: 13 -> 17; matrix products, arithmetic and copies ran while one was open for 5% -> 1% of each run, Pallas kernels for 16% -> 30%
where the time goes in v5:
time: 173 us; the launch traced here: 172 us
  Pallas kernels  62 us (36%)
  waiting for transfers between devices  53.3 us (31%)
  starting transfers between devices  42.8 us (25%)
  local copies, waits for them, and re-layouts  7.44 us (4%)
  other arithmetic  5.08 us (3%)
    ppermute x31, waiting for transfers between devices, swap(): return lax.ppermute(x, axis, [(i, i ^ bit) for i in range(n)])  49.9 us
    ppermute x31, starting transfers between devices, swap(): return lax.ppermute(x, axis, [(i, i ^ bit) for i in range(n)])  40.2 us
    pallas_call x1, Pallas kernels, body(): call(functools.partial(coarse_kernel, coarse_frames=nf, heads_axis=nh, re...  22.3 us
    unnamed x69, local copies, waits for them, and re-layouts  7.33 us
    pallas_call x1, Pallas kernels, body(): call(weight_kernel, [sds((padded, width), BF), sds((padded, pieces * SLOT...  5.77 us
    pallas_call x1, Pallas kernels, body(): call(functools.partial(gather_kernel, layout=layout, aligned=aligned), ou...  5.29 us
    pallas_call x1, Pallas kernels, body(): call(functools.partial(split_grad_kernel, late=True), wide, grid=(width /...  4.72 us
    pallas_call x1, Pallas kernels, body(): call(functools.partial(split_grad_kernel, late=False), [wide, sds((heads...  4.71 us
  transfers between devices with their start and end apart: 33, of which 17 were waited for; matrix products, arithmetic and copies ran while one was open for 1% of the time, Pallas kernels for 30%

profile of v5, /device:TPU:0, one launch (start us, length us, event | category | flops | bytes accessed | tf_op | source)
XLA Modules:
  0.0 172.3 jit_solution(3597934361655038870)
XLA Ops:
  0.6 2.2 %shard_map.152 = (bf16[2,3,8,640]{3,2,1,0:T(8,128)(2,1)}, bf16[2,3,8,640]{3,2,1,0:T(8,128)(2,1)}) custom-call(s32[1]{0:T(128)} %bitcast.me, bf16[2,2,320,128]{3,2,1,0:T(8,128)(2,1)} %bitcast.29, bf16[2,2,320,128]{3,2,1,0:T(8,128)(2,1)} %bitcast.32), custom_call_target="tpu_custom_call" | custom-call | tf_op jit(solution)/shard_map/pallas_call | solution.py:500
  5.3 4.0 %collective-permute-start.3 = (bf16[2,6,8,640]{3,2,1,0:T(8,128)(2,1)S(1)}, bf16[2,6,8,640]{3,2,1,0:T(8,128)(2,1)S(1)}, u32[]{:S(2)}, u32[]{:S(2)}) collective-permute-start(bf16[2,6,8,640]{3,2,1,0:T(8,128)(2,1)S(1)} %pad_maximum_fusion.7), channel_id=1, source_target_pairs={{0,16},{4,20},{8,24},{12,28},{16,0},{20,4},{24,8},{28,12},{1,17},{... | collective-permute-start | bytes 368648 | tf_op jit(solution)/shard_map/ppermute | solution.py:72
  9.2 6.3 %collective-permute-done.3 = bf16[2,6,8,640]{3,2,1,0:T(8,128)(2,1)S(1)} collective-permute-done((bf16[2,6,8,640]{3,2,1,0:T(8,128)(2,1)S(1)}, bf16[2,6,8,640]{3,2,1,0:T(8,128)(2,1)S(1)}, u32[]{:S(2)}, u32[]{:S(2)}) %collective-permute-start.3) | collective-permute-done | bytes 122912 | tf_op jit(solution)/shard_map/ppermute | solution.py:72
  18.1 5.8 %collective-permute-done.4 = bf16[2,12,8,640]{3,2,1,0:T(8,128)(2,1)S(1)} collective-permute-done((bf16[2,12,8,640]{3,2,1,0:T(8,128)(2,1)S(1)}, bf16[2,12,8,640]{3,2,1,0:T(8,128)(2,1)S(1)}, u32[]{:S(2)}, u32[]{:S(2)}) %collective-permute-start.4) | collective-permute-done | bytes 245792 | tf_op jit(solution)/shard_map/ppermute | solution.py:72
  26.8 3.8 %collective-permute-done.5 = bf16[1,24,8,640]{3,2,1,0:T(8,128)(2,1)S(1)} collective-permute-done((bf16[1,24,8,640]{3,2,1,0:T(8,128)(2,1)S(1)}, bf16[1,24,8,640]{3,2,1,0:T(8,128)(2,1)S(1)}, u32[]{:S(2)}, u32[]{:S(2)}) %collective-permute-start.5) | collective-permute-done | bytes 245792 | tf_op jit(solution)/shard_map/ppermute | solution.py:72
  39.3 3.4 %collective-permute-done.1.hi = bf16[4,320,128]{2,1,0:T(8,128)(2,1)S(1)} collective-permute-done((bf16[4,320,128]{2,1,0:T(8,128)(2,1)}, bf16[4,320,128]{2,1,0:T(8,128)(2,1)S(1)}, u32[]{:S(2)}, u32[]{:S(2)}) %collective-permute-start.1) | collective-permute-done | bytes 327712 | tf_op jit(solution)/shard_map/ppermute | solution.py:531
  43.5 4.5 %shard_map.154 = (bf16[2,2,320,128]{3,2,1,0:T(8,128)(2,1)}, f32[2,2,320,128]{3,2,1,0:T(8,128)}, bf16[4,128,320]{2,1,0:T(8,128)(2,1)}, bf16[4,128,320]{2,1,0:T(8,128)(2,1)}) custom-call(s32[2]{0:T(128)} %pad_add_fusion.me, bf16[2,2,320,128]{3,2,1,0:T(8,128)(2,1)} %bitcast.31, bf16[2,2,320,128]{3,2,1,0:T(8,128)(2,1)} %bitcast.34, ...), custom_call_target="tpu_custom_call" | custom-call | tf_op jit(solution)/shard_map/pallas_call | solution.py:533
  48.0 5.4 %collective-permute-start.16 = (bf16[4,128,320]{2,1,0:T(8,128)(2,1)}, bf16[4,128,320]{2,1,0:T(8,128)(2,1)S(1)}, u32[]{:S(2)}, u32[]{:S(2)}) collective-permute-start(bf16[4,128,320]{2,1,0:T(8,128)(2,1)} %get-tuple-element.77), channel_id=1, source_target_pairs={{0,4},{4,0},{8,12},{12,8},{16,20},{20,16},{24,28},{28,24},{1,5},{5... | collective-permute-start | bytes 983048 | tf_op jit(solution)/shard_map/ppermute | solution.py:72
  54.0 5.8 %shard_map.155 = (bf16[384,1280]{1,0:T(8,128)(2,1)}, bf16[384,1536]{1,0:T(8,128)(2,1)}, bf16[512,320]{1,0:T(8,128)(2,1)}, bf16[384,320]{1,0:T(8,128)(2,1)}, f32[320,128]{1,0:T(8,128)}) custom-call(bf16[320,1280]{1,0:T(8,128)(2,1)} %w_down.1, bf16[320,1280]{1,0:T(8,128)(2,1)} %w_embed.1, bf16[1,320]{1,0:T(2,128)(2,1)} %fusion.embed, ...), custom_call_target="tpu_custom_call" | custom-call | tf_op jit(solution)/shard_map/pallas_call | solution.py:513
  60.8 22.3 %shard_map.156 = (bf16[6,2,16,320]{3,2,1,0:T(8,128)(2,1)}, bf16[6,2,16,320]{3,2,1,0:T(8,128)(2,1)}, bf16[6,2,16,320]{3,2,1,0:T(8,128)(2,1)}, bf16[6,2,16,320]{3,...) custom-call(s32[2]{0:T(128)} %pad_add_fusion.me, ...), custom_call_target="tpu_custom_call" | custom-call | tf_op jit(solution)/shard_map/pallas_call | solution.py:636
  85.8 2.5 %collective-permute-start.17 = (bf16[128,320]{1,0:T(8,128)(2,1)}, bf16[128,320]{1,0:T(8,128)(2,1)S(1)}, u32[]{:S(2)}, u32[]{:S(2)}) collective-permute-start(bf16[128,320]{1,0:T(8,128)(2,1)} %get-tuple-element.79), channel_id=1, source_target_pairs={{0,8},{4,12},{8,0},{12,4},{16,24},{20,28},{24,16},{28,20},{1,9},{5... | collective-permute-start | bytes 245768 | tf_op jit(solution)/shard_map/ppermute | solution.py:72
  91.9 7.3 %collective-permute-done.18.refs_2_ = bf16[128,320]{1,0:T(8,128)(2,1)S(1)} collective-permute-done((bf16[128,320]{1,0:T(8,128)(2,1)}, bf16[128,320]{1,0:T(8,128)(2,1)S(1)}, u32[]{:S(2)}, u32[]{:S(2)}) %collective-permute-start.18) | collective-permute-done | bytes 81952 | tf_op jit(solution)/shard_map/ppermute | solution.py:72
  100.1 2.0 %shard_map.162 = (bf16[112,384]{1,0:T(8,128)(2,1)}, bf16[112,384]{1,0:T(8,128)(2,1)}, bf16[112,384]{1,0:T(8,128)(2,1)}, bf16[112,384]{1,0:T(8,128)(2,1)}) custom-call(s32[2]{0:T(128)} %pad_add_fusion.me, bf16[4,112,384]{2,1,0:T(8,128)(2,1)} %get-tuple-element.74.keep, bf16[4,112,384]{2,1,0:T(8,128)(2,1)} %copy-done.15, ...), custom_call_target="tpu_custom_call" | custom-call | tf_op jit(solution)/shard_map/pallas_call | solution.py:645
  111.7 2.9 %collective-permute-start.23 = (bf16[2,1,56,384]{3,2,1,0:T(8,128)(2,1)}, bf16[2,1,56,384]{3,2,1,0:T(8,128)(2,1)S(1)}, u32[]{:S(2)}, u32[]{:S(2)}) collective-permute-start(bf16[2,1,56,384]{3,2,1,0:T(8,128)(2,1)} %bitcast.35), channel_id=1, source_target_pairs={{0,16},{4,20},{8,24},{12,28},{16,0},{20,4},{24,8},{28,12},{1,17},{... | collective-permute-start | bytes 258056 | tf_op jit(solution)/shard_map/ppermute | solution.py:72
  114.6 2.7 %collective-permute-done.23 = bf16[2,1,56,384]{3,2,1,0:T(8,128)(2,1)S(1)} collective-permute-done((bf16[2,1,56,384]{3,2,1,0:T(8,128)(2,1)}, bf16[2,1,56,384]{3,2,1,0:T(8,128)(2,1)S(1)}, u32[]{:S(2)}, u32[]{:S(2)}) %collective-permute-start.23) | collective-permute-done | bytes 86048 | tf_op jit(solution)/shard_map/ppermute | solution.py:72
  118.2 1.9 %collective-permute-start.24 = (bf16[2,2,56,384]{3,2,1,0:T(8,128)(2,1)S(1)}, bf16[2,2,56,384]{3,2,1,0:T(8,128)(2,1)S(1)}, u32[]{:S(2)}, u32[]{:S(2)}) collective-permute-start(bf16[2,2,56,384]{3,2,1,0:T(8,128)(2,1)S(1)} %pad_maximum_fusion.6), channel_id=1, source_target_pairs={{0,8},{4,12},{8,0},{12,4},{16,24},{20,28},{24,16},{28,20},{1,9},{5... | collective-permute-start | bytes 516104 | tf_op jit(solution)/shard_map/ppermute | solution.py:72
  120.2 3.5 %collective-permute-done.24 = bf16[2,2,56,384]{3,2,1,0:T(8,128)(2,1)S(1)} collective-permute-done((bf16[2,2,56,384]{3,2,1,0:T(8,128)(2,1)S(1)}, bf16[2,2,56,384]{3,2,1,0:T(8,128)(2,1)S(1)}, u32[]{:S(2)}, u32[]{:S(2)}) %collective-permute-start.24) | collective-permute-done | bytes 172064 | tf_op jit(solution)/shard_map/ppermute | solution.py:72
  127.2 3.0 %collective-permute-done.25 = bf16[1,4,56,384]{3,2,1,0:T(8,128)(2,1)S(1)} collective-permute-done((bf16[1,4,56,384]{3,2,1,0:T(8,128)(2,1)S(1)}, bf16[1,4,56,384]{3,2,1,0:T(8,128)(2,1)S(1)}, u32[]{:S(2)}, u32[]{:S(2)}) %collective-permute-start.25) | collective-permute-done | bytes 172064 | tf_op jit(solution)/shard_map/ppermute | solution.py:72
  136.4 5.3 %collective-permute-done.9.refs_1_ = bf16[6,2,16,320]{3,2,1,0:T(8,128)(2,1)S(1)} collective-permute-done((bf16[6,2,16,320]{3,2,1,0:T(8,128)(2,1)S(1)}, bf16[6,2,16,320]{3,2,1,0:T(8,128)(2,1)S(1)}, u32[]{:S(2)}, u32[]{:S(2)}) %collective-permute-start.9) | collective-permute-done | bytes 122912 | tf_op jit(solution)/shard_map/ppermute | solution.py:72
  143.2 4.5 %collective-permute-done.11.refs_3_ = bf16[6,2,16,320]{3,2,1,0:T(8,128)(2,1)S(1)} collective-permute-done((bf16[6,2,16,320]{3,2,1,0:T(8,128)(2,1)S(1)}, bf16[6,2,16,320]{3,2,1,0:T(8,128)(2,1)S(1)}, u32[]{:S(2)}, u32[]{:S(2)}) %collective-permute-start.11) | collective-permute-done | bytes 122912 | tf_op jit(solution)/shard_map/ppermute | solution.py:72
  152.4 3.1 %shard_map.158 = (bf16[2,2,320,128]{3,2,1,0:T(8,128)(2,1)}, f32[2,2,320,128]{3,2,1,0:T(8,128)}) custom-call(s32[2]{0:T(128)} %pad_add_fusion.me, bf16[2,2,320,128]{3,2,1,0:T(8,128)(2,1)} %get-tuple-element.55.hidden, f32[2,2,320,128]{3,2,1,0:T(8,128)} %get-tuple-element.56.base, bf16[4,32,320]{2,1,0:T(8,128)(2,1)} %bitcast.38, bf16[4,32,320]{2,1,0:T(8,128)(2,1)} %bitcast.39, ...), custom_call_target="tpu_custom_call" | custom-call | tf_op jit(solution)/shard_map/pallas_call | solution.py:676
  156.5 4.7 %shard_map.159 = (f32[960,1280]{1,0:T(8,128)}, f32[320,1280]{1,0:T(8,128)}) custom-call(bf16[384,1280]{1,0:T(8,128)(2,1)} %get-tuple-element.61.refs_9_.refs_10_.refs_11_.down, bf16[384,1024]{1,0:T(8,128)(2,1)} %get-tuple-element.70.mix_a, bf16[384,1024]{1,0:T(8,128)(2,1)} %copy-done.1, bf16[320,320]{1,0:T(8,128)(2,1)} %get-tuple-element.71.refs_0_, ...), custom_call_target="tpu_custom_call" | custom-call | tf_op jit(solution)/shard_map/pallas_call | solution.py:690
  161.2 4.7 %shard_map.160 = f32[960,1280]{1,0:T(8,128)} custom-call(bf16[384,1280]{1,0:T(8,128)(2,1)} %get-tuple-element.61.refs_9_.refs_10_.refs_11_.down, bf16[384,1024]{1,0:T(8,128)(2,1)} %get-tuple-element.70.mix_a, bf16[384,1024]{1,0:T(8,128)(2,1)} %copy-done.1, f32[960,1280]{1,0:T(8,128)} %get-tuple-element.72.refs_0_), custom_call_target="tpu_custom_call", output_to_operand_aliasing={{}: (3, {})} | custom-call | tf_op jit(solution)/shard_map/pallas_call | solution.py:708
  167.0 5.3 %shard_map.164 = (f32[30,32,320]{2,1,0:T(8,128)}, f32[320,1280]{1,0:T(8,128)}, f32[320,1280]{1,0:T(8,128)}, f32[320,1280]{1,0:T(8,128)}) custom-call(s32[2]{0:T(128)} %pad_add_fusion.me, f32[320,128]{1,0:T(8,128)} %get-tuple-element.88.embed, bf16[2,4,56,384]{3,2,1,0:T(8,128)(2,1)} %copy-done.5, bf16[2,4,56,384]{3,2,1,0:T(8,128)(2,1)} %copy-done.10, ...), custom_call_target="tpu_custom_call" | custom-call | tf_op jit(solution)/shard_map/pallas_call | solution.py:736
  (138 shorter events, 53.6 us)
Async XLA Ops:
  5.3 10.3 %collective-permute-start.3 = (bf16[2,6,8,640]{3,2,1,0:T(8,128)(2,1)S(1)}, bf16[2,6,8,640]{3,2,1,0:T(8,128)(2,1)S(1)}, u32[]{:S(2)}, u32[]{:S(2)}) collective-permute-start(bf16[2,6,8,640]{3,2,1,0:T(8,128)(2,1)S(1)} %pad_maximum_fusion.7), channel_id=1, source_target_pairs={{0,16},{4,20},{8,24},{12,28},{16,0},{20,4},{24,8},{28,12},{1,17},{... | collective-permute-start | bytes 368648 | tf_op jit(solution)/shard_map/ppermute | solution.py:72
  16.4 7.5 %collective-permute-start.4 = (bf16[2,12,8,640]{3,2,1,0:T(8,128)(2,1)S(1)}, bf16[2,12,8,640]{3,2,1,0:T(8,128)(2,1)S(1)}, u32[]{:S(2)}, u32[]{:S(2)}) collective-permute-start(bf16[2,12,8,640]{3,2,1,0:T(8,128)(2,1)S(1)} %pad_maximum_fusion.5), channel_id=1, source_target_pairs={{0,8},{4,12},{8,0},{12,4},{16,24},{20,28},{24,16},{28,20},{1,9},{5... | collective-permute-start | bytes 737288 | tf_op jit(solution)/shard_map/ppermute | solution.py:72
  24.0 6.7 %collective-permute-start.5 = (bf16[1,24,8,640]{3,2,1,0:T(8,128)(2,1)S(1)}, bf16[1,24,8,640]{3,2,1,0:T(8,128)(2,1)S(1)}, u32[]{:S(2)}, u32[]{:S(2)}) collective-permute-start(bf16[1,24,8,640]{3,2,1,0:T(8,128)(2,1)S(1)} %get-tuple-element.97), channel_id=1, source_target_pairs={{0,1},{1,0},{2,3},{3,2},{4,5},{5,4},{6,7},{7,6},{8,9},{9,8},{10,11... | collective-permute-start | bytes 737288 | tf_op jit(solution)/shard_map/ppermute | solution.py:72
  25.3 6.5 %collective-permute-start.7 = (bf16[1,24,8,640]{3,2,1,0:T(8,128)(2,1)S(1)}, bf16[1,24,8,640]{3,2,1,0:T(8,128)(2,1)S(1)}, u32[]{:S(2)}, u32[]{:S(2)}) collective-permute-start(bf16[1,24,8,640]{3,2,1,0:T(8,128)(2,1)S(1)} %get-tuple-element.96), channel_id=1, source_target_pairs={{0,2},{1,3},{2,0},{3,1},{4,6},{5,7},{6,4},{7,5},{8,10},{9,11},{10,... | collective-permute-start | bytes 737288 | tf_op jit(solution)/shard_map/ppermute | solution.py:72
  30.7 29.1 %collective-permute-start.6 = (bf16[2,24,8,640]{3,2,1,0:T(8,128)(2,1)S(1)}, bf16[2,24,8,640]{3,2,1,0:T(8,128)(2,1)S(1)}, u32[]{:S(2)}, u32[]{:S(2)}) collective-permute-start(bf16[2,24,8,640]{3,2,1,0:T(8,128)(2,1)S(1)} %pad_maximum_fusion.first_a), channel_id=1, source_target_pairs={{0,2},{1,3},{2,0},{3,1},{4,6},{5,7},{6,4},{7,5},{8,10},{9,11},{10,... | collective-permute-start | bytes 1474568 | tf_op jit(solution)/shard_map/ppermute | solution.py:72
  31.9 28.0 %collective-permute-start.8 = (bf16[2,24,8,640]{3,2,1,0:T(8,128)(2,1)S(1)}, bf16[2,24,8,640]{3,2,1,0:T(8,128)(2,1)S(1)}, u32[]{:S(2)}, u32[]{:S(2)}) collective-permute-start(bf16[2,24,8,640]{3,2,1,0:T(8,128)(2,1)S(1)} %pad_maximum_fusion.1.second_a), channel_id=1, source_target_pairs={{0,1},{1,0},{2,3},{3,2},{4,5},{5,4},{6,7},{7,6},{8,9},{9,8},{10,11... | collective-permute-start | bytes 1474568 | tf_op jit(solution)/shard_map/ppermute | solution.py:72
  36.7 6.1 %collective-permute-start.1 = (bf16[4,320,128]{2,1,0:T(8,128)(2,1)}, bf16[4,320,128]{2,1,0:T(8,128)(2,1)S(1)}, u32[]{:S(2)}, u32[]{:S(2)}) collective-permute-start(bf16[4,320,128]{2,1,0:T(8,128)(2,1)} %get-tuple-element.54), channel_id=1, source_target_pairs={{4,0},{8,4},{12,8},{16,12},{20,16},{24,20},{28,24},{5,1},{9,5},{13... | collective-permute-start | bytes 983048 | tf_op jit(solution)/shard_map/ppermute | solution.py:531
  48.0 35.1 %collective-permute-start.16 = (bf16[4,128,320]{2,1,0:T(8,128)(2,1)}, bf16[4,128,320]{2,1,0:T(8,128)(2,1)S(1)}, u32[]{:S(2)}, u32[]{:S(2)}) collective-permute-start(bf16[4,128,320]{2,1,0:T(8,128)(2,1)} %get-tuple-element.77), channel_id=1, source_target_pairs={{0,4},{4,0},{8,12},{12,8},{16,20},{20,16},{24,28},{28,24},{1,5},{5... | collective-permute-start | bytes 983048 | tf_op jit(solution)/shard_map/ppermute | solution.py:72
  83.0 16.3 %collective-permute-start.15 = (bf16[4,112,384]{2,1,0:T(8,128)(2,1)}, bf16[4,112,384]{2,1,0:T(8,128)(2,1)S(1)}, u32[]{:S(2)}, u32[]{:S(2)}) collective-permute-start(bf16[4,112,384]{2,1,0:T(8,128)(2,1)} %get-tuple-element.75), channel_id=1, source_target_pairs={{0,4},{4,0},{8,12},{12,8},{16,20},{20,16},{24,28},{28,24},{1,5},{5... | collective-permute-start | bytes 1032200 | tf_op jit(solution)/shard_map/ppermute | solution.py:72
  85.8 6.2 %collective-permute-start.17 = (bf16[128,320]{1,0:T(8,128)(2,1)}, bf16[128,320]{1,0:T(8,128)(2,1)S(1)}, u32[]{:S(2)}, u32[]{:S(2)}) collective-permute-start(bf16[128,320]{1,0:T(8,128)(2,1)} %get-tuple-element.79), channel_id=1, source_target_pairs={{0,8},{4,12},{8,0},{12,4},{16,24},{20,28},{24,16},{28,20},{1,9},{5... | collective-permute-start | bytes 245768 | tf_op jit(solution)/shard_map/ppermute | solution.py:72
  88.3 11.0 %collective-permute-start.18 = (bf16[128,320]{1,0:T(8,128)(2,1)}, bf16[128,320]{1,0:T(8,128)(2,1)S(1)}, u32[]{:S(2)}, u32[]{:S(2)}) collective-permute-start(bf16[128,320]{1,0:T(8,128)(2,1)} %get-tuple-element.80), channel_id=1, source_target_pairs={{0,16},{4,20},{8,24},{12,28},{16,0},{20,4},{24,8},{28,12},{1,17},{... | collective-permute-start | bytes 245768 | tf_op jit(solution)/shard_map/ppermute | solution.py:72
  89.5 9.8 %collective-permute-start.19 = (bf16[128,320]{1,0:T(8,128)(2,1)}, bf16[128,320]{1,0:T(8,128)(2,1)S(1)}, u32[]{:S(2)}, u32[]{:S(2)}) collective-permute-start(bf16[128,320]{1,0:T(8,128)(2,1)} %get-tuple-element.81), channel_id=1, source_target_pairs={{0,24},{4,28},{8,16},{12,20},{16,8},{20,12},{24,0},{28,4},{1,25},{... | collective-permute-start | bytes 245768 | tf_op jit(solution)/shard_map/ppermute | solution.py:72
  125.7 6.1 %collective-permute-start.28 = (bf16[1,4,56,384]{3,2,1,0:T(8,128)(2,1)S(1)}, bf16[1,4,56,384]{3,2,1,0:T(8,128)(2,1)S(1)}, u32[]{:S(2)}, u32[]{:S(2)}) collective-permute-start(bf16[1,4,56,384]{3,2,1,0:T(8,128)(2,1)S(1)} %get-tuple-element.98), channel_id=1, source_target_pairs={{0,1},{1,0},{2,3},{3,2},{4,5},{5,4},{6,7},{7,6},{8,9},{9,8},{10,11... | collective-permute-start | bytes 516104 | tf_op jit(solution)/shard_map/ppermute | solution.py:72
  127.2 28.4 %collective-permute-start.13 = (bf16[384,1024]{1,0:T(8,128)(2,1)S(1)}, bf16[384,1024]{1,0:T(8,128)(2,1)S(1)}, u32[]{:S(2)}, u32[]{:S(2)}) collective-permute-start(bf16[384,1024]{1,0:T(8,128)(2,1)S(1)} %copy-done), channel_id=1, source_target_pairs={{0,4},{4,0},{8,12},{12,8},{16,20},{20,16},{24,28},{28,24},{1,5},{5... | collective-permute-start | bytes 2359304 | tf_op jit(solution)/shard_map/ppermute | solution.py:72
  130.2 20.0 %collective-permute-start.26 = (bf16[2,4,56,384]{3,2,1,0:T(8,128)(2,1)S(1)}, bf16[2,4,56,384]{3,2,1,0:T(8,128)(2,1)S(1)}, u32[]{:S(2)}, u32[]{:S(2)}) collective-permute-start(bf16[2,4,56,384]{3,2,1,0:T(8,128)(2,1)S(1)} %pad_maximum_fusion.3.refs_2_), channel_id=1, source_target_pairs={{0,1},{1,0},{2,3},{3,2},{4,5},{5,4},{6,7},{7,6},{8,9},{9,8},{10,11... | collective-permute-start | bytes 1032200 | tf_op jit(solution)/shard_map/ppermute | solution.py:72
  131.8 20.4 %collective-permute-start.29 = (bf16[2,4,56,384]{3,2,1,0:T(8,128)(2,1)S(1)}, bf16[2,4,56,384]{3,2,1,0:T(8,128)(2,1)S(1)}, u32[]{:S(2)}, u32[]{:S(2)}) collective-permute-start(bf16[2,4,56,384]{3,2,1,0:T(8,128)(2,1)S(1)} %pad_maximum_fusion.4.refs_0_), channel_id=1, source_target_pairs={{0,2},{1,3},{2,0},{3,1},{4,6},{5,7},{6,4},{7,5},{8,10},{9,11},{10,... | collective-permute-start | bytes 1032200 | tf_op jit(solution)/shard_map/ppermute | solution.py:72
  133.6 8.1 %collective-permute-start.9 = (bf16[6,2,16,320]{3,2,1,0:T(8,128)(2,1)S(1)}, bf16[6,2,16,320]{3,2,1,0:T(8,128)(2,1)S(1)}, u32[]{:S(2)}, u32[]{:S(2)}) collective-permute-start(bf16[6,2,16,320]{3,2,1,0:T(8,128)(2,1)S(1)} %copy-done.32), channel_id=1, source_target_pairs={{0,1},{1,0},{2,3},{3,2},{4,5},{5,4},{6,7},{7,6},{8,9},{9,8},{10,11... | collective-permute-start | bytes 368648 | tf_op jit(solution)/shard_map/ppermute | solution.py:72
  134.4 8.6 %collective-permute-start.10 = (bf16[6,2,16,320]{3,2,1,0:T(8,128)(2,1)S(1)}, bf16[6,2,16,320]{3,2,1,0:T(8,128)(2,1)S(1)}, u32[]{:S(2)}, u32[]{:S(2)}) collective-permute-start(bf16[6,2,16,320]{3,2,1,0:T(8,128)(2,1)S(1)} %copy-done.31), channel_id=1, source_target_pairs={{0,2},{1,3},{2,0},{3,1},{4,6},{5,7},{6,4},{7,5},{8,10},{9,11},{10,... | collective-permute-start | bytes 368648 | tf_op jit(solution)/shard_map/ppermute | solution.py:72
  141.6 6.0 %collective-permute-start.11 = (bf16[6,2,16,320]{3,2,1,0:T(8,128)(2,1)S(1)}, bf16[6,2,16,320]{3,2,1,0:T(8,128)(2,1)S(1)}, u32[]{:S(2)}, u32[]{:S(2)}) collective-permute-start(bf16[6,2,16,320]{3,2,1,0:T(8,128)(2,1)S(1)} %copy-done.30), channel_id=1, source_target_pairs={{0,3},{1,2},{2,1},{3,0},{4,7},{5,6},{6,5},{7,4},{8,11},{9,10},{10,... | collective-permute-start | bytes 368648 | tf_op jit(solution)/shard_map/ppermute | solution.py:72
  143.1 8.8 %collective-permute-start.14 = (bf16[320,320]{1,0:T(8,128)(2,1)S(1)}, bf16[320,320]{1,0:T(8,128)(2,1)S(1)}, u32[]{:S(2)}, u32[]{:S(2)}) collective-permute-start(bf16[320,320]{1,0:T(8,128)(2,1)S(1)} %copy-done.18), channel_id=1, source_target_pairs={{0,4},{4,0},{8,12},{12,8},{16,20},{20,16},{24,28},{28,24},{1,5},{5... | collective-permute-start | bytes 614408 | tf_op jit(solution)/shard_map/ppermute | solution.py:72
  150.3 15.7 %collective-permute-start.27 = (bf16[2,4,56,384]{3,2,1,0:T(8,128)(2,1)S(1)}, bf16[2,4,56,384]{3,2,1,0:T(8,128)(2,1)S(1)}, u32[]{:S(2)}, u32[]{:S(2)}) collective-permute-start(bf16[2,4,56,384]{3,2,1,0:T(8,128)(2,1)S(1)} %collective-permute-done.26.refs_3_), channel_id=1, source_target_pairs={{0,4},{4,0},{8,12},{12,8},{16,20},{20,16},{24,28},{28,24},{1,5},{5... | collective-permute-start | bytes 1032200 | tf_op jit(solution)/shard_map/ppermute | solution.py:72
  151.8 14.2 %collective-permute-start.30 = (bf16[2,4,56,384]{3,2,1,0:T(8,128)(2,1)S(1)}, bf16[2,4,56,384]{3,2,1,0:T(8,128)(2,1)S(1)}, u32[]{:S(2)}, u32[]{:S(2)}) collective-permute-start(bf16[2,4,56,384]{3,2,1,0:T(8,128)(2,1)S(1)} %pad_maximum_fusion.4.refs_0_), channel_id=1, source_target_pairs={{0,4},{4,0},{8,12},{12,8},{16,20},{20,16},{24,28},{28,24},{1,5},{5... | collective-permute-start | bytes 1032200 | tf_op jit(solution)/shard_map/ppermute | solution.py:72
  151.9 14.0 %collective-permute-start.32 = (bf16[2,4,56,384]{3,2,1,0:T(8,128)(2,1)S(1)}, bf16[2,4,56,384]{3,2,1,0:T(8,128)(2,1)S(1)}, u32[]{:S(2)}, u32[]{:S(2)}) collective-permute-start(bf16[2,4,56,384]{3,2,1,0:T(8,128)(2,1)S(1)} %pad_maximum_fusion.3.refs_2_), channel_id=1, source_target_pairs={{0,4},{4,0},{8,12},{12,8},{16,20},{20,16},{24,28},{28,24},{1,5},{5... | collective-permute-start | bytes 1032200 | tf_op jit(solution)/shard_map/ppermute | solution.py:72
  152.3 13.7 %collective-permute-start.31 = (bf16[2,4,56,384]{3,2,1,0:T(8,128)(2,1)S(1)}, bf16[2,4,56,384]{3,2,1,0:T(8,128)(2,1)S(1)}, u32[]{:S(2)}, u32[]{:S(2)}) collective-permute-start(bf16[2,4,56,384]{3,2,1,0:T(8,128)(2,1)S(1)} %collective-permute-done.29.refs_1_), channel_id=1, source_target_pairs={{0,4},{4,0},{8,12},{12,8},{16,20},{20,16},{24,28},{28,24},{1,5},{5... | collective-permute-start | bytes 1032200 | tf_op jit(solution)/shard_map/ppermute | solution.py:72
  (42 other events, 353.0 us)

commit v6 on v5

--- a/solution.py
+++ b/solution.py
@@ -422,7 +422,10 @@
 
 def gather_kernel(me, embed, *refs, layout, aligned):
     pieces = refs[:8]
-    time_out, down_rows, up_rows = refs[8], refs[-2], refs[-1]
+    if aligned:
+        results, (down_rows, up_rows, time_out, down_out, embed_out, up_out, sems) = refs[8:12], refs[12:]
+    else:
+        time_out, down_rows, up_rows = refs[8:]
     frame, head = me[0], me[1]
     chips, heads_axis, r1, p1, r3 = layout
     chans = time_out.shape[2]
@@ -446,14 +449,21 @@
                 time_out[owner] = value[2 * p1 : 2 * p1 + r3, 0:chans]
 
     if aligned:
-        down_out, embed_out, up_out = refs[9], refs[10], refs[11]
+        buffers = (time_out, down_out, embed_out, up_out)
+        copies = [pltpu.make_async_copy(buffers[i], results[i], sems.at[i]) for i in range(4)]
+        copies[0].start()
         lanes = down_rows.shape[2]
         eye = (lax.broadcasted_iota(jnp.int32, (lanes, lanes), 0) == lax.broadcasted_iota(jnp.int32, (lanes, lanes), 1))
         eye = eye.astype(F32).astype(BF)
         flipped = nt(eye, down_rows[...].reshape(devices * r1, lanes).astype(BF))
         down_out[...] = flipped[0:chans]
+        copies[1].start()
         embed_out[...] = embed[:, 0:1] * flipped[chans : chans + 1]
-        up_out[...] = nt(eye, up_rows[...].reshape(devices * r1, lanes).astype(BF))[0:chans]
+        copies[2].start()
+        up_out[...] = nt(eye[0:chans], up_rows[...].reshape(devices * r1, lanes).astype(BF))
+        copies[3].start()
+        for copy in copies:
+            copy.wait()
 
 
 def double(x, axis, bits, dim):
@@ -730,14 +740,15 @@
     scratch = []
     if aligned:
         outs += [sds((chans, width), F32), sds((w_embed.shape[0], width), F32), sds((chans, width), F32)]
-        scratch = [pltpu.VMEM(table, F32)] * 2
+        scratch = [pltpu.VMEM(table, F32)] * 2 + [pltpu.VMEM(x.shape, F32) for x in outs]
+        scratch.append(pltpu.SemaphoreType.DMA((4,)))
     else:
         outs += [sds(table, F32)] * 2
     got = call(
         functools.partial(gather_kernel, layout=layout, aligned=aligned),
         outs,
         in_specs=[smem()] + [vmem()] * 9,
-        out_specs=[vmem()] * len(outs),
+        out_specs=[pl.BlockSpec(memory_space=pl.ANY) if aligned else vmem()] * len(outs),
         scratch_shapes=scratch,
     )(me, embed_col, *shares, *mates)
     grad_time = got[0].reshape(w_time.shape)

time: 173 us -> 173 us (level)
  transfers between devices with their start and end apart: 33 -> 33, of which waited for: 17 -> 17; matrix products, arithmetic and copies ran while one was open for 1% -> 1% of each run, Pallas kernels for 30% -> 29%
where the time goes in v6:
time: 173 us; the launch traced here: 172 us
  Pallas kernels  62 us (36%)
  waiting for transfers between devices  53.3 us (31%)
  starting transfers between devices  42.8 us (25%)
  local copies, waits for them, and re-layouts  7.44 us (4%)
  other arithmetic  5.08 us (3%)
  between operations  1.78 us (1%)
    ppermute x31, waiting for transfers between devices, swap(): return lax.ppermute(x, axis, [(i, i ^ bit) for i in range(n)])  49.9 us
    ppermute x31, starting transfers between devices, swap(): return lax.ppermute(x, axis, [(i, i ^ bit) for i in range(n)])  40.2 us
    pallas_call x1, Pallas kernels, body(): call(functools.partial(coarse_kernel, coarse_frames=nf, heads_axis=nh, re...  22.3 us
    unnamed x69, local copies, waits for them, and re-layouts  7.33 us
    pallas_call x1, Pallas kernels, body(): call(weight_kernel, [sds((padded, width), BF), sds((padded, pieces * SLOT...  5.77 us
    pallas_call x1, Pallas kernels, body(): call(functools.partial(gather_kernel, layout=layout, aligned=aligned), ou...  5.31 us
    pallas_call x1, Pallas kernels, body(): call(functools.partial(split_grad_kernel, late=True), wide, grid=(width /...  4.72 us
    pallas_call x1, Pallas kernels, body(): call(functools.partial(split_grad_kernel, late=False), [wide, sds((heads...  4.71 us
  transfers between devices with their start and end apart: 33, of which 17 were waited for; matrix products, arithmetic and copies ran while one was open for 1% of the time, Pallas kernels for 29%

profile of v6, /device:TPU:0, one launch (start us, length us, event | category | flops | bytes accessed | tf_op | source)
XLA Modules:
  0.0 172.5 jit_solution(4868550688541313459)
XLA Ops:
  0.6 2.2 %shard_map.152 = (bf16[2,3,8,640]{3,2,1,0:T(8,128)(2,1)}, bf16[2,3,8,640]{3,2,1,0:T(8,128)(2,1)}) custom-call(s32[1]{0:T(128)} %bitcast.me, bf16[2,2,320,128]{3,2,1,0:T(8,128)(2,1)} %bitcast.29, bf16[2,2,320,128]{3,2,1,0:T(8,128)(2,1)} %bitcast.32), custom_call_target="tpu_custom_call" | custom-call | tf_op jit(solution)/shard_map/pallas_call | solution.py:510
  5.3 4.0 %collective-permute-start.3 = (bf16[2,6,8,640]{3,2,1,0:T(8,128)(2,1)S(1)}, bf16[2,6,8,640]{3,2,1,0:T(8,128)(2,1)S(1)}, u32[]{:S(2)}, u32[]{:S(2)}) collective-permute-start(bf16[2,6,8,640]{3,2,1,0:T(8,128)(2,1)S(1)} %pad_maximum_fusion.7), channel_id=1, source_target_pairs={{0,16},{4,20},{8,24},{12,28},{16,0},{20,4},{24,8},{28,12},{1,17},{... | collective-permute-start | bytes 368648 | tf_op jit(solution)/shard_map/ppermute | solution.py:72
  9.2 6.3 %collective-permute-done.3 = bf16[2,6,8,640]{3,2,1,0:T(8,128)(2,1)S(1)} collective-permute-done((bf16[2,6,8,640]{3,2,1,0:T(8,128)(2,1)S(1)}, bf16[2,6,8,640]{3,2,1,0:T(8,128)(2,1)S(1)}, u32[]{:S(2)}, u32[]{:S(2)}) %collective-permute-start.3) | collective-permute-done | bytes 122912 | tf_op jit(solution)/shard_map/ppermute | solution.py:72
  18.1 5.8 %collective-permute-done.4 = bf16[2,12,8,640]{3,2,1,0:T(8,128)(2,1)S(1)} collective-permute-done((bf16[2,12,8,640]{3,2,1,0:T(8,128)(2,1)S(1)}, bf16[2,12,8,640]{3,2,1,0:T(8,128)(2,1)S(1)}, u32[]{:S(2)}, u32[]{:S(2)}) %collective-permute-start.4) | collective-permute-done | bytes 245792 | tf_op jit(solution)/shard_map/ppermute | solution.py:72
  26.8 3.8 %collective-permute-done.5 = bf16[1,24,8,640]{3,2,1,0:T(8,128)(2,1)S(1)} collective-permute-done((bf16[1,24,8,640]{3,2,1,0:T(8,128)(2,1)S(1)}, bf16[1,24,8,640]{3,2,1,0:T(8,128)(2,1)S(1)}, u32[]{:S(2)}, u32[]{:S(2)}) %collective-permute-start.5) | collective-permute-done | bytes 245792 | tf_op jit(solution)/shard_map/ppermute | solution.py:72
  39.3 3.4 %collective-permute-done.1.hi = bf16[4,320,128]{2,1,0:T(8,128)(2,1)S(1)} collective-permute-done((bf16[4,320,128]{2,1,0:T(8,128)(2,1)}, bf16[4,320,128]{2,1,0:T(8,128)(2,1)S(1)}, u32[]{:S(2)}, u32[]{:S(2)}) %collective-permute-start.1) | collective-permute-done | bytes 327712 | tf_op jit(solution)/shard_map/ppermute | solution.py:541
  43.5 4.5 %shard_map.154 = (bf16[2,2,320,128]{3,2,1,0:T(8,128)(2,1)}, f32[2,2,320,128]{3,2,1,0:T(8,128)}, bf16[4,128,320]{2,1,0:T(8,128)(2,1)}, bf16[4,128,320]{2,1,0:T(8,128)(2,1)}) custom-call(s32[2]{0:T(128)} %pad_add_fusion.me, bf16[2,2,320,128]{3,2,1,0:T(8,128)(2,1)} %bitcast.31, bf16[2,2,320,128]{3,2,1,0:T(8,128)(2,1)} %bitcast.34, ...), custom_call_target="tpu_custom_call" | custom-call | tf_op jit(solution)/shard_map/pallas_call | solution.py:543
  48.0 5.4 %collective-permute-start.16 = (bf16[4,128,320]{2,1,0:T(8,128)(2,1)}, bf16[4,128,320]{2,1,0:T(8,128)(2,1)S(1)}, u32[]{:S(2)}, u32[]{:S(2)}) collective-permute-start(bf16[4,128,320]{2,1,0:T(8,128)(2,1)} %get-tuple-element.77), channel_id=1, source_target_pairs={{0,4},{4,0},{8,12},{12,8},{16,20},{20,16},{24,28},{28,24},{1,5},{5... | collective-permute-start | bytes 983048 | tf_op jit(solution)/shard_map/ppermute | solution.py:72
  54.0 5.8 %shard_map.155 = (bf16[384,1280]{1,0:T(8,128)(2,1)}, bf16[384,1536]{1,0:T(8,128)(2,1)}, bf16[512,320]{1,0:T(8,128)(2,1)}, bf16[384,320]{1,0:T(8,128)(2,1)}, f32[320,128]{1,0:T(8,128)}) custom-call(bf16[320,1280]{1,0:T(8,128)(2,1)} %w_down.1, bf16[320,1280]{1,0:T(8,128)(2,1)} %w_embed.1, bf16[1,320]{1,0:T(2,128)(2,1)} %fusion.embed, ...), custom_call_target="tpu_custom_call" | custom-call | tf_op jit(solution)/shard_map/pallas_call | solution.py:523
  60.8 22.3 %shard_map.156 = (bf16[6,2,16,320]{3,2,1,0:T(8,128)(2,1)}, bf16[6,2,16,320]{3,2,1,0:T(8,128)(2,1)}, bf16[6,2,16,320]{3,2,1,0:T(8,128)(2,1)}, bf16[6,2,16,320]{3,...) custom-call(s32[2]{0:T(128)} %pad_add_fusion.me, ...), custom_call_target="tpu_custom_call" | custom-call | tf_op jit(solution)/shard_map/pallas_call | solution.py:646
  85.8 2.5 %collective-permute-start.17 = (bf16[128,320]{1,0:T(8,128)(2,1)}, bf16[128,320]{1,0:T(8,128)(2,1)S(1)}, u32[]{:S(2)}, u32[]{:S(2)}) collective-permute-start(bf16[128,320]{1,0:T(8,128)(2,1)} %get-tuple-element.79), channel_id=1, source_target_pairs={{0,8},{4,12},{8,0},{12,4},{16,24},{20,28},{24,16},{28,20},{1,9},{5... | collective-permute-start | bytes 245768 | tf_op jit(solution)/shard_map/ppermute | solution.py:72
  91.9 7.3 %collective-permute-done.18.refs_2_ = bf16[128,320]{1,0:T(8,128)(2,1)S(1)} collective-permute-done((bf16[128,320]{1,0:T(8,128)(2,1)}, bf16[128,320]{1,0:T(8,128)(2,1)S(1)}, u32[]{:S(2)}, u32[]{:S(2)}) %collective-permute-start.18) | collective-permute-done | bytes 81952 | tf_op jit(solution)/shard_map/ppermute | solution.py:72
  100.1 2.0 %shard_map.162 = (bf16[112,384]{1,0:T(8,128)(2,1)}, bf16[112,384]{1,0:T(8,128)(2,1)}, bf16[112,384]{1,0:T(8,128)(2,1)}, bf16[112,384]{1,0:T(8,128)(2,1)}) custom-call(s32[2]{0:T(128)} %pad_add_fusion.me, bf16[4,112,384]{2,1,0:T(8,128)(2,1)} %get-tuple-element.74.keep, bf16[4,112,384]{2,1,0:T(8,128)(2,1)} %copy-done.15, ...), custom_call_target="tpu_custom_call" | custom-call | tf_op jit(solution)/shard_map/pallas_call | solution.py:655
  111.7 2.9 %collective-permute-start.23 = (bf16[2,1,56,384]{3,2,1,0:T(8,128)(2,1)}, bf16[2,1,56,384]{3,2,1,0:T(8,128)(2,1)S(1)}, u32[]{:S(2)}, u32[]{:S(2)}) collective-permute-start(bf16[2,1,56,384]{3,2,1,0:T(8,128)(2,1)} %bitcast.35), channel_id=1, source_target_pairs={{0,16},{4,20},{8,24},{12,28},{16,0},{20,4},{24,8},{28,12},{1,17},{... | collective-permute-start | bytes 258056 | tf_op jit(solution)/shard_map/ppermute | solution.py:72
  114.6 2.7 %collective-permute-done.23 = bf16[2,1,56,384]{3,2,1,0:T(8,128)(2,1)S(1)} collective-permute-done((bf16[2,1,56,384]{3,2,1,0:T(8,128)(2,1)}, bf16[2,1,56,384]{3,2,1,0:T(8,128)(2,1)S(1)}, u32[]{:S(2)}, u32[]{:S(2)}) %collective-permute-start.23) | collective-permute-done | bytes 86048 | tf_op jit(solution)/shard_map/ppermute | solution.py:72
  118.2 1.9 %collective-permute-start.24 = (bf16[2,2,56,384]{3,2,1,0:T(8,128)(2,1)S(1)}, bf16[2,2,56,384]{3,2,1,0:T(8,128)(2,1)S(1)}, u32[]{:S(2)}, u32[]{:S(2)}) collective-permute-start(bf16[2,2,56,384]{3,2,1,0:T(8,128)(2,1)S(1)} %pad_maximum_fusion.6), channel_id=1, source_target_pairs={{0,8},{4,12},{8,0},{12,4},{16,24},{20,28},{24,16},{28,20},{1,9},{5... | collective-permute-start | bytes 516104 | tf_op jit(solution)/shard_map/ppermute | solution.py:72
  120.2 3.5 %collective-permute-done.24 = bf16[2,2,56,384]{3,2,1,0:T(8,128)(2,1)S(1)} collective-permute-done((bf16[2,2,56,384]{3,2,1,0:T(8,128)(2,1)S(1)}, bf16[2,2,56,384]{3,2,1,0:T(8,128)(2,1)S(1)}, u32[]{:S(2)}, u32[]{:S(2)}) %collective-permute-start.24) | collective-permute-done | bytes 172064 | tf_op jit(solution)/shard_map/ppermute | solution.py:72
  127.2 3.0 %collective-permute-done.25 = bf16[1,4,56,384]{3,2,1,0:T(8,128)(2,1)S(1)} collective-permute-done((bf16[1,4,56,384]{3,2,1,0:T(8,128)(2,1)S(1)}, bf16[1,4,56,384]{3,2,1,0:T(8,128)(2,1)S(1)}, u32[]{:S(2)}, u32[]{:S(2)}) %collective-permute-start.25) | collective-permute-done | bytes 172064 | tf_op jit(solution)/shard_map/ppermute | solution.py:72
  136.4 5.3 %collective-permute-done.9.refs_1_ = bf16[6,2,16,320]{3,2,1,0:T(8,128)(2,1)S(1)} collective-permute-done((bf16[6,2,16,320]{3,2,1,0:T(8,128)(2,1)S(1)}, bf16[6,2,16,320]{3,2,1,0:T(8,128)(2,1)S(1)}, u32[]{:S(2)}, u32[]{:S(2)}) %collective-permute-start.9) | collective-permute-done | bytes 122912 | tf_op jit(solution)/shard_map/ppermute | solution.py:72
  143.2 4.5 %collective-permute-done.11.refs_3_ = bf16[6,2,16,320]{3,2,1,0:T(8,128)(2,1)S(1)} collective-permute-done((bf16[6,2,16,320]{3,2,1,0:T(8,128)(2,1)S(1)}, bf16[6,2,16,320]{3,2,1,0:T(8,128)(2,1)S(1)}, u32[]{:S(2)}, u32[]{:S(2)}) %collective-permute-start.11) | collective-permute-done | bytes 122912 | tf_op jit(solution)/shard_map/ppermute | solution.py:72
  152.4 3.1 %shard_map.158 = (bf16[2,2,320,128]{3,2,1,0:T(8,128)(2,1)}, f32[2,2,320,128]{3,2,1,0:T(8,128)}) custom-call(s32[2]{0:T(128)} %pad_add_fusion.me, bf16[2,2,320,128]{3,2,1,0:T(8,128)(2,1)} %get-tuple-element.55.hidden, f32[2,2,320,128]{3,2,1,0:T(8,128)} %get-tuple-element.56.base, bf16[4,32,320]{2,1,0:T(8,128)(2,1)} %bitcast.38, bf16[4,32,320]{2,1,0:T(8,128)(2,1)} %bitcast.39, ...), custom_call_target="tpu_custom_call" | custom-call | tf_op jit(solution)/shard_map/pallas_call | solution.py:686
  156.5 4.7 %shard_map.159 = (f32[960,1280]{1,0:T(8,128)}, f32[320,1280]{1,0:T(8,128)}) custom-call(bf16[384,1280]{1,0:T(8,128)(2,1)} %get-tuple-element.61.refs_9_.refs_10_.refs_11_.down, bf16[384,1024]{1,0:T(8,128)(2,1)} %get-tuple-element.70.mix_a, bf16[384,1024]{1,0:T(8,128)(2,1)} %copy-done.1, bf16[320,320]{1,0:T(8,128)(2,1)} %get-tuple-element.71.refs_0_, ...), custom_call_target="tpu_custom_call" | custom-call | tf_op jit(solution)/shard_map/pallas_call | solution.py:700
  161.2 4.7 %shard_map.160 = f32[960,1280]{1,0:T(8,128)} custom-call(bf16[384,1280]{1,0:T(8,128)(2,1)} %get-tuple-element.61.refs_9_.refs_10_.refs_11_.down, bf16[384,1024]{1,0:T(8,128)(2,1)} %get-tuple-element.70.mix_a, bf16[384,1024]{1,0:T(8,128)(2,1)} %copy-done.1, f32[960,1280]{1,0:T(8,128)} %get-tuple-element.72.refs_0_), custom_call_target="tpu_custom_call", output_to_operand_aliasing={{}: (3, {})} | custom-call | tf_op jit(solution)/shard_map/pallas_call | solution.py:718
  167.0 5.3 %shard_map.164 = (f32[30,32,320]{2,1,0:T(8,128)}, f32[320,1280]{1,0:T(8,128)}, f32[320,1280]{1,0:T(8,128)}, f32[320,1280]{1,0:T(8,128)}) custom-call(s32[2]{0:T(128)} %pad_add_fusion.me, f32[320,128]{1,0:T(8,128)} %get-tuple-element.88.embed, bf16[2,4,56,384]{3,2,1,0:T(8,128)(2,1)} %copy-done.5, bf16[2,4,56,384]{3,2,1,0:T(8,128)(2,1)} %copy-done.10, ...), custom_call_target="tpu_custom_call" | custom-call | tf_op jit(solution)/shard_map/pallas_call | solution.py:747
  (138 shorter events, 53.6 us)
Async XLA Ops:
  5.3 10.3 %collective-permute-start.3 = (bf16[2,6,8,640]{3,2,1,0:T(8,128)(2,1)S(1)}, bf16[2,6,8,640]{3,2,1,0:T(8,128)(2,1)S(1)}, u32[]{:S(2)}, u32[]{:S(2)}) collective-permute-start(bf16[2,6,8,640]{3,2,1,0:T(8,128)(2,1)S(1)} %pad_maximum_fusion.7), channel_id=1, source_target_pairs={{0,16},{4,20},{8,24},{12,28},{16,0},{20,4},{24,8},{28,12},{1,17},{... | collective-permute-start | bytes 368648 | tf_op jit(solution)/shard_map/ppermute | solution.py:72
  16.4 7.5 %collective-permute-start.4 = (bf16[2,12,8,640]{3,2,1,0:T(8,128)(2,1)S(1)}, bf16[2,12,8,640]{3,2,1,0:T(8,128)(2,1)S(1)}, u32[]{:S(2)}, u32[]{:S(2)}) collective-permute-start(bf16[2,12,8,640]{3,2,1,0:T(8,128)(2,1)S(1)} %pad_maximum_fusion.5), channel_id=1, source_target_pairs={{0,8},{4,12},{8,0},{12,4},{16,24},{20,28},{24,16},{28,20},{1,9},{5... | collective-permute-start | bytes 737288 | tf_op jit(solution)/shard_map/ppermute | solution.py:72
  24.0 6.7 %collective-permute-start.5 = (bf16[1,24,8,640]{3,2,1,0:T(8,128)(2,1)S(1)}, bf16[1,24,8,640]{3,2,1,0:T(8,128)(2,1)S(1)}, u32[]{:S(2)}, u32[]{:S(2)}) collective-permute-start(bf16[1,24,8,640]{3,2,1,0:T(8,128)(2,1)S(1)} %get-tuple-element.97), channel_id=1, source_target_pairs={{0,1},{1,0},{2,3},{3,2},{4,5},{5,4},{6,7},{7,6},{8,9},{9,8},{10,11... | collective-permute-start | bytes 737288 | tf_op jit(solution)/shard_map/ppermute | solution.py:72
  25.3 6.5 %collective-permute-start.7 = (bf16[1,24,8,640]{3,2,1,0:T(8,128)(2,1)S(1)}, bf16[1,24,8,640]{3,2,1,0:T(8,128)(2,1)S(1)}, u32[]{:S(2)}, u32[]{:S(2)}) collective-permute-start(bf16[1,24,8,640]{3,2,1,0:T(8,128)(2,1)S(1)} %get-tuple-element.96), channel_id=1, source_target_pairs={{0,2},{1,3},{2,0},{3,1},{4,6},{5,7},{6,4},{7,5},{8,10},{9,11},{10,... | collective-permute-start | bytes 737288 | tf_op jit(solution)/shard_map/ppermute | solution.py:72
  30.7 29.1 %collective-permute-start.6 = (bf16[2,24,8,640]{3,2,1,0:T(8,128)(2,1)S(1)}, bf16[2,24,8,640]{3,2,1,0:T(8,128)(2,1)S(1)}, u32[]{:S(2)}, u32[]{:S(2)}) collective-permute-start(bf16[2,24,8,640]{3,2,1,0:T(8,128)(2,1)S(1)} %pad_maximum_fusion.first_a), channel_id=1, source_target_pairs={{0,2},{1,3},{2,0},{3,1},{4,6},{5,7},{6,4},{7,5},{8,10},{9,11},{10,... | collective-permute-start | bytes 1474568 | tf_op jit(solution)/shard_map/ppermute | solution.py:72
  31.9 28.0 %collective-permute-start.8 = (bf16[2,24,8,640]{3,2,1,0:T(8,128)(2,1)S(1)}, bf16[2,24,8,640]{3,2,1,0:T(8,128)(2,1)S(1)}, u32[]{:S(2)}, u32[]{:S(2)}) collective-permute-start(bf16[2,24,8,640]{3,2,1,0:T(8,128)(2,1)S(1)} %pad_maximum_fusion.1.second_a), channel_id=1, source_target_pairs={{0,1},{1,0},{2,3},{3,2},{4,5},{5,4},{6,7},{7,6},{8,9},{9,8},{10,11... | collective-permute-start | bytes 1474568 | tf_op jit(solution)/shard_map/ppermute | solution.py:72
  36.7 6.1 %collective-permute-start.1 = (bf16[4,320,128]{2,1,0:T(8,128)(2,1)}, bf16[4,320,128]{2,1,0:T(8,128)(2,1)S(1)}, u32[]{:S(2)}, u32[]{:S(2)}) collective-permute-start(bf16[4,320,128]{2,1,0:T(8,128)(2,1)} %get-tuple-element.54), channel_id=1, source_target_pairs={{4,0},{8,4},{12,8},{16,12},{20,16},{24,20},{28,24},{5,1},{9,5},{13... | collective-permute-start | bytes 983048 | tf_op jit(solution)/shard_map/ppermute | solution.py:541
  48.0 35.1 %collective-permute-start.16 = (bf16[4,128,320]{2,1,0:T(8,128)(2,1)}, bf16[4,128,320]{2,1,0:T(8,128)(2,1)S(1)}, u32[]{:S(2)}, u32[]{:S(2)}) collective-permute-start(bf16[4,128,320]{2,1,0:T(8,128)(2,1)} %get-tuple-element.77), channel_id=1, source_target_pairs={{0,4},{4,0},{8,12},{12,8},{16,20},{20,16},{24,28},{28,24},{1,5},{5... | collective-permute-start | bytes 983048 | tf_op jit(solution)/shard_map/ppermute | solution.py:72
  83.0 16.3 %collective-permute-start.15 = (bf16[4,112,384]{2,1,0:T(8,128)(2,1)}, bf16[4,112,384]{2,1,0:T(8,128)(2,1)S(1)}, u32[]{:S(2)}, u32[]{:S(2)}) collective-permute-start(bf16[4,112,384]{2,1,0:T(8,128)(2,1)} %get-tuple-element.75), channel_id=1, source_target_pairs={{0,4},{4,0},{8,12},{12,8},{16,20},{20,16},{24,28},{28,24},{1,5},{5... | collective-permute-start | bytes 1032200 | tf_op jit(solution)/shard_map/ppermute | solution.py:72
  85.8 6.2 %collective-permute-start.17 = (bf16[128,320]{1,0:T(8,128)(2,1)}, bf16[128,320]{1,0:T(8,128)(2,1)S(1)}, u32[]{:S(2)}, u32[]{:S(2)}) collective-permute-start(bf16[128,320]{1,0:T(8,128)(2,1)} %get-tuple-element.79), channel_id=1, source_target_pairs={{0,8},{4,12},{8,0},{12,4},{16,24},{20,28},{24,16},{28,20},{1,9},{5... | collective-permute-start | bytes 245768 | tf_op jit(solution)/shard_map/ppermute | solution.py:72
  88.3 11.0 %collective-permute-start.18 = (bf16[128,320]{1,0:T(8,128)(2,1)}, bf16[128,320]{1,0:T(8,128)(2,1)S(1)}, u32[]{:S(2)}, u32[]{:S(2)}) collective-permute-start(bf16[128,320]{1,0:T(8,128)(2,1)} %get-tuple-element.80), channel_id=1, source_target_pairs={{0,16},{4,20},{8,24},{12,28},{16,0},{20,4},{24,8},{28,12},{1,17},{... | collective-permute-start | bytes 245768 | tf_op jit(solution)/shard_map/ppermute | solution.py:72
  89.5 9.8 %collective-permute-start.19 = (bf16[128,320]{1,0:T(8,128)(2,1)}, bf16[128,320]{1,0:T(8,128)(2,1)S(1)}, u32[]{:S(2)}, u32[]{:S(2)}) collective-permute-start(bf16[128,320]{1,0:T(8,128)(2,1)} %get-tuple-element.81), channel_id=1, source_target_pairs={{0,24},{4,28},{8,16},{12,20},{16,8},{20,12},{24,0},{28,4},{1,25},{... | collective-permute-start | bytes 245768 | tf_op jit(solution)/shard_map/ppermute | solution.py:72
  125.7 6.1 %collective-permute-start.28 = (bf16[1,4,56,384]{3,2,1,0:T(8,128)(2,1)S(1)}, bf16[1,4,56,384]{3,2,1,0:T(8,128)(2,1)S(1)}, u32[]{:S(2)}, u32[]{:S(2)}) collective-permute-start(bf16[1,4,56,384]{3,2,1,0:T(8,128)(2,1)S(1)} %get-tuple-element.98), channel_id=1, source_target_pairs={{0,1},{1,0},{2,3},{3,2},{4,5},{5,4},{6,7},{7,6},{8,9},{9,8},{10,11... | collective-permute-start | bytes 516104 | tf_op jit(solution)/shard_map/ppermute | solution.py:72
  127.2 28.4 %collective-permute-start.13 = (bf16[384,1024]{1,0:T(8,128)(2,1)S(1)}, bf16[384,1024]{1,0:T(8,128)(2,1)S(1)}, u32[]{:S(2)}, u32[]{:S(2)}) collective-permute-start(bf16[384,1024]{1,0:T(8,128)(2,1)S(1)} %copy-done), channel_id=1, source_target_pairs={{0,4},{4,0},{8,12},{12,8},{16,20},{20,16},{24,28},{28,24},{1,5},{5... | collective-permute-start | bytes 2359304 | tf_op jit(solution)/shard_map/ppermute | solution.py:72
  130.2 20.0 %collective-permute-start.26 = (bf16[2,4,56,384]{3,2,1,0:T(8,128)(2,1)S(1)}, bf16[2,4,56,384]{3,2,1,0:T(8,128)(2,1)S(1)}, u32[]{:S(2)}, u32[]{:S(2)}) collective-permute-start(bf16[2,4,56,384]{3,2,1,0:T(8,128)(2,1)S(1)} %pad_maximum_fusion.3.refs_2_), channel_id=1, source_target_pairs={{0,1},{1,0},{2,3},{3,2},{4,5},{5,4},{6,7},{7,6},{8,9},{9,8},{10,11... | collective-permute-start | bytes 1032200 | tf_op jit(solution)/shard_map/ppermute | solution.py:72
  131.8 20.4 %collective-permute-start.29 = (bf16[2,4,56,384]{3,2,1,0:T(8,128)(2,1)S(1)}, bf16[2,4,56,384]{3,2,1,0:T(8,128)(2,1)S(1)}, u32[]{:S(2)}, u32[]{:S(2)}) collective-permute-start(bf16[2,4,56,384]{3,2,1,0:T(8,128)(2,1)S(1)} %pad_maximum_fusion.4.refs_0_), channel_id=1, source_target_pairs={{0,2},{1,3},{2,0},{3,1},{4,6},{5,7},{6,4},{7,5},{8,10},{9,11},{10,... | collective-permute-start | bytes 1032200 | tf_op jit(solution)/shard_map/ppermute | solution.py:72
  133.6 8.1 %collective-permute-start.9 = (bf16[6,2,16,320]{3,2,1,0:T(8,128)(2,1)S(1)}, bf16[6,2,16,320]{3,2,1,0:T(8,128)(2,1)S(1)}, u32[]{:S(2)}, u32[]{:S(2)}) collective-permute-start(bf16[6,2,16,320]{3,2,1,0:T(8,128)(2,1)S(1)} %copy-done.32), channel_id=1, source_target_pairs={{0,1},{1,0},{2,3},{3,2},{4,5},{5,4},{6,7},{7,6},{8,9},{9,8},{10,11... | collective-permute-start | bytes 368648 | tf_op jit(solution)/shard_map/ppermute | solution.py:72
  134.4 8.6 %collective-permute-start.10 = (bf16[6,2,16,320]{3,2,1,0:T(8,128)(2,1)S(1)}, bf16[6,2,16,320]{3,2,1,0:T(8,128)(2,1)S(1)}, u32[]{:S(2)}, u32[]{:S(2)}) collective-permute-start(bf16[6,2,16,320]{3,2,1,0:T(8,128)(2,1)S(1)} %copy-done.31), channel_id=1, source_target_pairs={{0,2},{1,3},{2,0},{3,1},{4,6},{5,7},{6,4},{7,5},{8,10},{9,11},{10,... | collective-permute-start | bytes 368648 | tf_op jit(solution)/shard_map/ppermute | solution.py:72
  141.6 6.0 %collective-permute-start.11 = (bf16[6,2,16,320]{3,2,1,0:T(8,128)(2,1)S(1)}, bf16[6,2,16,320]{3,2,1,0:T(8,128)(2,1)S(1)}, u32[]{:S(2)}, u32[]{:S(2)}) collective-permute-start(bf16[6,2,16,320]{3,2,1,0:T(8,128)(2,1)S(1)} %copy-done.30), channel_id=1, source_target_pairs={{0,3},{1,2},{2,1},{3,0},{4,7},{5,6},{6,5},{7,4},{8,11},{9,10},{10,... | collective-permute-start | bytes 368648 | tf_op jit(solution)/shard_map/ppermute | solution.py:72
  143.1 8.8 %collective-permute-start.14 = (bf16[320,320]{1,0:T(8,128)(2,1)S(1)}, bf16[320,320]{1,0:T(8,128)(2,1)S(1)}, u32[]{:S(2)}, u32[]{:S(2)}) collective-permute-start(bf16[320,320]{1,0:T(8,128)(2,1)S(1)} %copy-done.18), channel_id=1, source_target_pairs={{0,4},{4,0},{8,12},{12,8},{16,20},{20,16},{24,28},{28,24},{1,5},{5... | collective-permute-start | bytes 614408 | tf_op jit(solution)/shard_map/ppermute | solution.py:72
  150.3 15.7 %collective-permute-start.27 = (bf16[2,4,56,384]{3,2,1,0:T(8,128)(2,1)S(1)}, bf16[2,4,56,384]{3,2,1,0:T(8,128)(2,1)S(1)}, u32[]{:S(2)}, u32[]{:S(2)}) collective-permute-start(bf16[2,4,56,384]{3,2,1,0:T(8,128)(2,1)S(1)} %collective-permute-done.26.refs_3_), channel_id=1, source_target_pairs={{0,4},{4,0},{8,12},{12,8},{16,20},{20,16},{24,28},{28,24},{1,5},{5... | collective-permute-start | bytes 1032200 | tf_op jit(solution)/shard_map/ppermute | solution.py:72
  151.8 14.2 %collective-permute-start.30 = (bf16[2,4,56,384]{3,2,1,0:T(8,128)(2,1)S(1)}, bf16[2,4,56,384]{3,2,1,0:T(8,128)(2,1)S(1)}, u32[]{:S(2)}, u32[]{:S(2)}) collective-permute-start(bf16[2,4,56,384]{3,2,1,0:T(8,128)(2,1)S(1)} %pad_maximum_fusion.4.refs_0_), channel_id=1, source_target_pairs={{0,4},{4,0},{8,12},{12,8},{16,20},{20,16},{24,28},{28,24},{1,5},{5... | collective-permute-start | bytes 1032200 | tf_op jit(solution)/shard_map/ppermute | solution.py:72
  151.9 14.0 %collective-permute-start.32 = (bf16[2,4,56,384]{3,2,1,0:T(8,128)(2,1)S(1)}, bf16[2,4,56,384]{3,2,1,0:T(8,128)(2,1)S(1)}, u32[]{:S(2)}, u32[]{:S(2)}) collective-permute-start(bf16[2,4,56,384]{3,2,1,0:T(8,128)(2,1)S(1)} %pad_maximum_fusion.3.refs_2_), channel_id=1, source_target_pairs={{0,4},{4,0},{8,12},{12,8},{16,20},{20,16},{24,28},{28,24},{1,5},{5... | collective-permute-start | bytes 1032200 | tf_op jit(solution)/shard_map/ppermute | solution.py:72
  152.3 13.7 %collective-permute-start.31 = (bf16[2,4,56,384]{3,2,1,0:T(8,128)(2,1)S(1)}, bf16[2,4,56,384]{3,2,1,0:T(8,128)(2,1)S(1)}, u32[]{:S(2)}, u32[]{:S(2)}) collective-permute-start(bf16[2,4,56,384]{3,2,1,0:T(8,128)(2,1)S(1)} %collective-permute-done.29.refs_1_), channel_id=1, source_target_pairs={{0,4},{4,0},{8,12},{12,8},{16,20},{20,16},{24,28},{28,24},{1,5},{5... | collective-permute-start | bytes 1032200 | tf_op jit(solution)/shard_map/ppermute | solution.py:72
  (42 other events, 353.0 us)

commit v7 on v6

--- a/solution.py
+++ b/solution.py
@@ -113,13 +113,11 @@
             send[color, item] = fold(tmp[item, pl.ds(base, quart), :])
 
 
-def edge_kernel(clip, cot, after, head, tail):
+def edge_kernel(cells, after, head, tail):
     del after
     for r in range(2):
-        head[r] = clip[0, r]
-        head[2 + r] = cot[0, r]
-        tail[r] = clip[1, r]
-        tail[2 + r] = cot[1, r]
+        head[r] = cells[0, r]
+        tail[r] = cells[1, r]
 
 
 def weight_kernel(w_down, w_embed, embed, w_qkv, w_out, w_up, down, mix, out_mix, direct, column):
@@ -150,39 +148,23 @@
     direct[...] = nt(full, up).astype(BF)
 
 
-def fine_kernel(me, clip, cot, lo, hi, w_time, hidden, base, keep, send, wide, grad, taps):
-    chans = w_time.shape[1]
-    columns = clip.shape[3]
+def fine_kernel(me, clip, cot, lo, hi, keep, send, wide, here, taps):
+    chans, columns = clip.shape[2], clip.shape[3]
+    cells = 2 * columns
     for t in range(4):
         for r in range(2):
             at = slice((2 * t + r) * columns, (2 * t + r + 1) * columns)
-            if t in (0, 3):
-                halo = lo if t == 0 else hi
-                wide[:, at] = halo[r]
-                grad[:, at] = halo[2 + r]
-            else:
-                wide[:, at] = clip[t - 1, r]
-                grad[:, at] = cot[t - 1, r]
-    cells = 2 * columns
+            wide[:, at] = lo[r] if t == 0 else (hi[r] if t == 3 else cot[t - 1, r])
+            if t in (1, 2):
+                here[:, (2 * t - 2 + r) * columns : (2 * t - 1 + r) * columns] = clip[t - 1, r]
     taps[3 * chans :, :] = jnp.zeros((taps.shape[0] - 3 * chans, chans), F32)
-    here = grad[:, cells : 3 * cells]
     for tap in range(3):
-        taps[tap * chans : (tap + 1) * chans, :] = nt(wide[:, tap * cells : (tap + 2) * cells], here)
+        taps[tap * chans : (tap + 1) * chans, :] = nt(here[...], wide[:, (2 - tap) * cells : (4 - tap) * cells])
     core = me[0] & 1
     share = keep.shape[1]
     for z in range(keep.shape[0]):
         keep[z] = taps[pl.ds(pl.multiple_of((2 * z + core) * share, share), share), :].astype(BF)
         send[z] = taps[pl.ds(pl.multiple_of((2 * z + 1 - core) * share, share), share), :].astype(BF)
-    acc = wide[:, cells : 3 * cells].astype(F32)
-    back = here.astype(F32)
-    for tap in range(3):
-        acc = acc + tn(w_time[tap], wide[:, tap * cells : (tap + 2) * cells])
-        back = back + nn(w_time[tap], grad[:, (2 - tap) * cells : (4 - tap) * cells])
-    for t in range(2):
-        for r in range(2):
-            at = slice((2 * t + r) * columns, (2 * t + r + 1) * columns)
-            hidden[t, r] = acc[:, at].astype(BF)
-            base[t, r] = back[:, at]
 
 
 def tap_kernel(me, keep, got, *outs):
@@ -259,6 +241,7 @@
     row = lax.broadcasted_iota(jnp.int32, (tokens, tokens), 0)
     col = lax.broadcasted_iota(jnp.int32, (tokens, tokens), 1)
     same = (row & (quart - 1)) == (col & (quart - 1))
+    ones = jnp.ones((tokens, tokens), BF)
     cases = [(color, n) for color in range(2) for n in range(heads)]
 
     def part_of(color, n, which):
@@ -273,9 +256,9 @@
     for i, (color, n) in enumerate(cases):
         scores = jnp.where(same, score[i] * scale, -jnp.inf)
         ex = jnp.exp(scores - jnp.max(scores, axis=1, keepdims=True))
-        probs = ex * (1.0 / jnp.sum(ex, axis=1, keepdims=True))
+        probs = ex * (1.0 / nn(ex.astype(BF), ones))
         dw = slope[i]
-        inner = jnp.sum(probs * dw, axis=1, keepdims=True)
+        inner = nn((probs * dw).astype(BF), ones)
         weight[i] = probs.astype(BF)
         delta[i] = (probs * (dw - inner) * scale).astype(BF)
     for i, (color, n) in enumerate(cases):
@@ -393,11 +376,26 @@
     qkv_out[...] = nn(flipped[...], down[...])
 
 
-def finish_kernel(me, hidden, base, own, other, w_time, output, grad_clip, rows, *, coarse_frames):
+def finish_kernel(me, clip, cot, clip_lo, clip_hi, cot_lo, cot_hi, own, other, w_time, output, grad_clip, wide, grad, rows, *, coarse_frames):
+    columns = clip.shape[3]
+    cells = 2 * columns
+    for t in range(4):
+        for r in range(2):
+            at = slice((2 * t + r) * columns, (2 * t + r + 1) * columns)
+            if t in (0, 3):
+                wide[:, at] = (clip_lo if t == 0 else clip_hi)[r]
+                grad[:, at] = (cot_lo if t == 0 else cot_hi)[r]
+            else:
+                wide[:, at] = clip[t - 1, r]
+                grad[:, at] = cot[t - 1, r]
+    hidden = wide[:, cells : 3 * cells].astype(F32)
+    base = grad[:, cells : 3 * cells].astype(F32)
+    for tap in range(3):
+        hidden = hidden + tn(w_time[tap], wide[:, tap * cells : (tap + 2) * cells])
+        base = base + nn(w_time[tap], grad[:, (2 - tap) * cells : (4 - tap) * cells])
     frame = me[0]
     core = frame & 1
     half = own.shape[1]
-    columns = hidden.shape[3]
     for i in range(4):
         rows[i, pl.ds(pl.multiple_of(core * half, half), half), :] = own[i].astype(F32)
         rows[i, pl.ds(pl.multiple_of((1 - core) * half, half), half), :] = other[i].astype(F32)
@@ -405,7 +403,8 @@
     fine = tn(rows[0].astype(BF), lift)
     for t in range(2):
         for r in range(2):
-            output[t, r] = (hidden[t, r].astype(F32) + fine).astype(BF)
+            at = slice((2 * t + r) * columns, (2 * t + r + 1) * columns)
+            output[t, r] = (hidden[:, at] + fine).astype(BF)
     before = (rows[1] * jnp.where(frame == 0, 0.0, 1.0)).astype(BF)
     here = rows[2].astype(BF)
     after = (rows[3] * jnp.where(frame == coarse_frames - 1, 0.0, 1.0)).astype(BF)
@@ -417,7 +416,8 @@
         low = (value - high.astype(F32)).astype(BF)
         add = (tn(high, lift) + tn(low, lift)) * 0.125
         for r in range(2):
-            grad_clip[t, r] = base[t, r] + add
+            at = slice((2 * t + r) * columns, (2 * t + r + 1) * columns)
+            grad_clip[t, r] = base[:, at] + add
 
 
 def gather_kernel(me, embed, *refs, layout, aligned):
@@ -531,27 +531,31 @@
         ],
     )(w_down, w_embed, embed[None, :], w_qkv_t, w_out, w_up_t)
 
-    head, tail = call(
-        edge_kernel,
-        [sds((4, chans, columns), BF)] * 2,
-        in_specs=[vmem(), vmem(), pl.BlockSpec(memory_space=pl.ANY)],
+    def halo(x, after):
+        head, tail = call(
+            edge_kernel,
+            [sds((2, chans, columns), BF)] * 2,
+            in_specs=[vmem(), pl.BlockSpec(memory_space=pl.ANY)],
+            out_specs=[vmem()] * 2,
+        )(x, after)
+        lo = lax.ppermute(tail, "frames", [(i, i + 1) for i in range(nf - 1)])
+        hi = lax.ppermute(head, "frames", [(i + 1, i) for i in range(nf - 1)])
+        return lo, hi
+
+    cot_lo, cot_hi = halo(cot_t, keep)
+    clip_lo, clip_hi = halo(clip_t, keep)
+    tap_rows = round_up(3 * chans, devices * 8)
+    tap_keep, tap_send = call(
+        fine_kernel,
+        [sds((chips, tap_rows // nf, chans), BF)] * 2,
+        in_specs=[smem()] + [vmem()] * 4,
         out_specs=[vmem()] * 2,
-    )(clip_t, cot_t, keep)
-    lo = lax.ppermute(tail, "frames", [(i, i + 1) for i in range(nf - 1)])
-    hi = lax.ppermute(head, "frames", [(i + 1, i) for i in range(nf - 1)])
-    tap_rows = round_up(3 * chans, devices * 8)
-    hidden, base, tap_keep, tap_send = call(
-        fine_kernel,
-        [
-            sds(clip_t.shape, BF),
-            sds(clip_t.shape, F32),
-            sds((chips, tap_rows // nf, chans), BF),
-            sds((chips, tap_rows // nf, chans), BF),
+        scratch_shapes=[
+            pltpu.VMEM((chans, 8 * columns), BF),
+            pltpu.VMEM((chans, 4 * columns), BF),
+            pltpu.VMEM((tap_rows, chans), F32),
         ],
-        in_specs=[smem()] + [vmem()] * 5,
-        out_specs=[vmem()] * 4,
-        scratch_shapes=[pltpu.VMEM((chans, 8 * columns), BF)] * 2 + [pltpu.VMEM((tap_rows, chans), F32)],
-    )(me, clip_t, cot_t, lo, hi, w_time)
+    )(me, clip_t, cot_t, cot_lo, cot_hi)
     share = tap_rows // nf
     tap_got = swap(tap_send, "frames", 1)
     tap_parts = call(
@@ -686,10 +690,10 @@
     output, grad_clip = call(
         functools.partial(finish_kernel, coarse_frames=nf),
         [sds(clip_t.shape, BF), sds(clip_t.shape, F32)],
-        in_specs=[smem()] + [vmem()] * 5,
+        in_specs=[smem()] + [vmem()] * 9,
         out_specs=[vmem()] * 2,
-        scratch_shapes=[pltpu.VMEM((4, half_c, chans), F32)],
-    )(me, hidden, base, mine4, other4, w_time)
+        scratch_shapes=[pltpu.VMEM((chans, 8 * columns), BF)] * 2 + [pltpu.VMEM((4, half_c, chans), F32)],
+    )(me, clip_t, cot_t, clip_lo, clip_hi, cot_lo, cot_hi, mine4, other4, w_time)
 
     mix_o = swap(mix_g, "frames", 1)
     att_o = swap(att_g, "frames", 1)

time: 173 us -> 170 us (0.983)
  waiting for transfers between devices: 53.3 us -> 48.3 us
    ppermute x31, waiting for transfers between devices: 49.9 us -> 45.1 us  [swap(): return lax.ppermute(x, axis, [(i, i ^ bit) for i in range(n)])]
    ppermute x2 -> x4, starting transfers between devices: 2.59 us -> 5.33 us  [the longest x2 2.75 us: halo(): hi = lax.ppermute(head, 'frames', [(i + 1, i) for i in range(nf - 1)])]
    unnamed x69 -> x73, local copies, waits for them, and re-layouts: 7.33 us -> 7.19 us
    pallas_call x2 -> x3, Pallas kernels: 6.47 us -> 6.43 us  [the longest x2 3.42 us: halo(): call(edge_kernel, [sds((2, chans, columns), BF)] * 2, in_specs=[vmem(), p...]
  transfers between devices with their start and end apart: 33 -> 35, of which waited for: 17 -> 14; matrix products, arithmetic and copies ran while one was open for 1% -> 1% of each run, Pallas kernels for 29% -> 30%
where the time goes in v7:
time: 170 us
  Pallas kernels  62.6 us (37%)
  waiting for transfers between devices  48.3 us (28%)
  starting transfers between devices  44.3 us (26%)
  local copies, waits for them, and re-layouts  7.3 us (4%)
  other arithmetic  5.05 us (3%)
  between operations  1.89 us (1%)
    ppermute x31, waiting for transfers between devices, swap(): return lax.ppermute(x, axis, [(i, i ^ bit) for i in range(n)])  45.1 us
    ppermute x31, starting transfers between devices, swap(): return lax.ppermute(x, axis, [(i, i ^ bit) for i in range(n)])  39 us
    pallas_call x1, Pallas kernels, body(): call(functools.partial(coarse_kernel, coarse_frames=nf, heads_axis=nh, re...  21.4 us
    unnamed x73, local copies, waits for them, and re-layouts  7.19 us
    pallas_call x1, Pallas kernels, body(): call(weight_kernel, [sds((padded, width), BF), sds((padded, pieces * SLOT...  5.77 us
    pallas_call x1, Pallas kernels, body(): call(functools.partial(gather_kernel, layout=layout, aligned=aligned), ou...  5.31 us
    pallas_call x1, Pallas kernels, body(): call(functools.partial(split_grad_kernel, late=True), wide, grid=(width /...  4.72 us
    pallas_call x1, Pallas kernels, body(): call(functools.partial(split_grad_kernel, late=False), [wide, sds((heads...  4.71 us
  transfers between devices with their start and end apart: 35, of which 14 were waited for; matrix products, arithmetic and copies ran while one was open for 1% of the time, Pallas kernels for 30%

profile of v7, /device:TPU:0, one launch (start us, length us, event | category | flops | bytes accessed | tf_op | source)
XLA Modules:
  0.0 169.5 jit_solution(9944741940578874350)
XLA Ops:
  0.6 2.2 %shard_map.152 = (bf16[2,3,8,640]{3,2,1,0:T(8,128)(2,1)}, bf16[2,3,8,640]{3,2,1,0:T(8,128)(2,1)}) custom-call(s32[1]{0:T(128)} %bitcast.me, bf16[2,2,320,128]{3,2,1,0:T(8,128)(2,1)} %bitcast.27, bf16[2,2,320,128]{3,2,1,0:T(8,128)(2,1)} %bitcast.31), custom_call_target="tpu_custom_call" | custom-call | tf_op jit(solution)/shard_map/pallas_call | solution.py:510
  5.3 4.0 %collective-permute-start.5 = (bf16[2,6,8,640]{3,2,1,0:T(8,128)(2,1)S(1)}, bf16[2,6,8,640]{3,2,1,0:T(8,128)(2,1)S(1)}, u32[]{:S(2)}, u32[]{:S(2)}) collective-permute-start(bf16[2,6,8,640]{3,2,1,0:T(8,128)(2,1)S(1)} %pad_maximum_fusion.7), channel_id=1, source_target_pairs={{0,16},{4,20},{8,24},{12,28},{16,0},{20,4},{24,8},{28,12},{1,17},{... | collective-permute-start | bytes 368648 | tf_op jit(solution)/shard_map/ppermute | solution.py:72
  9.2 6.3 %collective-permute-done.5 = bf16[2,6,8,640]{3,2,1,0:T(8,128)(2,1)S(1)} collective-permute-done((bf16[2,6,8,640]{3,2,1,0:T(8,128)(2,1)S(1)}, bf16[2,6,8,640]{3,2,1,0:T(8,128)(2,1)S(1)}, u32[]{:S(2)}, u32[]{:S(2)}) %collective-permute-start.5) | collective-permute-done | bytes 122912 | tf_op jit(solution)/shard_map/ppermute | solution.py:72
  18.1 5.8 %collective-permute-done.6 = bf16[2,12,8,640]{3,2,1,0:T(8,128)(2,1)S(1)} collective-permute-done((bf16[2,12,8,640]{3,2,1,0:T(8,128)(2,1)S(1)}, bf16[2,12,8,640]{3,2,1,0:T(8,128)(2,1)S(1)}, u32[]{:S(2)}, u32[]{:S(2)}) %collective-permute-start.6) | collective-permute-done | bytes 245792 | tf_op jit(solution)/shard_map/ppermute | solution.py:72
  26.8 3.8 %collective-permute-done.7 = bf16[1,24,8,640]{3,2,1,0:T(8,128)(2,1)S(1)} collective-permute-done((bf16[1,24,8,640]{3,2,1,0:T(8,128)(2,1)S(1)}, bf16[1,24,8,640]{3,2,1,0:T(8,128)(2,1)S(1)}, u32[]{:S(2)}, u32[]{:S(2)}) %collective-permute-start.7) | collective-permute-done | bytes 245792 | tf_op jit(solution)/shard_map/ppermute | solution.py:72
  39.1 3.2 %collective-permute-done.3.cot_hi.hi = bf16[2,320,128]{2,1,0:T(8,128)(2,1)S(1)} collective-permute-done((bf16[2,320,128]{2,1,0:T(8,128)(2,1)}, bf16[2,320,128]{2,1,0:T(8,128)(2,1)S(1)}, u32[]{:S(2)}, u32[]{:S(2)}) %collective-permute-start.3) | collective-permute-done | bytes 163872 | tf_op jit(solution)/shard_map/ppermute | solution.py:542
  42.9 3.0 %shard_map.161 = (bf16[4,128,320]{2,1,0:T(8,128)(2,1)}, bf16[4,128,320]{2,1,0:T(8,128)(2,1)}) custom-call(s32[2]{0:T(128)} %pad_add_fusion.me, bf16[2,2,320,128]{3,2,1,0:T(8,128)(2,1)} %bitcast.28, bf16[2,2,320,128]{3,2,1,0:T(8,128)(2,1)} %bitcast.33, bf16[2,320,128]{2,1,0:T(8,128)(2,1)} %copy-done.6, bf16[2,320,128]{2,1,0:T(8,128)(2,1)} %copy-done.7), custom_call_target="tpu_custom_call" | custom-call | tf_op jit(solution)/shard_map/pallas_call | solution.py:548
  45.9 3.9 %collective-permute-start.18 = (bf16[4,128,320]{2,1,0:T(8,128)(2,1)}, bf16[4,128,320]{2,1,0:T(8,128)(2,1)S(1)}, u32[]{:S(2)}, u32[]{:S(2)}) collective-permute-start(bf16[4,128,320]{2,1,0:T(8,128)(2,1)} %get-tuple-element.77), channel_id=1, source_target_pairs={{0,4},{4,0},{8,12},{12,8},{16,20},{20,16},{24,28},{28,24},{1,5},{5... | collective-permute-start | bytes 983048 | tf_op jit(solution)/shard_map/ppermute | solution.py:72
  50.5 5.8 %shard_map.155 = (bf16[384,1280]{1,0:T(8,128)(2,1)}, bf16[384,1536]{1,0:T(8,128)(2,1)}, bf16[512,320]{1,0:T(8,128)(2,1)}, bf16[384,320]{1,0:T(8,128)(2,1)}, f32[320,128]{1,0:T(8,128)}) custom-call(bf16[320,1280]{1,0:T(8,128)(2,1)} %w_down.1, bf16[320,1280]{1,0:T(8,128)(2,1)} %w_embed.1, bf16[1,320]{1,0:T(2,128)(2,1)} %fusion.embed, ...), custom_call_target="tpu_custom_call" | custom-call | tf_op jit(solution)/shard_map/pallas_call | solution.py:523
  57.2 21.4 %shard_map.156 = (bf16[6,2,16,320]{3,2,1,0:T(8,128)(2,1)}, bf16[6,2,16,320]{3,2,1,0:T(8,128)(2,1)}, bf16[6,2,16,320]{3,2,1,0:T(8,128)(2,1)}, bf16[6,2,16,320]{3,...) custom-call(s32[2]{0:T(128)} %pad_add_fusion.me, ...), custom_call_target="tpu_custom_call" | custom-call | tf_op jit(solution)/shard_map/pallas_call | solution.py:650
  79.5 1.9 %shard_map.162 = (bf16[128,320]{1,0:T(8,128)(2,1)}, bf16[128,320]{1,0:T(8,128)(2,1)}, bf16[128,320]{1,0:T(8,128)(2,1)}, bf16[128,320]{1,0:T(8,128)(2,1)}) custom-call(s32[2]{0:T(128)} %pad_add_fusion.me, bf16[4,128,320]{2,1,0:T(8,128)(2,1)} %get-tuple-element.76.keep, bf16[4,128,320]{2,1,0:T(8,128)(2,1)} %copy-done.10), custom_call_target="tpu_custom_call" | custom-call | tf_op jit(solution)/shard_map/pallas_call | solution.py:561
  81.4 2.5 %collective-permute-start.19 = (bf16[128,320]{1,0:T(8,128)(2,1)}, bf16[128,320]{1,0:T(8,128)(2,1)S(1)}, u32[]{:S(2)}, u32[]{:S(2)}) collective-permute-start(bf16[128,320]{1,0:T(8,128)(2,1)} %get-tuple-element.79), channel_id=1, source_target_pairs={{0,8},{4,12},{8,0},{12,4},{16,24},{20,28},{24,16},{28,20},{1,9},{5... | collective-permute-start | bytes 245768 | tf_op jit(solution)/shard_map/ppermute | solution.py:72
  87.5 7.3 %collective-permute-done.20.refs_2_ = bf16[128,320]{1,0:T(8,128)(2,1)S(1)} collective-permute-done((bf16[128,320]{1,0:T(8,128)(2,1)}, bf16[128,320]{1,0:T(8,128)(2,1)S(1)}, u32[]{:S(2)}, u32[]{:S(2)}) %collective-permute-start.20) | collective-permute-done | bytes 81952 | tf_op jit(solution)/shard_map/ppermute | solution.py:72
  95.7 2.1 %shard_map.163 = (bf16[112,384]{1,0:T(8,128)(2,1)}, bf16[112,384]{1,0:T(8,128)(2,1)}, bf16[112,384]{1,0:T(8,128)(2,1)}, bf16[112,384]{1,0:T(8,128)(2,1)}) custom-call(s32[2]{0:T(128)} %pad_add_fusion.me, bf16[4,112,384]{2,1,0:T(8,128)(2,1)} %get-tuple-element.74.keep, bf16[4,112,384]{2,1,0:T(8,128)(2,1)} %copy-done.17, ...), custom_call_target="tpu_custom_call" | custom-call | tf_op jit(solution)/shard_map/pallas_call | solution.py:659
  107.3 2.9 %collective-permute-start.25 = (bf16[2,1,56,384]{3,2,1,0:T(8,128)(2,1)}, bf16[2,1,56,384]{3,2,1,0:T(8,128)(2,1)S(1)}, u32[]{:S(2)}, u32[]{:S(2)}) collective-permute-start(bf16[2,1,56,384]{3,2,1,0:T(8,128)(2,1)} %bitcast.37), channel_id=1, source_target_pairs={{0,16},{4,20},{8,24},{12,28},{16,0},{20,4},{24,8},{28,12},{1,17},{... | collective-permute-start | bytes 258056 | tf_op jit(solution)/shard_map/ppermute | solution.py:72
  110.2 2.7 %collective-permute-done.25 = bf16[2,1,56,384]{3,2,1,0:T(8,128)(2,1)S(1)} collective-permute-done((bf16[2,1,56,384]{3,2,1,0:T(8,128)(2,1)}, bf16[2,1,56,384]{3,2,1,0:T(8,128)(2,1)S(1)}, u32[]{:S(2)}, u32[]{:S(2)}) %collective-permute-start.25) | collective-permute-done | bytes 86048 | tf_op jit(solution)/shard_map/ppermute | solution.py:72
  113.8 1.9 %collective-permute-start.26 = (bf16[2,2,56,384]{3,2,1,0:T(8,128)(2,1)S(1)}, bf16[2,2,56,384]{3,2,1,0:T(8,128)(2,1)S(1)}, u32[]{:S(2)}, u32[]{:S(2)}) collective-permute-start(bf16[2,2,56,384]{3,2,1,0:T(8,128)(2,1)S(1)} %pad_maximum_fusion.6), channel_id=1, source_target_pairs={{0,8},{4,12},{8,0},{12,4},{16,24},{20,28},{24,16},{28,20},{1,9},{5... | collective-permute-start | bytes 516104 | tf_op jit(solution)/shard_map/ppermute | solution.py:72
  115.8 3.5 %collective-permute-done.26 = bf16[2,2,56,384]{3,2,1,0:T(8,128)(2,1)S(1)} collective-permute-done((bf16[2,2,56,384]{3,2,1,0:T(8,128)(2,1)S(1)}, bf16[2,2,56,384]{3,2,1,0:T(8,128)(2,1)S(1)}, u32[]{:S(2)}, u32[]{:S(2)}) %collective-permute-start.26) | collective-permute-done | bytes 172064 | tf_op jit(solution)/shard_map/ppermute | solution.py:72
  127.5 2.0 %collective-permute-start.15 = (bf16[384,1024]{1,0:T(8,128)(2,1)S(1)}, bf16[384,1024]{1,0:T(8,128)(2,1)S(1)}, u32[]{:S(2)}, u32[]{:S(2)}) collective-permute-start(bf16[384,1024]{1,0:T(8,128)(2,1)S(1)} %copy-done), channel_id=1, source_target_pairs={{0,4},{4,0},{8,12},{12,8},{16,20},{20,16},{24,28},{28,24},{1,5},{5... | collective-permute-start | bytes 2359304 | tf_op jit(solution)/shard_map/ppermute | solution.py:72
  134.9 8.5 %collective-permute-done.13.refs_3_ = bf16[6,2,16,320]{3,2,1,0:T(8,128)(2,1)S(1)} collective-permute-done((bf16[6,2,16,320]{3,2,1,0:T(8,128)(2,1)S(1)}, bf16[6,2,16,320]{3,2,1,0:T(8,128)(2,1)S(1)}, u32[]{:S(2)}, u32[]{:S(2)}) %collective-permute-start.13) | collective-permute-done | bytes 122912 | tf_op jit(solution)/shard_map/ppermute | solution.py:72
  148.1 4.5 %shard_map.158 = (bf16[2,2,320,128]{3,2,1,0:T(8,128)(2,1)}, f32[2,2,320,128]{3,2,1,0:T(8,128)}) custom-call(s32[2]{0:T(128)} %pad_add_fusion.me, bf16[2,2,320,128]{3,2,1,0:T(8,128)(2,1)} %bitcast.30, bf16[2,2,320,128]{3,2,1,0:T(8,128)(2,1)} %bitcast.34, bf16[2,320,128]{2,1,0:T(8,128)(2,1)} %copy-done.20, bf16[2,320,128]{2,1,0:T(8,128)(2,1)} %copy-done.21, ...), custom_call_target="tpu_custom_call" | custom-call | tf_op jit(solution)/shard_map/pallas_call | solution.py:690
  153.5 4.7 %shard_map.159 = (f32[960,1280]{1,0:T(8,128)}, f32[320,1280]{1,0:T(8,128)}) custom-call(bf16[384,1280]{1,0:T(8,128)(2,1)} %get-tuple-element.61.refs_9_.refs_10_.refs_11_.down, bf16[384,1024]{1,0:T(8,128)(2,1)} %get-tuple-element.70.mix_a, bf16[384,1024]{1,0:T(8,128)(2,1)} %copy-done.1, bf16[320,320]{1,0:T(8,128)(2,1)} %get-tuple-element.71.refs_0_, ...), custom_call_target="tpu_custom_call" | custom-call | tf_op jit(solution)/shard_map/pallas_call | solution.py:704
  158.2 4.7 %shard_map.160 = f32[960,1280]{1,0:T(8,128)} custom-call(bf16[384,1280]{1,0:T(8,128)(2,1)} %get-tuple-element.61.refs_9_.refs_10_.refs_11_.down, bf16[384,1024]{1,0:T(8,128)(2,1)} %get-tuple-element.70.mix_a, bf16[384,1024]{1,0:T(8,128)(2,1)} %copy-done.1, f32[960,1280]{1,0:T(8,128)} %get-tuple-element.72.refs_0_), custom_call_target="tpu_custom_call", output_to_operand_aliasing={{}: (3, {})} | custom-call | tf_op jit(solution)/shard_map/pallas_call | solution.py:722
  164.0 5.3 %shard_map.165 = (f32[30,32,320]{2,1,0:T(8,128)}, f32[320,1280]{1,0:T(8,128)}, f32[320,1280]{1,0:T(8,128)}, f32[320,1280]{1,0:T(8,128)}) custom-call(s32[2]{0:T(128)} %pad_add_fusion.me, f32[320,128]{1,0:T(8,128)} %get-tuple-element.88.embed, bf16[2,4,56,384]{3,2,1,0:T(8,128)(2,1)} %copy-done.5, bf16[2,4,56,384]{3,2,1,0:T(8,128)(2,1)} %copy-done.12, ...), custom_call_target="tpu_custom_call" | custom-call | tf_op jit(solution)/shard_map/pallas_call | solution.py:751
  (147 shorter events, 53.6 us)
Async XLA Ops:
  5.3 10.3 %collective-permute-start.5 = (bf16[2,6,8,640]{3,2,1,0:T(8,128)(2,1)S(1)}, bf16[2,6,8,640]{3,2,1,0:T(8,128)(2,1)S(1)}, u32[]{:S(2)}, u32[]{:S(2)}) collective-permute-start(bf16[2,6,8,640]{3,2,1,0:T(8,128)(2,1)S(1)} %pad_maximum_fusion.7), channel_id=1, source_target_pairs={{0,16},{4,20},{8,24},{12,28},{16,0},{20,4},{24,8},{28,12},{1,17},{... | collective-permute-start | bytes 368648 | tf_op jit(solution)/shard_map/ppermute | solution.py:72
  16.4 7.5 %collective-permute-start.6 = (bf16[2,12,8,640]{3,2,1,0:T(8,128)(2,1)S(1)}, bf16[2,12,8,640]{3,2,1,0:T(8,128)(2,1)S(1)}, u32[]{:S(2)}, u32[]{:S(2)}) collective-permute-start(bf16[2,12,8,640]{3,2,1,0:T(8,128)(2,1)S(1)} %pad_maximum_fusion.5), channel_id=1, source_target_pairs={{0,8},{4,12},{8,0},{12,4},{16,24},{20,28},{24,16},{28,20},{1,9},{5... | collective-permute-start | bytes 737288 | tf_op jit(solution)/shard_map/ppermute | solution.py:72
  24.0 6.7 %collective-permute-start.7 = (bf16[1,24,8,640]{3,2,1,0:T(8,128)(2,1)S(1)}, bf16[1,24,8,640]{3,2,1,0:T(8,128)(2,1)S(1)}, u32[]{:S(2)}, u32[]{:S(2)}) collective-permute-start(bf16[1,24,8,640]{3,2,1,0:T(8,128)(2,1)S(1)} %get-tuple-element.97), channel_id=1, source_target_pairs={{0,1},{1,0},{2,3},{3,2},{4,5},{5,4},{6,7},{7,6},{8,9},{9,8},{10,11... | collective-permute-start | bytes 737288 | tf_op jit(solution)/shard_map/ppermute | solution.py:72
  25.3 6.5 %collective-permute-start.9 = (bf16[1,24,8,640]{3,2,1,0:T(8,128)(2,1)S(1)}, bf16[1,24,8,640]{3,2,1,0:T(8,128)(2,1)S(1)}, u32[]{:S(2)}, u32[]{:S(2)}) collective-permute-start(bf16[1,24,8,640]{3,2,1,0:T(8,128)(2,1)S(1)} %get-tuple-element.96), channel_id=1, source_target_pairs={{0,2},{1,3},{2,0},{3,1},{4,6},{5,7},{6,4},{7,5},{8,10},{9,11},{10,... | collective-permute-start | bytes 737288 | tf_op jit(solution)/shard_map/ppermute | solution.py:72
  30.7 25.5 %collective-permute-start.8 = (bf16[2,24,8,640]{3,2,1,0:T(8,128)(2,1)S(1)}, bf16[2,24,8,640]{3,2,1,0:T(8,128)(2,1)S(1)}, u32[]{:S(2)}, u32[]{:S(2)}) collective-permute-start(bf16[2,24,8,640]{3,2,1,0:T(8,128)(2,1)S(1)} %pad_maximum_fusion.first_a), channel_id=1, source_target_pairs={{0,2},{1,3},{2,0},{3,1},{4,6},{5,7},{6,4},{7,5},{8,10},{9,11},{10,... | collective-permute-start | bytes 1474568 | tf_op jit(solution)/shard_map/ppermute | solution.py:72
  31.9 24.4 %collective-permute-start.10 = (bf16[2,24,8,640]{3,2,1,0:T(8,128)(2,1)S(1)}, bf16[2,24,8,640]{3,2,1,0:T(8,128)(2,1)S(1)}, u32[]{:S(2)}, u32[]{:S(2)}) collective-permute-start(bf16[2,24,8,640]{3,2,1,0:T(8,128)(2,1)S(1)} %pad_maximum_fusion.1.second_a), channel_id=1, source_target_pairs={{0,1},{1,0},{2,3},{3,2},{4,5},{5,4},{6,7},{7,6},{8,9},{9,8},{10,11... | collective-permute-start | bytes 1474568 | tf_op jit(solution)/shard_map/ppermute | solution.py:72
  45.9 32.8 %collective-permute-start.18 = (bf16[4,128,320]{2,1,0:T(8,128)(2,1)}, bf16[4,128,320]{2,1,0:T(8,128)(2,1)S(1)}, u32[]{:S(2)}, u32[]{:S(2)}) collective-permute-start(bf16[4,128,320]{2,1,0:T(8,128)(2,1)} %get-tuple-element.77), channel_id=1, source_target_pairs={{0,4},{4,0},{8,12},{12,8},{16,20},{20,16},{24,28},{28,24},{1,5},{5... | collective-permute-start | bytes 983048 | tf_op jit(solution)/shard_map/ppermute | solution.py:72
  78.6 16.2 %collective-permute-start.17 = (bf16[4,112,384]{2,1,0:T(8,128)(2,1)}, bf16[4,112,384]{2,1,0:T(8,128)(2,1)S(1)}, u32[]{:S(2)}, u32[]{:S(2)}) collective-permute-start(bf16[4,112,384]{2,1,0:T(8,128)(2,1)} %get-tuple-element.75), channel_id=1, source_target_pairs={{0,4},{4,0},{8,12},{12,8},{16,20},{20,16},{24,28},{28,24},{1,5},{5... | collective-permute-start | bytes 1032200 | tf_op jit(solution)/shard_map/ppermute | solution.py:72
  83.9 11.0 %collective-permute-start.20 = (bf16[128,320]{1,0:T(8,128)(2,1)}, bf16[128,320]{1,0:T(8,128)(2,1)S(1)}, u32[]{:S(2)}, u32[]{:S(2)}) collective-permute-start(bf16[128,320]{1,0:T(8,128)(2,1)} %get-tuple-element.80), channel_id=1, source_target_pairs={{0,16},{4,20},{8,24},{12,28},{16,0},{20,4},{24,8},{28,12},{1,17},{... | collective-permute-start | bytes 245768 | tf_op jit(solution)/shard_map/ppermute | solution.py:72
  85.1 9.8 %collective-permute-start.21 = (bf16[128,320]{1,0:T(8,128)(2,1)}, bf16[128,320]{1,0:T(8,128)(2,1)S(1)}, u32[]{:S(2)}, u32[]{:S(2)}) collective-permute-start(bf16[128,320]{1,0:T(8,128)(2,1)} %get-tuple-element.81), channel_id=1, source_target_pairs={{0,24},{4,28},{8,16},{12,20},{16,8},{20,12},{24,0},{28,4},{1,25},{... | collective-permute-start | bytes 245768 | tf_op jit(solution)/shard_map/ppermute | solution.py:72
  120.3 7.2 %collective-permute-start.27 = (bf16[1,4,56,384]{3,2,1,0:T(8,128)(2,1)S(1)}, bf16[1,4,56,384]{3,2,1,0:T(8,128)(2,1)S(1)}, u32[]{:S(2)}, u32[]{:S(2)}) collective-permute-start(bf16[1,4,56,384]{3,2,1,0:T(8,128)(2,1)S(1)} %get-tuple-element.99), channel_id=1, source_target_pairs={{0,2},{1,3},{2,0},{3,1},{4,6},{5,7},{6,4},{7,5},{8,10},{9,11},{10,... | collective-permute-start | bytes 516104 | tf_op jit(solution)/shard_map/ppermute | solution.py:72
  121.3 8.3 %collective-permute-start.30 = (bf16[1,4,56,384]{3,2,1,0:T(8,128)(2,1)S(1)}, bf16[1,4,56,384]{3,2,1,0:T(8,128)(2,1)S(1)}, u32[]{:S(2)}, u32[]{:S(2)}) collective-permute-start(bf16[1,4,56,384]{3,2,1,0:T(8,128)(2,1)S(1)} %get-tuple-element.98), channel_id=1, source_target_pairs={{0,1},{1,0},{2,3},{3,2},{4,5},{5,4},{6,7},{7,6},{8,9},{9,8},{10,11... | collective-permute-start | bytes 516104 | tf_op jit(solution)/shard_map/ppermute | solution.py:72
  124.5 6.2 %collective-permute-start = (bf16[2,320,128]{2,1,0:T(8,128)(2,1)}, bf16[2,320,128]{2,1,0:T(8,128)(2,1)S(1)}, u32[]{:S(2)}, u32[]{:S(2)}) collective-permute-start(bf16[2,320,128]{2,1,0:T(8,128)(2,1)} %get-tuple-element.53), channel_id=1, source_target_pairs={{0,4},{4,8},{8,12},{12,16},{16,20},{20,24},{24,28},{1,5},{5,9},{9,... | collective-permute-start | bytes 491528 | tf_op jit(solution)/shard_map/ppermute | solution.py:541
  125.8 6.4 %collective-permute-start.11 = (bf16[6,2,16,320]{3,2,1,0:T(8,128)(2,1)S(1)}, bf16[6,2,16,320]{3,2,1,0:T(8,128)(2,1)S(1)}, u32[]{:S(2)}, u32[]{:S(2)}) collective-permute-start(bf16[6,2,16,320]{3,2,1,0:T(8,128)(2,1)S(1)} %copy-done.34), channel_id=1, source_target_pairs={{0,1},{1,0},{2,3},{3,2},{4,5},{5,4},{6,7},{7,6},{8,9},{9,8},{10,11... | collective-permute-start | bytes 368648 | tf_op jit(solution)/shard_map/ppermute | solution.py:72
  126.4 7.0 %collective-permute-start.12 = (bf16[6,2,16,320]{3,2,1,0:T(8,128)(2,1)S(1)}, bf16[6,2,16,320]{3,2,1,0:T(8,128)(2,1)S(1)}, u32[]{:S(2)}, u32[]{:S(2)}) collective-permute-start(bf16[6,2,16,320]{3,2,1,0:T(8,128)(2,1)S(1)} %copy-done.33), channel_id=1, source_target_pairs={{0,2},{1,3},{2,0},{3,1},{4,6},{5,7},{6,4},{7,5},{8,10},{9,11},{10,... | collective-permute-start | bytes 368648 | tf_op jit(solution)/shard_map/ppermute | solution.py:72
  127.5 25.1 %collective-permute-start.15 = (bf16[384,1024]{1,0:T(8,128)(2,1)S(1)}, bf16[384,1024]{1,0:T(8,128)(2,1)S(1)}, u32[]{:S(2)}, u32[]{:S(2)}) collective-permute-start(bf16[384,1024]{1,0:T(8,128)(2,1)S(1)} %copy-done), channel_id=1, source_target_pairs={{0,4},{4,0},{8,12},{12,8},{16,20},{20,16},{24,28},{28,24},{1,5},{5... | collective-permute-start | bytes 2359304 | tf_op jit(solution)/shard_map/ppermute | solution.py:72
  129.6 16.3 %collective-permute-start.28 = (bf16[2,4,56,384]{3,2,1,0:T(8,128)(2,1)S(1)}, bf16[2,4,56,384]{3,2,1,0:T(8,128)(2,1)S(1)}, u32[]{:S(2)}, u32[]{:S(2)}) collective-permute-start(bf16[2,4,56,384]{3,2,1,0:T(8,128)(2,1)S(1)} %pad_maximum_fusion.3.refs_2_), channel_id=1, source_target_pairs={{0,1},{1,0},{2,3},{3,2},{4,5},{5,4},{6,7},{7,6},{8,9},{9,8},{10,11... | collective-permute-start | bytes 1032200 | tf_op jit(solution)/shard_map/ppermute | solution.py:72
  130.8 17.2 %collective-permute-start.31 = (bf16[2,4,56,384]{3,2,1,0:T(8,128)(2,1)S(1)}, bf16[2,4,56,384]{3,2,1,0:T(8,128)(2,1)S(1)}, u32[]{:S(2)}, u32[]{:S(2)}) collective-permute-start(bf16[2,4,56,384]{3,2,1,0:T(8,128)(2,1)S(1)} %pad_maximum_fusion.4.refs_0_), channel_id=1, source_target_pairs={{0,2},{1,3},{2,0},{3,1},{4,6},{5,7},{6,4},{7,5},{8,10},{9,11},{10,... | collective-permute-start | bytes 1032200 | tf_op jit(solution)/shard_map/ppermute | solution.py:72
  132.3 11.0 %collective-permute-start.13 = (bf16[6,2,16,320]{3,2,1,0:T(8,128)(2,1)S(1)}, bf16[6,2,16,320]{3,2,1,0:T(8,128)(2,1)S(1)}, u32[]{:S(2)}, u32[]{:S(2)}) collective-permute-start(bf16[6,2,16,320]{3,2,1,0:T(8,128)(2,1)S(1)} %copy-done.32), channel_id=1, source_target_pairs={{0,3},{1,2},{2,1},{3,0},{4,7},{5,6},{6,5},{7,4},{8,11},{9,10},{10,... | collective-permute-start | bytes 368648 | tf_op jit(solution)/shard_map/ppermute | solution.py:72
  133.4 12.5 %collective-permute-start.1 = (bf16[2,320,128]{2,1,0:T(8,128)(2,1)}, bf16[2,320,128]{2,1,0:T(8,128)(2,1)S(1)}, u32[]{:S(2)}, u32[]{:S(2)}) collective-permute-start(bf16[2,320,128]{2,1,0:T(8,128)(2,1)} %get-tuple-element.54), channel_id=1, source_target_pairs={{4,0},{8,4},{12,8},{16,12},{20,16},{24,20},{28,24},{5,1},{9,5},{13... | collective-permute-start | bytes 491528 | tf_op jit(solution)/shard_map/ppermute | solution.py:542
  146.0 17.0 %collective-permute-start.29 = (bf16[2,4,56,384]{3,2,1,0:T(8,128)(2,1)S(1)}, bf16[2,4,56,384]{3,2,1,0:T(8,128)(2,1)S(1)}, u32[]{:S(2)}, u32[]{:S(2)}) collective-permute-start(bf16[2,4,56,384]{3,2,1,0:T(8,128)(2,1)S(1)} %collective-permute-done.28.refs_3_), channel_id=1, source_target_pairs={{0,4},{4,0},{8,12},{12,8},{16,20},{20,16},{24,28},{28,24},{1,5},{5... | collective-permute-start | bytes 1032200 | tf_op jit(solution)/shard_map/ppermute | solution.py:72
  147.4 15.5 %collective-permute-start.32 = (bf16[2,4,56,384]{3,2,1,0:T(8,128)(2,1)S(1)}, bf16[2,4,56,384]{3,2,1,0:T(8,128)(2,1)S(1)}, u32[]{:S(2)}, u32[]{:S(2)}) collective-permute-start(bf16[2,4,56,384]{3,2,1,0:T(8,128)(2,1)S(1)} %pad_maximum_fusion.4.refs_0_), channel_id=1, source_target_pairs={{0,4},{4,0},{8,12},{12,8},{16,20},{20,16},{24,28},{28,24},{1,5},{5... | collective-permute-start | bytes 1032200 | tf_op jit(solution)/shard_map/ppermute | solution.py:72
  147.6 15.4 %collective-permute-start.34 = (bf16[2,4,56,384]{3,2,1,0:T(8,128)(2,1)S(1)}, bf16[2,4,56,384]{3,2,1,0:T(8,128)(2,1)S(1)}, u32[]{:S(2)}, u32[]{:S(2)}) collective-permute-start(bf16[2,4,56,384]{3,2,1,0:T(8,128)(2,1)S(1)} %pad_maximum_fusion.3.refs_2_), channel_id=1, source_target_pairs={{0,4},{4,0},{8,12},{12,8},{16,20},{20,16},{24,28},{28,24},{1,5},{5... | collective-permute-start | bytes 1032200 | tf_op jit(solution)/shard_map/ppermute | solution.py:72
  148.0 15.0 %collective-permute-start.33 = (bf16[2,4,56,384]{3,2,1,0:T(8,128)(2,1)S(1)}, bf16[2,4,56,384]{3,2,1,0:T(8,128)(2,1)S(1)}, u32[]{:S(2)}, u32[]{:S(2)}) collective-permute-start(bf16[2,4,56,384]{3,2,1,0:T(8,128)(2,1)S(1)} %collective-permute-done.31.refs_1_), channel_id=1, source_target_pairs={{0,4},{4,0},{8,12},{12,8},{16,20},{20,16},{24,28},{28,24},{1,5},{5... | collective-permute-start | bytes 1032200 | tf_op jit(solution)/shard_map/ppermute | solution.py:72
  (46 other events, 385.5 us)

commit v8 on v7

--- a/solution.py
+++ b/solution.py
@@ -148,7 +148,8 @@
     direct[...] = nt(full, up).astype(BF)
 
 
-def fine_kernel(me, clip, cot, lo, hi, keep, send, wide, here, taps):
+def fine_kernel(me, clip, cot, lo, hi, *refs):
+    outs, (wide, here, taps) = refs[:-3], refs[-3:]
     chans, columns = clip.shape[2], clip.shape[3]
     cells = 2 * columns
     for t in range(4):
@@ -160,17 +161,22 @@
     taps[3 * chans :, :] = jnp.zeros((taps.shape[0] - 3 * chans, chans), F32)
     for tap in range(3):
         taps[tap * chans : (tap + 1) * chans, :] = nt(here[...], wide[:, (2 - tap) * cells : (4 - tap) * cells])
-    core = me[0] & 1
-    share = keep.shape[1]
-    for z in range(keep.shape[0]):
-        keep[z] = taps[pl.ds(pl.multiple_of((2 * z + core) * share, share), share), :].astype(BF)
-        send[z] = taps[pl.ds(pl.multiple_of((2 * z + 1 - core) * share, share), share), :].astype(BF)
-
-
-def tap_kernel(me, keep, got, *outs):
+    pair = outs[0].shape[0]
     for d, out in enumerate(outs):
         at = (me[0] >> 1) ^ d
-        out[...] = (keep[at].astype(F32) + got[at].astype(F32)).astype(BF)
+        out[...] = taps[pl.ds(pl.multiple_of(at * pair, pair), pair), :].astype(BF)
+
+
+def tap_kernel(me, *refs):
+    parts, (keep, send) = refs[:-2], refs[-2:]
+    share = keep.shape[0]
+    core = me[0] & 1
+    for dest, which in ((keep, core), (send, 1 - core)):
+        rows = pl.ds(pl.multiple_of(which * share, share), share)
+        acc = parts[0][rows, :].astype(F32)
+        for ref in parts[1:]:
+            acc = acc + ref[rows, :].astype(F32)
+        dest[...] = acc.astype(BF)
 
 
 def coarse_kernel(
@@ -545,11 +551,11 @@
     cot_lo, cot_hi = halo(cot_t, keep)
     clip_lo, clip_hi = halo(clip_t, keep)
     tap_rows = round_up(3 * chans, devices * 8)
-    tap_keep, tap_send = call(
+    tap_parts = call(
         fine_kernel,
-        [sds((chips, tap_rows // nf, chans), BF)] * 2,
+        [sds((2 * tap_rows // nf, chans), BF)] * chips,
         in_specs=[smem()] + [vmem()] * 4,
-        out_specs=[vmem()] * 2,
+        out_specs=[vmem()] * chips,
         scratch_shapes=[
             pltpu.VMEM((chans, 8 * columns), BF),
             pltpu.VMEM((chans, 4 * columns), BF),
@@ -557,16 +563,16 @@
         ],
     )(me, clip_t, cot_t, cot_lo, cot_hi)
     share = tap_rows // nf
-    tap_got = swap(tap_send, "frames", 1)
-    tap_parts = call(
+    tap_got = [tap_parts[0]]
+    for d in range(1, chips):
+        tap_got.append(swap(tap_parts[d], "frames", 2 * d))
+    tap_keep, tap_send = call(
         tap_kernel,
-        [sds((share, chans), BF)] * chips,
-        in_specs=[smem(), vmem(), vmem()],
-        out_specs=[vmem()] * chips,
-    )(me, tap_keep, tap_got)
-    taps = [tap_parts[0]]
-    for d in range(1, chips):
-        taps.append(swap(tap_parts[d], "frames", 2 * d))
+        [sds((share, chans), BF)] * 2,
+        in_specs=[smem()] + [vmem()] * chips,
+        out_specs=[vmem()] * 2,
+    )(me, *tap_got)
+    taps = (tap_keep, swap(tap_send, "frames", 1))
 
     chip_rows = 2 * width // nf
     r1 = width // devices
@@ -657,9 +663,9 @@
 
     d_got = swap(d_send, "frames", 1)
     ordered = call(
-        functools.partial(order_kernel, at=2 * p1, taps=chips),
+        functools.partial(order_kernel, at=2 * p1, taps=2),
         [sds((piece_rows, padded), BF)] * nh,
-        in_specs=[smem()] + [vmem()] * (2 + chips),
+        in_specs=[smem()] + [vmem()] * 4,
         out_specs=[vmem()] * nh,
     )(me, d_keep, d_got, *taps)
     got = []

time: 170 us -> 177 us (1.041)
  waiting for transfers between devices: 48.3 us -> 53.1 us
  starting transfers between devices: 44.3 us -> 46.3 us
    ppermute x31, waiting for transfers between devices: 45.1 us -> 53.1 us  [swap(): return lax.ppermute(x, axis, [(i, i ^ bit) for i in range(n)])]
    ppermute x2, waiting for transfers between devices: 3.22 us -> 0.01 us  [halo(): hi = lax.ppermute(head, 'frames', [(i + 1, i) for i in range(nf - 1)])]
    ppermute x31, starting transfers between devices: 39 us -> 41 us  [swap(): return lax.ppermute(x, axis, [(i, i ^ bit) for i in range(n)])]
  transfers between devices with their start and end apart: 35 -> 35, of which waited for: 14 -> 14; matrix products, arithmetic and copies ran while one was open for 1% -> 1% of each run, Pallas kernels for 30% -> 29%
where the time goes in v8:
time: 177 us
  Pallas kernels  62.4 us (35%)
  waiting for transfers between devices  53.1 us (30%)
  starting transfers between devices  46.3 us (26%)
  local copies, waits for them, and re-layouts  7.97 us (5%)
  other arithmetic  5.05 us (3%)
  between operations  1.81 us (1%)
    ppermute x31, waiting for transfers between devices, swap(): return lax.ppermute(x, axis, [(i, i ^ bit) for i in range(n)])  53.1 us
    ppermute x31, starting transfers between devices, swap(): return lax.ppermute(x, axis, [(i, i ^ bit) for i in range(n)])  41 us
    pallas_call x1, Pallas kernels, body(): call(functools.partial(coarse_kernel, coarse_frames=nf, heads_axis=nh, re...  21.4 us
    unnamed x73, local copies, waits for them, and re-layouts  7.86 us
    pallas_call x1, Pallas kernels, body(): call(weight_kernel, [sds((padded, width), BF), sds((padded, pieces * SLOT...  5.77 us
    pallas_call x1, Pallas kernels, body(): call(functools.partial(gather_kernel, layout=layout, aligned=aligned), ou...  5.31 us
    pallas_call x1, Pallas kernels, body(): call(functools.partial(split_grad_kernel, late=True), wide, grid=(width /...  4.72 us
    pallas_call x1, Pallas kernels, body(): call(functools.partial(split_grad_kernel, late=False), [wide, sds((heads...  4.71 us
  transfers between devices with their start and end apart: 35, of which 14 were waited for; matrix products, arithmetic and copies ran while one was open for 1% of the time, Pallas kernels for 29%

profile of v8, /device:TPU:0, one launch (start us, length us, event | category | flops | bytes accessed | tf_op | source)
XLA Modules:
  0.0 176.6 jit_solution(15063939326066927509)
XLA Ops:
  0.6 2.2 %shard_map.152 = (bf16[2,3,8,640]{3,2,1,0:T(8,128)(2,1)}, bf16[2,3,8,640]{3,2,1,0:T(8,128)(2,1)}) custom-call(s32[1]{0:T(128)} %bitcast.me, bf16[2,2,320,128]{3,2,1,0:T(8,128)(2,1)} %bitcast.27, bf16[2,2,320,128]{3,2,1,0:T(8,128)(2,1)} %bitcast.31), custom_call_target="tpu_custom_call" | custom-call | tf_op jit(solution)/shard_map/pallas_call | solution.py:516
  5.3 4.0 %collective-permute-start.5 = (bf16[2,6,8,640]{3,2,1,0:T(8,128)(2,1)S(1)}, bf16[2,6,8,640]{3,2,1,0:T(8,128)(2,1)S(1)}, u32[]{:S(2)}, u32[]{:S(2)}) collective-permute-start(bf16[2,6,8,640]{3,2,1,0:T(8,128)(2,1)S(1)} %pad_maximum_fusion.7), channel_id=1, source_target_pairs={{0,16},{4,20},{8,24},{12,28},{16,0},{20,4},{24,8},{28,12},{1,17},{... | collective-permute-start | bytes 368648 | tf_op jit(solution)/shard_map/ppermute | solution.py:72
  9.2 6.3 %collective-permute-done.5 = bf16[2,6,8,640]{3,2,1,0:T(8,128)(2,1)S(1)} collective-permute-done((bf16[2,6,8,640]{3,2,1,0:T(8,128)(2,1)S(1)}, bf16[2,6,8,640]{3,2,1,0:T(8,128)(2,1)S(1)}, u32[]{:S(2)}, u32[]{:S(2)}) %collective-permute-start.5) | collective-permute-done | bytes 122912 | tf_op jit(solution)/shard_map/ppermute | solution.py:72
  18.1 5.8 %collective-permute-done.6 = bf16[2,12,8,640]{3,2,1,0:T(8,128)(2,1)S(1)} collective-permute-done((bf16[2,12,8,640]{3,2,1,0:T(8,128)(2,1)S(1)}, bf16[2,12,8,640]{3,2,1,0:T(8,128)(2,1)S(1)}, u32[]{:S(2)}, u32[]{:S(2)}) %collective-permute-start.6) | collective-permute-done | bytes 245792 | tf_op jit(solution)/shard_map/ppermute | solution.py:72
  26.8 3.8 %collective-permute-done.7 = bf16[1,24,8,640]{3,2,1,0:T(8,128)(2,1)S(1)} collective-permute-done((bf16[1,24,8,640]{3,2,1,0:T(8,128)(2,1)S(1)}, bf16[1,24,8,640]{3,2,1,0:T(8,128)(2,1)S(1)}, u32[]{:S(2)}, u32[]{:S(2)}) %collective-permute-start.7) | collective-permute-done | bytes 245792 | tf_op jit(solution)/shard_map/ppermute | solution.py:72
  39.1 5.8 %shard_map.155 = (bf16[384,1280]{1,0:T(8,128)(2,1)}, bf16[384,1536]{1,0:T(8,128)(2,1)}, bf16[512,320]{1,0:T(8,128)(2,1)}, bf16[384,320]{1,0:T(8,128)(2,1)}, f32[320,128]{1,0:T(8,128)}) custom-call(bf16[320,1280]{1,0:T(8,128)(2,1)} %w_down.1, bf16[320,1280]{1,0:T(8,128)(2,1)} %w_embed.1, bf16[1,320]{1,0:T(2,128)(2,1)} %fusion.embed, ...), custom_call_target="tpu_custom_call" | custom-call | tf_op jit(solution)/shard_map/pallas_call | solution.py:529
  46.4 21.4 %shard_map.156 = (bf16[6,2,16,320]{3,2,1,0:T(8,128)(2,1)}, bf16[6,2,16,320]{3,2,1,0:T(8,128)(2,1)}, bf16[6,2,16,320]{3,2,1,0:T(8,128)(2,1)}, bf16[6,2,16,320]{3,...) custom-call(s32[2]{0:T(128)} %pad_add_fusion.me, ...), custom_call_target="tpu_custom_call" | custom-call | tf_op jit(solution)/shard_map/pallas_call | solution.py:656
  67.9 3.5 %collective-permute-start.17 = (bf16[4,112,384]{2,1,0:T(8,128)(2,1)}, bf16[4,112,384]{2,1,0:T(8,128)(2,1)S(1)}, u32[]{:S(2)}, u32[]{:S(2)}) collective-permute-start(bf16[4,112,384]{2,1,0:T(8,128)(2,1)} %get-tuple-element.75), channel_id=1, source_target_pairs={{0,4},{4,0},{8,12},{12,8},{16,20},{20,16},{24,28},{28,24},{1,5},{5... | collective-permute-start | bytes 1032200 | tf_op jit(solution)/shard_map/ppermute | solution.py:72
  72.7 2.8 %shard_map.161 = (bf16[256,320]{1,0:T(8,128)(2,1)}, bf16[256,320]{1,0:T(8,128)(2,1)}, bf16[256,320]{1,0:T(8,128)(2,1)}, bf16[256,320]{1,0:T(8,128)(2,1)}) custom-call(s32[2]{0:T(128)} %pad_add_fusion.me, bf16[2,2,320,128]{3,2,1,0:T(8,128)(2,1)} %bitcast.28, bf16[2,2,320,128]{3,2,1,0:T(8,128)(2,1)} %bitcast.33, bf16[2,320,128]{2,1,0:T(8,128)(2,1)} %copy-done.6, ...), custom_call_target="tpu_custom_call" | custom-call | tf_op jit(solution)/shard_map/pallas_call | solution.py:554
  75.5 2.5 %collective-permute-start.18 = (bf16[256,320]{1,0:T(8,128)(2,1)}, bf16[256,320]{1,0:T(8,128)(2,1)S(1)}, u32[]{:S(2)}, u32[]{:S(2)}) collective-permute-start(bf16[256,320]{1,0:T(8,128)(2,1)} %get-tuple-element.77), channel_id=1, source_target_pairs={{0,8},{4,12},{8,0},{12,4},{16,24},{20,28},{24,16},{28,20},{1,9},{5... | collective-permute-start | bytes 491528 | tf_op jit(solution)/shard_map/ppermute | solution.py:72
  78.1 2.5 %collective-permute-start.19 = (bf16[256,320]{1,0:T(8,128)(2,1)}, bf16[256,320]{1,0:T(8,128)(2,1)S(1)}, u32[]{:S(2)}, u32[]{:S(2)}) collective-permute-start(bf16[256,320]{1,0:T(8,128)(2,1)} %get-tuple-element.78), channel_id=1, source_target_pairs={{0,16},{4,20},{8,24},{12,28},{16,0},{20,4},{24,8},{28,12},{1,17},{... | collective-permute-start | bytes 491528 | tf_op jit(solution)/shard_map/ppermute | solution.py:72
  80.6 6.6 %collective-permute-done.18.refs_1_ = bf16[256,320]{1,0:T(8,128)(2,1)S(1)} collective-permute-done((bf16[256,320]{1,0:T(8,128)(2,1)}, bf16[256,320]{1,0:T(8,128)(2,1)S(1)}, u32[]{:S(2)}, u32[]{:S(2)}) %collective-permute-start.18) | collective-permute-done | bytes 163872 | tf_op jit(solution)/shard_map/ppermute | solution.py:72
  87.1 8.3 %collective-permute-done.19.refs_2_ = bf16[256,320]{1,0:T(8,128)(2,1)S(1)} collective-permute-done((bf16[256,320]{1,0:T(8,128)(2,1)}, bf16[256,320]{1,0:T(8,128)(2,1)S(1)}, u32[]{:S(2)}, u32[]{:S(2)}) %collective-permute-start.19) | collective-permute-done | bytes 163872 | tf_op jit(solution)/shard_map/ppermute | solution.py:72
  100.4 2.0 %shard_map.163 = (bf16[112,384]{1,0:T(8,128)(2,1)}, bf16[112,384]{1,0:T(8,128)(2,1)}, bf16[112,384]{1,0:T(8,128)(2,1)}, bf16[112,384]{1,0:T(8,128)(2,1)}) custom-call(s32[2]{0:T(128)} %pad_add_fusion.me, bf16[4,112,384]{2,1,0:T(8,128)(2,1)} %get-tuple-element.74.keep, bf16[4,112,384]{2,1,0:T(8,128)(2,1)} %copy-done.16, ...), custom_call_target="tpu_custom_call" | custom-call | tf_op jit(solution)/shard_map/pallas_call | solution.py:665
  111.9 5.0 %collective-permute-start.25 = (bf16[2,1,56,384]{3,2,1,0:T(8,128)(2,1)}, bf16[2,1,56,384]{3,2,1,0:T(8,128)(2,1)S(1)}, u32[]{:S(2)}, u32[]{:S(2)}) collective-permute-start(bf16[2,1,56,384]{3,2,1,0:T(8,128)(2,1)} %bitcast.37), channel_id=1, source_target_pairs={{0,16},{4,20},{8,24},{12,28},{16,0},{20,4},{24,8},{28,12},{1,17},{... | collective-permute-start | bytes 258056 | tf_op jit(solution)/shard_map/ppermute | solution.py:72
  116.9 2.7 %collective-permute-done.25 = bf16[2,1,56,384]{3,2,1,0:T(8,128)(2,1)S(1)} collective-permute-done((bf16[2,1,56,384]{3,2,1,0:T(8,128)(2,1)}, bf16[2,1,56,384]{3,2,1,0:T(8,128)(2,1)S(1)}, u32[]{:S(2)}, u32[]{:S(2)}) %collective-permute-start.25) | collective-permute-done | bytes 86048 | tf_op jit(solution)/shard_map/ppermute | solution.py:72
  120.5 2.0 %collective-permute-start.26 = (bf16[2,2,56,384]{3,2,1,0:T(8,128)(2,1)S(1)}, bf16[2,2,56,384]{3,2,1,0:T(8,128)(2,1)S(1)}, u32[]{:S(2)}, u32[]{:S(2)}) collective-permute-start(bf16[2,2,56,384]{3,2,1,0:T(8,128)(2,1)S(1)} %pad_maximum_fusion.6), channel_id=1, source_target_pairs={{0,8},{4,12},{8,0},{12,4},{16,24},{20,28},{24,16},{28,20},{1,9},{5... | collective-permute-start | bytes 516104 | tf_op jit(solution)/shard_map/ppermute | solution.py:72
  122.5 3.5 %collective-permute-done.26 = bf16[2,2,56,384]{3,2,1,0:T(8,128)(2,1)S(1)} collective-permute-done((bf16[2,2,56,384]{3,2,1,0:T(8,128)(2,1)S(1)}, bf16[2,2,56,384]{3,2,1,0:T(8,128)(2,1)S(1)}, u32[]{:S(2)}, u32[]{:S(2)}) %collective-permute-start.26) | collective-permute-done | bytes 172064 | tf_op jit(solution)/shard_map/ppermute | solution.py:72
  134.2 2.1 %collective-permute-start.15 = (bf16[384,1024]{1,0:T(8,128)(2,1)S(1)}, bf16[384,1024]{1,0:T(8,128)(2,1)S(1)}, u32[]{:S(2)}, u32[]{:S(2)}) collective-permute-start(bf16[384,1024]{1,0:T(8,128)(2,1)S(1)} %copy-done), channel_id=1, source_target_pairs={{0,4},{4,0},{8,12},{12,8},{16,20},{20,16},{24,28},{28,24},{1,5},{5... | collective-permute-start | bytes 2359304 | tf_op jit(solution)/shard_map/ppermute | solution.py:72
  141.6 8.8 %collective-permute-done.13.refs_3_ = bf16[6,2,16,320]{3,2,1,0:T(8,128)(2,1)S(1)} collective-permute-done((bf16[6,2,16,320]{3,2,1,0:T(8,128)(2,1)S(1)}, bf16[6,2,16,320]{3,2,1,0:T(8,128)(2,1)S(1)}, u32[]{:S(2)}, u32[]{:S(2)}) %collective-permute-start.13) | collective-permute-done | bytes 122912 | tf_op jit(solution)/shard_map/ppermute | solution.py:72
  155.2 4.5 %shard_map.158 = (bf16[2,2,320,128]{3,2,1,0:T(8,128)(2,1)}, f32[2,2,320,128]{3,2,1,0:T(8,128)}) custom-call(s32[2]{0:T(128)} %pad_add_fusion.me, bf16[2,2,320,128]{3,2,1,0:T(8,128)(2,1)} %bitcast.30, bf16[2,2,320,128]{3,2,1,0:T(8,128)(2,1)} %bitcast.34, bf16[2,320,128]{2,1,0:T(8,128)(2,1)} %copy-done.22, bf16[2,320,128]{2,1,0:T(8,128)(2,1)} %copy-done.23, ...), custom_call_target="tpu_custom_call" | custom-call | tf_op jit(solution)/shard_map/pallas_call | solution.py:696
  160.6 4.7 %shard_map.159 = (f32[960,1280]{1,0:T(8,128)}, f32[320,1280]{1,0:T(8,128)}) custom-call(bf16[384,1280]{1,0:T(8,128)(2,1)} %get-tuple-element.61.refs_9_.refs_10_.refs_11_.down, bf16[384,1024]{1,0:T(8,128)(2,1)} %get-tuple-element.70.mix_a, bf16[384,1024]{1,0:T(8,128)(2,1)} %copy-done.1, bf16[320,320]{1,0:T(8,128)(2,1)} %get-tuple-element.71.refs_0_, ...), custom_call_target="tpu_custom_call" | custom-call | tf_op jit(solution)/shard_map/pallas_call | solution.py:710
  165.3 4.7 %shard_map.160 = f32[960,1280]{1,0:T(8,128)} custom-call(bf16[384,1280]{1,0:T(8,128)(2,1)} %get-tuple-element.61.refs_9_.refs_10_.refs_11_.down, bf16[384,1024]{1,0:T(8,128)(2,1)} %get-tuple-element.70.mix_a, bf16[384,1024]{1,0:T(8,128)(2,1)} %copy-done.1, f32[960,1280]{1,0:T(8,128)} %get-tuple-element.72.refs_0_), custom_call_target="tpu_custom_call", output_to_operand_aliasing={{}: (3, {})} | custom-call | tf_op jit(solution)/shard_map/pallas_call | solution.py:728
  171.1 5.3 %shard_map.165 = (f32[30,32,320]{2,1,0:T(8,128)}, f32[320,1280]{1,0:T(8,128)}, f32[320,1280]{1,0:T(8,128)}, f32[320,1280]{1,0:T(8,128)}) custom-call(s32[2]{0:T(128)} %pad_add_fusion.me, f32[320,128]{1,0:T(8,128)} %get-tuple-element.88.embed, bf16[2,4,56,384]{3,2,1,0:T(8,128)(2,1)} %copy-done.5, bf16[2,4,56,384]{3,2,1,0:T(8,128)(2,1)} %copy-done.11, ...), custom_call_target="tpu_custom_call" | custom-call | tf_op jit(solution)/shard_map/pallas_call | solution.py:757
  (147 shorter events, 54.1 us)
Async XLA Ops:
  5.3 10.3 %collective-permute-start.5 = (bf16[2,6,8,640]{3,2,1,0:T(8,128)(2,1)S(1)}, bf16[2,6,8,640]{3,2,1,0:T(8,128)(2,1)S(1)}, u32[]{:S(2)}, u32[]{:S(2)}) collective-permute-start(bf16[2,6,8,640]{3,2,1,0:T(8,128)(2,1)S(1)} %pad_maximum_fusion.7), channel_id=1, source_target_pairs={{0,16},{4,20},{8,24},{12,28},{16,0},{20,4},{24,8},{28,12},{1,17},{... | collective-permute-start | bytes 368648 | tf_op jit(solution)/shard_map/ppermute | solution.py:72
  16.4 7.5 %collective-permute-start.6 = (bf16[2,12,8,640]{3,2,1,0:T(8,128)(2,1)S(1)}, bf16[2,12,8,640]{3,2,1,0:T(8,128)(2,1)S(1)}, u32[]{:S(2)}, u32[]{:S(2)}) collective-permute-start(bf16[2,12,8,640]{3,2,1,0:T(8,128)(2,1)S(1)} %pad_maximum_fusion.5), channel_id=1, source_target_pairs={{0,8},{4,12},{8,0},{12,4},{16,24},{20,28},{24,16},{28,20},{1,9},{5... | collective-permute-start | bytes 737288 | tf_op jit(solution)/shard_map/ppermute | solution.py:72
  24.0 6.7 %collective-permute-start.7 = (bf16[1,24,8,640]{3,2,1,0:T(8,128)(2,1)S(1)}, bf16[1,24,8,640]{3,2,1,0:T(8,128)(2,1)S(1)}, u32[]{:S(2)}, u32[]{:S(2)}) collective-permute-start(bf16[1,24,8,640]{3,2,1,0:T(8,128)(2,1)S(1)} %get-tuple-element.97), channel_id=1, source_target_pairs={{0,1},{1,0},{2,3},{3,2},{4,5},{5,4},{6,7},{7,6},{8,9},{9,8},{10,11... | collective-permute-start | bytes 737288 | tf_op jit(solution)/shard_map/ppermute | solution.py:72
  30.7 14.8 %collective-permute-start.8 = (bf16[2,24,8,640]{3,2,1,0:T(8,128)(2,1)S(1)}, bf16[2,24,8,640]{3,2,1,0:T(8,128)(2,1)S(1)}, u32[]{:S(2)}, u32[]{:S(2)}) collective-permute-start(bf16[2,24,8,640]{3,2,1,0:T(8,128)(2,1)S(1)} %pad_maximum_fusion.first_a), channel_id=1, source_target_pairs={{0,2},{1,3},{2,0},{3,1},{4,6},{5,7},{6,4},{7,5},{8,10},{9,11},{10,... | collective-permute-start | bytes 1474568 | tf_op jit(solution)/shard_map/ppermute | solution.py:72
  31.9 13.6 %collective-permute-start.10 = (bf16[2,24,8,640]{3,2,1,0:T(8,128)(2,1)S(1)}, bf16[2,24,8,640]{3,2,1,0:T(8,128)(2,1)S(1)}, u32[]{:S(2)}, u32[]{:S(2)}) collective-permute-start(bf16[2,24,8,640]{3,2,1,0:T(8,128)(2,1)S(1)} %pad_maximum_fusion.1.second_a), channel_id=1, source_target_pairs={{0,1},{1,0},{2,3},{3,2},{4,5},{5,4},{6,7},{7,6},{8,9},{9,8},{10,11... | collective-permute-start | bytes 1474568 | tf_op jit(solution)/shard_map/ppermute | solution.py:72
  35.1 36.3 %collective-permute-start.2 = (bf16[2,320,128]{2,1,0:T(8,128)(2,1)}, bf16[2,320,128]{2,1,0:T(8,128)(2,1)S(1)}, u32[]{:S(2)}, u32[]{:S(2)}) collective-permute-start(bf16[2,320,128]{2,1,0:T(8,128)(2,1)} %get-tuple-element.55), channel_id=1, source_target_pairs={{0,4},{4,8},{8,12},{12,16},{16,20},{20,24},{24,28},{1,5},{5,9},{9,... | collective-permute-start | bytes 491528 | tf_op jit(solution)/shard_map/ppermute | solution.py:547
  36.4 35.0 %collective-permute-start.3 = (bf16[2,320,128]{2,1,0:T(8,128)(2,1)}, bf16[2,320,128]{2,1,0:T(8,128)(2,1)S(1)}, u32[]{:S(2)}, u32[]{:S(2)}) collective-permute-start(bf16[2,320,128]{2,1,0:T(8,128)(2,1)} %get-tuple-element.56), channel_id=1, source_target_pairs={{4,0},{8,4},{12,8},{16,12},{20,16},{24,20},{28,24},{5,1},{9,5},{13... | collective-permute-start | bytes 491528 | tf_op jit(solution)/shard_map/ppermute | solution.py:548
  67.9 31.8 %collective-permute-start.17 = (bf16[4,112,384]{2,1,0:T(8,128)(2,1)}, bf16[4,112,384]{2,1,0:T(8,128)(2,1)S(1)}, u32[]{:S(2)}, u32[]{:S(2)}) collective-permute-start(bf16[4,112,384]{2,1,0:T(8,128)(2,1)} %get-tuple-element.75), channel_id=1, source_target_pairs={{0,4},{4,0},{8,12},{12,8},{16,20},{20,16},{24,28},{28,24},{1,5},{5... | collective-permute-start | bytes 1032200 | tf_op jit(solution)/shard_map/ppermute | solution.py:72
  75.5 11.6 %collective-permute-start.18 = (bf16[256,320]{1,0:T(8,128)(2,1)}, bf16[256,320]{1,0:T(8,128)(2,1)S(1)}, u32[]{:S(2)}, u32[]{:S(2)}) collective-permute-start(bf16[256,320]{1,0:T(8,128)(2,1)} %get-tuple-element.77), channel_id=1, source_target_pairs={{0,8},{4,12},{8,0},{12,4},{16,24},{20,28},{24,16},{28,20},{1,9},{5... | collective-permute-start | bytes 491528 | tf_op jit(solution)/shard_map/ppermute | solution.py:72
  78.1 17.4 %collective-permute-start.19 = (bf16[256,320]{1,0:T(8,128)(2,1)}, bf16[256,320]{1,0:T(8,128)(2,1)S(1)}, u32[]{:S(2)}, u32[]{:S(2)}) collective-permute-start(bf16[256,320]{1,0:T(8,128)(2,1)} %get-tuple-element.78), channel_id=1, source_target_pairs={{0,16},{4,20},{8,24},{12,28},{16,0},{20,4},{24,8},{28,12},{1,17},{... | collective-permute-start | bytes 491528 | tf_op jit(solution)/shard_map/ppermute | solution.py:72
  80.6 14.8 %collective-permute-start.20 = (bf16[256,320]{1,0:T(8,128)(2,1)}, bf16[256,320]{1,0:T(8,128)(2,1)S(1)}, u32[]{:S(2)}, u32[]{:S(2)}) collective-permute-start(bf16[256,320]{1,0:T(8,128)(2,1)} %get-tuple-element.79), channel_id=1, source_target_pairs={{0,24},{4,28},{8,16},{12,20},{16,8},{20,12},{24,0},{28,4},{1,25},{... | collective-permute-start | bytes 491528 | tf_op jit(solution)/shard_map/ppermute | solution.py:72
  111.9 7.7 %collective-permute-start.25 = (bf16[2,1,56,384]{3,2,1,0:T(8,128)(2,1)}, bf16[2,1,56,384]{3,2,1,0:T(8,128)(2,1)S(1)}, u32[]{:S(2)}, u32[]{:S(2)}) collective-permute-start(bf16[2,1,56,384]{3,2,1,0:T(8,128)(2,1)} %bitcast.37), channel_id=1, source_target_pairs={{0,16},{4,20},{8,24},{12,28},{16,0},{20,4},{24,8},{28,12},{1,17},{... | collective-permute-start | bytes 258056 | tf_op jit(solution)/shard_map/ppermute | solution.py:72
  127.0 7.2 %collective-permute-start.27 = (bf16[1,4,56,384]{3,2,1,0:T(8,128)(2,1)S(1)}, bf16[1,4,56,384]{3,2,1,0:T(8,128)(2,1)S(1)}, u32[]{:S(2)}, u32[]{:S(2)}) collective-permute-start(bf16[1,4,56,384]{3,2,1,0:T(8,128)(2,1)S(1)} %get-tuple-element.99), channel_id=1, source_target_pairs={{0,2},{1,3},{2,0},{3,1},{4,6},{5,7},{6,4},{7,5},{8,10},{9,11},{10,... | collective-permute-start | bytes 516104 | tf_op jit(solution)/shard_map/ppermute | solution.py:72
  128.1 8.2 %collective-permute-start.30 = (bf16[1,4,56,384]{3,2,1,0:T(8,128)(2,1)S(1)}, bf16[1,4,56,384]{3,2,1,0:T(8,128)(2,1)S(1)}, u32[]{:S(2)}, u32[]{:S(2)}) collective-permute-start(bf16[1,4,56,384]{3,2,1,0:T(8,128)(2,1)S(1)} %get-tuple-element.98), channel_id=1, source_target_pairs={{0,1},{1,0},{2,3},{3,2},{4,5},{5,4},{6,7},{7,6},{8,9},{9,8},{10,11... | collective-permute-start | bytes 516104 | tf_op jit(solution)/shard_map/ppermute | solution.py:72
  133.2 6.9 %collective-permute-start.12 = (bf16[6,2,16,320]{3,2,1,0:T(8,128)(2,1)S(1)}, bf16[6,2,16,320]{3,2,1,0:T(8,128)(2,1)S(1)}, u32[]{:S(2)}, u32[]{:S(2)}) collective-permute-start(bf16[6,2,16,320]{3,2,1,0:T(8,128)(2,1)S(1)} %copy-done.33), channel_id=1, source_target_pairs={{0,2},{1,3},{2,0},{3,1},{4,6},{5,7},{6,4},{7,5},{8,10},{9,11},{10,... | collective-permute-start | bytes 368648 | tf_op jit(solution)/shard_map/ppermute | solution.py:72
  134.2 25.5 %collective-permute-start.15 = (bf16[384,1024]{1,0:T(8,128)(2,1)S(1)}, bf16[384,1024]{1,0:T(8,128)(2,1)S(1)}, u32[]{:S(2)}, u32[]{:S(2)}) collective-permute-start(bf16[384,1024]{1,0:T(8,128)(2,1)S(1)} %copy-done), channel_id=1, source_target_pairs={{0,4},{4,0},{8,12},{12,8},{16,20},{20,16},{24,28},{28,24},{1,5},{5... | collective-permute-start | bytes 2359304 | tf_op jit(solution)/shard_map/ppermute | solution.py:72
  136.3 16.7 %collective-permute-start.28 = (bf16[2,4,56,384]{3,2,1,0:T(8,128)(2,1)S(1)}, bf16[2,4,56,384]{3,2,1,0:T(8,128)(2,1)S(1)}, u32[]{:S(2)}, u32[]{:S(2)}) collective-permute-start(bf16[2,4,56,384]{3,2,1,0:T(8,128)(2,1)S(1)} %pad_maximum_fusion.3.refs_2_), channel_id=1, source_target_pairs={{0,1},{1,0},{2,3},{3,2},{4,5},{5,4},{6,7},{7,6},{8,9},{9,8},{10,11... | collective-permute-start | bytes 1032200 | tf_op jit(solution)/shard_map/ppermute | solution.py:72
  137.7 17.3 %collective-permute-start.31 = (bf16[2,4,56,384]{3,2,1,0:T(8,128)(2,1)S(1)}, bf16[2,4,56,384]{3,2,1,0:T(8,128)(2,1)S(1)}, u32[]{:S(2)}, u32[]{:S(2)}) collective-permute-start(bf16[2,4,56,384]{3,2,1,0:T(8,128)(2,1)S(1)} %pad_maximum_fusion.4.refs_0_), channel_id=1, source_target_pairs={{0,2},{1,3},{2,0},{3,1},{4,6},{5,7},{6,4},{7,5},{8,10},{9,11},{10,... | collective-permute-start | bytes 1032200 | tf_op jit(solution)/shard_map/ppermute | solution.py:72
  138.9 11.5 %collective-permute-start.13 = (bf16[6,2,16,320]{3,2,1,0:T(8,128)(2,1)S(1)}, bf16[6,2,16,320]{3,2,1,0:T(8,128)(2,1)S(1)}, u32[]{:S(2)}, u32[]{:S(2)}) collective-permute-start(bf16[6,2,16,320]{3,2,1,0:T(8,128)(2,1)S(1)} %copy-done.32), channel_id=1, source_target_pairs={{0,3},{1,2},{2,1},{3,0},{4,7},{5,6},{6,5},{7,4},{8,11},{9,10},{10,... | collective-permute-start | bytes 368648 | tf_op jit(solution)/shard_map/ppermute | solution.py:72
  140.1 12.8 %collective-permute-start.1 = (bf16[2,320,128]{2,1,0:T(8,128)(2,1)}, bf16[2,320,128]{2,1,0:T(8,128)(2,1)S(1)}, u32[]{:S(2)}, u32[]{:S(2)}) collective-permute-start(bf16[2,320,128]{2,1,0:T(8,128)(2,1)} %get-tuple-element.54), channel_id=1, source_target_pairs={{4,0},{8,4},{12,8},{16,12},{20,16},{24,20},{28,24},{5,1},{9,5},{13... | collective-permute-start | bytes 491528 | tf_op jit(solution)/shard_map/ppermute | solution.py:548
  153.0 17.0 %collective-permute-start.29 = (bf16[2,4,56,384]{3,2,1,0:T(8,128)(2,1)S(1)}, bf16[2,4,56,384]{3,2,1,0:T(8,128)(2,1)S(1)}, u32[]{:S(2)}, u32[]{:S(2)}) collective-permute-start(bf16[2,4,56,384]{3,2,1,0:T(8,128)(2,1)S(1)} %collective-permute-done.28.refs_3_), channel_id=1, source_target_pairs={{0,4},{4,0},{8,12},{12,8},{16,20},{20,16},{24,28},{28,24},{1,5},{5... | collective-permute-start | bytes 1032200 | tf_op jit(solution)/shard_map/ppermute | solution.py:72
  154.5 15.5 %collective-permute-start.32 = (bf16[2,4,56,384]{3,2,1,0:T(8,128)(2,1)S(1)}, bf16[2,4,56,384]{3,2,1,0:T(8,128)(2,1)S(1)}, u32[]{:S(2)}, u32[]{:S(2)}) collective-permute-start(bf16[2,4,56,384]{3,2,1,0:T(8,128)(2,1)S(1)} %pad_maximum_fusion.4.refs_0_), channel_id=1, source_target_pairs={{0,4},{4,0},{8,12},{12,8},{16,20},{20,16},{24,28},{28,24},{1,5},{5... | collective-permute-start | bytes 1032200 | tf_op jit(solution)/shard_map/ppermute | solution.py:72
  154.7 15.4 %collective-permute-start.34 = (bf16[2,4,56,384]{3,2,1,0:T(8,128)(2,1)S(1)}, bf16[2,4,56,384]{3,2,1,0:T(8,128)(2,1)S(1)}, u32[]{:S(2)}, u32[]{:S(2)}) collective-permute-start(bf16[2,4,56,384]{3,2,1,0:T(8,128)(2,1)S(1)} %pad_maximum_fusion.3.refs_2_), channel_id=1, source_target_pairs={{0,4},{4,0},{8,12},{12,8},{16,20},{20,16},{24,28},{28,24},{1,5},{5... | collective-permute-start | bytes 1032200 | tf_op jit(solution)/shard_map/ppermute | solution.py:72
  155.0 15.0 %collective-permute-start.33 = (bf16[2,4,56,384]{3,2,1,0:T(8,128)(2,1)S(1)}, bf16[2,4,56,384]{3,2,1,0:T(8,128)(2,1)S(1)}, u32[]{:S(2)}, u32[]{:S(2)}) collective-permute-start(bf16[2,4,56,384]{3,2,1,0:T(8,128)(2,1)S(1)} %collective-permute-done.31.refs_1_), channel_id=1, source_target_pairs={{0,4},{4,0},{8,12},{12,8},{16,20},{20,16},{24,28},{28,24},{1,5},{5... | collective-permute-start | bytes 1032200 | tf_op jit(solution)/shard_map/ppermute | solution.py:72
  (46 other events, 368.0 us)

commit v9 on v8

--- a/solution.py
+++ b/solution.py
@@ -654,9 +654,7 @@
     )
     rest = (p1, r3, piece_rows, panes, shift)
     results = call(
-        functools.partial(coarse_kernel, coarse_frames=nf, heads_axis=nh, rest=rest),
-        outs,
-        grid_spec=grid_spec,
+        functools.partial(coarse_kernel, coarse_frames=nf, heads_axis=nh, rest=rest), outs, grid_spec=grid_spec
     )(me, *sides, *statics, *[x for x in cells for _ in range(panes)])
     local = results[:nh]
     mix_g, att_g, d_keep, d_send = results[nh:]

time: 177 us -> 177 us (level)
  no operation moved by 1% of the time
where the time goes in v9:
time: 177 us
  Pallas kernels  62.4 us (35%)
  waiting for transfers between devices  53.1 us (30%)
  starting transfers between devices  46.3 us (26%)
  local copies, waits for them, and re-layouts  7.97 us (5%)
  other arithmetic  5.05 us (3%)
  between operations  1.81 us (1%)
    ppermute x31, waiting for transfers between devices, swap(): return lax.ppermute(x, axis, [(i, i ^ bit) for i in range(n)])  53.1 us
    ppermute x31, starting transfers between devices, swap(): return lax.ppermute(x, axis, [(i, i ^ bit) for i in range(n)])  41 us
    pallas_call x1, Pallas kernels, body(): call(functools.partial(coarse_kernel, coarse_frames=nf, heads_axis=nh, re...  21.4 us
    unnamed x73, local copies, waits for them, and re-layouts  7.86 us
    pallas_call x1, Pallas kernels, body(): call(weight_kernel, [sds((padded, width), BF), sds((padded, pieces * SLOT...  5.77 us
    pallas_call x1, Pallas kernels, body(): call(functools.partial(gather_kernel, layout=layout, aligned=aligned), ou...  5.31 us
    pallas_call x1, Pallas kernels, body(): call(functools.partial(split_grad_kernel, late=True), wide, grid=(width /...  4.72 us
    pallas_call x1, Pallas kernels, body(): call(functools.partial(split_grad_kernel, late=False), [wide, sds((heads...  4.71 us
  transfers between devices with their start and end apart: 35, of which 14 were waited for; matrix products, arithmetic and copies ran while one was open for 1% of the time, Pallas kernels for 29%

profile of v9, /device:TPU:0, one launch (start us, length us, event | category | flops | bytes accessed | tf_op | source)
XLA Modules:
  0.0 176.6 jit_solution(15063939326066927509)
XLA Ops:
  0.6 2.2 %shard_map.152 = (bf16[2,3,8,640]{3,2,1,0:T(8,128)(2,1)}, bf16[2,3,8,640]{3,2,1,0:T(8,128)(2,1)}) custom-call(s32[1]{0:T(128)} %bitcast.me, bf16[2,2,320,128]{3,2,1,0:T(8,128)(2,1)} %bitcast.27, bf16[2,2,320,128]{3,2,1,0:T(8,128)(2,1)} %bitcast.31), custom_call_target="tpu_custom_call" | custom-call | tf_op jit(solution)/shard_map/pallas_call | solution.py:516
  5.3 4.0 %collective-permute-start.5 = (bf16[2,6,8,640]{3,2,1,0:T(8,128)(2,1)S(1)}, bf16[2,6,8,640]{3,2,1,0:T(8,128)(2,1)S(1)}, u32[]{:S(2)}, u32[]{:S(2)}) collective-permute-start(bf16[2,6,8,640]{3,2,1,0:T(8,128)(2,1)S(1)} %pad_maximum_fusion.7), channel_id=1, source_target_pairs={{0,16},{4,20},{8,24},{12,28},{16,0},{20,4},{24,8},{28,12},{1,17},{... | collective-permute-start | bytes 368648 | tf_op jit(solution)/shard_map/ppermute | solution.py:72
  9.2 6.3 %collective-permute-done.5 = bf16[2,6,8,640]{3,2,1,0:T(8,128)(2,1)S(1)} collective-permute-done((bf16[2,6,8,640]{3,2,1,0:T(8,128)(2,1)S(1)}, bf16[2,6,8,640]{3,2,1,0:T(8,128)(2,1)S(1)}, u32[]{:S(2)}, u32[]{:S(2)}) %collective-permute-start.5) | collective-permute-done | bytes 122912 | tf_op jit(solution)/shard_map/ppermute | solution.py:72
  18.1 5.8 %collective-permute-done.6 = bf16[2,12,8,640]{3,2,1,0:T(8,128)(2,1)S(1)} collective-permute-done((bf16[2,12,8,640]{3,2,1,0:T(8,128)(2,1)S(1)}, bf16[2,12,8,640]{3,2,1,0:T(8,128)(2,1)S(1)}, u32[]{:S(2)}, u32[]{:S(2)}) %collective-permute-start.6) | collective-permute-done | bytes 245792 | tf_op jit(solution)/shard_map/ppermute | solution.py:72
  26.8 3.8 %collective-permute-done.7 = bf16[1,24,8,640]{3,2,1,0:T(8,128)(2,1)S(1)} collective-permute-done((bf16[1,24,8,640]{3,2,1,0:T(8,128)(2,1)S(1)}, bf16[1,24,8,640]{3,2,1,0:T(8,128)(2,1)S(1)}, u32[]{:S(2)}, u32[]{:S(2)}) %collective-permute-start.7) | collective-permute-done | bytes 245792 | tf_op jit(solution)/shard_map/ppermute | solution.py:72
  39.1 5.8 %shard_map.155 = (bf16[384,1280]{1,0:T(8,128)(2,1)}, bf16[384,1536]{1,0:T(8,128)(2,1)}, bf16[512,320]{1,0:T(8,128)(2,1)}, bf16[384,320]{1,0:T(8,128)(2,1)}, f32[320,128]{1,0:T(8,128)}) custom-call(bf16[320,1280]{1,0:T(8,128)(2,1)} %w_down.1, bf16[320,1280]{1,0:T(8,128)(2,1)} %w_embed.1, bf16[1,320]{1,0:T(2,128)(2,1)} %fusion.embed, ...), custom_call_target="tpu_custom_call" | custom-call | tf_op jit(solution)/shard_map/pallas_call | solution.py:529
  46.4 21.4 %shard_map.156 = (bf16[6,2,16,320]{3,2,1,0:T(8,128)(2,1)}, bf16[6,2,16,320]{3,2,1,0:T(8,128)(2,1)}, bf16[6,2,16,320]{3,2,1,0:T(8,128)(2,1)}, bf16[6,2,16,320]{3,...) custom-call(s32[2]{0:T(128)} %pad_add_fusion.me, ...), custom_call_target="tpu_custom_call" | custom-call | tf_op jit(solution)/shard_map/pallas_call | solution.py:656
  67.9 3.5 %collective-permute-start.17 = (bf16[4,112,384]{2,1,0:T(8,128)(2,1)}, bf16[4,112,384]{2,1,0:T(8,128)(2,1)S(1)}, u32[]{:S(2)}, u32[]{:S(2)}) collective-permute-start(bf16[4,112,384]{2,1,0:T(8,128)(2,1)} %get-tuple-element.75), channel_id=1, source_target_pairs={{0,4},{4,0},{8,12},{12,8},{16,20},{20,16},{24,28},{28,24},{1,5},{5... | collective-permute-start | bytes 1032200 | tf_op jit(solution)/shard_map/ppermute | solution.py:72
  72.7 2.8 %shard_map.161 = (bf16[256,320]{1,0:T(8,128)(2,1)}, bf16[256,320]{1,0:T(8,128)(2,1)}, bf16[256,320]{1,0:T(8,128)(2,1)}, bf16[256,320]{1,0:T(8,128)(2,1)}) custom-call(s32[2]{0:T(128)} %pad_add_fusion.me, bf16[2,2,320,128]{3,2,1,0:T(8,128)(2,1)} %bitcast.28, bf16[2,2,320,128]{3,2,1,0:T(8,128)(2,1)} %bitcast.33, bf16[2,320,128]{2,1,0:T(8,128)(2,1)} %copy-done.6, ...), custom_call_target="tpu_custom_call" | custom-call | tf_op jit(solution)/shard_map/pallas_call | solution.py:554
  75.5 2.5 %collective-permute-start.18 = (bf16[256,320]{1,0:T(8,128)(2,1)}, bf16[256,320]{1,0:T(8,128)(2,1)S(1)}, u32[]{:S(2)}, u32[]{:S(2)}) collective-permute-start(bf16[256,320]{1,0:T(8,128)(2,1)} %get-tuple-element.77), channel_id=1, source_target_pairs={{0,8},{4,12},{8,0},{12,4},{16,24},{20,28},{24,16},{28,20},{1,9},{5... | collective-permute-start | bytes 491528 | tf_op jit(solution)/shard_map/ppermute | solution.py:72
  78.1 2.5 %collective-permute-start.19 = (bf16[256,320]{1,0:T(8,128)(2,1)}, bf16[256,320]{1,0:T(8,128)(2,1)S(1)}, u32[]{:S(2)}, u32[]{:S(2)}) collective-permute-start(bf16[256,320]{1,0:T(8,128)(2,1)} %get-tuple-element.78), channel_id=1, source_target_pairs={{0,16},{4,20},{8,24},{12,28},{16,0},{20,4},{24,8},{28,12},{1,17},{... | collective-permute-start | bytes 491528 | tf_op jit(solution)/shard_map/ppermute | solution.py:72
  80.6 6.6 %collective-permute-done.18.refs_1_ = bf16[256,320]{1,0:T(8,128)(2,1)S(1)} collective-permute-done((bf16[256,320]{1,0:T(8,128)(2,1)}, bf16[256,320]{1,0:T(8,128)(2,1)S(1)}, u32[]{:S(2)}, u32[]{:S(2)}) %collective-permute-start.18) | collective-permute-done | bytes 163872 | tf_op jit(solution)/shard_map/ppermute | solution.py:72
  87.1 8.3 %collective-permute-done.19.refs_2_ = bf16[256,320]{1,0:T(8,128)(2,1)S(1)} collective-permute-done((bf16[256,320]{1,0:T(8,128)(2,1)}, bf16[256,320]{1,0:T(8,128)(2,1)S(1)}, u32[]{:S(2)}, u32[]{:S(2)}) %collective-permute-start.19) | collective-permute-done | bytes 163872 | tf_op jit(solution)/shard_map/ppermute | solution.py:72
  100.4 2.0 %shard_map.163 = (bf16[112,384]{1,0:T(8,128)(2,1)}, bf16[112,384]{1,0:T(8,128)(2,1)}, bf16[112,384]{1,0:T(8,128)(2,1)}, bf16[112,384]{1,0:T(8,128)(2,1)}) custom-call(s32[2]{0:T(128)} %pad_add_fusion.me, bf16[4,112,384]{2,1,0:T(8,128)(2,1)} %get-tuple-element.74.keep, bf16[4,112,384]{2,1,0:T(8,128)(2,1)} %copy-done.16, ...), custom_call_target="tpu_custom_call" | custom-call | tf_op jit(solution)/shard_map/pallas_call | solution.py:663
  111.9 5.0 %collective-permute-start.25 = (bf16[2,1,56,384]{3,2,1,0:T(8,128)(2,1)}, bf16[2,1,56,384]{3,2,1,0:T(8,128)(2,1)S(1)}, u32[]{:S(2)}, u32[]{:S(2)}) collective-permute-start(bf16[2,1,56,384]{3,2,1,0:T(8,128)(2,1)} %bitcast.37), channel_id=1, source_target_pairs={{0,16},{4,20},{8,24},{12,28},{16,0},{20,4},{24,8},{28,12},{1,17},{... | collective-permute-start | bytes 258056 | tf_op jit(solution)/shard_map/ppermute | solution.py:72
  116.9 2.7 %collective-permute-done.25 = bf16[2,1,56,384]{3,2,1,0:T(8,128)(2,1)S(1)} collective-permute-done((bf16[2,1,56,384]{3,2,1,0:T(8,128)(2,1)}, bf16[2,1,56,384]{3,2,1,0:T(8,128)(2,1)S(1)}, u32[]{:S(2)}, u32[]{:S(2)}) %collective-permute-start.25) | collective-permute-done | bytes 86048 | tf_op jit(solution)/shard_map/ppermute | solution.py:72
  120.5 2.0 %collective-permute-start.26 = (bf16[2,2,56,384]{3,2,1,0:T(8,128)(2,1)S(1)}, bf16[2,2,56,384]{3,2,1,0:T(8,128)(2,1)S(1)}, u32[]{:S(2)}, u32[]{:S(2)}) collective-permute-start(bf16[2,2,56,384]{3,2,1,0:T(8,128)(2,1)S(1)} %pad_maximum_fusion.6), channel_id=1, source_target_pairs={{0,8},{4,12},{8,0},{12,4},{16,24},{20,28},{24,16},{28,20},{1,9},{5... | collective-permute-start | bytes 516104 | tf_op jit(solution)/shard_map/ppermute | solution.py:72
  122.5 3.5 %collective-permute-done.26 = bf16[2,2,56,384]{3,2,1,0:T(8,128)(2,1)S(1)} collective-permute-done((bf16[2,2,56,384]{3,2,1,0:T(8,128)(2,1)S(1)}, bf16[2,2,56,384]{3,2,1,0:T(8,128)(2,1)S(1)}, u32[]{:S(2)}, u32[]{:S(2)}) %collective-permute-start.26) | collective-permute-done | bytes 172064 | tf_op jit(solution)/shard_map/ppermute | solution.py:72
  134.2 2.1 %collective-permute-start.15 = (bf16[384,1024]{1,0:T(8,128)(2,1)S(1)}, bf16[384,1024]{1,0:T(8,128)(2,1)S(1)}, u32[]{:S(2)}, u32[]{:S(2)}) collective-permute-start(bf16[384,1024]{1,0:T(8,128)(2,1)S(1)} %copy-done), channel_id=1, source_target_pairs={{0,4},{4,0},{8,12},{12,8},{16,20},{20,16},{24,28},{28,24},{1,5},{5... | collective-permute-start | bytes 2359304 | tf_op jit(solution)/shard_map/ppermute | solution.py:72
  141.6 8.8 %collective-permute-done.13.refs_3_ = bf16[6,2,16,320]{3,2,1,0:T(8,128)(2,1)S(1)} collective-permute-done((bf16[6,2,16,320]{3,2,1,0:T(8,128)(2,1)S(1)}, bf16[6,2,16,320]{3,2,1,0:T(8,128)(2,1)S(1)}, u32[]{:S(2)}, u32[]{:S(2)}) %collective-permute-start.13) | collective-permute-done | bytes 122912 | tf_op jit(solution)/shard_map/ppermute | solution.py:72
  155.2 4.5 %shard_map.158 = (bf16[2,2,320,128]{3,2,1,0:T(8,128)(2,1)}, f32[2,2,320,128]{3,2,1,0:T(8,128)}) custom-call(s32[2]{0:T(128)} %pad_add_fusion.me, bf16[2,2,320,128]{3,2,1,0:T(8,128)(2,1)} %bitcast.30, bf16[2,2,320,128]{3,2,1,0:T(8,128)(2,1)} %bitcast.34, bf16[2,320,128]{2,1,0:T(8,128)(2,1)} %copy-done.22, bf16[2,320,128]{2,1,0:T(8,128)(2,1)} %copy-done.23, ...), custom_call_target="tpu_custom_call" | custom-call | tf_op jit(solution)/shard_map/pallas_call | solution.py:694
  160.6 4.7 %shard_map.159 = (f32[960,1280]{1,0:T(8,128)}, f32[320,1280]{1,0:T(8,128)}) custom-call(bf16[384,1280]{1,0:T(8,128)(2,1)} %get-tuple-element.61.refs_9_.refs_10_.refs_11_.down, bf16[384,1024]{1,0:T(8,128)(2,1)} %get-tuple-element.70.mix_a, bf16[384,1024]{1,0:T(8,128)(2,1)} %copy-done.1, bf16[320,320]{1,0:T(8,128)(2,1)} %get-tuple-element.71.refs_0_, ...), custom_call_target="tpu_custom_call" | custom-call | tf_op jit(solution)/shard_map/pallas_call | solution.py:708
  165.3 4.7 %shard_map.160 = f32[960,1280]{1,0:T(8,128)} custom-call(bf16[384,1280]{1,0:T(8,128)(2,1)} %get-tuple-element.61.refs_9_.refs_10_.refs_11_.down, bf16[384,1024]{1,0:T(8,128)(2,1)} %get-tuple-element.70.mix_a, bf16[384,1024]{1,0:T(8,128)(2,1)} %copy-done.1, f32[960,1280]{1,0:T(8,128)} %get-tuple-element.72.refs_0_), custom_call_target="tpu_custom_call", output_to_operand_aliasing={{}: (3, {})} | custom-call | tf_op jit(solution)/shard_map/pallas_call | solution.py:726
  171.1 5.3 %shard_map.165 = (f32[30,32,320]{2,1,0:T(8,128)}, f32[320,1280]{1,0:T(8,128)}, f32[320,1280]{1,0:T(8,128)}, f32[320,1280]{1,0:T(8,128)}) custom-call(s32[2]{0:T(128)} %pad_add_fusion.me, f32[320,128]{1,0:T(8,128)} %get-tuple-element.88.embed, bf16[2,4,56,384]{3,2,1,0:T(8,128)(2,1)} %copy-done.5, bf16[2,4,56,384]{3,2,1,0:T(8,128)(2,1)} %copy-done.11, ...), custom_call_target="tpu_custom_call" | custom-call | tf_op jit(solution)/shard_map/pallas_call | solution.py:755
  (147 shorter events, 54.1 us)
Async XLA Ops:
  5.3 10.3 %collective-permute-start.5 = (bf16[2,6,8,640]{3,2,1,0:T(8,128)(2,1)S(1)}, bf16[2,6,8,640]{3,2,1,0:T(8,128)(2,1)S(1)}, u32[]{:S(2)}, u32[]{:S(2)}) collective-permute-start(bf16[2,6,8,640]{3,2,1,0:T(8,128)(2,1)S(1)} %pad_maximum_fusion.7), channel_id=1, source_target_pairs={{0,16},{4,20},{8,24},{12,28},{16,0},{20,4},{24,8},{28,12},{1,17},{... | collective-permute-start | bytes 368648 | tf_op jit(solution)/shard_map/ppermute | solution.py:72
  16.4 7.5 %collective-permute-start.6 = (bf16[2,12,8,640]{3,2,1,0:T(8,128)(2,1)S(1)}, bf16[2,12,8,640]{3,2,1,0:T(8,128)(2,1)S(1)}, u32[]{:S(2)}, u32[]{:S(2)}) collective-permute-start(bf16[2,12,8,640]{3,2,1,0:T(8,128)(2,1)S(1)} %pad_maximum_fusion.5), channel_id=1, source_target_pairs={{0,8},{4,12},{8,0},{12,4},{16,24},{20,28},{24,16},{28,20},{1,9},{5... | collective-permute-start | bytes 737288 | tf_op jit(solution)/shard_map/ppermute | solution.py:72
  24.0 6.7 %collective-permute-start.7 = (bf16[1,24,8,640]{3,2,1,0:T(8,128)(2,1)S(1)}, bf16[1,24,8,640]{3,2,1,0:T(8,128)(2,1)S(1)}, u32[]{:S(2)}, u32[]{:S(2)}) collective-permute-start(bf16[1,24,8,640]{3,2,1,0:T(8,128)(2,1)S(1)} %get-tuple-element.97), channel_id=1, source_target_pairs={{0,1},{1,0},{2,3},{3,2},{4,5},{5,4},{6,7},{7,6},{8,9},{9,8},{10,11... | collective-permute-start | bytes 737288 | tf_op jit(solution)/shard_map/ppermute | solution.py:72
  30.7 14.8 %collective-permute-start.8 = (bf16[2,24,8,640]{3,2,1,0:T(8,128)(2,1)S(1)}, bf16[2,24,8,640]{3,2,1,0:T(8,128)(2,1)S(1)}, u32[]{:S(2)}, u32[]{:S(2)}) collective-permute-start(bf16[2,24,8,640]{3,2,1,0:T(8,128)(2,1)S(1)} %pad_maximum_fusion.first_a), channel_id=1, source_target_pairs={{0,2},{1,3},{2,0},{3,1},{4,6},{5,7},{6,4},{7,5},{8,10},{9,11},{10,... | collective-permute-start | bytes 1474568 | tf_op jit(solution)/shard_map/ppermute | solution.py:72
  31.9 13.6 %collective-permute-start.10 = (bf16[2,24,8,640]{3,2,1,0:T(8,128)(2,1)S(1)}, bf16[2,24,8,640]{3,2,1,0:T(8,128)(2,1)S(1)}, u32[]{:S(2)}, u32[]{:S(2)}) collective-permute-start(bf16[2,24,8,640]{3,2,1,0:T(8,128)(2,1)S(1)} %pad_maximum_fusion.1.second_a), channel_id=1, source_target_pairs={{0,1},{1,0},{2,3},{3,2},{4,5},{5,4},{6,7},{7,6},{8,9},{9,8},{10,11... | collective-permute-start | bytes 1474568 | tf_op jit(solution)/shard_map/ppermute | solution.py:72
  35.1 36.3 %collective-permute-start.2 = (bf16[2,320,128]{2,1,0:T(8,128)(2,1)}, bf16[2,320,128]{2,1,0:T(8,128)(2,1)S(1)}, u32[]{:S(2)}, u32[]{:S(2)}) collective-permute-start(bf16[2,320,128]{2,1,0:T(8,128)(2,1)} %get-tuple-element.55), channel_id=1, source_target_pairs={{0,4},{4,8},{8,12},{12,16},{16,20},{20,24},{24,28},{1,5},{5,9},{9,... | collective-permute-start | bytes 491528 | tf_op jit(solution)/shard_map/ppermute | solution.py:547
  36.4 35.0 %collective-permute-start.3 = (bf16[2,320,128]{2,1,0:T(8,128)(2,1)}, bf16[2,320,128]{2,1,0:T(8,128)(2,1)S(1)}, u32[]{:S(2)}, u32[]{:S(2)}) collective-permute-start(bf16[2,320,128]{2,1,0:T(8,128)(2,1)} %get-tuple-element.56), channel_id=1, source_target_pairs={{4,0},{8,4},{12,8},{16,12},{20,16},{24,20},{28,24},{5,1},{9,5},{13... | collective-permute-start | bytes 491528 | tf_op jit(solution)/shard_map/ppermute | solution.py:548
  67.9 31.8 %collective-permute-start.17 = (bf16[4,112,384]{2,1,0:T(8,128)(2,1)}, bf16[4,112,384]{2,1,0:T(8,128)(2,1)S(1)}, u32[]{:S(2)}, u32[]{:S(2)}) collective-permute-start(bf16[4,112,384]{2,1,0:T(8,128)(2,1)} %get-tuple-element.75), channel_id=1, source_target_pairs={{0,4},{4,0},{8,12},{12,8},{16,20},{20,16},{24,28},{28,24},{1,5},{5... | collective-permute-start | bytes 1032200 | tf_op jit(solution)/shard_map/ppermute | solution.py:72
  75.5 11.6 %collective-permute-start.18 = (bf16[256,320]{1,0:T(8,128)(2,1)}, bf16[256,320]{1,0:T(8,128)(2,1)S(1)}, u32[]{:S(2)}, u32[]{:S(2)}) collective-permute-start(bf16[256,320]{1,0:T(8,128)(2,1)} %get-tuple-element.77), channel_id=1, source_target_pairs={{0,8},{4,12},{8,0},{12,4},{16,24},{20,28},{24,16},{28,20},{1,9},{5... | collective-permute-start | bytes 491528 | tf_op jit(solution)/shard_map/ppermute | solution.py:72
  78.1 17.4 %collective-permute-start.19 = (bf16[256,320]{1,0:T(8,128)(2,1)}, bf16[256,320]{1,0:T(8,128)(2,1)S(1)}, u32[]{:S(2)}, u32[]{:S(2)}) collective-permute-start(bf16[256,320]{1,0:T(8,128)(2,1)} %get-tuple-element.78), channel_id=1, source_target_pairs={{0,16},{4,20},{8,24},{12,28},{16,0},{20,4},{24,8},{28,12},{1,17},{... | collective-permute-start | bytes 491528 | tf_op jit(solution)/shard_map/ppermute | solution.py:72
  80.6 14.8 %collective-permute-start.20 = (bf16[256,320]{1,0:T(8,128)(2,1)}, bf16[256,320]{1,0:T(8,128)(2,1)S(1)}, u32[]{:S(2)}, u32[]{:S(2)}) collective-permute-start(bf16[256,320]{1,0:T(8,128)(2,1)} %get-tuple-element.79), channel_id=1, source_target_pairs={{0,24},{4,28},{8,16},{12,20},{16,8},{20,12},{24,0},{28,4},{1,25},{... | collective-permute-start | bytes 491528 | tf_op jit(solution)/shard_map/ppermute | solution.py:72
  111.9 7.7 %collective-permute-start.25 = (bf16[2,1,56,384]{3,2,1,0:T(8,128)(2,1)}, bf16[2,1,56,384]{3,2,1,0:T(8,128)(2,1)S(1)}, u32[]{:S(2)}, u32[]{:S(2)}) collective-permute-start(bf16[2,1,56,384]{3,2,1,0:T(8,128)(2,1)} %bitcast.37), channel_id=1, source_target_pairs={{0,16},{4,20},{8,24},{12,28},{16,0},{20,4},{24,8},{28,12},{1,17},{... | collective-permute-start | bytes 258056 | tf_op jit(solution)/shard_map/ppermute | solution.py:72
  127.0 7.2 %collective-permute-start.27 = (bf16[1,4,56,384]{3,2,1,0:T(8,128)(2,1)S(1)}, bf16[1,4,56,384]{3,2,1,0:T(8,128)(2,1)S(1)}, u32[]{:S(2)}, u32[]{:S(2)}) collective-permute-start(bf16[1,4,56,384]{3,2,1,0:T(8,128)(2,1)S(1)} %get-tuple-element.99), channel_id=1, source_target_pairs={{0,2},{1,3},{2,0},{3,1},{4,6},{5,7},{6,4},{7,5},{8,10},{9,11},{10,... | collective-permute-start | bytes 516104 | tf_op jit(solution)/shard_map/ppermute | solution.py:72
  128.1 8.2 %collective-permute-start.30 = (bf16[1,4,56,384]{3,2,1,0:T(8,128)(2,1)S(1)}, bf16[1,4,56,384]{3,2,1,0:T(8,128)(2,1)S(1)}, u32[]{:S(2)}, u32[]{:S(2)}) collective-permute-start(bf16[1,4,56,384]{3,2,1,0:T(8,128)(2,1)S(1)} %get-tuple-element.98), channel_id=1, source_target_pairs={{0,1},{1,0},{2,3},{3,2},{4,5},{5,4},{6,7},{7,6},{8,9},{9,8},{10,11... | collective-permute-start | bytes 516104 | tf_op jit(solution)/shard_map/ppermute | solution.py:72
  133.2 6.9 %collective-permute-start.12 = (bf16[6,2,16,320]{3,2,1,0:T(8,128)(2,1)S(1)}, bf16[6,2,16,320]{3,2,1,0:T(8,128)(2,1)S(1)}, u32[]{:S(2)}, u32[]{:S(2)}) collective-permute-start(bf16[6,2,16,320]{3,2,1,0:T(8,128)(2,1)S(1)} %copy-done.33), channel_id=1, source_target_pairs={{0,2},{1,3},{2,0},{3,1},{4,6},{5,7},{6,4},{7,5},{8,10},{9,11},{10,... | collective-permute-start | bytes 368648 | tf_op jit(solution)/shard_map/ppermute | solution.py:72
  134.2 25.5 %collective-permute-start.15 = (bf16[384,1024]{1,0:T(8,128)(2,1)S(1)}, bf16[384,1024]{1,0:T(8,128)(2,1)S(1)}, u32[]{:S(2)}, u32[]{:S(2)}) collective-permute-start(bf16[384,1024]{1,0:T(8,128)(2,1)S(1)} %copy-done), channel_id=1, source_target_pairs={{0,4},{4,0},{8,12},{12,8},{16,20},{20,16},{24,28},{28,24},{1,5},{5... | collective-permute-start | bytes 2359304 | tf_op jit(solution)/shard_map/ppermute | solution.py:72
  136.3 16.7 %collective-permute-start.28 = (bf16[2,4,56,384]{3,2,1,0:T(8,128)(2,1)S(1)}, bf16[2,4,56,384]{3,2,1,0:T(8,128)(2,1)S(1)}, u32[]{:S(2)}, u32[]{:S(2)}) collective-permute-start(bf16[2,4,56,384]{3,2,1,0:T(8,128)(2,1)S(1)} %pad_maximum_fusion.3.refs_2_), channel_id=1, source_target_pairs={{0,1},{1,0},{2,3},{3,2},{4,5},{5,4},{6,7},{7,6},{8,9},{9,8},{10,11... | collective-permute-start | bytes 1032200 | tf_op jit(solution)/shard_map/ppermute | solution.py:72
  137.7 17.3 %collective-permute-start.31 = (bf16[2,4,56,384]{3,2,1,0:T(8,128)(2,1)S(1)}, bf16[2,4,56,384]{3,2,1,0:T(8,128)(2,1)S(1)}, u32[]{:S(2)}, u32[]{:S(2)}) collective-permute-start(bf16[2,4,56,384]{3,2,1,0:T(8,128)(2,1)S(1)} %pad_maximum_fusion.4.refs_0_), channel_id=1, source_target_pairs={{0,2},{1,3},{2,0},{3,1},{4,6},{5,7},{6,4},{7,5},{8,10},{9,11},{10,... | collective-permute-start | bytes 1032200 | tf_op jit(solution)/shard_map/ppermute | solution.py:72
  138.9 11.5 %collective-permute-start.13 = (bf16[6,2,16,320]{3,2,1,0:T(8,128)(2,1)S(1)}, bf16[6,2,16,320]{3,2,1,0:T(8,128)(2,1)S(1)}, u32[]{:S(2)}, u32[]{:S(2)}) collective-permute-start(bf16[6,2,16,320]{3,2,1,0:T(8,128)(2,1)S(1)} %copy-done.32), channel_id=1, source_target_pairs={{0,3},{1,2},{2,1},{3,0},{4,7},{5,6},{6,5},{7,4},{8,11},{9,10},{10,... | collective-permute-start | bytes 368648 | tf_op jit(solution)/shard_map/ppermute | solution.py:72
  140.1 12.8 %collective-permute-start.1 = (bf16[2,320,128]{2,1,0:T(8,128)(2,1)}, bf16[2,320,128]{2,1,0:T(8,128)(2,1)S(1)}, u32[]{:S(2)}, u32[]{:S(2)}) collective-permute-start(bf16[2,320,128]{2,1,0:T(8,128)(2,1)} %get-tuple-element.54), channel_id=1, source_target_pairs={{4,0},{8,4},{12,8},{16,12},{20,16},{24,20},{28,24},{5,1},{9,5},{13... | collective-permute-start | bytes 491528 | tf_op jit(solution)/shard_map/ppermute | solution.py:548
  153.0 17.0 %collective-permute-start.29 = (bf16[2,4,56,384]{3,2,1,0:T(8,128)(2,1)S(1)}, bf16[2,4,56,384]{3,2,1,0:T(8,128)(2,1)S(1)}, u32[]{:S(2)}, u32[]{:S(2)}) collective-permute-start(bf16[2,4,56,384]{3,2,1,0:T(8,128)(2,1)S(1)} %collective-permute-done.28.refs_3_), channel_id=1, source_target_pairs={{0,4},{4,0},{8,12},{12,8},{16,20},{20,16},{24,28},{28,24},{1,5},{5... | collective-permute-start | bytes 1032200 | tf_op jit(solution)/shard_map/ppermute | solution.py:72
  154.5 15.5 %collective-permute-start.32 = (bf16[2,4,56,384]{3,2,1,0:T(8,128)(2,1)S(1)}, bf16[2,4,56,384]{3,2,1,0:T(8,128)(2,1)S(1)}, u32[]{:S(2)}, u32[]{:S(2)}) collective-permute-start(bf16[2,4,56,384]{3,2,1,0:T(8,128)(2,1)S(1)} %pad_maximum_fusion.4.refs_0_), channel_id=1, source_target_pairs={{0,4},{4,0},{8,12},{12,8},{16,20},{20,16},{24,28},{28,24},{1,5},{5... | collective-permute-start | bytes 1032200 | tf_op jit(solution)/shard_map/ppermute | solution.py:72
  154.7 15.4 %collective-permute-start.34 = (bf16[2,4,56,384]{3,2,1,0:T(8,128)(2,1)S(1)}, bf16[2,4,56,384]{3,2,1,0:T(8,128)(2,1)S(1)}, u32[]{:S(2)}, u32[]{:S(2)}) collective-permute-start(bf16[2,4,56,384]{3,2,1,0:T(8,128)(2,1)S(1)} %pad_maximum_fusion.3.refs_2_), channel_id=1, source_target_pairs={{0,4},{4,0},{8,12},{12,8},{16,20},{20,16},{24,28},{28,24},{1,5},{5... | collective-permute-start | bytes 1032200 | tf_op jit(solution)/shard_map/ppermute | solution.py:72
  155.0 15.0 %collective-permute-start.33 = (bf16[2,4,56,384]{3,2,1,0:T(8,128)(2,1)S(1)}, bf16[2,4,56,384]{3,2,1,0:T(8,128)(2,1)S(1)}, u32[]{:S(2)}, u32[]{:S(2)}) collective-permute-start(bf16[2,4,56,384]{3,2,1,0:T(8,128)(2,1)S(1)} %collective-permute-done.31.refs_1_), channel_id=1, source_target_pairs={{0,4},{4,0},{8,12},{12,8},{16,20},{20,16},{24,28},{28,24},{1,5},{5... | collective-permute-start | bytes 1032200 | tf_op jit(solution)/shard_map/ppermute | solution.py:72
  (46 other events, 368.0 us)
